TPU v7x, 32 devices: a whole 2x2x4 slice. The times are simulated.
32 devices in a mesh: seq: 16 (over z, y, x), head: 2 (over core).
Axes of the slice: x: 2, y: 2, z: 4, core: 2. Of those that a mesh axis runs over, the one named last changes fastest.
Arguments:
- block_input: bfloat16 [8192, 768], P('seq', 'head'), may hold values from -6 to 6
- starts: int32 [8192], P('seq'), may hold values from 0 to 1, as said below
- decay_rate: float32 [12, 8192], P('head', 'seq'), may hold values from 0 to 1
- norm1_gain: float32 [768], replicated, may hold values from 0.5 to 1.5
- norm1_bias: float32 [768], replicated, may hold values from -1.5 to 1.5
- q_weight: bfloat16 [768, 768], P(None, 'head'), may hold values from -0.21875 to 0.21875
- k_weight: bfloat16 [768, 768], P(None, 'head'), may hold values from -0.21875 to 0.21875
- v_weight: bfloat16 [768, 768], P(None, 'head'), may hold values from -0.21875 to 0.21875
- shift_kernel: bfloat16 [64, 768], P(None, 'head'), may hold values from -0.75 to 0.75
- out_weight: bfloat16 [768, 768], P(None, 'head'), may hold values from -0.3125 to 0.3125
- norm2_gain: float32 [768], replicated, may hold values from 0.5 to 1.5
- norm2_bias: float32 [768], replicated, may hold values from -1.5 to 1.5
- up_weight: bfloat16 [768, 3072], P(None, 'head'), may hold values from -0.21875 to 0.21875
- down_weight: bfloat16 [768, 3072], P(None, 'head'), may hold values from -0.109375 to 0.109375
- out_grad: bfloat16 [8192, 768], P('seq', 'head'), may hold values from -6 to 6
Outputs:
- block_output: bfloat16 [8192, 768], P('seq', 'head')
- input_grad: bfloat16 [8192, 768], P('seq', 'head')
- norm1_gain_grad: float32 [768], replicated
- norm1_bias_grad: float32 [768], replicated
- q_weight_grad: float32 [768, 768], P('seq', 'head')
- k_weight_grad: float32 [768, 768], P('seq', 'head')
- v_weight_grad: float32 [768, 768], P('seq', 'head')
- shift_kernel_grad: float32 [64, 768], P(None, 'head')
- out_weight_grad: float32 [768, 768], P('seq', 'head')
- norm2_gain_grad: float32 [768], replicated
- norm2_bias_grad: float32 [768], replicated
- up_weight_grad: float32 [768, 3072], P('seq', 'head')
- down_weight_grad: float32 [768, 3072], P('seq', 'head')
Inputs may be any that keep to these rules, and one draw needn't show every extreme that they name: `starts`: the first token is 1.
All inputs are finite; a program needn't handle non-finite values.
Results may differ from a plain program's by a relative error of at most 0.017.
Values may be sent and summed in bfloat16 or wider, within the bound.
No kernel may reach another device: no remote copies, remote signals or barrier semaphores. Data moves between devices by JAX's collectives and lax.ppermute only.
A program may use at most 192 MiB of HBM per device.

v0:
```python
import jax
import jax.numpy as jnp
from jax import lax
from jax.sharding import PartitionSpec as P

NORM_EPS = 1e-05
RATE_CAP = 0.05
FAR_BACK = 1 << 20
HIGHEST = lax.Precision.HIGHEST


def passed_along(array, axis, by):
    count = lax.axis_size(axis)
    pairs = [(i, i + by) for i in range(count) if 0 <= i + by < count]
    return lax.ppermute(array, axis, pairs)


def entering(array, axis, combine, identity, reverse):
    count, mine = (lax.axis_size(axis), lax.axis_index(axis))
    everything = jax.tree.map(
        lambda part, kind: lax.all_gather(part.astype(kind), axis),
        array,
        (jnp.bfloat16, jnp.bfloat16),
    )
    start = jax.tree.map(
        lambda part, zero: jnp.broadcast_to(jnp.asarray(zero, part.dtype), part.shape),
        array,
        identity,
    )

    def lap(k, before):
        at = count - 1 - k if reverse else k
        reached = at > mine if reverse else at < mine
        new = combine(
            before, jax.tree.map(lambda part, own: part[at].astype(own.dtype), everything, array)
        )
        return jax.tree.map(lambda a, b: jnp.where(reached, a, b), new, before)

    return lax.fori_loop(0, count, lap, start)


def as_sent(array):
    return jax.tree.map(lambda a: a.astype(jnp.bfloat16) if a.dtype == jnp.float32 else a, array)


def norm_forward(rows_in, gain_vec, bias_vec):
    center = rows_in - jnp.mean(rows_in, axis=-1, keepdims=True)
    inverse = lax.rsqrt(jnp.mean(center * center, axis=-1, keepdims=True) + NORM_EPS)
    unit_rows = center * inverse
    return (unit_rows * gain_vec + bias_vec, unit_rows, inverse)


def norm_backward(grad_rows, unit_rows, inverse, gain_vec):
    scaled = grad_rows * gain_vec
    return inverse * (
        scaled
        - jnp.mean(scaled, axis=-1, keepdims=True)
        - unit_rows * jnp.mean(scaled * unit_rows, axis=-1, keepdims=True)
    )


def gelu_tanh(pre_act):
    return jax.nn.gelu(pre_act, approximate=True)


def chain(earlier_part, later_part):
    return (
        earlier_part[0] * later_part[0],
        later_part[0][:, None, None] * earlier_part[1] + later_part[1],
    )


def local(
    block_input,
    starts,
    decay_rate,
    norm1_gain,
    norm1_bias,
    q_weight,
    k_weight,
    v_weight,
    shift_kernel,
    out_weight,
    norm2_gain,
    norm2_bias,
    up_weight,
    down_weight,
    out_grad,
):
    tok_rows, half_width = block_input.shape
    head_count = decay_rate.shape[0]
    head_width = half_width // head_count
    tap_count = shift_kernel.shape[0]
    edge_rows = tap_count - 1
    block_len = 512
    block_count = tok_rows // block_len
    head_size = lax.axis_size("head")
    head_index = lax.axis_index("head")
    full_width = half_width * head_size
    own_start = head_index * half_width
    row_count = tok_rows // head_size
    row_start = head_index * row_count
    position = jnp.arange(tok_rows, dtype=jnp.int32)
    last_start = lax.cummax(jnp.where(starts > 0, position, -FAR_BACK), axis=0)
    distance = position - last_start
    tail_mask = (position[tok_rows - edge_rows :] >= last_start[tok_rows - 1]).astype(jnp.float32)[
        :, None
    ]
    whole_input, whole_grad = (
        lax.all_gather(block_input, "head", axis=1, tiled=True),
        lax.all_gather(out_grad, "head", axis=1, tiled=True),
    )
    normed_one, unit_one, inverse_one = norm_forward(
        whole_input.astype(jnp.float32), norm1_gain, norm1_bias
    )
    normed_one = normed_one.astype(jnp.bfloat16)
    query_rows = jnp.dot(normed_one, q_weight, preferred_element_type=jnp.float32).astype(
        jnp.bfloat16
    )
    key_rows = jnp.dot(normed_one, k_weight, preferred_element_type=jnp.float32).astype(
        jnp.bfloat16
    )
    value_rows = jnp.dot(normed_one, v_weight, preferred_element_type=jnp.float32).astype(
        jnp.bfloat16
    )
    tail_send = (key_rows[tok_rows - edge_rows :] * tail_mask).astype(jnp.bfloat16)
    prev_tail = passed_along(tail_send, "seq", 1)
    padded = jnp.concatenate([prev_tail, key_rows], axis=0)
    kernel = shift_kernel.astype(jnp.float32)
    shifted = jnp.zeros((tok_rows, half_width), jnp.float32)
    for tap_index in range(tap_count):
        keep_mask = (distance >= tap_index).astype(jnp.float32)[:, None]
        shifted = shifted + keep_mask * kernel[tap_index][None, :] * padded[
            edge_rows - tap_index : edge_rows - tap_index + tok_rows
        ].astype(jnp.float32)
    gain_in = jnp.sqrt(-jnp.expm1(-2.0 * jnp.minimum(decay_rate, RATE_CAP)))
    scaled_key = (shifted.reshape(tok_rows, head_count, head_width) * gain_in.T[:, :, None]).astype(
        jnp.bfloat16
    )
    query_blocks = query_rows.reshape(block_count, block_len, head_count, head_width)
    key_blocks = scaled_key.reshape(block_count, block_len, head_count, head_width)
    value_blocks = value_rows.reshape(block_count, block_len, head_count, head_width)
    cumulative = jnp.cumsum(
        decay_rate.reshape(head_count, block_count, block_len).transpose(1, 0, 2), axis=-1
    )
    doc_index = jnp.cumsum(starts.reshape(block_count, block_len), axis=1, dtype=jnp.int32)
    place_rows = jnp.arange(block_len, dtype=jnp.int32)
    same_doc = (doc_index[:, :, None] == doc_index[:, None, :]) & (
        place_rows[:, None] >= place_rows[None, :]
    )[None]
    decay_mat = jnp.where(
        same_doc[:, None],
        jnp.exp(jnp.minimum(cumulative[:, :, None, :] - cumulative[:, :, :, None], 0.0)),
        0.0,
    )
    first_w = jnp.where(doc_index[:, None, :] == 0, jnp.exp(-cumulative), 0.0)
    last_w = jnp.where(
        doc_index[:, None, :] == doc_index[:, None, -1:],
        jnp.exp(cumulative - cumulative[:, :, -1:]),
        0.0,
    )
    block_gate = jnp.where(doc_index[:, -1:] == 0, jnp.exp(-cumulative[:, :, -1]), 0.0)
    first_rows = first_w.transpose(0, 2, 1)[..., None]
    last_rows = last_w.transpose(0, 2, 1)[..., None]
    scores = jnp.einsum(
        "bthd,bshd->bhts", query_blocks, key_blocks, preferred_element_type=jnp.float32
    )
    weights_low = (scores * decay_mat).astype(jnp.bfloat16)
    inside = jnp.einsum(
        "bhts,bshd->bthd", weights_low, value_blocks, preferred_element_type=jnp.float32
    )
    value_float = value_blocks.astype(jnp.float32)
    weighted_key = key_blocks.astype(jnp.float32) * last_rows
    block_state = jnp.einsum("bshd,bshe->bhde", weighted_key, value_float, precision=HIGHEST)
    carried = jnp.zeros((head_count, head_width, head_width), jnp.float32)
    through = jnp.ones((head_count,), jnp.float32)
    block_index = 0
    local_inits = [carried]
    pass_factors = [through]
    carried = block_gate[block_index][:, None, None] * carried + block_state[block_index]
    through = through * block_gate[block_index]
    identity = (
        jnp.ones((head_count,), jnp.float32),
        jnp.zeros((head_count, head_width, head_width), jnp.float32),
    )
    prefix_gate, incoming = entering((through, carried), "seq", chain, identity, False)
    pass_stack = jnp.stack(pass_factors)[:, :, None, None]
    block_init = jnp.stack(local_inits) + pass_stack * incoming[None]
    query_float = query_blocks.astype(jnp.float32)
    from_state = jnp.einsum("bthd,bhde->bthe", query_float, block_init, precision=HIGHEST)
    mixed_rows = (
        (0.125 * (inside + first_rows * from_state))
        .reshape(tok_rows, half_width)
        .astype(jnp.bfloat16)
    )
    attn_part = jnp.einsum("th,dh->td", mixed_rows, out_weight, preferred_element_type=jnp.float32)
    attn_own = lax.psum_scatter(
        attn_part.astype(jnp.bfloat16), "head", scatter_dimension=1, tiled=True
    ).astype(jnp.float32)
    residual = block_input.astype(jnp.float32) + attn_own
    whole_resid = lax.all_gather(residual.astype(jnp.bfloat16), "head", axis=1, tiled=True).astype(
        residual.dtype
    )
    normed_two, unit_two, inverse_two = norm_forward(whole_resid, norm2_gain, norm2_bias)
    normed_two = normed_two.astype(jnp.bfloat16)
    pre_act = jnp.dot(normed_two, up_weight, preferred_element_type=jnp.float32)
    hidden = gelu_tanh(pre_act).astype(jnp.bfloat16)
    ffn_part = jnp.einsum("tf,df->td", hidden, down_weight, preferred_element_type=jnp.float32)
    ffn_own = lax.psum_scatter(
        ffn_part.astype(jnp.bfloat16), "head", scatter_dimension=1, tiled=True
    ).astype(jnp.float32)
    block_output = (residual + ffn_own).astype(jnp.bfloat16)
    hidden_grad = jnp.dot(whole_grad, down_weight, preferred_element_type=jnp.float32)
    gelu_value, gelu_pull = jax.vjp(gelu_tanh, pre_act)
    pre_grad = gelu_pull(hidden_grad)[0].astype(jnp.bfloat16)
    down_grad = jnp.einsum("td,tf->df", whole_grad, hidden, preferred_element_type=jnp.float32)
    up_grad = jnp.einsum("td,tf->df", normed_two, pre_grad, preferred_element_type=jnp.float32)
    ffn_total = (
        lax.psum_scatter(up_grad, "seq", scatter_dimension=0, tiled=True),
        lax.psum_scatter(down_grad, "seq", scatter_dimension=0, tiled=True),
    )
    norm2_part = jnp.einsum("tf,df->td", pre_grad, up_weight, preferred_element_type=jnp.float32)
    norm2_full = lax.psum(norm2_part.astype(jnp.bfloat16), "head").astype(jnp.float32)
    norm2_half = lax.dynamic_slice_in_dim(norm2_full, row_start, row_count, axis=0)
    unit_half = lax.dynamic_slice_in_dim(unit_two, row_start, row_count, axis=0)
    gain2_grad = jnp.sum(norm2_half * unit_half, axis=0)
    bias2_grad = jnp.sum(norm2_half, axis=0)
    resid_back = norm_backward(norm2_full, unit_two, inverse_two, norm2_gain)
    resid_grad = out_grad.astype(jnp.float32) + lax.dynamic_slice_in_dim(
        resid_back, own_start, half_width, axis=1
    )
    branch_grad = resid_grad.astype(jnp.bfloat16)
    whole_branch = lax.all_gather(branch_grad, "head", axis=1, tiled=True)
    mixed_grad = jnp.dot(whole_branch, out_weight, preferred_element_type=jnp.float32).astype(
        jnp.bfloat16
    )
    out_w_grad = jnp.einsum(
        "td,th->dh", whole_branch, mixed_rows, preferred_element_type=jnp.float32
    )
    grad_low = (mixed_grad * 0.125).reshape(block_count, block_len, head_count, head_width)
    grad_float = grad_low.astype(jnp.float32)
    prob_grad = jnp.einsum(
        "bthd,bshd->bhts", grad_low, value_blocks, preferred_element_type=jnp.float32
    )
    score_grad = (prob_grad * decay_mat).astype(jnp.bfloat16)
    value_grad = jnp.einsum(
        "bhts,bthd->bshd", weights_low, grad_low, preferred_element_type=jnp.float32
    )
    query_grad = jnp.einsum(
        "bhts,bshd->bthd", score_grad, key_blocks, preferred_element_type=jnp.float32
    )
    key_scaled_grad = jnp.einsum(
        "bhts,bthd->bshd", score_grad, query_blocks, preferred_element_type=jnp.float32
    )
    query_grad = query_grad + first_rows * jnp.einsum(
        "bthe,bhde->bthd", grad_float, block_init, precision=HIGHEST
    )
    init_grad = jnp.einsum(
        "bthd,bthe->bhde", query_float * first_rows, grad_float, precision=HIGHEST
    )
    local_sum = jnp.sum(pass_stack * init_grad, axis=0)
    later_gate, later_grad = entering((through, local_sum), "seq", chain, identity, True)
    running = later_grad
    state_grad_list = [running] * block_count
    for block_index in reversed(range(block_count)):
        state_grad_list[block_index] = running
        running = block_gate[block_index][:, None, None] * running + init_grad[block_index]
    state_grad = jnp.stack(state_grad_list)
    key_scaled_grad = key_scaled_grad + last_rows * jnp.einsum(
        "bhde,bshe->bshd", state_grad, value_float, precision=HIGHEST
    )
    value_grad = value_grad + jnp.einsum(
        "bhde,bshd->bshe", state_grad, weighted_key, precision=HIGHEST
    )
    query_grad_low = query_grad.reshape(tok_rows, half_width).astype(jnp.bfloat16)
    value_grad_low = value_grad.reshape(tok_rows, half_width).astype(jnp.bfloat16)
    shifted_grad = (
        key_scaled_grad.reshape(tok_rows, head_count, head_width) * gain_in.T[:, :, None]
    ).reshape(tok_rows, half_width)
    grad_wide = jnp.pad(shifted_grad, ((edge_rows, edge_rows), (0, 0)))
    distance_wide = jnp.pad(distance, (edge_rows, edge_rows), constant_values=-1)
    span_rows = tok_rows + edge_rows
    padded_grad = jnp.zeros((span_rows, half_width), jnp.float32)
    for tap_index in range(tap_count):
        tap_mask = (distance_wide[tap_index : tap_index + span_rows] >= tap_index)[:, None]
        padded_grad = padded_grad + kernel[tap_index][None, :] * jnp.where(
            tap_mask, grad_wide[tap_index : tap_index + span_rows], 0.0
        )
    kernel_rows = []
    for tap_index in range(tap_count):
        keep_mask = (distance >= tap_index)[:, None]
        kernel_rows.append(
            jnp.sum(
                jnp.where(
                    keep_mask,
                    shifted_grad
                    * padded[edge_rows - tap_index : edge_rows - tap_index + tok_rows].astype(
                        jnp.float32
                    ),
                    0.0,
                ),
                axis=0,
            )
        )
    kernel_grad = jnp.stack(kernel_rows)
    back_edge = passed_along(as_sent(padded_grad[:edge_rows]), "seq", -1)
    key_grad = padded_grad[edge_rows:].at[tok_rows - edge_rows :].add(back_edge * tail_mask)
    key_grad_low = key_grad.astype(jnp.bfloat16)
    q_grad = jnp.einsum("td,th->dh", normed_one, query_grad_low, preferred_element_type=jnp.float32)
    k_grad = jnp.einsum("td,th->dh", normed_one, key_grad_low, preferred_element_type=jnp.float32)
    v_grad = jnp.einsum("td,th->dh", normed_one, value_grad_low, preferred_element_type=jnp.float32)
    norm1_part = jnp.einsum(
        "th,dh->td", query_grad_low, q_weight, preferred_element_type=jnp.float32
    )
    norm1_part = norm1_part + jnp.einsum(
        "th,dh->td", key_grad_low, k_weight, preferred_element_type=jnp.float32
    )
    norm1_part = norm1_part + jnp.einsum(
        "th,dh->td", value_grad_low, v_weight, preferred_element_type=jnp.float32
    )
    norm1_full = lax.psum(norm1_part.astype(jnp.bfloat16), "head").astype(jnp.float32)
    norm1_half = lax.dynamic_slice_in_dim(norm1_full, row_start, row_count, axis=0)
    unit_one_half = lax.dynamic_slice_in_dim(unit_one, row_start, row_count, axis=0)
    gain1_grad = jnp.sum(norm1_half * unit_one_half, axis=0)
    bias1_grad = jnp.sum(norm1_half, axis=0)
    input_back = norm_backward(norm1_full, unit_one, inverse_one, norm1_gain)
    input_grad = (
        resid_grad + lax.dynamic_slice_in_dim(input_back, own_start, half_width, axis=1)
    ).astype(jnp.bfloat16)
    kernel_full = lax.dynamic_update_slice_in_dim(
        jnp.zeros((tap_count, full_width), jnp.float32), kernel_grad, own_start, axis=1
    )
    small_total = lax.psum(
        (kernel_full, gain1_grad, bias1_grad, gain2_grad, bias2_grad), ("seq", "head")
    )
    kernel_total = lax.dynamic_slice_in_dim(small_total[0], own_start, half_width, axis=1)
    mixer_total = (
        lax.psum_scatter(q_grad, "seq", scatter_dimension=0, tiled=True),
        lax.psum_scatter(k_grad, "seq", scatter_dimension=0, tiled=True),
        lax.psum_scatter(v_grad, "seq", scatter_dimension=0, tiled=True),
        lax.psum_scatter(out_w_grad, "seq", scatter_dimension=0, tiled=True),
    )
    return (
        block_output,
        input_grad,
        small_total[1],
        small_total[2],
        mixer_total[0],
        mixer_total[1],
        mixer_total[2],
        kernel_total,
        mixer_total[3],
        small_total[3],
        small_total[4],
        ffn_total[0],
        ffn_total[1],
    )


def solution(mesh):
    in_specs = (
        P("seq", "head"),
        P("seq"),
        P("head", "seq"),
        P(),
        P(),
        P(None, "head"),
        P(None, "head"),
        P(None, "head"),
        P(None, "head"),
        P(None, "head"),
        P(),
        P(),
        P(None, "head"),
        P(None, "head"),
        P("seq", "head"),
    )
    out_specs = (
        P("seq", "head"),
        P("seq", "head"),
        P(),
        P(),
        P("seq", "head"),
        P("seq", "head"),
        P("seq", "head"),
        P(None, "head"),
        P("seq", "head"),
        P(),
        P(),
        P("seq", "head"),
        P("seq", "head"),
    )
    return jax.shard_map(local, mesh=mesh, in_specs=in_specs, out_specs=out_specs, check_vma=False)
```

profile of v0, /device:TPU:0, one launch (start us, length us, event | category | flops | bytes accessed | tf_op | source)
XLA Modules:
  0.0 1358.3 jit_solution(6649271378398197888)
XLA Ops:
  9.3 2.6 all_gather.26
  16.4 5.4 collective-permute-start
  28.9 3.2 reduce-window.29
  41.6 1.8 select_bitcast_fusion.1
  45.9 2.6 convolution_convert_fusion.5
  55.3 38.5 %all-gather = bf16[16,6,1]{1,2,0:T(2,128)(2,1)S(1)} all-gather(bf16[1,6,1]{1,2,0:T(2,128)(2,1)} %get-tuple-element.706), channel_id=2, replica_groups=mesh['seq'=16,'head'=2] {'seq'}, dimensions={0}, use_global_device_ids=true | all-gather | bytes 204 | tf_op jit(solution)/shard_map/all_gather | solution.py:21
  95.5 20.1 %fusion.384 = f32[512,384]{1,0:T(8,128)} fusion(bf16[512,384]{1,0:T(8,128)(2,1)S(1)} %convolution_convert_fusion.4, bf16[63,384]{1,0:T(8,128)(2,1)} %collective-permute-done, f32[384]{0:T(512)} %get-tuple-element.477, f32[512]{0:T(512)} %get-tuple-element.895, f32[384]{0:T(512)} %get-tuple-element.478, f32[512]{0:T(512)} %get-tuple-element.893, ...), kind=kLoop, calls=%fused_computation.676 | loop fusion | flops 87293952 | bytes 1457408 | tf_op jit(solution)/shard_map/add | solution.py:133
  115.7 2.3 copy.80
  121.5 49.9 %all-gather.1 = bf16[96,64,64]{2,1,0:T(8,128)(2,1)} all-gather(bf16[6,64,64]{2,1,0:T(8,128)(2,1)S(1)} %fusion.27), channel_id=3, replica_groups=mesh['seq'=16,'head'=2] {'seq'}, dimensions={0}, use_global_device_ids=true | all-gather | bytes 835584 | tf_op jit(solution)/shard_map/all_gather | solution.py:21
  171.4 47.0 %while.31 = (s32[]{:T(128)}, f32[6,64,64]{2,1,0:T(8,128)}, s32[]{:T(128)}, bf16[16,6]{1,0:T(8,128)(2,1)}, bf16[16,6,64,64]{3,2,1,0:T(8,128)(2,1)}, /*index=5*/s32[]{:T(128)}, s32[]{:T(128)}) while((s32[]{:T(128)}, f32[6,64,64]{2,1,0:T(8,128)}, s32[]{:T(128)}, bf16[16,6]{1,0:T(8,128)(2,1)}, bf16[16,6,64,64]{3,2,1,0:T(8,128)(2,1)}, ...), condition=%wide.region_9.10_spmd.clone, body=%wide.region_8.9_spmd.clone.sunk | while | flops 122890 | bytes 245925 | solution.py:39
  187.2 1.7 fusion.690
  190.2 1.7 fusion.690
  204.9 1.7 fusion.690
  218.4 3.3 multiply_convert_fusion.1
  225.8 2.3 copy.100
  228.2 2.6 all_gather.30
  231.7 4.7 fusion.628
  236.4 2.0 copy.101
  239.7 2.4 all_gather.29
  242.7 4.5 fusion.8
  248.4 2.3 convolution_convert_fusion
  255.8 13.1 all-reduce.7.cloned.1.call-done
  268.9 1.8 fusion.485
  272.0 2.5 all_gather.31
  276.0 3.3 multiply_convert_fusion
  279.3 53.8 %all-gather.2 = bf16[96,64,64]{2,1,0:T(8,128)(2,1)} all-gather(bf16[6,64,64]{2,1,0:T(8,128)(2,1)S(1)} %convolution_convert_fusion.7), channel_id=4, replica_groups=mesh['seq'=16,'head'=2] {'seq'}, dimensions={0}, use_global_device_ids=true | all-gather | bytes 835584 | tf_op jit(solution)/shard_map/all_gather | solution.py:21
  333.1 27.3 %while.32 = (s32[]{:T(128)}, f32[6,64,64]{2,1,0:T(8,128)S(1)}, s32[]{:T(128)}, bf16[16,6]{1,0:T(8,128)(2,1)}, bf16[16,6,64,64]{3,2,1,0:T(8,128)(2,1)}, /*index=5*/s32[]{:T(128)}, s32[]{:T(128)}, s32[]{:T(128)}, s32[]{:T(128)}) while((s32[]{:T(128)}, f32[6,64,64]{2,1,0:T(8,128)S(1)}, s32[]{:T(128)}, bf16[16,6]{1,0:T(8,128)(2,1)}, ...), condition=%wide.region_18.19_spmd.clone, body=%wide.region_17.18_spmd.clone.sunk | while | flops 122894 | bytes 245987 | solution.py:39
  360.9 3.4 fusion.16
  364.3 2.3 copy.91
  366.7 2.3 fusion.402
  369.1 2.1 fusion.410
  376.9 1.8 fusion.284
  378.8 1.8 fusion.292
  380.7 1.8 fusion.325
  382.6 1.8 fusion.333
  384.5 1.9 fusion.341
  386.5 1.9 fusion.349
  388.5 1.9 fusion.357
  390.5 1.9 fusion.365
  392.5 1.9 fusion.386
  394.5 1.9 fusion.394
  399.3 5.5 convolution_convert_fusion.1
  404.8 2.4 copy.102
  408.6 2.6 fusion.25
  411.5 17.0 %fusion.183 = f32[575,384]{1,0:T(8,128)} fusion(f32[512,384]{1,0:T(8,128)S(1)} %get-tuple-element.564, f32[384]{0:T(512)S(1)} %copy-done.54, f32[384]{0:T(512)S(1)} %copy-done.55, f32[384]{0:T(512)S(1)} %copy-done.56, f32[384]{0:T(512)S(1)} %copy-done.57, f32[384]{0:T(512)S(1)} %copy-done.58, f32[384]{0:T(512)S(1)} %copy-done.59, f32[384]{0:T(512)S(1)} %copy-done.60, ...), kind=kLoop, calls=%fused_computation.475 | loop fusion | flops 42172800 | bytes 1804736 | tf_op jit(solution)/shard_map/add | solution.py:286
  431.3 3.1 fusion.24
  434.5 1.8 fusion.629
  438.4 2.7 add_convert_fusion
  442.9 2.8 fusion.632
  449.5 5.1 fusion.488
  455.8 5.8 convolution_bitcast_fusion
  461.6 6.1 copy.104
  469.5 49.5 %all-reduce.11.cloned.1.call-done = f32[64,768]{1,0:T(8,128)} async-done(((f32[64,768]{1,0:T(8,128)}), f32[64,768]{1,0:T(8,128)}) %all-reduce.11.cloned.1.call-update) | async-done | bytes 196624 | tf_op jit(solution)/shard_map/psum | solution.py:333
  520.6 9.8 reduce-scatter.27.cloned.1.call-done
  532.5 20.6 %all-reduce.9.cloned.1.call-done = bf16[512,768]{1,0:T(8,128)(2,1)} async-done(((bf16[512,768]{1,0:T(8,128)(2,1)}), bf16[512,768]{1,0:T(8,128)(2,1)}) %all-reduce.9.cloned.1.call-update) | async-done | bytes 786448 | tf_op jit(solution)/shard_map/psum | solution.py:321
  554.4 2.6 fusion.483
  558.2 41.0 %all-reduce.2 = (f32[768]{0:T(1024)}, f32[768]{0:T(1024)}, f32[768]{0:T(1024)}, f32[768]{0:T(1024)}) all-reduce(f32[768]{0:T(1024)S(1)} %get-tuple-element.407, f32[768]{0:T(1024)S(1)} %get-tuple-element.406, f32[768]{0:T(1024)S(1)} %get-tuple-element.405, ...), channel_id=1, replica_groups=mesh['seq'=16,'head'=2] {'seq','head'}, use_global_device_ids=true, to_apply=%region_23.24 | all-reduce | flops 3072 | bytes 24576 | tf_op jit(solution)/shard_map/psum | solution.py:333
  599.2 2.7 fusion.414
  601.9 81.2 %reduce-scatter.19.cloned.1.call-done = f32[48,384]{1,0:T(8,128)} async-done(((f32[768,384]{1,0:T(8,128)}), f32[48,384]{1,0:T(8,128)}) %reduce-scatter.19.cloned.1.call-update) | async-done | bytes 73744 | tf_op jit(solution)/shard_map/reduce_scatter | solution.py:340
  683.1 128.0 %reduce-scatter.21.cloned.1.call-done = f32[48,384]{1,0:T(8,128)} async-done(((f32[768,384]{1,0:T(8,128)}), f32[48,384]{1,0:T(8,128)}) %reduce-scatter.21.cloned.1.call-update) | async-done | bytes 73744 | tf_op jit(solution)/shard_map/reduce_scatter | solution.py:341
  811.1 127.9 %reduce-scatter.15.cloned.1.call-done = f32[48,384]{1,0:T(8,128)} async-done(((f32[768,384]{1,0:T(8,128)}), f32[48,384]{1,0:T(8,128)}) %reduce-scatter.15.cloned.1.call-update) | async-done | bytes 73744 | tf_op jit(solution)/shard_map/reduce_scatter | solution.py:338
  939.0 128.0 %reduce-scatter.17.cloned.1.call-done = f32[48,384]{1,0:T(8,128)} async-done(((f32[768,384]{1,0:T(8,128)}), f32[48,384]{1,0:T(8,128)}) %reduce-scatter.17.cloned.1.call-update) | async-done | bytes 73744 | tf_op jit(solution)/shard_map/reduce_scatter | solution.py:339
  1067.1 141.6 %reduce-scatter.23.cloned.1.call-done = f32[48,1536]{1,0:T(8,128)} async-done(((f32[768,1536]{1,0:T(8,128)}), f32[48,1536]{1,0:T(8,128)}) %reduce-scatter.23.cloned.1.call-update) | async-done | bytes 294928 | tf_op jit(solution)/shard_map/reduce_scatter | solution.py:219
  1208.7 142.6 %reduce-scatter.29.cloned.1.call-done = f32[48,1536]{1,0:T(8,128)} async-done(((f32[768,1536]{1,0:T(8,128)}), f32[48,1536]{1,0:T(8,128)}) %reduce-scatter.29.cloned.1.call-update) | async-done | bytes 294928
  (599 shorter events, 149.9 us)
Async XLA Ops:
  7.2 235.5 %copy-start = (bf16[768,1536]{1,0:T(8,128)(2,1)S(1)}, bf16[768,1536]{1,0:T(8,128)(2,1)}, u32[]{:S(2)}) copy-start(bf16[768,1536]{1,0:T(8,128)(2,1)} %param.33) | copy-start | bytes 7077892
  7.2 229.2 %reduce-scatter.25.cloned.1.call-start = ((), (), s32[]{:S(2)}) async-start(), calls=%async_computation.16 | async-start | bytes 1179648
  12.1 10.8 copy-start.48
  12.1 12.9 copy-start.46
  16.4 79.1 %collective-permute-start = (bf16[63,384]{1,0:T(8,128)(2,1)}, bf16[63,384]{1,0:T(8,128)(2,1)}, u32[]{:S(2)}, u32[]{:S(2)}) collective-permute-start(bf16[63,384]{1,0:T(8,128)(2,1)} %multiply_convert_fusion.4), channel_id=1, source_target_pairs={{0,2},{2,4},{4,6},{6,8},{8,10},{10,12},{12,14},{14,16},{16,18},{18... | collective-permute-start | bytes 145160 | tf_op jit(solution)/shard_map/ppermute | solution.py:15
  39.0 10.4 copy-start.98
  39.0 11.0 copy-start.4
  39.0 11.0 copy-start.37
  228.1 40.7 %all-reduce.7.cloned.1.call-start = ((), (), s32[]{:S(2)}) async-start(), calls=%async_computation.8 | async-start | bytes 1572864 | tf_op jit(solution)/shard_map/psum | solution.py:223
  250.7 18.2 %copy-start.7 = (bf16[512,768]{1,0:T(8,128)(2,1)S(1)}, bf16[512,768]{1,0:T(8,128)(2,1)}, u32[]{:S(2)}) copy-start(bf16[512,768]{1,0:T(8,128)(2,1)} %copy-done.6) | copy-start | bytes 2359300
  250.7 18.2 %copy-start.91 = (f32[512]{0:T(512)S(1)}, f32[512]{0:T(512)}, u32[]{:S(2)}) copy-start(f32[512]{0:T(512)} %copy-done.90) | copy-start | bytes 6148
  250.7 18.2 %copy-start.94 = (f32[512]{0:T(512)S(1)}, f32[512]{0:T(512)}, u32[]{:S(2)}) copy-start(f32[512]{0:T(512)} %copy-done.93) | copy-start | bytes 6148
  250.7 18.2 %copy-start.102 = (f32[768]{0:T(1024)S(1)}, f32[768]{0:T(1024)}, u32[]{:S(2)}) copy-start(f32[768]{0:T(1024)} %param.31) | copy-start | bytes 9220
  250.7 268.3 %all-reduce.11.cloned.1.call-start = ((), (), s32[]{:S(2)}) async-start(), calls=%async_computation.13 | async-start | bytes 393216 | tf_op jit(solution)/shard_map/psum | solution.py:333
  255.8 15.0 %copy-start.31 = (bf16[512,384]{1,0:T(8,128)(2,1)S(1)}, bf16[512,384]{1,0:T(8,128)(2,1)}, u32[]{:S(2)}) copy-start(bf16[512,384]{1,0:T(8,128)(2,1)} %param.35) | copy-start | bytes 1179652
  279.3 81.1 %copy-start.45 = (f32[1,512,6]{1,2,0:T(8,128)S(1)}, f32[1,512,6]{1,2,0:T(8,128)}, u32[]{:S(2)}) copy-start(f32[1,512,6]{1,2,0:T(8,128)} %copy.87) | copy-start | bytes 36868
  369.0 7.8 copy-start.140
  369.0 7.8 copy-start.141
  369.0 7.8 copy-start.142
  369.1 7.8 copy-start.143
  375.0 7.5 copy-start.128
  375.0 7.5 copy-start.129
  376.8 7.6 copy-start.124
  376.9 7.6 copy-start.125
  376.9 7.6 copy-start.126
  376.9 7.6 copy-start.127
  378.7 7.7 copy-start.120
  378.7 7.7 copy-start.121
  378.8 7.7 copy-start.122
  378.8 7.7 copy-start.123
  380.6 7.8 copy-start.116
  380.6 7.8 copy-start.117
  380.7 7.8 copy-start.118
  380.7 7.8 copy-start.119
  382.6 7.9 copy-start.112
  382.6 7.9 copy-start.113
  382.6 7.9 copy-start.114
  382.6 7.9 copy-start.115
  384.5 7.9 copy-start.108
  384.5 7.9 copy-start.109
  384.5 7.9 copy-start.110
  384.5 7.9 copy-start.111
  386.5 8.0 copy-start.104
  386.5 8.0 copy-start.105
  386.5 8.0 copy-start.106
  386.5 8.0 copy-start.107
  388.5 8.0 copy-start.159
  388.5 8.0 copy-start.160
  388.5 8.0 copy-start.161
  399.1 131.3 %reduce-scatter.27.cloned.1.call-start = ((), (), s32[]{:S(2)}) async-start(), calls=%async_computation.17 | async-start | bytes 1179648
  407.2 145.8 %all-reduce.9.cloned.1.call-start = ((), (), s32[]{:S(2)}) async-start(), calls=%async_computation.9 | async-start | bytes 1572864 | tf_op jit(solution)/shard_map/psum | solution.py:321
  408.6 19.9 %copy-start.9 = (f32[6,64,64]{2,1,0:T(8,128)S(1)}, f32[6,64,64]{2,1,0:T(8,128)}, u32[]{:S(2)}) copy-start(f32[6,64,64]{2,1,0:T(8,128)} %get-tuple-element.251) | copy-start | bytes 294916
  429.9 6.5 collective-permute-start.1
  441.1 242.0 %reduce-scatter.19.cloned.1.call-start = ((), (), s32[]{:S(2)}) async-start(), calls=%async_computation.12 | async-start | bytes 1253376 | tf_op jit(solution)/shard_map/reduce_scatter | solution.py:340
  442.8 368.3 %reduce-scatter.21.cloned.1.call-start = ((), (), s32[]{:S(2)}) async-start(), calls=%async_computation.14 | async-start | bytes 1253376 | tf_op jit(solution)/shard_map/reduce_scatter | solution.py:341
  445.7 493.4 %reduce-scatter.15.cloned.1.call-start = ((), (), s32[]{:S(2)}) async-start(), calls=%async_computation.10 | async-start | bytes 1253376 | tf_op jit(solution)/shard_map/reduce_scatter | solution.py:338
  447.4 619.6 %reduce-scatter.17.cloned.1.call-start = ((), (), s32[]{:S(2)}) async-start(), calls=%async_computation.11 | async-start | bytes 1253376 | tf_op jit(solution)/shard_map/reduce_scatter | solution.py:339
  449.2 759.6 %reduce-scatter.23.cloned.1.call-start = ((), (), s32[]{:S(2)}) async-start(), calls=%async_computation.15 | async-start | bytes 5013504 | tf_op jit(solution)/shard_map/reduce_scatter | solution.py:219
  454.7 896.7 %reduce-scatter.29.cloned.1.call-start = ((), (), s32[]{:S(2)}) async-start(), calls=%async_computation.18 | async-start | bytes 5013504
  467.8 63.8 %copy-start.26 = (bf16[512,384]{1,0:T(8,128)(2,1)S(1)}, bf16[512,384]{1,0:T(8,128)(2,1)}, u32[]{:S(2)}) copy-start(bf16[512,384]{1,0:T(8,128)(2,1)} %copy.101) | copy-start | bytes 1179652
  467.8 63.8 %copy-start.27 = (bf16[512,384]{1,0:T(8,128)(2,1)S(1)}, bf16[512,384]{1,0:T(8,128)(2,1)}, u32[]{:S(2)}) copy-start(bf16[512,384]{1,0:T(8,128)(2,1)} %param.21) | copy-start | bytes 1179652
  530.3 24.0 %copy-start.50 = (f32[512]{0:T(512)S(1)}, f32[512]{0:T(512)}, u32[]{:S(2)}) copy-start(f32[512]{0:T(512)} %copy-done.49) | copy-start | bytes 6148
  530.3 24.0 %copy-start.52 = (f32[512]{0:T(512)S(1)}, f32[512]{0:T(512)}, u32[]{:S(2)}) copy-start(f32[512]{0:T(512)} %copy-done.51) | copy-start | bytes 6148
  554.4 796.9 %copy-start.1 = (bf16[768,1536]{1,0:T(8,128)(2,1)S(1)}, bf16[768,1536]{1,0:T(8,128)(2,1)}, u32[]{:S(2)}) copy-start(bf16[768,1536]{1,0:T(8,128)(2,1)} %param.33) | copy-start | bytes 7077892
  (124 other events, 451.3 us)
Sparse Core Ops, SparseCore 0:
  228.3 5.6 reduce-scatter.24
  250.9 17.9 all-reduce.6
  399.2 119.7 all-reduce.10
  521.1 9.1 reduce-scatter.26
  532.6 20.3 all-reduce.8
  558.2 124.8 reduce-scatter.18
  688.4 122.6 reduce-scatter.20
  816.4 122.5 reduce-scatter.14
  944.4 122.6 reduce-scatter.16
  1072.7 136.0 reduce-scatter.22
  1215.3 136.0 reduce-scatter.28
where the time goes:
time: 1370 us; the launch traced here: 1360 us
  waiting for transfers between devices  843 us (62%)
  blocking collectives  193 us (14%)
  other arithmetic  176 us (13%)
  matrix products  68.4 us (5%)
  local copies, waits for them, and re-layouts  51.1 us (4%)
  between operations  18.6 us (1%)
    unnamed x14, waiting for transfers between devices  153 us
    all_gather x3, blocking collectives, entering(): lax.all_gather(part.astype(kind), axis)  142 us
    reduce_scatter x1, waiting for transfers between devices, local(): lax.psum_scatter(up_grad, 'seq', scatter_dimension=0, tiled=True)  142 us
    reduce_scatter x1, waiting for transfers between devices, local(): lax.psum_scatter(k_grad, 'seq', scatter_dimension=0, tiled=True)  128 us
    reduce_scatter x1, waiting for transfers between devices, local(): lax.psum_scatter(out_w_grad, 'seq', scatter_dimension=0, tiled=True)  128 us
    reduce_scatter x1, waiting for transfers between devices, local(): lax.psum_scatter(q_grad, 'seq', scatter_dimension=0, tiled=True)  128 us
    reduce_scatter x1, waiting for transfers between devices, local(): lax.psum_scatter(v_grad, 'seq', scatter_dimension=0, tiled=True)  81.2 us
    psum x1, waiting for transfers between devices, local(): lax.psum((kernel_full, gain1_grad, bias1_grad, gain2_grad, bias2_grad), (...  49.5 us
  transfers between devices with their start and end apart: 13, of which 10 were waited for; matrix products, arithmetic and copies ran while one was open for 9% of the time, Pallas kernels for 0%

commit v1 on v0

v1 whole, which is shorter than its diff:
```python
import functools

import jax
import jax.numpy as jnp
from jax import lax
from jax.experimental import pallas as pl
from jax.experimental.pallas import tpu as pltpu
from jax.sharding import PartitionSpec as P

NORM_EPS = 1e-05
RATE_CAP = 0.05
LANES = 128
STEP = 64
FAR = float(1 << 20)
GELU_SCALE = 0.7978845608028654
GELU_CUBE = 0.044715
F32 = jnp.float32
BF16 = jnp.bfloat16

NN = (((1,), (0,)), ((), ()))
NT = (((1,), (1,)), ((), ()))
TN = (((0,), (0,)), ((), ()))


def mm(a, b, dims=NN):
    return lax.dot_general(a, b, dims, preferred_element_type=F32)


def shape(dims, kind):
    return pltpu.HBM(dims, kind)


def shape(dims, kind):
    return jax.ShapeDtypeStruct(dims, kind)


FEW = pl.BlockSpec(memory_space=pltpu.SMEM)


def whole(array):
    dims = array.shape
    return pl.BlockSpec(dims, lambda *_: (0,) * len(dims), pipeline_mode=pl.Buffered(1))


def run(body, outs, *ins, scratch=(), scalars=0, grid=(1,), in_specs=None, out_specs=None, mib=16,
        us=1.0, far=()):
    many = isinstance(outs, (tuple, list))
    held = [pltpu.with_memory_space_constraint(x, pltpu.HBM) if i in far else x for i, x in enumerate(ins)]
    if in_specs is None:
        in_specs = [None] * (len(ins) - scalars)
    if out_specs is None:
        out_specs = (None,) * len(outs) if many else None
    in_specs = [spec or whole(x) for spec, x in zip(in_specs, ins[scalars:])]
    pick = lambda spec, x: spec or whole(x)
    out_specs = tuple(map(pick, out_specs, outs)) if many else pick(out_specs, outs)
    return pl.pallas_call(
        body, out_shape=outs, grid=grid, in_specs=[FEW] * scalars + list(in_specs), out_specs=out_specs,
        scratch_shapes=list(scratch), compiler_params=pltpu.CompilerParams(vmem_limit_bytes=mib << 20),
        cost_estimate=pl.CostEstimate(flops=int(us * 1e9), transcendentals=0, bytes_accessed=int(us * 3e6)))(*held)


def after(value, *first):
    return lax.optimization_barrier((value,) + first)[0]


def lanes(width):
    return range(0, width, LANES)


def half_of(ref, h, width):
    return ref.at[:, pl.ds(pl.multiple_of(h * width, LANES), width)]


def digits_of(count):
    digits, stride = [], 1
    while count > 1:
        radix = 4 if count % 4 == 0 else (2 if count % 2 == 0 else count)
        digits.append((stride, radix))
        stride, count = stride * radix, count // radix
    return digits


def turned(array, stride, radix, by):
    pairs = []
    for i in range(lax.axis_size("seq")):
        member = i // stride % radix
        pairs.append((i, i + ((member + by) % radix - member) * stride))
    return lax.ppermute(array, "seq", pairs)


def crossed(array, stride, radix, mask):
    pairs = []
    for i in range(lax.axis_size("seq")):
        member = i // stride % radix
        pairs.append((i, i + ((member ^ mask) - member) * stride))
    return lax.ppermute(array, "seq", pairs)


def swapped(array):
    count = lax.axis_size("head")
    return lax.ppermute(array, "head", [(i, (i + 1) % count) for i in range(count)])


def passed_along(array, by):
    count = lax.axis_size("seq")
    return lax.ppermute(array, "seq", [(i, i + by) for i in range(count) if 0 <= i + by < count])


def member_at(place_ref, stride, radix):
    return lax.rem(lax.div(place_ref[0], stride), radix)


def send_pieces(pieces, stride, radix):
    return [pieces[0]] + [turned(pieces[by], stride, radix, by) for by in range(1, radix)]


def bits_of(count):
    return [1 << k for k in range(count.bit_length() - 1)]


def mirrored(array, stride):
    pairs = [(i, i ^ stride) for i in range(lax.axis_size("seq"))]
    return lax.ppermute(array, "seq", pairs)


def halve(total, bit, keep, send, low):
    for g in range(keep.shape[0]):
        at = g // low * 2 * low + g % low
        keep[g] = total[at + bit * low].astype(BF16)
        send[g] = total[at + (1 - bit) * low].astype(BF16)


def split_shapes(count, rows, widths):
    return tuple(shape((count // 2, rows, w), BF16) for w in widths for _ in range(2))


def half_width(width):
    return -(-width // (2 * LANES)) * LANES


def put_rows(total, at, grad):
    rows = total.shape[1]
    for s in range(total.shape[0]):
        total[s, :, at : at + grad.shape[1]] = grad[s * rows : (s + 1) * rows]


def both_halves(total, place_ref, outs):
    middle = outs[0].shape[2]
    halve(total.at[:, :, :middle], member_at(place_ref, 1, 2), outs[0], outs[1], 1)
    halve(total.at[:, :, middle:], member_at(place_ref, 2, 2), outs[2], outs[3], 2)


def grads_kernel(spans, place_ref, *refs):
    lefts, rights, outs, total = refs[: len(spans)], refs[len(spans) : 2 * len(spans)], refs[-5:-1], refs[-1]
    for left, right, at in zip(lefts, rights, spans):
        put_rows(total, at, mm(left[...], right[...], TN))
    both_halves(total, place_ref, outs)


def grad_halves(place, pairs, us):
    count = lax.axis_size("seq")
    depth = pairs[0][0].shape[1]
    spans, width = [], 0
    for _, right in pairs:
        spans.append(width)
        width += right.shape[1]
    middle = half_width(width)
    rows = depth // count
    return run(
        functools.partial(grads_kernel, spans), split_shapes(count, rows, (middle, width - middle)),
        place, *[left for left, _ in pairs], *[right for _, right in pairs],
        scalars=1, scratch=[pltpu.VMEM((count, rows, width), F32)], mib=24, us=us)


def fold_rest(place, halves, got, at, widths):
    bits = bits_of(lax.axis_size("seq"))
    while True:
        halves = fold_bit(place, halves, got, at, widths)
        at += 1
        if at >= len(bits):
            return halves
        got = mirrored(halves[1], bits[at])


def down_kernel(place_ref, grad_ref, hidden_ref, down_ref, resid_ref, *refs):
    outs, own_ref, send_ref, total, part = refs[:4], refs[4], refs[5], refs[6], refs[7]
    part[...] = mm(hidden_ref[...], down_ref[...], NT)
    width = own_ref.shape[1]
    h = place_ref[1]
    own_ref[...] = half_of(part, h, width)[...] + half_of(resid_ref, h, width)[...]
    send_ref[...] = half_of(part, 1 - h, width)[...].astype(BF16)
    put_rows(total, 0, mm(grad_ref[...], hidden_ref[...], TN))
    both_halves(total, place_ref, outs)


def cross_kernel(place_ref, keep_a, got_a, keep_b, got_b, *refs):
    outs, sum_a, sum_b = refs[:4], refs[4], refs[5]
    for keep, got, total in ((keep_a, got_a, sum_a), (keep_b, got_b, sum_b)):
        for g in range(total.shape[0]):
            total[g] = keep[g].astype(F32) + got[g].astype(F32)
    halve(sum_a, member_at(place_ref, 2, 2), outs[0], outs[1], 1)
    halve(sum_b, member_at(place_ref, 1, 2), outs[2], outs[3], 1)


def cross(place, halves, got_a, got_b):
    keep_a, _, keep_b, _ = halves
    count, rows, _ = keep_a.shape
    return run(
        cross_kernel, split_shapes(count, rows, (keep_a.shape[2], keep_b.shape[2])),
        place, keep_a, got_a, keep_b, got_b, scalars=1,
        scratch=[pltpu.VMEM(keep_a.shape, F32), pltpu.VMEM(keep_b.shape, F32)], us=8)


def join_kernel(stride, place_ref, keep_a, got_a, keep_b, got_b, *refs):
    outs, total = refs[:-1], refs[-1]
    middle = keep_a.shape[2]
    for g in range(total.shape[0]):
        total[g, :, :middle] = keep_a[g].astype(F32) + got_a[g].astype(F32)
        total[g, :, middle:] = keep_b[g].astype(F32) + got_b[g].astype(F32)
    put_folded(stride, total, place_ref, outs)


def fold_kernel(stride, place_ref, keep, got, *refs):
    outs, total = refs[:-1], refs[-1]
    for g in range(total.shape[0]):
        total[g] = keep[g].astype(F32) + got[g].astype(F32)
    put_folded(stride, total, place_ref, outs)


def put_folded(stride, total, place_ref, outs):
    if stride:
        halve(total, member_at(place_ref, stride, 2), outs[0], outs[1], 1)
        return
    begin = 0
    for out in outs:
        out[...] = total[0, :, begin : begin + out.shape[1]]
        begin += out.shape[1]


def fold_outs(entries, rows, widths):
    if entries == 1:
        return tuple(shape((rows, w), F32) for w in widths)
    return split_shapes(entries, rows, (sum(widths),))


def join(place, halves, got_a, got_b, widths):
    keep_a, _, keep_b, _ = halves
    entries, rows, _ = keep_a.shape
    bits = bits_of(lax.axis_size("seq"))
    last = entries == 1
    return run(
        functools.partial(join_kernel, 0 if last else bits[2]), fold_outs(entries, rows, widths), place,
        keep_a, got_a, keep_b, got_b, scalars=1, scratch=[pltpu.VMEM((entries, rows, sum(widths)), F32)], us=8)


def fold_bit(place, halves, got, at, widths):
    keep = halves[0]
    entries, rows, _ = keep.shape
    bits = bits_of(lax.axis_size("seq"))
    last = entries == 1
    return run(
        functools.partial(fold_kernel, 0 if last else bits[at + 1]), fold_outs(entries, rows, widths), place,
        keep, got, scalars=1, scratch=[pltpu.VMEM((entries, rows, sum(widths)), F32)], us=8)


def add_kernel(stage, later, rows, place_ref, *refs):
    radix = stage[1]
    got, outs, total, sorted_parts = refs[:radix], refs[radix:-2], refs[-2], refs[-1]
    entries = total.shape[0]
    for g in range(entries):
        at = slice(g * rows, (g + 1) * rows)
        acc = got[0][at].astype(F32)
        for by in range(1, radix):
            acc = acc + got[by][at].astype(F32)
        total[g] = acc
    tail = [m.at[entries * rows :] for m in got]
    shared = in_order(member_at(place_ref, *stage), tail, sorted_parts)
    if later:
        put_messages(total, shared, later[1], member_at(place_ref, *later), outs)
    else:
        outs[0][...] = total[0]
        outs[1][...] = shared[:STEP]
        put_vectors(shared[STEP:], outs[2:4])
        put_vectors(shared[STEP + 8 :], outs[4:])


def put_messages(total, shared, radix, member, outs):
    rows = total.shape[1]
    for by in range(radix):
        to = lax.rem(member + by, radix)
        groups = total.shape[0] // radix
        for g in range(groups):
            outs[by][g * rows : (g + 1) * rows] = total[g * radix + to].astype(BF16)
        outs[by][groups * rows :] = shared.astype(BF16)


def add_messages(place, got, at, rows):
    stages = digits_of(lax.axis_size("seq"))
    radix = stages[at][1]
    depth, width = got[0].shape
    extra = STEP + 16
    entries = (depth - extra) // rows
    later = ()
    if at + 1 < len(stages):
        later = stages[at + 1]
        outs = (shape((entries // later[1] * rows + extra, width), BF16),) * later[1]
    else:
        outs = (shape((rows, width), F32), shape((STEP, width), F32)) + (shape((2 * width,), F32),) * 4
    return run(
        functools.partial(add_kernel, stages[at], later, rows), outs, place, *got, scalars=1,
        scratch=[pltpu.VMEM((entries, rows, width), F32), pltpu.VMEM((radix, extra, width), F32)], us=8)


def in_order(member, got, sorted_parts):
    radix = len(got)
    for by in range(radix):
        sorted_parts[lax.rem(member + radix - by, radix)] = got[by][...].astype(F32)
    acc = sorted_parts[0]
    for c in range(1, radix):
        acc = acc + sorted_parts[c]
    return acc


def put_vectors(rows_in, outs):
    width = rows_in.shape[1]
    for k, out in enumerate(outs):
        out[:width] = rows_in[k]
        out[width:] = rows_in[k + 2]


def flat_rows(sums, width):
    return jnp.concatenate([sums[:, :width], sums[:, width:]], axis=0)


def chained(first, second):
    return first[0] * second[0], second[0] * first[1] + second[1]


def link(stage, reverse, place_ref, messages, before, want_total):
    radix = stage[1]
    member = member_at(place_ref, *stage)
    if reverse:
        member = radix - 1 - member
    rows = messages[0].shape[0] - 16
    pairs = []
    for m in messages:
        whole = m[...].astype(F32)
        pairs.append((whole[rows : rows + 1], whole[:rows]))
    none = (jnp.ones_like(pairs[0][0]), jnp.zeros_like(pairs[0][1]))

    def side(use):
        acc = none
        for by in range(radix - 1, 0, -1):
            kept = use(by)
            part = (jnp.where(kept, pairs[by][0], none[0]), jnp.where(kept, pairs[by][1], none[1]))
            acc = chained(acc, part)
        return acc

    lower = side(lambda by: by <= member)
    before = chained(lower, tuple(b[...] for b in before)) if before else lower
    if not want_total:
        return before, None
    return before, chained(chained(lower, pairs[0]), side(lambda by: by > member))


def link_kernel(stage, reverse, place_ref, *refs):
    messages, held, outs = refs[: stage[1]], refs[stage[1] : -3], refs[-3:]
    before, total = link(stage, reverse, place_ref, messages, held, True)
    outs[0][...], outs[1][...] = before
    rows = outs[1].shape[0]
    outs[2][:rows] = total[1].astype(BF16)
    outs[2][rows:] = jnp.broadcast_to(total[0], (outs[2].shape[0] - rows, total[0].shape[1])).astype(BF16)


def scan_send(message, at, reverse):
    stride, radix = digits_of(lax.axis_size("seq"))[at]
    return [message] + [
        turned(message, stride, radix, (radix - by) if reverse else by) for by in range(1, radix)
    ]


def scan_link(place, got, before, at, reverse):
    stage = digits_of(lax.axis_size("seq"))[at]
    rows, width = got[0].shape
    outs = run(functools.partial(link_kernel, stage, reverse),
               (shape((1, width), F32), shape((rows - 16, width), F32), shape((rows, width), BF16)),
               place, *got, *before, scalars=1, us=8)
    return outs[:2], outs[2]


def split_parts(x, count):
    parts = []
    for _ in range(count):
        low = x.astype(BF16)
        parts.append(low)
        x = x - low.astype(F32)
    return parts


def side_kernel(starts_ref, decay_ref, beta_ref, lamr_ref, lamc_ref, docr_ref, docc_ref, dist_ref,
                beta_out, first_out, last_out, gate_out, tri, same, wide):
    tok = starts_ref.shape[0]
    heads = decay_ref.shape[0]
    head_pairs = lamc_ref.shape[0] // tok
    width = beta_out.shape[1]
    row = lax.broadcasted_iota(jnp.int32, (tok, tok), 0)
    col = lax.broadcasted_iota(jnp.int32, (tok, tok), 1)
    tri[...] = (col <= row).astype(F32).astype(BF16)
    begins = jnp.broadcast_to(row_of(starts_ref).astype(F32), (LANES, tok)).astype(BF16)
    doc_col = mm(tri[...], begins, NT)
    doc_row = mm(begins[:16], tri[...], NT)[:8]
    docr_ref[...] = doc_row
    docc_ref[...] = doc_col
    wide[...] = jnp.zeros_like(wide)
    wide[:heads] = decay_ref[...]
    lam_col = jnp.zeros((tok, LANES), F32)
    lam_row = jnp.zeros((16, tok), F32)
    for part in split_parts(wide[...], 3):
        lam_col = lam_col + mm(tri[...], part, NT)
        lam_row = lam_row + mm(part[:16], tri[...], NT)
    lamr_ref[...] = jnp.zeros_like(lamr_ref)
    for p in range(head_pairs):
        lamr_ref[8 * p : 8 * p + 2] = lam_row[2 * p : 2 * p + 2]
        lamc_ref[p * tok : (p + 1) * tok] = lam_col if p == 0 else pltpu.roll(lam_col, LANES - 2 * p, 1)
    ones = jnp.ones((tok, LANES), BF16)
    alike = doc_col[:, :1] == doc_row[:1]
    same[...] = jnp.where(alike & (col <= row), 1.0, 0.0).astype(BF16)
    behind = mm(same[...], ones)
    dist_ref[...] = jnp.where(doc_col == 0.0, FAR, behind - 1.0)
    lam_end = lam_col[tok - 1 :]
    doc_end = doc_col[tok - 1 :]
    first = jnp.where(doc_col == 0.0, jnp.exp(-lam_col), 0.0)
    last = jnp.where(doc_col == doc_end, jnp.exp(lam_col - lam_end), 0.0)
    spread = (lax.broadcasted_iota(jnp.int32, (LANES, width), 0)
              == lax.broadcasted_iota(jnp.int32, (LANES, width), 1) // (width // heads))
    spread = spread.astype(F32).astype(BF16)
    for ref, value in ((first_out, first), (last_out, last)):
        parts = split_parts(value, 2)
        ref[...] = mm(parts[0], spread) + mm(parts[1], spread)
    wide[:heads] = beta_ref[...]
    eye = (row == col).astype(F32).astype(BF16)
    beta_col = jnp.zeros((tok, LANES), F32)
    for part in split_parts(wide[...], 2):
        beta_col = beta_col + mm(eye, part, NT)
    parts = split_parts(beta_col, 2)
    beta_out[...] = mm(parts[0], spread) + mm(parts[1], spread)
    gate_out[...] = first_out[tok - 16 :].astype(BF16)


def row_of(ref):
    return ref[...].reshape(1, ref.shape[0])


def norm_rows(rows_in):
    count = rows_in.shape[1]
    center = rows_in - jnp.sum(rows_in, axis=1, keepdims=True) * (1.0 / count)
    spread = jnp.sum(center * center, axis=1, keepdims=True) * (1.0 / count)
    inverse = lax.rsqrt(spread + NORM_EPS)
    return center * inverse, inverse


def norm_back(grad_rows, unit_rows, inverse, gain_vec):
    scale = 1.0 / grad_rows.shape[1]
    scaled = grad_rows * gain_vec
    return inverse * (scaled - jnp.sum(scaled, axis=1, keepdims=True) * scale
                      - unit_rows * (jnp.sum(scaled * unit_rows, axis=1, keepdims=True) * scale))


def by_rows(tok, body, size=64):
    def step(i, carry):
        body(pl.ds(pl.multiple_of(i * size, size), size))
        return carry

    lax.fori_loop(0, tok // size, step, 0)


def in_kernel(place_ref, own_ref, other_ref, gain_ref, bias_ref, wq_ref, wk_ref, wv_ref, docc_ref,
              normed_ref, q_ref, k_ref, v_ref, tail_ref, rows):
    h = place_ref[1]
    tok, width = own_ref.shape
    half_of(rows, h, width)[...] = own_ref[...]
    half_of(rows, 1 - h, width)[...] = other_ref[...]

    def norm(at):
        unit, _ = norm_rows(rows[at].astype(F32))
        normed_ref[at] = (unit * row_of(gain_ref) + row_of(bias_ref)).astype(BF16)

    by_rows(tok, norm)
    normed = normed_ref[...]
    k_ref[...] = mm(normed, wk_ref[...]).astype(BF16)
    keep = docc_ref[tok - STEP :] == docc_ref[tok - 1 :]
    for l in lanes(width):
        tail_ref[:, l : l + LANES] = jnp.where(
            keep, k_ref[tok - STEP :, l : l + LANES].astype(F32), 0.0).astype(BF16)
    q_ref[...] = mm(normed, wq_ref[...]).astype(BF16)
    v_ref[...] = mm(normed, wv_ref[...]).astype(BF16)


def filter_chunk(keys, taps, dist, count, t0):
    def group(a, acc):
        acc = list(acc)
        for b in range(8):
            j = a * 8 + b
            keep = dist >= j.astype(F32)
            for l in range(count):
                x = keys[l, pl.ds(STEP + t0 - a * 8 - b, STEP), :]
                acc[l] = acc[l] + jnp.where(keep, x * taps[l, pl.ds(j, 1), :], 0.0)
        return tuple(acc)

    return lax.fori_loop(0, 8, group, tuple(jnp.zeros((STEP, LANES), F32) for _ in range(count)))


def filter_kernel(k_ref, taps_ref, dist_ref, beta_ref, out_ref, keys, taps):
    tok, width = k_ref.shape
    count = width // LANES
    for l in range(count):
        keys[l, STEP:] = k_ref[:, l * LANES : (l + 1) * LANES].astype(F32)
        taps[l] = taps_ref[:, l * LANES : (l + 1) * LANES].astype(F32)
    out_ref[:STEP] = jnp.zeros((STEP, width), BF16)

    def chunk(c, carry):
        t0 = pl.multiple_of(c * STEP, STEP)
        at = pl.ds(t0, STEP)
        acc = filter_chunk(keys, taps, dist_ref[at], count, t0)
        for l in range(count):
            span = slice(l * LANES, (l + 1) * LANES)
            out_ref[at, span] = (acc[l] * beta_ref[at, span]).astype(BF16)
        return carry

    lax.fori_loop(1, tok // STEP, chunk, 0)


def fold(square, low):
    return jnp.where(low, square[:STEP], square[STEP:])


def unfold(flat, low):
    return jnp.concatenate([jnp.where(low, flat, 0.0), jnp.where(low, 0.0, flat)], axis=0)


def low_lanes(rows):
    return lax.broadcasted_iota(jnp.int32, (rows, LANES), 1) < STEP


def state_kernel(part_ref, tail_ref, k_ref, taps_ref, dist_ref, beta_ref, last_ref, v_ref, gate_ref,
                 sk_ref, message_ref, keys, taps):
    tok, width = part_ref.shape
    count = width // LANES
    for l in range(count):
        span = slice(l * LANES, (l + 1) * LANES)
        keys[l, :STEP] = tail_ref[:, span].astype(F32)
        keys[l, STEP:] = k_ref[:STEP, span].astype(F32)
        taps[l] = taps_ref[:, span].astype(F32)
    sk_ref[...] = part_ref[...]
    acc = filter_chunk(keys, taps, dist_ref[:STEP], count, 0)
    low = low_lanes(STEP)
    for l in range(count):
        span = slice(l * LANES, (l + 1) * LANES)
        sk_ref[:STEP, span] = (acc[l] * beta_ref[:STEP, span]).astype(BF16)
        weighted = (sk_ref[:, span].astype(F32) * last_ref[:, span]).astype(BF16)
        message_ref[:STEP, span] = fold(mm(weighted, v_ref[:, span], TN), low).astype(BF16)
    message_ref[STEP:] = gate_ref[...]


def kept_pairs(docc_ref, docr_ref):
    tok = docc_ref.shape[0]
    order = lax.broadcasted_iota(jnp.int32, (tok, tok), 0) >= lax.broadcasted_iota(jnp.int32, (tok, tok), 1)
    return (docc_ref[:, :1] == docr_ref[:1]) & order


def own_lanes(x, low, e):
    return jnp.where(low if e == 0 else ~low, x.astype(F32), 0.0).astype(BF16)


def decay_of(lamr_ref, lamc_ref, keep, e):
    span = jnp.minimum(lamr_ref[e : e + 1] - lamc_ref[:, e : e + 1], 0.0)
    return jnp.where(keep, jnp.exp(span), 0.0)


def inside_kernel(q_ref, k_ref, v_ref, lamr_ref, lamc_ref, docr_ref, docc_ref, out_ref):
    low = low_lanes(q_ref.shape[0])
    keep = kept_pairs(docc_ref, docr_ref)
    outs = []
    for e in range(2):
        score = mm(own_lanes(q_ref[...], low, e), k_ref[...], NT)
        outs.append(mm((score * decay_of(lamr_ref, lamc_ref, keep, e)).astype(BF16), v_ref[...]))
    out_ref[...] = jnp.where(low, outs[0], outs[1])


def mixed_kernel(stage, place_ref, inside_ref, q_ref, first_ref, *refs):
    (state_ref, mixed_ref) = refs[-2:]
    before, _ = link(stage, False, place_ref, refs[: stage[1]], refs[stage[1] : -2], False)
    state_ref[...] = before[1]
    low = low_lanes(STEP)
    for l in lanes(q_ref.shape[1]):
        span = slice(l, l + LANES)
        square = unfold(state_ref[:, span], low).astype(BF16)
        mixed_ref[:, span] = (0.125 * (inside_ref[:, span] + first_ref[:, span] * mm(q_ref[:, span], square))
                              ).astype(BF16)


def hidden_grad_kernel(place_ref, own_ref, other_ref, down_ref, out_ref, full_ref):
    @pl.when(pl.program_id(0) == 0)
    def _():
        width = own_ref.shape[1]
        half_of(full_ref, place_ref[1], width)[...] = own_ref[...]
        half_of(full_ref, 1 - place_ref[1], width)[...] = other_ref[...]

    out_ref[...] = mm(full_ref[...], down_ref[...]).astype(BF16)


def ffn_kernel(place_ref, own_ref, other_ref, mix_own_ref, mix_other_ref, out_own_ref, out_other_ref, gain_ref,
               bias_ref, up_ref, hg_ref, resid_ref, normed_ref, hidden_ref, pre_ref, part_ref, rows, acc):
    h = place_ref[1]
    step = pl.program_id(0)
    tok, width = own_ref.shape

    @pl.when(step == 0)
    def _():
        half_of(rows, h, width)[...] = own_ref[...]
        half_of(rows, 1 - h, width)[...] = other_ref[...]
        resid_ref[...] = mm(mix_own_ref[...], out_own_ref[...], NT) + mm(mix_other_ref[...], out_other_ref[...], NT)

        def norm(at):
            resid = rows[at].astype(F32) + resid_ref[at]
            resid_ref[at] = resid
            unit, _ = norm_rows(resid)
            normed_ref[at] = (unit * row_of(gain_ref) + row_of(bias_ref)).astype(BF16)

        by_rows(tok, norm)
        acc[...] = jnp.zeros_like(acc)

    pre = mm(normed_ref[...], up_ref[...])
    square = pre * pre
    bent = jnp.tanh(GELU_SCALE * (pre + GELU_CUBE * (square * pre)))
    outer = 0.5 * (1.0 + bent)
    hidden_ref[...] = (pre * outer).astype(BF16)
    slope = outer + 0.5 * pre * (1.0 - bent * bent) * (GELU_SCALE * (1.0 + 3.0 * GELU_CUBE * square))
    pre_ref[...] = (hg_ref[...].astype(F32) * slope).astype(BF16)
    acc[...] += mm(pre_ref[...], up_ref[...], NT)

    @pl.when(step == pl.num_programs(0) - 1)
    def _():
        part_ref[...] = acc[...].astype(BF16)


def norm2_kernel(place_ref, part_ref, got_ref, resid_ref, grad_ref, gain_ref, out_w_ref, q_ref, first_ref,
                 gate_ref, resid_grad_ref, branch_ref, g_ref, sums_ref, message_ref, rows):
    h = place_ref[1]
    tok, width = q_ref.shape
    sums_ref[...] = jnp.zeros_like(sums_ref)

    def norm(at):
        back = part_ref[at].astype(F32) + got_ref[at].astype(F32)
        unit, inverse = norm_rows(resid_ref[at])
        grad = grad_ref[at].astype(F32) + norm_back(back, unit, inverse, row_of(gain_ref))
        rows[at] = grad
        branch_ref[at] = grad.astype(BF16)
        sums_ref[0:1] += jnp.sum(back * unit, axis=0, keepdims=True)
        sums_ref[1:2] += jnp.sum(back, axis=0, keepdims=True)

    by_rows(tok, norm)
    resid_grad_ref[...] = half_of(rows, h, width)[...]
    g_ref[...] = (0.125 * mm(branch_ref[...], out_w_ref[...]).astype(BF16).astype(F32)).astype(BF16)
    low = low_lanes(STEP)
    for l in lanes(width):
        span = slice(l, l + LANES)
        weighted = (q_ref[:, span].astype(F32) * first_ref[:, span]).astype(BF16)
        message_ref[:STEP, span] = fold(mm(weighted, g_ref[:, span], TN), low).astype(BF16)
    message_ref[STEP:] = gate_ref[...]


def back_kernel(q_ref, k_ref, v_ref, g_ref, lamr_ref, lamc_ref, docr_ref, docc_ref, first_ref, state_ref,
                dq_ref, dk_ref, dv_ref):
    low = low_lanes(q_ref.shape[0])
    keep = kept_pairs(docc_ref, docr_ref)
    square = unfold(state_ref[...], low_lanes(STEP)).astype(BF16)
    outs = []
    for e in range(2):
        decay = decay_of(lamr_ref, lamc_ref, keep, e)
        prob = (mm(own_lanes(q_ref[...], low, e), k_ref[...], NT) * decay).astype(BF16)
        score = (mm(own_lanes(g_ref[...], low, e), v_ref[...], NT) * decay).astype(BF16)
        outs.append((mm(score, k_ref[...]), mm(score, q_ref[...], TN), mm(prob, g_ref[...], TN)))
    from_state = first_ref[...] * mm(g_ref[...], square, NT)
    dq_ref[...] = (jnp.where(low, outs[0][0], outs[1][0]) + from_state).astype(BF16)
    dk_ref[...] = jnp.where(low, outs[0][1], outs[1][1])
    dv_ref[...] = jnp.where(low, outs[0][2], outs[1][2])


def filter_back_chunk(sg, keys, taps, ahead, sums, count, s0):
    held = [keys[l, pl.ds(s0, STEP), :] for l in range(count)]

    def group(a, acc):
        acc = list(acc)
        for b in range(8):
            j = a * 8 + b
            keep = ahead > j.astype(F32)
            for l in range(count):
                u = jnp.where(keep, sg[l, pl.ds(s0 + a * 8 + b, STEP), :], 0.0)
                acc[l] = acc[l] + u * taps[l, pl.ds(j, 1), :]
                sums[l, j] += jnp.sum((held[l] * u).reshape(STEP // 8, 8, LANES), axis=0)
        return tuple(acc)

    return lax.fori_loop(0, 8, group, tuple(jnp.zeros((STEP, LANES), F32) for _ in range(count)))


def reach(docr_ref, docc_ref, ahead_ref):
    tok = docc_ref.shape[0]
    order = lax.broadcasted_iota(jnp.int32, (tok, tok), 0) <= lax.broadcasted_iota(jnp.int32, (tok, tok), 1)
    same = jnp.where((docc_ref[:, :1] == docr_ref[:1]) & order, 1.0, 0.0).astype(BF16)
    ahead_ref[STEP:] = mm(same, jnp.ones((tok, LANES), BF16))
    unbroken = jnp.sum(jnp.where(docr_ref[:1] == 0.0, 1.0, 0.0), axis=1, keepdims=True)
    ahead_ref[:STEP] = unbroken + STEP - lax.broadcasted_iota(jnp.int32, (STEP, LANES), 0).astype(F32)


def carry_kernel(stage, place_ref, dk_ref, dv_ref, k_ref, v_ref, last_ref, beta_ref, docr_ref, docc_ref, taps_ref,
                 tail_ref, ffn_own_ref, ffn_other_ref, *refs):
    value_ref, sg_ref, edge_ref, sums, ahead_ref, block_ref, taps, keys = refs[-8:]
    block_ref[...] = (ffn_own_ref[...] + ffn_other_ref[...].astype(F32)).astype(BF16)
    reach(docr_ref, docc_ref, ahead_ref)
    before, _ = link(stage, True, place_ref, refs[: stage[1]], refs[stage[1] : -8], False)
    state = before[1]
    tok, width = dk_ref.shape
    count = width // LANES
    low = low_lanes(STEP)
    for l in range(count):
        span = slice(l * LANES, (l + 1) * LANES)
        square = unfold(state[:, span], low).astype(BF16)
        last = last_ref[:, span]
        value_ref[:, span] = (dv_ref[:, span] + last * mm(k_ref[:, span], square)).astype(BF16)
        sg_ref[l, :STEP] = jnp.zeros((STEP, LANES), F32)
        sg_ref[l, STEP : STEP + tok] = beta_ref[:, span] * (
            dk_ref[:, span] + last * mm(v_ref[:, span], square, NT))
        sg_ref[l, STEP + tok :] = jnp.zeros((STEP, LANES), F32)
        keys[l] = tail_ref[:, span].astype(F32)
        taps[l] = taps_ref[:, span].astype(F32)
    sums[...] = jnp.zeros_like(sums)
    acc = filter_back_chunk(sg_ref, keys, taps, ahead_ref[:STEP], sums, count, 0)
    for l in range(count):
        edge_ref[:, l * LANES : (l + 1) * LANES] = acc[l].astype(BF16)


def filter_back_kernel(sg_ref, k_ref, ahead_ref, taps_ref, sums_in, sums2_ref, grad_ref, small_ref, keys, taps, sums):
    tok, width = k_ref.shape
    count = width // LANES
    for l in range(count):
        span = slice(l * LANES, (l + 1) * LANES)
        keys[l, STEP:] = k_ref[:, span].astype(F32)
        taps[l] = taps_ref[:, span].astype(F32)
    sums[...] = sums_in[...]

    def chunk(c, carry):
        s0 = pl.multiple_of(c * STEP, STEP)
        acc = filter_back_chunk(sg_ref, keys, taps, ahead_ref[pl.ds(s0, STEP)], sums, count, s0)
        for l in range(count):
            grad_ref[pl.ds(s0 - STEP, STEP), l * LANES : (l + 1) * LANES] = acc[l]
        return carry

    lax.fori_loop(1, tok // STEP + 1, chunk, 0)
    for l in range(count):
        small_ref[:STEP, l * LANES : (l + 1) * LANES] = jnp.sum(sums[l], axis=1)
    small_ref[STEP:] = jnp.zeros_like(small_ref[STEP:])
    small_ref[STEP : STEP + 4] = flat_rows(sums2_ref[:2], width)


def out_kernel(place_ref, grad_ref, edge_ref, docc_ref, dq_ref, dv_ref, wq_ref, wk_ref, wv_ref, own_ref, other_ref,
               key_ref, part_ref, rows, total, sums_ref):
    h = place_ref[1]
    tok, width = own_ref.shape
    keep = docc_ref[tok - STEP :] == docc_ref[tok - 1 :]
    key_ref[: tok - STEP] = grad_ref[: tok - STEP].astype(BF16)
    for l in lanes(width):
        span = slice(l, l + LANES)
        edge = jnp.where(keep, edge_ref[:, span].astype(F32), 0.0)
        key_ref[tok - STEP :, span] = (grad_ref[tok - STEP :, span] + edge).astype(BF16)
    total[...] = (mm(dq_ref[...], wq_ref[...], NT) + mm(dv_ref[...], wv_ref[...], NT)
                  + mm(key_ref[...], wk_ref[...], NT))
    part_ref[:tok] = total[...].astype(BF16)
    half_of(rows, h, width)[...] = own_ref[...]
    half_of(rows, 1 - h, width)[...] = other_ref[...]
    sums_ref[...] = jnp.zeros_like(sums_ref)

    def norm(at):
        unit, _ = norm_rows(rows[at].astype(F32))
        sums_ref[0:1] += jnp.sum(total[at] * unit, axis=0, keepdims=True)
        sums_ref[1:2] += jnp.sum(total[at], axis=0, keepdims=True)

    by_rows(tok, norm)
    part_ref[tok:] = sums_ref[...].astype(BF16)


def key_grads_kernel(stage, place_ref, normed_ref, key_ref, small_ref, part_ref, got_ref, *refs):
    radix = stage[1]
    outs, total, shared = refs[:radix], refs[-2], refs[-1]
    put_rows(total, 0, mm(normed_ref[...], key_ref[...], TN))
    tok, width = key_ref.shape
    sums = part_ref[tok:].astype(F32) + got_ref[tok:].astype(F32)
    shared[...] = small_ref[...]
    shared[STEP + 8 : STEP + 12] = flat_rows(sums[:2], width)
    put_messages(total, shared[...], radix, member_at(place_ref, *stage), outs)


def input_kernel(place_ref, part_ref, got_ref, own_ref, other_ref, gain_ref, resid_grad_ref, out_ref, rows, back):
    h = place_ref[1]
    tok, width = own_ref.shape
    half_of(rows, h, width)[...] = own_ref[...]
    half_of(rows, 1 - h, width)[...] = other_ref[...]

    def norm(at):
        unit, inverse = norm_rows(rows[at].astype(F32))
        grad = part_ref[at].astype(F32) + got_ref[at].astype(F32)
        back[at] = norm_back(grad, unit, inverse, row_of(gain_ref))

    by_rows(tok, norm)
    out_ref[...] = (half_of(back, h, width)[...] + resid_grad_ref[...]).astype(BF16)


def local(block_input, starts, decay_rate, norm1_gain, norm1_bias, q_weight, k_weight, v_weight,
          shift_kernel, out_weight, norm2_gain, norm2_bias, up_weight, down_weight, out_grad):
    tok, width = block_input.shape
    heads = decay_rate.shape[0]
    full = 2 * width
    hidden_width = up_weight.shape[1]
    count = width // LANES
    seqs = lax.axis_size("seq")
    place = jnp.stack([lax.axis_index("seq"), lax.axis_index("head")]).astype(jnp.int32)
    gain1, bias1, gain2, bias2 = norm1_gain, norm1_bias, norm2_gain, norm2_bias
    vm = pltpu.VMEM

    stages = digits_of(seqs)
    other_input = swapped(block_input)
    other_grad = swapped(out_grad)
    other_out = swapped(out_weight)
    beta = jnp.sqrt(-jnp.expm1(-2.0 * jnp.minimum(decay_rate, RATE_CAP)))
    lamr, lamc, docr, docc, dist, beta_w, first_w, last_w, gate_w = run(
        side_kernel,
        (shape((8 * count, tok), F32), shape((count * tok, LANES), F32), shape((8, tok), F32),
         shape((tok, LANES), F32), shape((tok, LANES), F32),
         shape((tok, width), F32), shape((tok, width), F32), shape((tok, width), F32), shape((16, width), BF16)),
        starts, decay_rate, beta,
        scratch=[vm((tok, tok), BF16), vm((tok, tok), BF16), vm((LANES, tok), F32)], us=2.7)
    other_input = after(other_input, docc)
    normed1, query, key, value, tail = run(
        in_kernel,
        (shape((tok, full), BF16),) + (shape((tok, width), BF16),) * 3 + (shape((STEP, width), BF16),),
        place, block_input, other_input, gain1, bias1, q_weight, k_weight, v_weight, docc,
        scratch=[vm((tok, full), BF16)], scalars=1, us=3.0)
    prev_tail = passed_along(tail, 1)
    scaled_part = run(
        filter_kernel, shape((tok, width), BF16), key, shift_kernel, dist, beta_w,
        scratch=[vm((count, tok + STEP, LANES), F32), vm((count, STEP, LANES), F32)], us=5.4)
    prev_tail = after(prev_tail, scaled_part)
    scaled, message = run(
        state_kernel, (shape((tok, width), BF16), shape((STEP + 16, width), BF16)),
        scaled_part, prev_tail, key, shift_kernel, dist, beta_w, last_w, value, gate_w,
        scratch=[vm((count, 2 * STEP, LANES), F32), vm((count, STEP, LANES), F32)], us=1.7)
    pair_spec = pl.BlockSpec((tok, LANES), lambda p: (0, p))
    lamr_spec = pl.BlockSpec((8, tok), lambda p: (p, 0))
    lamc_spec = pl.BlockSpec((tok, LANES), lambda p: (p, 0))
    state_spec = pl.BlockSpec((STEP, LANES), lambda p: (0, p))
    tile = 512

    before = ()
    got = scan_send(message, 0, False)
    hidden_grad, grad_full = run(
        hidden_grad_kernel, (shape((tok, hidden_width), BF16), shape((tok, full), BF16)),
        place, out_grad, after(other_grad, message), down_weight, scalars=1,
        grid=(hidden_width // tile,), in_specs=[None, None, pl.BlockSpec((full, tile), lambda i: (0, i))],
        out_specs=(pl.BlockSpec((tok, tile), lambda i: (0, i)), None), us=2.5)
    last_got = [after(g, hidden_grad) for g in got]
    for at in range(len(stages) - 1):
        before, message = scan_link(place, last_got, before, at, False)
        last_got = scan_send(message, at + 1, False)
    query_late = after(query, message)
    inside = run(
        inside_kernel, shape((tok, width), F32), query_late, scaled, value, lamr, lamc, docr, docc,
        grid=(count,),
        in_specs=[pair_spec] * 3 + [lamr_spec, lamc_spec, None, None], out_specs=pair_spec, us=3.5)
    last_got = [after(g, inside) for g in last_got]
    state, mixed = run(
        functools.partial(mixed_kernel, stages[-1]), (shape((STEP, width), F32), shape((tok, width), BF16)),
        place, inside, query, first_w, *last_got, *before, scalars=1, us=1.2)
    mixed_other = swapped(mixed)

    wide_tile = pl.BlockSpec((full, tile), lambda i: (0, i))
    tok_tile = pl.BlockSpec((tok, tile), lambda i: (0, i))
    resid, normed2, hidden, pre_grad, part2 = run(
        ffn_kernel,
        (shape((tok, full), F32), shape((tok, full), BF16), shape((tok, hidden_width), BF16),
         shape((tok, hidden_width), BF16), shape((tok, full), BF16)),
        place, block_input, other_input, mixed, mixed_other, out_weight, other_out, gain2, bias2, up_weight, hidden_grad,
        scratch=[vm((tok, full), BF16), vm((tok, full), F32)], scalars=1, mib=24,
        grid=(hidden_width // tile,),
        in_specs=[None] * 8 + [wide_tile, tok_tile],
        out_specs=(None, None, tok_tile, tok_tile, None), us=10.8)
    got2 = swapped(part2)
    *down_halves, ffn_own, ffn_send = run(
        down_kernel,
        split_shapes(seqs, full // seqs, (half_width(hidden_width), hidden_width - half_width(hidden_width)))
        + (shape((tok, width), F32), shape((tok, width), BF16)),
        place, grad_full, hidden, down_weight, resid, scalars=1,
        scratch=[vm((seqs, full // seqs, hidden_width), F32), vm((tok, full), F32)], mib=24, us=4.0)
    got2 = after(got2, ffn_own)
    resid_grad, branch, g_low, sums2, message = run(
        norm2_kernel,
        (shape((tok, width), F32), shape((tok, full), BF16), shape((tok, width), BF16), shape((8, full), F32),
         shape((STEP + 16, width), BF16)),
        place, part2, got2, resid, grad_full, gain2, out_weight, query, first_w, gate_w,
        scratch=[vm((tok, full), F32)], scalars=1, us=3.2)
    before = ()
    got = scan_send(message, 0, True)
    ffn_other = swapped(after(ffn_send, message))
    up_halves = grad_halves(place, [(after(normed2, message), pre_grad)], 2.5)
    got = [after(g, up_halves[0]) for g in got]
    for at in range(len(stages) - 1):
        before, message = scan_link(place, got, before, at, True)
        got = scan_send(message, at + 1, True)
    down_got = mirrored(after(down_halves[1], message), 1), mirrored(after(down_halves[3], message), 2)
    query_late = after(query, message)
    query_grad, dk_part, dv_part = run(
        back_kernel, (shape((tok, width), BF16), shape((tok, width), F32), shape((tok, width), F32)),
        query_late, scaled, value, g_low, lamr, lamc, docr, docc, first_w, state,
        grid=(count,),
        in_specs=[pair_spec] * 4 + [lamr_spec, lamc_spec, None, None, pair_spec, state_spec],
        out_specs=(pair_spec,) * 3, us=5.6)
    got = [after(g, query_grad) for g in got]
    value_grad, shifted_grad, edge, sums, ahead, block_output = run(
        functools.partial(carry_kernel, stages[-1]),
        (shape((tok, width), BF16), shape((count, tok + 2 * STEP, LANES), F32), shape((STEP, width), BF16),
         shape((count, STEP, 8, LANES), F32), shape((tok + STEP, LANES), F32), shape((tok, width), BF16)),
        place, dk_part, dv_part, scaled, value, last_w, beta_w, docr, docc, shift_kernel, prev_tail, ffn_own, ffn_other,
        *got, *before, scalars=1,
        scratch=[vm((count, STEP, LANES), F32), vm((count, STEP, LANES), F32)], us=2.4)
    got_edge = passed_along(edge, -1)
    mix_halves = grad_halves(place, [(branch, mixed), (normed1, query_grad), (normed1, after(value_grad, edge))], 2.6)
    mix_widths, ffn_widths = (width,) * 3, (hidden_width,)
    down_got = [after(g, mix_halves[0]) for g in down_got]
    down_halves = cross(place, down_halves, *down_got)
    down_got = mirrored(down_halves[1], 2), mirrored(down_halves[3], 1)
    up_got = mirrored(after(up_halves[1], down_halves[0]), 1), mirrored(after(up_halves[3], down_halves[0]), 2)
    sums = after(sums, down_halves[0])
    key_rows, small_rows = run(
        filter_back_kernel, (shape((tok, width), F32), shape((STEP + 16, width), F32)),
        shifted_grad, key, ahead, shift_kernel, sums, sums2,
        scratch=[vm((count, tok + STEP, LANES), F32), vm((count, STEP, LANES), F32),
                 vm((count, STEP, 8, LANES), F32)], us=12.0)
    down_got = [after(g, key_rows) for g in down_got]
    down_halves = join(place, down_halves, *down_got, ffn_widths)
    down_got = mirrored(down_halves[1], 4)
    up_got = [after(g, down_halves[0]) for g in up_got]
    up_halves = cross(place, up_halves, *up_got)
    up_got = mirrored(up_halves[1], 2), mirrored(up_halves[3], 1)
    got_edge = after(got_edge, up_halves[0])
    key_grad, part1 = run(
        out_kernel, (shape((tok, width), BF16), shape((tok + 8, full), BF16)),
        place, key_rows, got_edge, docc, query_grad, value_grad, q_weight, k_weight, v_weight, block_input, other_input,
        scratch=[vm((tok, full), BF16), vm((tok, full), F32), vm((8, full), F32)], scalars=1, us=3.2)
    got1 = swapped(part1)
    up_got = [after(g, key_grad) for g in up_got]
    up_halves = join(place, up_halves, *up_got, ffn_widths)
    up_got = mirrored(up_halves[1], 4)
    mix_got = mirrored(after(mix_halves[1], up_halves[0]), 1), mirrored(after(mix_halves[3], up_halves[0]), 2)
    down_halves = fold_bit(place, down_halves, after(down_got, up_halves[0]), 2, ffn_widths)
    down_got = mirrored(down_halves[1], 8)
    rows = full // seqs
    radix = stages[0][1]
    key_messages = run(
        functools.partial(key_grads_kernel, stages[0]),
        (shape((seqs // radix * rows + STEP + 16, width), BF16),) * radix,
        place, normed1, key_grad, small_rows, part1, after(got1, down_halves[0]), scalars=1,
        scratch=[vm((seqs, rows, width), F32), vm((STEP + 16, width), F32)], us=1.4)
    key_got = send_pieces(key_messages, *stages[0])
    input_grad = run(
        input_kernel, shape((tok, width), BF16),
        place, part1, after(got1, key_messages[0]), block_input, other_input, gain1, resid_grad, scalars=1,
        scratch=[vm((tok, full), BF16), vm((tok, full), F32)], us=3.2)
    mix_got = [after(g, input_grad) for g in mix_got]
    mix_halves = cross(place, mix_halves, *mix_got)
    mix_got = mirrored(mix_halves[1], 2), mirrored(mix_halves[3], 1)
    up_halves = fold_bit(place, up_halves, after(up_got, mix_halves[0]), 2, ffn_widths)
    up_got = mirrored(up_halves[1], 8)
    (down_total,) = fold_rest(place, down_halves, after(down_got, up_halves[0]), 3, ffn_widths)
    key_got = [after(g, down_total) for g in key_got]
    key_messages = add_messages(place, key_got, 0, rows)
    key_got = send_pieces(key_messages, *stages[1])
    mix_got = [after(g, key_messages[0]) for g in mix_got]
    mix_halves = join(place, mix_halves, *mix_got, mix_widths)
    mix_got = mirrored(mix_halves[1], 4)
    (up_total,) = fold_rest(place, up_halves, after(up_got, mix_halves[0]), 3, ffn_widths)
    mix_halves = fold_bit(place, mix_halves, after(mix_got, up_total), 2, mix_widths)
    mix_got = mirrored(mix_halves[1], 8)
    key_got = [after(g, mix_halves[0]) for g in key_got]
    for at in range(1, len(stages) - 1):
        key_got = send_pieces(add_messages(place, key_got, at, rows), *stages[at + 1])
    k_total, taps_total, gain2_grad, bias2_grad, gain1_grad, bias1_grad = add_messages(
        place, key_got, len(stages) - 1, rows)
    out_total, q_total, v_total = fold_rest(place, mix_halves, after(mix_got, k_total), 3, mix_widths)
    return (block_output, input_grad, gain1_grad, bias1_grad, q_total, k_total, v_total, taps_total, out_total,
            gain2_grad, bias2_grad, up_total, down_total)


def solution(mesh):
    both, head = P("seq", "head"), P(None, "head")
    in_specs = (both, P("seq"), P("head", "seq"), P(), P(), head, head, head, head, head, P(), P(), head, head, both)
    out_specs = (both, both, P(), P(), both, both, both, head, both, P(), P(), both, both)
    return jax.shard_map(local, mesh=mesh, in_specs=in_specs, out_specs=out_specs, check_vma=False)
```

time: 1370 us -> 169 us (0.12)
  waiting for transfers between devices: 843 us -> 27.4 us
  blocking collectives: 193 us -> 0 us
  other arithmetic: 176 us -> 0.81 us
  Pallas kernels: 0 us -> 83.8 us
  matrix products: 68.4 us -> 0 us
  local copies, waits for them, and re-layouts: 51.1 us -> 1.46 us
  starting transfers between devices: 7.71 us -> 54.1 us
  between operations: 18.6 us -> 1.19 us
    reduce_scatter x5 -> x0, waiting for transfers between devices: 607 us -> none  [the longest x1 142 us: local(): lax.psum_scatter(up_grad, 'seq', scatter_dimension=0, tiled=True)]
    unnamed x14 -> x0, waiting for transfers between devices: 153 us -> none
    all_gather x7 -> x0, blocking collectives: 152 us -> none  [the longest x3 142 us: entering(): lax.all_gather(part.astype(kind), axis)]
    pallas_call x0 -> x34, Pallas kernels: none -> 83.8 us  [run(): pl.pallas_call(body, out_shape=outs, grid=grid, in_specs=[FEW] * scalars...]
    psum x3 -> x0, waiting for transfers between devices: 83.2 us -> none  [the longest x1 49.5 us: local(): lax.psum((kernel_full, gain1_grad, bias1_grad, gain2_grad, bias2_grad), (...]
    dot_general x30 -> x0, matrix products: 68.4 us -> none  [the longest x1 5.84 us: local(): jnp.einsum('td,tf->df', whole_grad, hidden, preferred_element_type=jnp.fl...]
    ppermute x2 -> x45, starting transfers between devices: 6.79 us -> 54.1 us  [the longest x18 23.5 us: mirrored(): return lax.ppermute(array, 'seq', pairs)]
    select_n x32 -> x0, other arithmetic: 43.7 us -> none  [lap(): return jax.tree.map(lambda a, b: jnp.where(reached, a, b), new, before)]
  transfers between devices with their start and end apart: 13 -> 45, of which waited for: 10 -> 17; matrix products, arithmetic and copies ran while one was open for 9% -> 0% of each run, Pallas kernels for 0% -> 41%
where the time goes in v1:
time: 169 us
  Pallas kernels  83.8 us (50%)
  starting transfers between devices  54.1 us (32%)
  waiting for transfers between devices  27.4 us (16%)
    pallas_call x34, Pallas kernels, run(): pl.pallas_call(body, out_shape=outs, grid=grid, in_specs=[FEW] * scalars...  83.8 us
    ppermute x18, starting transfers between devices, mirrored(): return lax.ppermute(array, 'seq', pairs)  23.5 us
    ppermute x18, starting transfers between devices, turned(): return lax.ppermute(array, 'seq', pairs)  23.4 us
    ppermute x18, waiting for transfers between devices, mirrored(): return lax.ppermute(array, 'seq', pairs)  16.8 us
    ppermute x18, waiting for transfers between devices, turned(): return lax.ppermute(array, 'seq', pairs)  8.89 us
    ppermute x2, starting transfers between devices, passed_along(): lax.ppermute(array, 'seq', [(i, i + by) for i in range(count) if 0 <= i +...  5.75 us
  transfers between devices with their start and end apart: 45, of which 17 were waited for; matrix products, arithmetic and copies ran while one was open for 0% of the time, Pallas kernels for 41%

profile of v1, /device:TPU:0, one launch (start us, length us, event | category | flops | bytes accessed | tf_op | source)
XLA Modules:
  0.0 168.8 jit_solution(14447072223882689289)
XLA Ops:
  1.7 0.7 negate_sqrt_fusion.beta_ref
  3.9 2.6 %shard_map.246 = (f32[24,512]{1,0:T(8,128)S(1)}, f32[1536,128]{1,0:T(8,128)S(1)}, f32[8,512]{1,0:T(8,128)S(1)}, f32[512,128]{1,0:T(8,128)S(1)}, f32[512,128]{1,0...) custom-call(s32[512]{0:T(512)S(1)} %copy-done.14, ...), custom_call_target="tpu_custom_call" | custom-call | flops 2700000000 | bytes 8100000 | tf_op jit(solution)/shard_map/pallas_call | solution.py:56
  6.6 3.6 %shard_map.247 = (bf16[512,768]{1,0:T(8,128)(2,1)S(1)}, bf16[512,384]{1,0:T(8,128)(2,1)S(1)}, bf16[512,384]{1,0:T(8,128)(2,1)S(1)}, bf16[512,384]{1,0:T(8,128)(2,1)S(1)}, bf16[64,384]{1,0:T(8,128)(2,1)S(1)}) custom-call(s32[2]{0:T(128)S(1)} %pad_add_fusion.place_ref, bf16[512,384]{1,0:T(8,128)(2,1)S(1)} %copy-done.8, ...), custom_call_target="tpu_custom_call" | custom-call | flops 3000000000 | bytes 9000000 | tf_op jit(solution)/shard_map/pallas_call | solution.py:56
  10.2 4.5 %collective-permute-start.1 = (bf16[64,384]{1,0:T(8,128)(2,1)S(1)}, bf16[64,384]{1,0:T(8,128)(2,1)S(1)}, u32[]{:S(2)}, u32[]{:S(2)}) collective-permute-start(bf16[64,384]{1,0:T(8,128)(2,1)S(1)} %get-tuple-element.184), channel_id=1, source_target_pairs={{0,2},{2,4},{4,6},{6,8},{8,10},{10,12},{12,14},{14,16},{16,18},{18... | collective-permute-start | bytes 147464 | tf_op jit(solution)/shard_map/ppermute | solution.py:106
  14.7 5.5 %shard_map.248.part_ref = bf16[512,384]{1,0:T(8,128)(2,1)S(1)} custom-call(bf16[512,384]{1,0:T(8,128)(2,1)S(1)} %get-tuple-element.181.k_ref, bf16[64,384]{1,0:T(8,128)(2,1)S(1)} %copy-done.9, f32[512,128]{1,0:T(8,128)S(1)} %get-tuple-element.182.dist_ref, f32[512,384]{1,0:T(8,128)S(1)} %get-tuple-element.183.beta_ref), custom_call_target="tpu_custom_call" | custom-call | flops 5400000000 | bytes 16200000 | tf_op jit(solution)/shard_map/pallas_call | solution.py:56
  20.2 1.1 shard_map.249
  21.3 2.5 %collective-permute-start.5 = (bf16[80,384]{1,0:T(8,128)(2,1)S(1)}, bf16[80,384]{1,0:T(8,128)(2,1)S(1)}, u32[]{:S(2)}, u32[]{:S(2)}) collective-permute-start(bf16[80,384]{1,0:T(8,128)(2,1)S(1)} %get-tuple-element.192.refs_0_), channel_id=1, source_target_pairs={{0,6},{2,0},{4,2},{6,4},{8,14},{10,8},{12,10},{14,12},{16,22},{18,... | collective-permute-start | bytes 184328 | tf_op jit(solution)/shard_map/ppermute | solution.py:88
  25.0 2.6 %shard_map.250 = (bf16[512,1536]{1,0:T(8,128)(2,1)S(1)}, bf16[512,768]{1,0:T(8,128)(2,1)S(1)}) custom-call(s32[2]{0:T(128)S(1)} %pad_add_fusion.place_ref, bf16[512,384]{1,0:T(8,128)(2,1)S(1)} %copy-done.7, bf16[512,384]{1,0:T(8,128)(2,1)S(1)} %collective-permute-done.2.other_ref, bf16[768,1536]{1,0:T(8,128)(2,1)S(1)} %copy-done.2), custom_call_target="tpu_custom_call" | custom-call | flops 2500000000 | bytes 7500000 | tf_op jit(solution)/shard_map/pallas_call | solution.py:56
  27.6 1.2 collective-permute-done.4.refs_2_
  28.7 0.7 collective-permute-done.3.refs_1_
  30.1 3.7 %collective-permute-start.8 = (bf16[80,384]{1,0:T(8,128)(2,1)S(1)}, bf16[80,384]{1,0:T(8,128)(2,1)S(1)}, u32[]{:S(2)}, u32[]{:S(2)}) collective-permute-start(bf16[80,384]{1,0:T(8,128)(2,1)S(1)} %get-tuple-element.203.refs_0_), channel_id=1, source_target_pairs={{0,24},{2,26},{4,28},{6,30},{8,0},{10,2},{12,4},{14,6},{16,8},{18,... | collective-permute-start | bytes 184328 | tf_op jit(solution)/shard_map/ppermute | solution.py:88
  33.8 1.0 collective-permute-start.6
  34.8 2.9 %shard_map.252.inside_ref = f32[512,384]{1,0:T(8,128)S(1)} custom-call(bf16[512,384]{1,0:T(8,128)(2,1)S(1)} %get-tuple-element.226.q_ref, bf16[512,384]{1,0:T(8,128)(2,1)S(1)} %get-tuple-element.198.k_ref, bf16[512,384]{1,0:T(8,128)(2,1)S(1)} %get-tuple-element.187.v_ref, f32[24,512]{1,0:T(8,128)S(1)} %get-tuple-element.199.lamr_ref, ...), custom_call_target="tpu_custom_call" | custom-call | flops 3500000000 | bytes 10500000 | tf_op jit(solution)/shard_map/pallas_call | solution.py:56
  37.8 1.2 collective-permute-done.7.refs_2_
  38.9 0.9 collective-permute-done.6.refs_1_
  39.8 0.8 shard_map.253
  40.8 1.7 %collective-permute-done.9.mix_other_ref = bf16[512,384]{1,0:T(8,128)(2,1)S(1)} collective-permute-done((bf16[512,384]{1,0:T(8,128)(2,1)S(1)}, bf16[512,384]{1,0:T(8,128)(2,1)S(1)}, u32[]{:S(2)}, u32[]{:S(2)}) %collective-permute-start.9) | collective-permute-done | bytes 393248 | tf_op jit(solution)/shard_map/ppermute | solution.py:101
  42.5 8.8 %shard_map.254 = (f32[512,768]{1,0:T(8,128)S(1)}, bf16[512,768]{1,0:T(8,128)(2,1)S(1)}, bf16[512,1536]{1,0:T(8,128)(2,1)S(1)}, bf16[512,1536]{1,0:T(8,128)(2,1)S(1)}, bf16[512,768]{1,0:T(8,128)(2,1)S(1)}) custom-call(s32[2]{0:T(128)S(1)} %pad_add_fusion.place_ref, bf16[512,384]{1,0:T(8,128)(2,1)S(1)} %copy-done.8, ...), custom_call_target="tpu_custom_call" | custom-call | flops 10800000000 | bytes 32400000 | tf_op jit(solution)/shard_map/pallas_call | solution.py:56
  51.5 4.1 %shard_map.255 = (bf16[8,48,768]{2,1,0:T(8,128)(2,1)S(1)}, bf16[8,48,768]{2,1,0:T(8,128)(2,1)S(1)}, bf16[8,48,768]{2,1,0:T(8,128)(2,1)S(1)}, bf16[8,48,768]{2,1,...) custom-call(s32[2]{0:T(128)S(1)} %pad_add_fusion.place_ref, ...), custom_call_target="tpu_custom_call" | custom-call | flops 4000000000 | bytes 12000000 | tf_op jit(solution)/shard_map/pallas_call | solution.py:56
  55.6 3.8 %shard_map.256 = (f32[512,384]{1,0:T(8,128)S(1)}, bf16[512,768]{1,0:T(8,128)(2,1)S(1)}, bf16[512,384]{1,0:T(8,128)(2,1)S(1)}, f32[8,768]{1,0:T(8,128)S(1)}, bf16[80,384]{1,0:T(8,128)(2,1)S(1)}) custom-call(s32[2]{0:T(128)S(1)} %pad_add_fusion.place_ref, bf16[512,768]{1,0:T(8,128)(2,1)S(1)} %get-tuple-element.210.part_ref, ...), custom_call_target="tpu_custom_call" | custom-call | flops 3200000000 | bytes 9600000 | tf_op jit(solution)/shard_map/pallas_call | solution.py:56
  59.6 1.0 collective-permute-start.13
  60.5 2.8 %collective-permute-start.12 = (bf16[80,384]{1,0:T(8,128)(2,1)S(1)}, bf16[80,384]{1,0:T(8,128)(2,1)S(1)}, u32[]{:S(2)}, u32[]{:S(2)}) collective-permute-start(bf16[80,384]{1,0:T(8,128)(2,1)S(1)} %get-tuple-element.221.refs_0_), channel_id=1, source_target_pairs={{0,6},{2,0},{4,2},{6,4},{8,14},{10,8},{12,10},{14,12},{16,22},{18,... | collective-permute-start | bytes 184328 | tf_op jit(solution)/shard_map/ppermute | solution.py:88
  63.3 2.4 %shard_map.257 = (bf16[8,48,768]{2,1,0:T(8,128)(2,1)S(1)}, bf16[8,48,768]{2,1,0:T(8,128)(2,1)S(1)}, bf16[8,48,768]{2,1,0:T(8,128)(2,1)S(1)}, bf16[8,48,768]{2,1,0:T(8,128)(2,1)S(1)}) custom-call(s32[2]{0:T(128)S(1)} %pad_add_fusion.place_ref, bf16[512,768]{1,0:T(8,128)(2,1)S(1)} %get-tuple-element.218.refs_0_, bf16[512,1536]{1,0:T(8,128)(2,1)S(1)} %get-tuple-element.219.refs_1_), custom_call_target="tpu_custom_call" | custom-call | flops 2500000000 | bytes 7500000 | tf_op jit(solution)/shard_map/pallas_call | solution.py:56
  66.6 1.3 collective-permute-start.17
  67.9 2.4 %collective-permute-start.16 = (bf16[80,384]{1,0:T(8,128)(2,1)S(1)}, bf16[80,384]{1,0:T(8,128)(2,1)S(1)}, u32[]{:S(2)}, u32[]{:S(2)}) collective-permute-start(bf16[80,384]{1,0:T(8,128)(2,1)S(1)} %get-tuple-element.234.refs_0_), channel_id=1, source_target_pairs={{0,24},{2,26},{4,28},{6,30},{8,0},{10,2},{12,4},{14,6},{16,8},{18,... | collective-permute-start | bytes 184328 | tf_op jit(solution)/shard_map/ppermute | solution.py:88
  70.3 2.5 %collective-permute-start.19 = (bf16[8,48,768]{2,1,0:T(8,128)(2,1)S(1)}, bf16[8,48,768]{2,1,0:T(8,128)(2,1)S(1)}, u32[]{:S(2)}, u32[]{:S(2)}) collective-permute-start(bf16[8,48,768]{2,1,0:T(8,128)(2,1)S(1)} %get-tuple-element.246), channel_id=1, source_target_pairs={{0,2},{2,0},{4,6},{6,4},{8,10},{10,8},{12,14},{14,12},{16,18},{18,... | collective-permute-start | bytes 1769480 | tf_op jit(solution)/shard_map/ppermute | solution.py:123
  73.3 1.1 collective-permute-start.20
  74.5 5.5 %shard_map.259 = (bf16[512,384]{1,0:T(8,128)(2,1)S(1)}, f32[512,384]{1,0:T(8,128)S(1)}, f32[512,384]{1,0:T(8,128)S(1)}) custom-call(bf16[512,384]{1,0:T(8,128)(2,1)S(1)} %get-tuple-element.226.q_ref, bf16[512,384]{1,0:T(8,128)(2,1)S(1)} %get-tuple-element.198.k_ref, bf16[512,384]{1,0:T(8,128)(2,1)S(1)} %get-tuple-element.187.v_ref, ...), custom_call_target="tpu_custom_call" | custom-call | flops 5600000000 | bytes 16800000 | tf_op jit(solution)/shard_map/pallas_call | solution.py:56
  80.0 3.4 %shard_map.260 = (bf16[512,384]{1,0:T(8,128)(2,1)S(1)}, f32[3,640,128]{2,1,0:T(8,128)S(1)}, bf16[64,384]{1,0:T(8,128)(2,1)S(1)}, f32[3,64,8,128]{3,2,1,0:T(8,128...) custom-call(s32[2]{0:T(128)S(1)} %pad_add_fusion.place_ref, f32[512,384]{1,0:T(8,128)S(1)} %get-tuple-element.229.dk_ref, ...), custom_call_target="tpu_custom_call" | custom-call | flops 2400000000 | bytes 7200000 | tf_op jit(solution)/shard_map/pallas_call | solution.py:56
  83.4 1.3 collective-permute-start.21
  84.7 2.6 %shard_map.261 = (bf16[8,48,640]{2,1,0:T(8,128)(2,1)S(1)}, bf16[8,48,640]{2,1,0:T(8,128)(2,1)S(1)}, bf16[8,48,512]{2,1,0:T(8,128)(2,1)S(1)}, bf16[8,48,512]{2,1,0:T(8,128)(2,1)S(1)}) custom-call(s32[2]{0:T(128)S(1)} %pad_add_fusion.place_ref, bf16[512,768]{1,0:T(8,128)(2,1)S(1)} %get-tuple-element.247.refs_0_, ...), custom_call_target="tpu_custom_call" | custom-call | flops 2600000000 | bytes 7800000 | tf_op jit(solution)/shard_map/pallas_call | solution.py:56
  87.8 0.9 shard_map.262
  88.7 3.7 %collective-permute-start.23 = (bf16[4,48,768]{2,1,0:T(8,128)(2,1)S(1)}, bf16[4,48,768]{2,1,0:T(8,128)(2,1)S(1)}, u32[]{:S(2)}, u32[]{:S(2)}) collective-permute-start(bf16[4,48,768]{2,1,0:T(8,128)(2,1)S(1)} %get-tuple-element.264), channel_id=1, source_target_pairs={{0,4},{2,6},{4,0},{6,2},{8,12},{10,14},{12,8},{14,10},{16,20},{18,... | collective-permute-start | bytes 884744 | tf_op jit(solution)/shard_map/ppermute | solution.py:123
  92.4 2.0 %collective-permute-start.22 = (bf16[8,48,768]{2,1,0:T(8,128)(2,1)S(1)}, bf16[8,48,768]{2,1,0:T(8,128)(2,1)S(1)}, u32[]{:S(2)}, u32[]{:S(2)}) collective-permute-start(bf16[8,48,768]{2,1,0:T(8,128)(2,1)S(1)} %get-tuple-element.263), channel_id=1, source_target_pairs={{0,2},{2,0},{4,6},{6,4},{8,10},{10,8},{12,14},{14,12},{16,18},{18,... | collective-permute-start | bytes 1769480 | tf_op jit(solution)/shard_map/ppermute | solution.py:123
  94.5 11.7 %shard_map.263 = (f32[512,384]{1,0:T(8,128)S(1)}, f32[80,384]{1,0:T(8,128)S(1)}) custom-call(f32[3,640,128]{2,1,0:T(8,128)S(1)} %get-tuple-element.241.sg_ref, bf16[512,384]{1,0:T(8,128)(2,1)S(1)} %get-tuple-element.181.k_ref, f32[576,128]{1,0:T(8,128)S(1)} %get-tuple-element.242.ahead_ref, bf16[64,384]{1,0:T(8,128)(2,1)S(1)} %copy-done.9, ...), custom_call_target="tpu_custom_call" | custom-call | flops 12000000000 | bytes 36000000 | tf_op jit(solution)/shard_map/pallas_call | solution.py:56
  106.2 0.7 shard_map.264
  107.0 2.5 %collective-permute-start.27 = (bf16[2,48,1536]{2,1,0:T(8,128)(2,1)S(1)}, bf16[2,48,1536]{2,1,0:T(8,128)(2,1)S(1)}, u32[]{:S(2)}, u32[]{:S(2)}) collective-permute-start(bf16[2,48,1536]{2,1,0:T(8,128)(2,1)S(1)} %get-tuple-element.280), channel_id=1, source_target_pairs={{0,8},{2,10},{4,12},{6,14},{8,0},{10,2},{12,4},{14,6},{16,24},{18,... | collective-permute-start | bytes 884744 | tf_op jit(solution)/shard_map/ppermute | solution.py:123
  109.5 0.9 collective-permute-done.22.got_a
  110.4 0.9 shard_map.265
  111.9 1.7 %collective-permute-start.29 = (bf16[4,48,768]{2,1,0:T(8,128)(2,1)S(1)}, bf16[4,48,768]{2,1,0:T(8,128)(2,1)S(1)}, u32[]{:S(2)}, u32[]{:S(2)}) collective-permute-start(bf16[4,48,768]{2,1,0:T(8,128)(2,1)S(1)} %get-tuple-element.284), channel_id=1, source_target_pairs={{0,2},{2,0},{4,6},{6,4},{8,10},{10,8},{12,14},{14,12},{16,18},{18,... | collective-permute-start | bytes 884744 | tf_op jit(solution)/shard_map/ppermute | solution.py:123
  113.7 3.7 %shard_map.266 = (bf16[512,384]{1,0:T(8,128)(2,1)S(1)}, bf16[520,768]{1,0:T(8,128)(2,1)S(1)}) custom-call(s32[2]{0:T(128)S(1)} %pad_add_fusion.place_ref, f32[512,384]{1,0:T(8,128)S(1)} %get-tuple-element.261.grad_ref, bf16[64,384]{1,0:T(8,128)(2,1)S(1)} %collective-permute-done.21.edge_ref, f32[512,128]{1,0:T(8,128)S(1)} %get-tuple-element.178.docc_ref, ...), custom_call_target="tpu_custom_call" | custom-call | flops 3200000000 | bytes 9600000 | tf_op jit(solution)/shard_map/pallas_call | solution.py:56
  118.7 0.7 shard_map.267
  119.4 1.8 %collective-permute-start.32 = (bf16[8,48,640]{2,1,0:T(8,128)(2,1)S(1)}, bf16[8,48,640]{2,1,0:T(8,128)(2,1)S(1)}, u32[]{:S(2)}, u32[]{:S(2)}) collective-permute-start(bf16[8,48,640]{2,1,0:T(8,128)(2,1)S(1)} %get-tuple-element.296), channel_id=1, source_target_pairs={{0,2},{2,0},{4,6},{6,4},{8,10},{10,8},{12,14},{14,12},{16,18},{18,... | collective-permute-start | bytes 1474568 | tf_op jit(solution)/shard_map/ppermute | solution.py:123
  121.9 1.8 %collective-permute-start.30 = (bf16[1,48,1536]{2,1,0:T(8,128)(2,1)S(1)}, bf16[1,48,1536]{2,1,0:T(8,128)(2,1)S(1)}, u32[]{:S(2)}, u32[]{:S(2)}) collective-permute-start(bf16[1,48,1536]{2,1,0:T(8,128)(2,1)S(1)} %get-tuple-element.293), channel_id=1, source_target_pairs={{0,16},{2,18},{4,20},{6,22},{8,24},{10,26},{12,28},{14,30},{16,0},... | collective-permute-start | bytes 442376 | tf_op jit(solution)/shard_map/ppermute | solution.py:123
  123.7 0.8 collective-permute-start.31
  124.9 1.3 shard_map.269
  126.2 3.7 %shard_map.270 = bf16[512,384]{1,0:T(8,128)(2,1)} custom-call(s32[2]{0:T(128)S(1)} %pad_add_fusion.place_ref, bf16[520,768]{1,0:T(8,128)(2,1)S(1)} %get-tuple-element.277.part_ref, bf16[520,768]{1,0:T(8,128)(2,1)S(1)} %collective-permute-done.26.got_ref, bf16[512,384]{1,0:T(8,128)(2,1)S(1)} %copy-done.8, ...), custom_call_target="tpu_custom_call" | custom-call | flops 3200000000 | bytes 9600000 | tf_op jit(solution)/shard_map/pallas_call | solution.py:56
  129.9 3.7 %collective-permute-done.33.got_b = bf16[8,48,512]{2,1,0:T(8,128)(2,1)S(1)} collective-permute-done((bf16[8,48,512]{2,1,0:T(8,128)(2,1)S(1)}, bf16[8,48,512]{2,1,0:T(8,128)(2,1)S(1)}, u32[]{:S(2)}, u32[]{:S(2)}) %collective-permute-start.33) | collective-permute-done | bytes 393248 | tf_op jit(solution)/shard_map/ppermute | solution.py:123
  133.6 0.8 shard_map.271
  135.5 1.0 collective-permute-start.35
  136.5 2.0 %collective-permute-start.36 = (bf16[272,384]{1,0:T(8,128)(2,1)S(1)}, bf16[272,384]{1,0:T(8,128)(2,1)S(1)}, u32[]{:S(2)}, u32[]{:S(2)}) collective-permute-start(bf16[272,384]{1,0:T(8,128)(2,1)S(1)} %get-tuple-element.311), channel_id=1, source_target_pairs={{0,6},{2,0},{4,2},{6,4},{8,14},{10,8},{12,10},{14,12},{16,22},{18,... | collective-permute-start | bytes 626696 | tf_op jit(solution)/shard_map/ppermute | solution.py:88
  138.5 1.3 shard_map.273
  139.7 1.6 collective-permute-start.40
  141.4 2.7 %collective-permute-done.34.refs_1_ = bf16[272,384]{1,0:T(8,128)(2,1)S(1)} collective-permute-done((bf16[272,384]{1,0:T(8,128)(2,1)S(1)}, bf16[272,384]{1,0:T(8,128)(2,1)S(1)}, u32[]{:S(2)}, u32[]{:S(2)}) %collective-permute-start.34) | collective-permute-done | bytes 208928 | tf_op jit(solution)/shard_map/ppermute | solution.py:88
  144.5 1.3 collective-permute-done.35.refs_2_
  146.9 1.4 collective-permute-done.38.got_b
  148.4 2.4 %collective-permute-start.42 = (bf16[128,384]{1,0:T(8,128)(2,1)S(1)}, bf16[128,384]{1,0:T(8,128)(2,1)S(1)}, u32[]{:S(2)}, u32[]{:S(2)}) collective-permute-start(bf16[128,384]{1,0:T(8,128)(2,1)S(1)} %get-tuple-element.328), channel_id=1, source_target_pairs={{0,16},{2,18},{4,20},{6,22},{8,24},{10,26},{12,28},{14,30},{16,0},... | collective-permute-start | bytes 294920 | tf_op jit(solution)/shard_map/ppermute | solution.py:88
  150.8 1.6 collective-permute-start.43
  153.6 1.3 shard_map.276
  154.9 5.2 %collective-permute-done.39.got = bf16[2,48,1152]{2,1,0:T(8,128)(2,1)S(1)} collective-permute-done((bf16[2,48,1152]{2,1,0:T(8,128)(2,1)S(1)}, bf16[2,48,1152]{2,1,0:T(8,128)(2,1)S(1)}, u32[]{:S(2)}, u32[]{:S(2)}) %collective-permute-start.39) | collective-permute-done | bytes 221216 | tf_op jit(solution)/shard_map/ppermute | solution.py:123
  160.7 1.8 %collective-permute-start.44 = (bf16[1,48,1152]{2,1,0:T(8,128)(2,1)S(1)}, bf16[1,48,1152]{2,1,0:T(8,128)(2,1)S(1)}, u32[]{:S(2)}, u32[]{:S(2)}) collective-permute-start(bf16[1,48,1152]{2,1,0:T(8,128)(2,1)S(1)} %get-tuple-element.334), channel_id=1, source_target_pairs={{0,16},{2,18},{4,20},{6,22},{8,24},{10,26},{12,28},{14,30},{16,0},... | collective-permute-start | bytes 331784 | tf_op jit(solution)/shard_map/ppermute | solution.py:123
  162.5 1.3 shard_map.278
  163.8 3.8 %collective-permute-done.44.got = bf16[1,48,1152]{2,1,0:T(8,128)(2,1)S(1)} collective-permute-done((bf16[1,48,1152]{2,1,0:T(8,128)(2,1)S(1)}, bf16[1,48,1152]{2,1,0:T(8,128)(2,1)S(1)}, u32[]{:S(2)}, u32[]{:S(2)}) %collective-permute-start.44) | collective-permute-done | bytes 110624 | tf_op jit(solution)/shard_map/ppermute | solution.py:123
  167.6 1.2 shard_map.279
  (92 shorter events, 14.1 us)
Async XLA Ops:
  0.6 24.3 %collective-permute-start.2 = (bf16[512,384]{1,0:T(8,128)(2,1)}, bf16[512,384]{1,0:T(8,128)(2,1)S(1)}, u32[]{:S(2)}, u32[]{:S(2)}) collective-permute-start(bf16[512,384]{1,0:T(8,128)(2,1)} %own_ref.6), channel_id=1, source_target_pairs={{0,1},{1,0},{2,3},{3,2},{4,5},{5,4},{6,7},{7,6},{8,9},{9,8},{10,11... | collective-permute-start | bytes 1179656 | tf_op jit(solution)/shard_map/ppermute | solution.py:101
  1.2 5.3 %collective-permute-start = (bf16[512,384]{1,0:T(8,128)(2,1)}, bf16[512,384]{1,0:T(8,128)(2,1)S(1)}, u32[]{:S(2)}, u32[]{:S(2)}) collective-permute-start(bf16[512,384]{1,0:T(8,128)(2,1)} %own_ref.9), channel_id=1, source_target_pairs={{0,1},{1,0},{2,3},{3,2},{4,5},{5,4},{6,7},{7,6},{8,9},{9,8},{10,11... | collective-permute-start | bytes 1179656 | tf_op jit(solution)/shard_map/ppermute | solution.py:101
  1.2 39.5 %collective-permute-start.10 = (bf16[768,384]{1,0:T(8,128)(2,1)}, bf16[768,384]{1,0:T(8,128)(2,1)S(1)}, u32[]{:S(2)}, u32[]{:S(2)}) collective-permute-start(bf16[768,384]{1,0:T(8,128)(2,1)} %out_w_ref.1), channel_id=1, source_target_pairs={{0,1},{1,0},{2,3},{3,2},{4,5},{5,4},{6,7},{7,6},{8,9},{9,8},{10,11... | collective-permute-start | bytes 1769480 | tf_op jit(solution)/shard_map/ppermute | solution.py:101
  2.5 0.7 copy-start
  3.2 0.7 copy-start.14
  3.9 2.6 %copy-start.4 = (bf16[768,384]{1,0:T(8,128)(2,1)S(1)}, bf16[768,384]{1,0:T(8,128)(2,1)}, u32[]{:S(2)}) copy-start(bf16[768,384]{1,0:T(8,128)(2,1)} %wq_ref.3) | copy-start | bytes 1769476
  3.9 2.6 %copy-start.5 = (bf16[768,384]{1,0:T(8,128)(2,1)S(1)}, bf16[768,384]{1,0:T(8,128)(2,1)}, u32[]{:S(2)}) copy-start(bf16[768,384]{1,0:T(8,128)(2,1)} %wk_ref.3) | copy-start | bytes 1769476
  3.9 2.6 %copy-start.6 = (bf16[768,384]{1,0:T(8,128)(2,1)S(1)}, bf16[768,384]{1,0:T(8,128)(2,1)}, u32[]{:S(2)}) copy-start(bf16[768,384]{1,0:T(8,128)(2,1)} %wv_ref.3) | copy-start | bytes 1769476
  3.9 2.6 %copy-start.8 = (bf16[512,384]{1,0:T(8,128)(2,1)S(1)}, bf16[512,384]{1,0:T(8,128)(2,1)}, u32[]{:S(2)}) copy-start(bf16[512,384]{1,0:T(8,128)(2,1)} %own_ref.9) | copy-start | bytes 1179652
  3.9 2.6 %copy-start.10 = (f32[768]{0:T(1024)S(1)}, f32[768]{0:T(1024)}, u32[]{:S(2)}) copy-start(f32[768]{0:T(1024)} %bias_ref.2) | copy-start | bytes 9220
  3.9 2.6 %copy-start.13 = (f32[768]{0:T(1024)S(1)}, f32[768]{0:T(1024)}, u32[]{:S(2)}) copy-start(f32[768]{0:T(1024)} %gain_ref.7) | copy-start | bytes 9220
  6.6 8.1 %copy-start.9 = (bf16[64,384]{1,0:T(8,128)(2,1)S(1)}, bf16[64,384]{1,0:T(8,128)(2,1)}, u32[]{:S(2)}) copy-start(bf16[64,384]{1,0:T(8,128)(2,1)} %taps_ref.7) | copy-start | bytes 147460
  10.2 10.0 %collective-permute-start.1 = (bf16[64,384]{1,0:T(8,128)(2,1)S(1)}, bf16[64,384]{1,0:T(8,128)(2,1)S(1)}, u32[]{:S(2)}, u32[]{:S(2)}) collective-permute-start(bf16[64,384]{1,0:T(8,128)(2,1)S(1)} %get-tuple-element.184), channel_id=1, source_target_pairs={{0,2},{2,4},{4,6},{6,8},{8,10},{10,12},{12,14},{14,16},{16,18},{18... | collective-permute-start | bytes 147464 | tf_op jit(solution)/shard_map/ppermute | solution.py:106
  20.2 4.8 %copy-start.2 = (bf16[768,1536]{1,0:T(8,128)(2,1)S(1)}, bf16[768,1536]{1,0:T(8,128)(2,1)}, u32[]{:S(2)}) copy-start(bf16[768,1536]{1,0:T(8,128)(2,1)} %down_ref.3) | copy-start | bytes 7077892
  20.2 4.8 %copy-start.7 = (bf16[512,384]{1,0:T(8,128)(2,1)S(1)}, bf16[512,384]{1,0:T(8,128)(2,1)}, u32[]{:S(2)}) copy-start(bf16[512,384]{1,0:T(8,128)(2,1)} %own_ref.6) | copy-start | bytes 1179652
  21.3 6.2 %collective-permute-start.5 = (bf16[80,384]{1,0:T(8,128)(2,1)S(1)}, bf16[80,384]{1,0:T(8,128)(2,1)S(1)}, u32[]{:S(2)}, u32[]{:S(2)}) collective-permute-start(bf16[80,384]{1,0:T(8,128)(2,1)S(1)} %get-tuple-element.192.refs_0_), channel_id=1, source_target_pairs={{0,6},{2,0},{4,2},{6,4},{8,14},{10,8},{12,10},{14,12},{16,22},{18,... | collective-permute-start | bytes 184328 | tf_op jit(solution)/shard_map/ppermute | solution.py:88
  23.8 4.9 %collective-permute-start.4 = (bf16[80,384]{1,0:T(8,128)(2,1)S(1)}, bf16[80,384]{1,0:T(8,128)(2,1)S(1)}, u32[]{:S(2)}, u32[]{:S(2)}) collective-permute-start(bf16[80,384]{1,0:T(8,128)(2,1)S(1)} %get-tuple-element.192.refs_0_), channel_id=1, source_target_pairs={{0,4},{2,6},{4,0},{6,2},{8,12},{10,14},{12,8},{14,10},{16,20},{18,... | collective-permute-start | bytes 184328 | tf_op jit(solution)/shard_map/ppermute | solution.py:88
  24.3 5.1 %collective-permute-start.3 = (bf16[80,384]{1,0:T(8,128)(2,1)S(1)}, bf16[80,384]{1,0:T(8,128)(2,1)S(1)}, u32[]{:S(2)}, u32[]{:S(2)}) collective-permute-start(bf16[80,384]{1,0:T(8,128)(2,1)S(1)} %get-tuple-element.192.refs_0_), channel_id=1, source_target_pairs={{0,2},{2,4},{4,6},{6,0},{8,10},{10,12},{12,14},{14,8},{16,18},{18,... | collective-permute-start | bytes 184328 | tf_op jit(solution)/shard_map/ppermute | solution.py:88
  30.1 7.6 %collective-permute-start.8 = (bf16[80,384]{1,0:T(8,128)(2,1)S(1)}, bf16[80,384]{1,0:T(8,128)(2,1)S(1)}, u32[]{:S(2)}, u32[]{:S(2)}) collective-permute-start(bf16[80,384]{1,0:T(8,128)(2,1)S(1)} %get-tuple-element.203.refs_0_), channel_id=1, source_target_pairs={{0,24},{2,26},{4,28},{6,30},{8,0},{10,2},{12,4},{14,6},{16,8},{18,... | collective-permute-start | bytes 184328 | tf_op jit(solution)/shard_map/ppermute | solution.py:88
  33.8 5.1 %collective-permute-start.7 = (bf16[80,384]{1,0:T(8,128)(2,1)S(1)}, bf16[80,384]{1,0:T(8,128)(2,1)S(1)}, u32[]{:S(2)}, u32[]{:S(2)}) collective-permute-start(bf16[80,384]{1,0:T(8,128)(2,1)S(1)} %get-tuple-element.203.refs_0_), channel_id=1, source_target_pairs={{0,16},{2,18},{4,20},{6,22},{8,24},{10,26},{12,28},{14,30},{16,0},... | collective-permute-start | bytes 184328 | tf_op jit(solution)/shard_map/ppermute | solution.py:88
  33.8 6.0 %collective-permute-start.6 = (bf16[80,384]{1,0:T(8,128)(2,1)S(1)}, bf16[80,384]{1,0:T(8,128)(2,1)S(1)}, u32[]{:S(2)}, u32[]{:S(2)}) collective-permute-start(bf16[80,384]{1,0:T(8,128)(2,1)S(1)} %get-tuple-element.203.refs_0_), channel_id=1, source_target_pairs={{0,8},{2,10},{4,12},{6,14},{8,16},{10,18},{12,20},{14,22},{16,24},... | collective-permute-start | bytes 184328 | tf_op jit(solution)/shard_map/ppermute | solution.py:88
  39.8 2.6 %copy-start.1 = (bf16[768,1536]{1,0:T(8,128)(2,1)S(1)}, bf16[768,1536]{1,0:T(8,128)(2,1)}, u32[]{:S(2)}) copy-start(bf16[768,1536]{1,0:T(8,128)(2,1)} %up_ref.1) | copy-start | bytes 7077892
  39.8 2.6 %copy-start.3 = (bf16[768,384]{1,0:T(8,128)(2,1)S(1)}, bf16[768,384]{1,0:T(8,128)(2,1)}, u32[]{:S(2)}) copy-start(bf16[768,384]{1,0:T(8,128)(2,1)} %out_w_ref.1) | copy-start | bytes 1769476
  39.8 2.6 %copy-start.11 = (f32[768]{0:T(1024)S(1)}, f32[768]{0:T(1024)}, u32[]{:S(2)}) copy-start(f32[768]{0:T(1024)} %bias_ref.3) | copy-start | bytes 9220
  39.8 2.6 %copy-start.12 = (f32[768]{0:T(1024)S(1)}, f32[768]{0:T(1024)}, u32[]{:S(2)}) copy-start(f32[768]{0:T(1024)} %gain_ref.6) | copy-start | bytes 9220
  40.7 1.8 %collective-permute-start.9 = (bf16[512,384]{1,0:T(8,128)(2,1)S(1)}, bf16[512,384]{1,0:T(8,128)(2,1)S(1)}, u32[]{:S(2)}, u32[]{:S(2)}) collective-permute-start(bf16[512,384]{1,0:T(8,128)(2,1)S(1)} %get-tuple-element.209.mix_own_ref.refs_3_), channel_id=1, source_target_pairs={{0,1},{1,0},{2,3},{3,2},{4,5},{5,4},{6,7},{7,6},{8,9},{9,8},{10,11... | collective-permute-start | bytes 1179656 | tf_op jit(solution)/shard_map/ppermute | solution.py:101
  51.3 4.3 %collective-permute-start.11 = (bf16[512,768]{1,0:T(8,128)(2,1)S(1)}, bf16[512,768]{1,0:T(8,128)(2,1)S(1)}, u32[]{:S(2)}, u32[]{:S(2)}) collective-permute-start(bf16[512,768]{1,0:T(8,128)(2,1)S(1)} %get-tuple-element.210.part_ref), channel_id=1, source_target_pairs={{0,1},{1,0},{2,3},{3,2},{4,5},{5,4},{6,7},{7,6},{8,9},{9,8},{10,11... | collective-permute-start | bytes 2359304 | tf_op jit(solution)/shard_map/ppermute | solution.py:101
  59.4 6.4 %collective-permute-start.14 = (bf16[80,384]{1,0:T(8,128)(2,1)S(1)}, bf16[80,384]{1,0:T(8,128)(2,1)S(1)}, u32[]{:S(2)}, u32[]{:S(2)}) collective-permute-start(bf16[80,384]{1,0:T(8,128)(2,1)S(1)} %get-tuple-element.221.refs_0_), channel_id=1, source_target_pairs={{0,2},{2,4},{4,6},{6,0},{8,10},{10,12},{12,14},{14,8},{16,18},{18,... | collective-permute-start | bytes 184328 | tf_op jit(solution)/shard_map/ppermute | solution.py:88
  59.6 6.2 %collective-permute-start.13 = (bf16[80,384]{1,0:T(8,128)(2,1)S(1)}, bf16[80,384]{1,0:T(8,128)(2,1)S(1)}, u32[]{:S(2)}, u32[]{:S(2)}) collective-permute-start(bf16[80,384]{1,0:T(8,128)(2,1)S(1)} %get-tuple-element.221.refs_0_), channel_id=1, source_target_pairs={{0,4},{2,6},{4,0},{6,2},{8,12},{10,14},{12,8},{14,10},{16,20},{18,... | collective-permute-start | bytes 184328 | tf_op jit(solution)/shard_map/ppermute | solution.py:88
  60.5 5.2 %collective-permute-start.12 = (bf16[80,384]{1,0:T(8,128)(2,1)S(1)}, bf16[80,384]{1,0:T(8,128)(2,1)S(1)}, u32[]{:S(2)}, u32[]{:S(2)}) collective-permute-start(bf16[80,384]{1,0:T(8,128)(2,1)S(1)} %get-tuple-element.221.refs_0_), channel_id=1, source_target_pairs={{0,6},{2,0},{4,2},{6,4},{8,14},{10,8},{12,10},{14,12},{16,22},{18,... | collective-permute-start | bytes 184328 | tf_op jit(solution)/shard_map/ppermute | solution.py:88
  66.4 6.9 %collective-permute-start.18 = (bf16[80,384]{1,0:T(8,128)(2,1)S(1)}, bf16[80,384]{1,0:T(8,128)(2,1)S(1)}, u32[]{:S(2)}, u32[]{:S(2)}) collective-permute-start(bf16[80,384]{1,0:T(8,128)(2,1)S(1)} %get-tuple-element.234.refs_0_), channel_id=1, source_target_pairs={{0,8},{2,10},{4,12},{6,14},{8,16},{10,18},{12,20},{14,22},{16,24},... | collective-permute-start | bytes 184328 | tf_op jit(solution)/shard_map/ppermute | solution.py:88
  66.5 13.5 %collective-permute-start.15 = (bf16[512,384]{1,0:T(8,128)(2,1)S(1)}, bf16[512,384]{1,0:T(8,128)(2,1)S(1)}, u32[]{:S(2)}, u32[]{:S(2)}) collective-permute-start(bf16[512,384]{1,0:T(8,128)(2,1)S(1)} %get-tuple-element.232), channel_id=1, source_target_pairs={{0,1},{1,0},{2,3},{3,2},{4,5},{5,4},{6,7},{7,6},{8,9},{9,8},{10,11... | collective-permute-start | bytes 1179656 | tf_op jit(solution)/shard_map/ppermute | solution.py:101
  66.6 13.4 %collective-permute-start.17 = (bf16[80,384]{1,0:T(8,128)(2,1)S(1)}, bf16[80,384]{1,0:T(8,128)(2,1)S(1)}, u32[]{:S(2)}, u32[]{:S(2)}) collective-permute-start(bf16[80,384]{1,0:T(8,128)(2,1)S(1)} %get-tuple-element.234.refs_0_), channel_id=1, source_target_pairs={{0,16},{2,18},{4,20},{6,22},{8,24},{10,26},{12,28},{14,30},{16,0},... | collective-permute-start | bytes 184328 | tf_op jit(solution)/shard_map/ppermute | solution.py:88
  67.9 12.1 %collective-permute-start.16 = (bf16[80,384]{1,0:T(8,128)(2,1)S(1)}, bf16[80,384]{1,0:T(8,128)(2,1)S(1)}, u32[]{:S(2)}, u32[]{:S(2)}) collective-permute-start(bf16[80,384]{1,0:T(8,128)(2,1)S(1)} %get-tuple-element.234.refs_0_), channel_id=1, source_target_pairs={{0,24},{2,26},{4,28},{6,30},{8,0},{10,2},{12,4},{14,6},{16,8},{18,... | collective-permute-start | bytes 184328 | tf_op jit(solution)/shard_map/ppermute | solution.py:88
  70.3 16.9 %collective-permute-start.19 = (bf16[8,48,768]{2,1,0:T(8,128)(2,1)S(1)}, bf16[8,48,768]{2,1,0:T(8,128)(2,1)S(1)}, u32[]{:S(2)}, u32[]{:S(2)}) collective-permute-start(bf16[8,48,768]{2,1,0:T(8,128)(2,1)S(1)} %get-tuple-element.246), channel_id=1, source_target_pairs={{0,2},{2,0},{4,6},{6,4},{8,10},{10,8},{12,14},{14,12},{16,18},{18,... | collective-permute-start | bytes 1769480 | tf_op jit(solution)/shard_map/ppermute | solution.py:123
  73.3 14.5 %collective-permute-start.20 = (bf16[8,48,768]{2,1,0:T(8,128)(2,1)S(1)}, bf16[8,48,768]{2,1,0:T(8,128)(2,1)S(1)}, u32[]{:S(2)}, u32[]{:S(2)}) collective-permute-start(bf16[8,48,768]{2,1,0:T(8,128)(2,1)S(1)} %get-tuple-element.256), channel_id=1, source_target_pairs={{0,4},{2,6},{4,0},{6,2},{8,12},{10,14},{12,8},{14,10},{16,20},{18,... | collective-permute-start | bytes 1769480 | tf_op jit(solution)/shard_map/ppermute | solution.py:123
  83.4 27.9 %collective-permute-start.21 = (bf16[64,384]{1,0:T(8,128)(2,1)S(1)}, bf16[64,384]{1,0:T(8,128)(2,1)S(1)}, u32[]{:S(2)}, u32[]{:S(2)}) collective-permute-start(bf16[64,384]{1,0:T(8,128)(2,1)S(1)} %get-tuple-element.250), channel_id=1, source_target_pairs={{2,0},{4,2},{6,4},{8,6},{10,8},{12,10},{14,12},{16,14},{18,16},{20... | collective-permute-start | bytes 147464 | tf_op jit(solution)/shard_map/ppermute | solution.py:106
  88.7 17.5 %collective-permute-start.23 = (bf16[4,48,768]{2,1,0:T(8,128)(2,1)S(1)}, bf16[4,48,768]{2,1,0:T(8,128)(2,1)S(1)}, u32[]{:S(2)}, u32[]{:S(2)}) collective-permute-start(bf16[4,48,768]{2,1,0:T(8,128)(2,1)S(1)} %get-tuple-element.264), channel_id=1, source_target_pairs={{0,4},{2,6},{4,0},{6,2},{8,12},{10,14},{12,8},{14,10},{16,20},{18,... | collective-permute-start | bytes 884744 | tf_op jit(solution)/shard_map/ppermute | solution.py:123
  92.4 13.8 %collective-permute-start.24 = (bf16[4,48,768]{2,1,0:T(8,128)(2,1)S(1)}, bf16[4,48,768]{2,1,0:T(8,128)(2,1)S(1)}, u32[]{:S(2)}, u32[]{:S(2)}) collective-permute-start(bf16[4,48,768]{2,1,0:T(8,128)(2,1)S(1)} %get-tuple-element.267), channel_id=1, source_target_pairs={{0,2},{2,0},{4,6},{6,4},{8,10},{10,8},{12,14},{14,12},{16,18},{18,... | collective-permute-start | bytes 884744 | tf_op jit(solution)/shard_map/ppermute | solution.py:123
  92.4 17.9 %collective-permute-start.22 = (bf16[8,48,768]{2,1,0:T(8,128)(2,1)S(1)}, bf16[8,48,768]{2,1,0:T(8,128)(2,1)S(1)}, u32[]{:S(2)}, u32[]{:S(2)}) collective-permute-start(bf16[8,48,768]{2,1,0:T(8,128)(2,1)S(1)} %get-tuple-element.263), channel_id=1, source_target_pairs={{0,2},{2,0},{4,6},{6,4},{8,10},{10,8},{12,14},{14,12},{16,18},{18,... | collective-permute-start | bytes 1769480 | tf_op jit(solution)/shard_map/ppermute | solution.py:123
  94.4 15.9 %collective-permute-start.25 = (bf16[8,48,768]{2,1,0:T(8,128)(2,1)S(1)}, bf16[8,48,768]{2,1,0:T(8,128)(2,1)S(1)}, u32[]{:S(2)}, u32[]{:S(2)}) collective-permute-start(bf16[8,48,768]{2,1,0:T(8,128)(2,1)S(1)} %get-tuple-element.273), channel_id=1, source_target_pairs={{0,4},{2,6},{4,0},{6,2},{8,12},{10,14},{12,8},{14,10},{16,20},{18,... | collective-permute-start | bytes 1769480 | tf_op jit(solution)/shard_map/ppermute | solution.py:123
  107.0 12.4 %collective-permute-start.27 = (bf16[2,48,1536]{2,1,0:T(8,128)(2,1)S(1)}, bf16[2,48,1536]{2,1,0:T(8,128)(2,1)S(1)}, u32[]{:S(2)}, u32[]{:S(2)}) collective-permute-start(bf16[2,48,1536]{2,1,0:T(8,128)(2,1)S(1)} %get-tuple-element.280), channel_id=1, source_target_pairs={{0,8},{2,10},{4,12},{6,14},{8,0},{10,2},{12,4},{14,6},{16,24},{18,... | collective-permute-start | bytes 884744 | tf_op jit(solution)/shard_map/ppermute | solution.py:123
  111.3 6.8 %collective-permute-start.28 = (bf16[4,48,768]{2,1,0:T(8,128)(2,1)S(1)}, bf16[4,48,768]{2,1,0:T(8,128)(2,1)S(1)}, u32[]{:S(2)}, u32[]{:S(2)}) collective-permute-start(bf16[4,48,768]{2,1,0:T(8,128)(2,1)S(1)} %get-tuple-element.281), channel_id=1, source_target_pairs={{0,4},{2,6},{4,0},{6,2},{8,12},{10,14},{12,8},{14,10},{16,20},{18,... | collective-permute-start | bytes 884744 | tf_op jit(solution)/shard_map/ppermute | solution.py:123
  111.9 6.7 %collective-permute-start.29 = (bf16[4,48,768]{2,1,0:T(8,128)(2,1)S(1)}, bf16[4,48,768]{2,1,0:T(8,128)(2,1)S(1)}, u32[]{:S(2)}, u32[]{:S(2)}) collective-permute-start(bf16[4,48,768]{2,1,0:T(8,128)(2,1)S(1)} %get-tuple-element.284), channel_id=1, source_target_pairs={{0,2},{2,0},{4,6},{6,4},{8,10},{10,8},{12,14},{14,12},{16,18},{18,... | collective-permute-start | bytes 884744 | tf_op jit(solution)/shard_map/ppermute | solution.py:123
  117.3 7.6 %collective-permute-start.26 = (bf16[520,768]{1,0:T(8,128)(2,1)S(1)}, bf16[520,768]{1,0:T(8,128)(2,1)S(1)}, u32[]{:S(2)}, u32[]{:S(2)}) collective-permute-start(bf16[520,768]{1,0:T(8,128)(2,1)S(1)} %get-tuple-element.277.part_ref), channel_id=1, source_target_pairs={{0,1},{1,0},{2,3},{3,2},{4,5},{5,4},{6,7},{7,6},{8,9},{9,8},{10,11... | collective-permute-start | bytes 2396168 | tf_op jit(solution)/shard_map/ppermute | solution.py:101
  119.4 14.2 %collective-permute-start.32 = (bf16[8,48,640]{2,1,0:T(8,128)(2,1)S(1)}, bf16[8,48,640]{2,1,0:T(8,128)(2,1)S(1)}, u32[]{:S(2)}, u32[]{:S(2)}) collective-permute-start(bf16[8,48,640]{2,1,0:T(8,128)(2,1)S(1)} %get-tuple-element.296), channel_id=1, source_target_pairs={{0,2},{2,0},{4,6},{6,4},{8,10},{10,8},{12,14},{14,12},{16,18},{18,... | collective-permute-start | bytes 1474568 | tf_op jit(solution)/shard_map/ppermute | solution.py:123
  121.9 13.2 %collective-permute-start.30 = (bf16[1,48,1536]{2,1,0:T(8,128)(2,1)S(1)}, bf16[1,48,1536]{2,1,0:T(8,128)(2,1)S(1)}, u32[]{:S(2)}, u32[]{:S(2)}) collective-permute-start(bf16[1,48,1536]{2,1,0:T(8,128)(2,1)S(1)} %get-tuple-element.293), channel_id=1, source_target_pairs={{0,16},{2,18},{4,20},{6,22},{8,24},{10,26},{12,28},{14,30},{16,0},... | collective-permute-start | bytes 442376 | tf_op jit(solution)/shard_map/ppermute | solution.py:123
  123.7 10.8 %collective-permute-start.31 = (bf16[2,48,1536]{2,1,0:T(8,128)(2,1)S(1)}, bf16[2,48,1536]{2,1,0:T(8,128)(2,1)S(1)}, u32[]{:S(2)}, u32[]{:S(2)}) collective-permute-start(bf16[2,48,1536]{2,1,0:T(8,128)(2,1)S(1)} %get-tuple-element.294), channel_id=1, source_target_pairs={{0,8},{2,10},{4,12},{6,14},{8,0},{10,2},{12,4},{14,6},{16,24},{18,... | collective-permute-start | bytes 884744 | tf_op jit(solution)/shard_map/ppermute | solution.py:123
  124.5 9.1 %collective-permute-start.33 = (bf16[8,48,512]{2,1,0:T(8,128)(2,1)S(1)}, bf16[8,48,512]{2,1,0:T(8,128)(2,1)S(1)}, u32[]{:S(2)}, u32[]{:S(2)}) collective-permute-start(bf16[8,48,512]{2,1,0:T(8,128)(2,1)S(1)} %get-tuple-element.300), channel_id=1, source_target_pairs={{0,4},{2,6},{4,0},{6,2},{8,12},{10,14},{12,8},{14,10},{16,20},{18,... | collective-permute-start | bytes 1179656 | tf_op jit(solution)/shard_map/ppermute | solution.py:123
  135.1 9.0 %collective-permute-start.34 = (bf16[272,384]{1,0:T(8,128)(2,1)S(1)}, bf16[272,384]{1,0:T(8,128)(2,1)S(1)}, u32[]{:S(2)}, u32[]{:S(2)}) collective-permute-start(bf16[272,384]{1,0:T(8,128)(2,1)S(1)} %get-tuple-element.307), channel_id=1, source_target_pairs={{0,2},{2,4},{4,6},{6,0},{8,10},{10,12},{12,14},{14,8},{16,18},{18,... | collective-permute-start | bytes 626696 | tf_op jit(solution)/shard_map/ppermute | solution.py:88
  135.5 10.3 %collective-permute-start.35 = (bf16[272,384]{1,0:T(8,128)(2,1)S(1)}, bf16[272,384]{1,0:T(8,128)(2,1)S(1)}, u32[]{:S(2)}, u32[]{:S(2)}) collective-permute-start(bf16[272,384]{1,0:T(8,128)(2,1)S(1)} %get-tuple-element.309), channel_id=1, source_target_pairs={{0,4},{2,6},{4,0},{6,2},{8,12},{10,14},{12,8},{14,10},{16,20},{18,... | collective-permute-start | bytes 626696 | tf_op jit(solution)/shard_map/ppermute | solution.py:88
  136.5 9.7 %collective-permute-start.36 = (bf16[272,384]{1,0:T(8,128)(2,1)S(1)}, bf16[272,384]{1,0:T(8,128)(2,1)S(1)}, u32[]{:S(2)}, u32[]{:S(2)}) collective-permute-start(bf16[272,384]{1,0:T(8,128)(2,1)S(1)} %get-tuple-element.311), channel_id=1, source_target_pairs={{0,6},{2,0},{4,2},{6,4},{8,14},{10,8},{12,10},{14,12},{16,22},{18,... | collective-permute-start | bytes 626696 | tf_op jit(solution)/shard_map/ppermute | solution.py:88
  139.7 13.4 %collective-permute-start.40 = (bf16[1,48,1536]{2,1,0:T(8,128)(2,1)S(1)}, bf16[1,48,1536]{2,1,0:T(8,128)(2,1)S(1)}, u32[]{:S(2)}, u32[]{:S(2)}) collective-permute-start(bf16[1,48,1536]{2,1,0:T(8,128)(2,1)S(1)} %get-tuple-element.321), channel_id=1, source_target_pairs={{0,16},{2,18},{4,20},{6,22},{8,24},{10,26},{12,28},{14,30},{16,0},... | collective-permute-start | bytes 442376 | tf_op jit(solution)/shard_map/ppermute | solution.py:123
  141.4 7.0 %collective-permute-start.38 = (bf16[4,48,512]{2,1,0:T(8,128)(2,1)S(1)}, bf16[4,48,512]{2,1,0:T(8,128)(2,1)S(1)}, u32[]{:S(2)}, u32[]{:S(2)}) collective-permute-start(bf16[4,48,512]{2,1,0:T(8,128)(2,1)S(1)} %get-tuple-element.317), channel_id=1, source_target_pairs={{0,2},{2,0},{4,6},{6,4},{8,10},{10,8},{12,14},{14,12},{16,18},{18,... | collective-permute-start | bytes 589832 | tf_op jit(solution)/shard_map/ppermute | solution.py:123
  144.1 8.3 %collective-permute-start.37 = (bf16[4,48,640]{2,1,0:T(8,128)(2,1)S(1)}, bf16[4,48,640]{2,1,0:T(8,128)(2,1)S(1)}, u32[]{:S(2)}, u32[]{:S(2)}) collective-permute-start(bf16[4,48,640]{2,1,0:T(8,128)(2,1)S(1)} %get-tuple-element.314), channel_id=1, source_target_pairs={{0,4},{2,6},{4,0},{6,2},{8,12},{10,14},{12,8},{14,10},{16,20},{18,... | collective-permute-start | bytes 737288 | tf_op jit(solution)/shard_map/ppermute | solution.py:123
  148.3 12.4 %collective-permute-start.41 = (bf16[128,384]{1,0:T(8,128)(2,1)S(1)}, bf16[128,384]{1,0:T(8,128)(2,1)S(1)}, u32[]{:S(2)}, u32[]{:S(2)}) collective-permute-start(bf16[128,384]{1,0:T(8,128)(2,1)S(1)} %get-tuple-element.326), channel_id=1, source_target_pairs={{0,8},{2,10},{4,12},{6,14},{8,16},{10,18},{12,20},{14,22},{16,24},... | collective-permute-start | bytes 294920 | tf_op jit(solution)/shard_map/ppermute | solution.py:88
  148.4 12.3 %collective-permute-start.42 = (bf16[128,384]{1,0:T(8,128)(2,1)S(1)}, bf16[128,384]{1,0:T(8,128)(2,1)S(1)}, u32[]{:S(2)}, u32[]{:S(2)}) collective-permute-start(bf16[128,384]{1,0:T(8,128)(2,1)S(1)} %get-tuple-element.328), channel_id=1, source_target_pairs={{0,16},{2,18},{4,20},{6,22},{8,24},{10,26},{12,28},{14,30},{16,0},... | collective-permute-start | bytes 294920 | tf_op jit(solution)/shard_map/ppermute | solution.py:88
  150.8 9.9 %collective-permute-start.43 = (bf16[128,384]{1,0:T(8,128)(2,1)S(1)}, bf16[128,384]{1,0:T(8,128)(2,1)S(1)}, u32[]{:S(2)}, u32[]{:S(2)}) collective-permute-start(bf16[128,384]{1,0:T(8,128)(2,1)S(1)} %get-tuple-element.330), channel_id=1, source_target_pairs={{0,24},{2,26},{4,28},{6,30},{8,0},{10,2},{12,4},{14,6},{16,8},{18,... | collective-permute-start | bytes 294920 | tf_op jit(solution)/shard_map/ppermute | solution.py:88
  153.1 6.9 %collective-permute-start.39 = (bf16[2,48,1152]{2,1,0:T(8,128)(2,1)S(1)}, bf16[2,48,1152]{2,1,0:T(8,128)(2,1)S(1)}, u32[]{:S(2)}, u32[]{:S(2)}) collective-permute-start(bf16[2,48,1152]{2,1,0:T(8,128)(2,1)S(1)} %get-tuple-element.320), channel_id=1, source_target_pairs={{0,8},{2,10},{4,12},{6,14},{8,0},{10,2},{12,4},{14,6},{16,24},{18,... | collective-permute-start | bytes 663560 | tf_op jit(solution)/shard_map/ppermute | solution.py:123
  160.7 6.9 %collective-permute-start.44 = (bf16[1,48,1152]{2,1,0:T(8,128)(2,1)S(1)}, bf16[1,48,1152]{2,1,0:T(8,128)(2,1)S(1)}, u32[]{:S(2)}, u32[]{:S(2)}) collective-permute-start(bf16[1,48,1152]{2,1,0:T(8,128)(2,1)S(1)} %get-tuple-element.334), channel_id=1, source_target_pairs={{0,16},{2,18},{4,20},{6,22},{8,24},{10,26},{12,28},{14,30},{16,0},... | collective-permute-start | bytes 331784 | tf_op jit(solution)/shard_map/ppermute | solution.py:123

commit v2 on v1

--- a/solution.py
+++ b/solution.py
@@ -110,32 +110,44 @@
     return lax.rem(lax.div(place_ref[0], stride), radix)
 
 
-def send_pieces(pieces, stride, radix):
-    return [pieces[0]] + [turned(pieces[by], stride, radix, by) for by in range(1, radix)]
-
-
-def bits_of(count):
-    return [1 << k for k in range(count.bit_length() - 1)]
-
-
-def mirrored(array, stride):
-    pairs = [(i, i ^ stride) for i in range(lax.axis_size("seq"))]
-    return lax.ppermute(array, "seq", pairs)
-
-
-def halve(total, bit, keep, send, low):
-    for g in range(keep.shape[0]):
-        at = g // low * 2 * low + g % low
-        keep[g] = total[at + bit * low].astype(BF16)
-        send[g] = total[at + (1 - bit) * low].astype(BF16)
-
-
-def split_shapes(count, rows, widths):
-    return tuple(shape((count // 2, rows, w), BF16) for w in widths for _ in range(2))
-
-
-def half_width(width):
-    return -(-width // (2 * LANES)) * LANES
+def strides_of(count):
+    bits = [1 << k for k in range(count.bit_length() - 1)]
+    order = []
+    for k in range(0, len(bits) - 1, 2):
+        order += [(bits[k], bits[k + 1]), (bits[k + 1], bits[k])]
+    return order + [(b, b) for b in bits[len(order) :]]
+
+
+def mirrored(array, at):
+    count, cores = lax.axis_size("seq"), lax.axis_size("head")
+    strides = strides_of(count)[at]
+    pairs = [(i * cores + h, (i ^ strides[h % 2]) * cores + h) for i in range(count) for h in range(cores)]
+    return lax.ppermute(array, ("seq", "head"), pairs)
+
+
+def pick(place_ref, first, second):
+    return jnp.where(place_ref[1] == 0, first, second)
+
+
+def halved(place_ref, at, count):
+    pairs = strides_of(count)
+    left = count >> at
+    bit = pick(place_ref, *(lax.rem(lax.div(place_ref[0], stride), 2) for stride in pairs[at]))
+    split = at % 2 == 0 and pairs[at][0] != pairs[at][1]
+    places = []
+    for g in range(left // 2):
+        if split:
+            base, low = pick(place_ref, 2 * g, g // 2 * 4 + g % 2), pick(place_ref, 1, 2)
+        else:
+            base, low = 2 * g, 1
+        places.append((base + bit * low, base + (1 - bit) * low))
+    return places
+
+
+def put_halves(place_ref, at, count, total, keep, send):
+    for g, (mine, other) in enumerate(halved(place_ref, at, count)):
+        keep[g] = total[mine].astype(BF16)
+        send[g] = total[other].astype(BF16)
 
 
 def put_rows(total, at, grad):
@@ -144,92 +156,38 @@
         total[s, :, at : at + grad.shape[1]] = grad[s * rows : (s + 1) * rows]
 
 
-def both_halves(total, place_ref, outs):
-    middle = outs[0].shape[2]
-    halve(total.at[:, :, :middle], member_at(place_ref, 1, 2), outs[0], outs[1], 1)
-    halve(total.at[:, :, middle:], member_at(place_ref, 2, 2), outs[2], outs[3], 2)
+def half_shapes(entries, rows, width):
+    return (shape((entries // 2, rows, width), BF16),) * 2
 
 
 def grads_kernel(spans, place_ref, *refs):
-    lefts, rights, outs, total = refs[: len(spans)], refs[len(spans) : 2 * len(spans)], refs[-5:-1], refs[-1]
+    lefts, rights, (keep, send), total = refs[: len(spans)], refs[len(spans) : 2 * len(spans)], refs[-3:-1], refs[-1]
     for left, right, at in zip(lefts, rights, spans):
         put_rows(total, at, mm(left[...], right[...], TN))
-    both_halves(total, place_ref, outs)
-
-
-def grad_halves(place, pairs, us):
-    count = lax.axis_size("seq")
-    depth = pairs[0][0].shape[1]
-    spans, width = [], 0
-    for _, right in pairs:
-        spans.append(width)
-        width += right.shape[1]
-    middle = half_width(width)
-    rows = depth // count
-    return run(
-        functools.partial(grads_kernel, spans), split_shapes(count, rows, (middle, width - middle)),
-        place, *[left for left, _ in pairs], *[right for _, right in pairs],
-        scalars=1, scratch=[pltpu.VMEM((count, rows, width), F32)], mib=24, us=us)
-
-
-def fold_rest(place, halves, got, at, widths):
-    bits = bits_of(lax.axis_size("seq"))
-    while True:
-        halves = fold_bit(place, halves, got, at, widths)
-        at += 1
-        if at >= len(bits):
-            return halves
-        got = mirrored(halves[1], bits[at])
-
-
-def down_kernel(place_ref, grad_ref, hidden_ref, down_ref, resid_ref, *refs):
-    outs, own_ref, send_ref, total, part = refs[:4], refs[4], refs[5], refs[6], refs[7]
+    put_halves(place_ref, 0, total.shape[0], total, keep, send)
+
+
+def up_kernel(spans, place_ref, *refs):
+    grads_kernel(spans, place_ref, *refs[:4], *refs[6:8], refs[-1])
+    refs[8][...] = (refs[4][...] + refs[5][...].astype(F32)).astype(BF16)
+
+
+def down_kernel(place_ref, grad_ref, hidden_ref, down_ref, resid_ref, keep, send, own_ref, send_ref, total, part):
     part[...] = mm(hidden_ref[...], down_ref[...], NT)
     width = own_ref.shape[1]
     h = place_ref[1]
     own_ref[...] = half_of(part, h, width)[...] + half_of(resid_ref, h, width)[...]
     send_ref[...] = half_of(part, 1 - h, width)[...].astype(BF16)
     put_rows(total, 0, mm(grad_ref[...], hidden_ref[...], TN))
-    both_halves(total, place_ref, outs)
-
-
-def cross_kernel(place_ref, keep_a, got_a, keep_b, got_b, *refs):
-    outs, sum_a, sum_b = refs[:4], refs[4], refs[5]
-    for keep, got, total in ((keep_a, got_a, sum_a), (keep_b, got_b, sum_b)):
-        for g in range(total.shape[0]):
-            total[g] = keep[g].astype(F32) + got[g].astype(F32)
-    halve(sum_a, member_at(place_ref, 2, 2), outs[0], outs[1], 1)
-    halve(sum_b, member_at(place_ref, 1, 2), outs[2], outs[3], 1)
-
-
-def cross(place, halves, got_a, got_b):
-    keep_a, _, keep_b, _ = halves
-    count, rows, _ = keep_a.shape
-    return run(
-        cross_kernel, split_shapes(count, rows, (keep_a.shape[2], keep_b.shape[2])),
-        place, keep_a, got_a, keep_b, got_b, scalars=1,
-        scratch=[pltpu.VMEM(keep_a.shape, F32), pltpu.VMEM(keep_b.shape, F32)], us=8)
-
-
-def join_kernel(stride, place_ref, keep_a, got_a, keep_b, got_b, *refs):
-    outs, total = refs[:-1], refs[-1]
-    middle = keep_a.shape[2]
-    for g in range(total.shape[0]):
-        total[g, :, :middle] = keep_a[g].astype(F32) + got_a[g].astype(F32)
-        total[g, :, middle:] = keep_b[g].astype(F32) + got_b[g].astype(F32)
-    put_folded(stride, total, place_ref, outs)
-
-
-def fold_kernel(stride, place_ref, keep, got, *refs):
+    put_halves(place_ref, 0, total.shape[0], total, keep, send)
+
+
+def fold_kernel(at, count, place_ref, keep_ref, got_ref, *refs):
     outs, total = refs[:-1], refs[-1]
     for g in range(total.shape[0]):
-        total[g] = keep[g].astype(F32) + got[g].astype(F32)
-    put_folded(stride, total, place_ref, outs)
-
-
-def put_folded(stride, total, place_ref, outs):
-    if stride:
-        halve(total, member_at(place_ref, stride, 2), outs[0], outs[1], 1)
+        total[g] = keep_ref[g].astype(F32) + got_ref[g].astype(F32)
+    if total.shape[0] > 1:
+        put_halves(place_ref, at + 1, count, total, *outs)
         return
     begin = 0
     for out in outs:
@@ -237,99 +195,66 @@
         begin += out.shape[1]
 
 
-def fold_outs(entries, rows, widths):
-    if entries == 1:
-        return tuple(shape((rows, w), F32) for w in widths)
-    return split_shapes(entries, rows, (sum(widths),))
-
-
-def join(place, halves, got_a, got_b, widths):
-    keep_a, _, keep_b, _ = halves
-    entries, rows, _ = keep_a.shape
-    bits = bits_of(lax.axis_size("seq"))
-    last = entries == 1
-    return run(
-        functools.partial(join_kernel, 0 if last else bits[2]), fold_outs(entries, rows, widths), place,
-        keep_a, got_a, keep_b, got_b, scalars=1, scratch=[pltpu.VMEM((entries, rows, sum(widths)), F32)], us=8)
-
-
-def fold_bit(place, halves, got, at, widths):
-    keep = halves[0]
-    entries, rows, _ = keep.shape
-    bits = bits_of(lax.axis_size("seq"))
-    last = entries == 1
-    return run(
-        functools.partial(fold_kernel, 0 if last else bits[at + 1]), fold_outs(entries, rows, widths), place,
-        keep, got, scalars=1, scratch=[pltpu.VMEM((entries, rows, sum(widths)), F32)], us=8)
-
-
-def add_kernel(stage, later, rows, place_ref, *refs):
-    radix = stage[1]
-    got, outs, total, sorted_parts = refs[:radix], refs[radix:-2], refs[-2], refs[-1]
-    entries = total.shape[0]
+def folded(place, keep, got, at, widths, us):
+    entries, rows, width = keep.shape
+    outs = half_shapes(entries, rows, width) if entries > 1 else tuple(shape((rows, w), F32) for w in widths)
+    return run(functools.partial(fold_kernel, at, lax.axis_size("seq")), outs, place, keep, got, scalars=1,
+               scratch=[pltpu.VMEM((entries, rows, width), F32)], us=us)
+
+
+def folded_last(place, keep, got, at, widths, us):
+    while True:
+        res = folded(place, keep, got, at, widths, us)
+        if keep.shape[0] == 1:
+            return res
+        keep, got, at = res[0], mirrored(res[1], at + 1), at + 1
+
+
+def put_messages(place_ref, at, count, total, shared, keep, send):
+    rows = total.shape[1]
+    places = halved(place_ref, at, count)
+    for g, (mine, other) in enumerate(places):
+        keep[g * rows : (g + 1) * rows] = total[mine].astype(BF16)
+        send[g * rows : (g + 1) * rows] = total[other].astype(BF16)
+    end = len(places) * rows
+    keep[end:] = shared.astype(BF16)
+    send[end:] = shared.astype(BF16)
+
+
+def message_kernel(at, count, place_ref, keep_ref, got_ref, *refs):
+    outs, total = refs[:-1], refs[-1]
+    entries, rows, _ = total.shape
     for g in range(entries):
-        at = slice(g * rows, (g + 1) * rows)
-        acc = got[0][at].astype(F32)
-        for by in range(1, radix):
-            acc = acc + got[by][at].astype(F32)
-        total[g] = acc
-    tail = [m.at[entries * rows :] for m in got]
-    shared = in_order(member_at(place_ref, *stage), tail, sorted_parts)
-    if later:
-        put_messages(total, shared, later[1], member_at(place_ref, *later), outs)
+        span = slice(g * rows, (g + 1) * rows)
+        total[g] = keep_ref[span].astype(F32) + got_ref[span].astype(F32)
+    shared = keep_ref[entries * rows :].astype(F32) + got_ref[entries * rows :].astype(F32)
+    if entries > 1:
+        put_messages(place_ref, at + 1, count, total, shared, *outs)
+        return
+    outs[0][...] = total[0]
+    outs[1][...] = shared[:STEP]
+    outs[2][...] = shared[STEP:]
+
+
+def folded_message(place, keep, got, at, rows, us):
+    depth, width = keep.shape
+    extra = STEP + 8
+    entries = (depth - extra) // rows
+    if entries > 1:
+        outs = (shape((entries // 2 * rows + extra, width), BF16),) * 2
     else:
-        outs[0][...] = total[0]
-        outs[1][...] = shared[:STEP]
-        put_vectors(shared[STEP:], outs[2:4])
-        put_vectors(shared[STEP + 8 :], outs[4:])
-
-
-def put_messages(total, shared, radix, member, outs):
-    rows = total.shape[1]
-    for by in range(radix):
-        to = lax.rem(member + by, radix)
-        groups = total.shape[0] // radix
-        for g in range(groups):
-            outs[by][g * rows : (g + 1) * rows] = total[g * radix + to].astype(BF16)
-        outs[by][groups * rows :] = shared.astype(BF16)
-
-
-def add_messages(place, got, at, rows):
-    stages = digits_of(lax.axis_size("seq"))
-    radix = stages[at][1]
-    depth, width = got[0].shape
-    extra = STEP + 16
-    entries = (depth - extra) // rows
-    later = ()
-    if at + 1 < len(stages):
-        later = stages[at + 1]
-        outs = (shape((entries // later[1] * rows + extra, width), BF16),) * later[1]
-    else:
-        outs = (shape((rows, width), F32), shape((STEP, width), F32)) + (shape((2 * width,), F32),) * 4
-    return run(
-        functools.partial(add_kernel, stages[at], later, rows), outs, place, *got, scalars=1,
-        scratch=[pltpu.VMEM((entries, rows, width), F32), pltpu.VMEM((radix, extra, width), F32)], us=8)
-
-
-def in_order(member, got, sorted_parts):
-    radix = len(got)
-    for by in range(radix):
-        sorted_parts[lax.rem(member + radix - by, radix)] = got[by][...].astype(F32)
-    acc = sorted_parts[0]
-    for c in range(1, radix):
-        acc = acc + sorted_parts[c]
-    return acc
-
-
-def put_vectors(rows_in, outs):
-    width = rows_in.shape[1]
+        outs = (shape((rows, width), F32), shape((STEP, width), F32), shape((8, width), F32))
+    return run(functools.partial(message_kernel, at, lax.axis_size("seq")), outs, place, keep, got, scalars=1,
+               scratch=[pltpu.VMEM((entries, rows, width), F32)], us=us)
+
+
+def vector_kernel(place_ref, own_ref, other_ref, *outs):
+    h = place_ref[1]
+    width = own_ref.shape[1]
+    own, other = own_ref[...], other_ref[...]
     for k, out in enumerate(outs):
-        out[:width] = rows_in[k]
-        out[width:] = rows_in[k + 2]
-
-
-def flat_rows(sums, width):
-    return jnp.concatenate([sums[:, :width], sums[:, width:]], axis=0)
+        out[:width] = jnp.where(h == 0, own[k], other[k])
+        out[width:] = jnp.where(h == 0, other[k], own[k])
 
 
 def chained(first, second):
@@ -444,7 +369,7 @@
         beta_col = beta_col + mm(eye, part, NT)
     parts = split_parts(beta_col, 2)
     beta_out[...] = mm(parts[0], spread) + mm(parts[1], spread)
-    gate_out[...] = first_out[tok - 16 :].astype(BF16)
+    gate_out[...] = jnp.broadcast_to(first_out[tok - 1 :], gate_out.shape).astype(BF16)
 
 
 def row_of(ref):
@@ -714,11 +639,10 @@
 
 
 def carry_kernel(stage, place_ref, dk_ref, dv_ref, k_ref, v_ref, last_ref, beta_ref, docr_ref, docc_ref, taps_ref,
-                 tail_ref, ffn_own_ref, ffn_other_ref, *refs):
-    value_ref, sg_ref, edge_ref, sums, ahead_ref, block_ref, taps, keys = refs[-8:]
-    block_ref[...] = (ffn_own_ref[...] + ffn_other_ref[...].astype(F32)).astype(BF16)
+                 tail_ref, *refs):
+    value_ref, sg_ref, edge_ref, sums, ahead_ref, taps, keys = refs[-7:]
     reach(docr_ref, docc_ref, ahead_ref)
-    before, _ = link(stage, True, place_ref, refs[: stage[1]], refs[stage[1] : -8], False)
+    before, _ = link(stage, True, place_ref, refs[: stage[1]], refs[stage[1] : -7], False)
     state = before[1]
     tok, width = dk_ref.shape
     count = width // LANES
@@ -740,7 +664,7 @@
         edge_ref[:, l * LANES : (l + 1) * LANES] = acc[l].astype(BF16)
 
 
-def filter_back_kernel(sg_ref, k_ref, ahead_ref, taps_ref, sums_in, sums2_ref, grad_ref, small_ref, keys, taps, sums):
+def filter_back_kernel(sg_ref, k_ref, ahead_ref, taps_ref, sums_in, grad_ref, taps_grad_ref, keys, taps, sums):
     tok, width = k_ref.shape
     count = width // LANES
     for l in range(count):
@@ -758,9 +682,7 @@
 
     lax.fori_loop(1, tok // STEP + 1, chunk, 0)
     for l in range(count):
-        small_ref[:STEP, l * LANES : (l + 1) * LANES] = jnp.sum(sums[l], axis=1)
-    small_ref[STEP:] = jnp.zeros_like(small_ref[STEP:])
-    small_ref[STEP : STEP + 4] = flat_rows(sums2_ref[:2], width)
+        taps_grad_ref[:, l * LANES : (l + 1) * LANES] = jnp.sum(sums[l], axis=1)
 
 
 def out_kernel(place_ref, grad_ref, edge_ref, docc_ref, dq_ref, dv_ref, wq_ref, wk_ref, wv_ref, own_ref, other_ref,
@@ -789,15 +711,15 @@
     part_ref[tok:] = sums_ref[...].astype(BF16)
 
 
-def key_grads_kernel(stage, place_ref, normed_ref, key_ref, small_ref, part_ref, got_ref, *refs):
-    radix = stage[1]
-    outs, total, shared = refs[:radix], refs[-2], refs[-1]
+def key_grads_kernel(place_ref, normed_ref, key_ref, taps_ref, sums2_ref, part_ref, got_ref, keep, send, total, shared):
     put_rows(total, 0, mm(normed_ref[...], key_ref[...], TN))
     tok, width = key_ref.shape
-    sums = part_ref[tok:].astype(F32) + got_ref[tok:].astype(F32)
-    shared[...] = small_ref[...]
-    shared[STEP + 8 : STEP + 12] = flat_rows(sums[:2], width)
-    put_messages(total, shared[...], radix, member_at(place_ref, *stage), outs)
+    shared[STEP:] = jnp.zeros_like(shared[STEP:])
+    shared[:STEP] = taps_ref[...]
+    sums1 = part_ref[tok:].astype(F32) + got_ref[tok:].astype(F32)
+    for at, sums in ((STEP, sums1), (STEP + 2, sums2_ref[...])):
+        shared[at : at + 2] = jnp.where(place_ref[1] == 0, sums[:2, :width], sums[:2, width:])
+    put_messages(place_ref, 0, total.shape[0], total, shared[...], keep, send)
 
 
 def input_kernel(place_ref, part_ref, got_ref, own_ref, other_ref, gain_ref, resid_grad_ref, out_ref, rows, back):
@@ -894,107 +816,111 @@
         in_specs=[None] * 8 + [wide_tile, tok_tile],
         out_specs=(None, None, tok_tile, tok_tile, None), us=10.8)
     got2 = swapped(part2)
-    *down_halves, ffn_own, ffn_send = run(
+    rows = full // seqs
+    up_width = hidden_width + width
+    down_keep, down_send, ffn_own, ffn_send = run(
         down_kernel,
-        split_shapes(seqs, full // seqs, (half_width(hidden_width), hidden_width - half_width(hidden_width)))
-        + (shape((tok, width), F32), shape((tok, width), BF16)),
+        half_shapes(seqs, rows, hidden_width) + (shape((tok, width), F32), shape((tok, width), BF16)),
         place, grad_full, hidden, down_weight, resid, scalars=1,
-        scratch=[vm((seqs, full // seqs, hidden_width), F32), vm((tok, full), F32)], mib=24, us=4.0)
+        scratch=[vm((seqs, rows, hidden_width), F32), vm((tok, full), F32)], mib=24, us=4.1)
+    down_got = mirrored(down_send, 0)
+    ffn_other = swapped(ffn_send)
     got2 = after(got2, ffn_own)
     resid_grad, branch, g_low, sums2, message = run(
         norm2_kernel,
         (shape((tok, width), F32), shape((tok, full), BF16), shape((tok, width), BF16), shape((8, full), F32),
          shape((STEP + 16, width), BF16)),
         place, part2, got2, resid, grad_full, gain2, out_weight, query, first_w, gate_w,
-        scratch=[vm((tok, full), F32)], scalars=1, us=3.2)
+        scratch=[vm((tok, full), F32)], scalars=1, us=3.9)
     before = ()
     got = scan_send(message, 0, True)
-    ffn_other = swapped(after(ffn_send, message))
-    up_halves = grad_halves(place, [(after(normed2, message), pre_grad)], 2.5)
-    got = [after(g, up_halves[0]) for g in got]
+    up_keep, up_send, block_output = run(
+        functools.partial(up_kernel, (0, hidden_width)),
+        half_shapes(seqs, rows, up_width) + (shape((tok, width), BF16),),
+        place, after(normed2, message), branch, pre_grad, mixed, ffn_own, ffn_other, scalars=1,
+        scratch=[vm((seqs, rows, up_width), F32)], mib=24, us=3.2)
+    down_keep, down_send = folded(place, down_keep, after(down_got, block_output), 0, (), 4)
+    down_got = mirrored(down_send, 1)
+    got = [after(g, down_keep) for g in got]
     for at in range(len(stages) - 1):
         before, message = scan_link(place, got, before, at, True)
         got = scan_send(message, at + 1, True)
-    down_got = mirrored(after(down_halves[1], message), 1), mirrored(after(down_halves[3], message), 2)
+    up_got = mirrored(after(up_send, message), 0)
     query_late = after(query, message)
     query_grad, dk_part, dv_part = run(
         back_kernel, (shape((tok, width), BF16), shape((tok, width), F32), shape((tok, width), F32)),
         query_late, scaled, value, g_low, lamr, lamc, docr, docc, first_w, state,
         grid=(count,),
         in_specs=[pair_spec] * 4 + [lamr_spec, lamc_spec, None, None, pair_spec, state_spec],
-        out_specs=(pair_spec,) * 3, us=5.6)
+        out_specs=(pair_spec,) * 3, us=2.14)
     got = [after(g, query_grad) for g in got]
-    value_grad, shifted_grad, edge, sums, ahead, block_output = run(
+    value_grad, shifted_grad, edge, sums, ahead = run(
         functools.partial(carry_kernel, stages[-1]),
         (shape((tok, width), BF16), shape((count, tok + 2 * STEP, LANES), F32), shape((STEP, width), BF16),
-         shape((count, STEP, 8, LANES), F32), shape((tok + STEP, LANES), F32), shape((tok, width), BF16)),
-        place, dk_part, dv_part, scaled, value, last_w, beta_w, docr, docc, shift_kernel, prev_tail, ffn_own, ffn_other,
+         shape((count, STEP, 8, LANES), F32), shape((tok + STEP, LANES), F32)),
+        place, dk_part, dv_part, scaled, value, last_w, beta_w, docr, docc, shift_kernel, prev_tail,
         *got, *before, scalars=1,
-        scratch=[vm((count, STEP, LANES), F32), vm((count, STEP, LANES), F32)], us=2.4)
+        scratch=[vm((count, STEP, LANES), F32), vm((count, STEP, LANES), F32)], us=1.0)
     got_edge = passed_along(edge, -1)
-    mix_halves = grad_halves(place, [(branch, mixed), (normed1, query_grad), (normed1, after(value_grad, edge))], 2.6)
-    mix_widths, ffn_widths = (width,) * 3, (hidden_width,)
-    down_got = [after(g, mix_halves[0]) for g in down_got]
-    down_halves = cross(place, down_halves, *down_got)
-    down_got = mirrored(down_halves[1], 2), mirrored(down_halves[3], 1)
-    up_got = mirrored(after(up_halves[1], down_halves[0]), 1), mirrored(after(up_halves[3], down_halves[0]), 2)
-    sums = after(sums, down_halves[0])
-    key_rows, small_rows = run(
-        filter_back_kernel, (shape((tok, width), F32), shape((STEP + 16, width), F32)),
-        shifted_grad, key, ahead, shift_kernel, sums, sums2,
+    down_keep, down_send = folded(place, down_keep, after(down_got, edge), 1, (), 8)
+    down_got = mirrored(down_send, 2)
+    mix_keep, mix_send = run(
+        functools.partial(grads_kernel, (0, width)), half_shapes(seqs, rows, 2 * width),
+        place, normed1, normed1, query_grad, after(value_grad, down_keep), scalars=1,
+        scratch=[vm((seqs, rows, 2 * width), F32)], us=1.9)
+    mix_got = mirrored(mix_send, 0)
+    key_rows, taps_grad = run(
+        filter_back_kernel, (shape((tok, width), F32), shape((STEP, width), F32)),
+        shifted_grad, key, ahead, shift_kernel, after(sums, mix_keep),
         scratch=[vm((count, tok + STEP, LANES), F32), vm((count, STEP, LANES), F32),
-                 vm((count, STEP, 8, LANES), F32)], us=12.0)
-    down_got = [after(g, key_rows) for g in down_got]
-    down_halves = join(place, down_halves, *down_got, ffn_widths)
-    down_got = mirrored(down_halves[1], 4)
-    up_got = [after(g, down_halves[0]) for g in up_got]
-    up_halves = cross(place, up_halves, *up_got)
-    up_got = mirrored(up_halves[1], 2), mirrored(up_halves[3], 1)
-    got_edge = after(got_edge, up_halves[0])
+                 vm((count, STEP, 8, LANES), F32)], us=4.7)
+    up_keep, up_send = folded(place, up_keep, after(up_got, key_rows), 0, (), 0.2)
+    up_got = mirrored(up_send, 1)
+    down_keep, down_send = folded(place, down_keep, after(down_got, up_keep), 2, (), 2)
+    down_got = mirrored(down_send, 3)
+    mix_keep, mix_send = folded(place, mix_keep, after(mix_got, down_keep), 0, (), 2)
+    mix_got = mirrored(mix_send, 1)
     key_grad, part1 = run(
         out_kernel, (shape((tok, width), BF16), shape((tok + 8, full), BF16)),
-        place, key_rows, got_edge, docc, query_grad, value_grad, q_weight, k_weight, v_weight, block_input, other_input,
-        scratch=[vm((tok, full), BF16), vm((tok, full), F32), vm((8, full), F32)], scalars=1, us=3.2)
+        place, key_rows, after(got_edge, mix_keep), docc, query_grad, value_grad, q_weight, k_weight, v_weight,
+        block_input, other_input,
+        scratch=[vm((tok, full), BF16), vm((tok, full), F32), vm((8, full), F32)], scalars=1, us=3.6)
     got1 = swapped(part1)
-    up_got = [after(g, key_grad) for g in up_got]
-    up_halves = join(place, up_halves, *up_got, ffn_widths)
-    up_got = mirrored(up_halves[1], 4)
-    mix_got = mirrored(after(mix_halves[1], up_halves[0]), 1), mirrored(after(mix_halves[3], up_halves[0]), 2)
-    down_halves = fold_bit(place, down_halves, after(down_got, up_halves[0]), 2, ffn_widths)
-    down_got = mirrored(down_halves[1], 8)
-    rows = full // seqs
-    radix = stages[0][1]
-    key_messages = run(
-        functools.partial(key_grads_kernel, stages[0]),
-        (shape((seqs // radix * rows + STEP + 16, width), BF16),) * radix,
-        place, normed1, key_grad, small_rows, part1, after(got1, down_halves[0]), scalars=1,
-        scratch=[vm((seqs, rows, width), F32), vm((STEP + 16, width), F32)], us=1.4)
-    key_got = send_pieces(key_messages, *stages[0])
+    up_keep, up_send = folded(place, up_keep, after(up_got, key_grad), 1, (), 8)
+    up_got = mirrored(up_send, 2)
+    key_keep, key_send = run(
+        key_grads_kernel, (shape((seqs // 2 * rows + STEP + 8, width), BF16),) * 2,
+        place, normed1, key_grad, taps_grad, sums2, part1, after(got1, up_keep), scalars=1,
+        scratch=[vm((seqs, rows, width), F32), vm((STEP + 8, width), F32)], us=1.3)
+    key_got = mirrored(key_send, 0)
     input_grad = run(
         input_kernel, shape((tok, width), BF16),
-        place, part1, after(got1, key_messages[0]), block_input, other_input, gain1, resid_grad, scalars=1,
-        scratch=[vm((tok, full), BF16), vm((tok, full), F32)], us=3.2)
-    mix_got = [after(g, input_grad) for g in mix_got]
-    mix_halves = cross(place, mix_halves, *mix_got)
-    mix_got = mirrored(mix_halves[1], 2), mirrored(mix_halves[3], 1)
-    up_halves = fold_bit(place, up_halves, after(up_got, mix_halves[0]), 2, ffn_widths)
-    up_got = mirrored(up_halves[1], 8)
-    (down_total,) = fold_rest(place, down_halves, after(down_got, up_halves[0]), 3, ffn_widths)
-    key_got = [after(g, down_total) for g in key_got]
-    key_messages = add_messages(place, key_got, 0, rows)
-    key_got = send_pieces(key_messages, *stages[1])
-    mix_got = [after(g, key_messages[0]) for g in mix_got]
-    mix_halves = join(place, mix_halves, *mix_got, mix_widths)
-    mix_got = mirrored(mix_halves[1], 4)
-    (up_total,) = fold_rest(place, up_halves, after(up_got, mix_halves[0]), 3, ffn_widths)
-    mix_halves = fold_bit(place, mix_halves, after(mix_got, up_total), 2, mix_widths)
-    mix_got = mirrored(mix_halves[1], 8)
-    key_got = [after(g, mix_halves[0]) for g in key_got]
-    for at in range(1, len(stages) - 1):
-        key_got = send_pieces(add_messages(place, key_got, at, rows), *stages[at + 1])
-    k_total, taps_total, gain2_grad, bias2_grad, gain1_grad, bias1_grad = add_messages(
-        place, key_got, len(stages) - 1, rows)
-    out_total, q_total, v_total = fold_rest(place, mix_halves, after(mix_got, k_total), 3, mix_widths)
+        place, part1, after(got1, key_keep), block_input, other_input, gain1, resid_grad, scalars=1,
+        scratch=[vm((tok, full), BF16), vm((tok, full), F32)], us=3.7)
+    mix_keep, mix_send = folded(place, mix_keep, after(mix_got, input_grad), 1, (), 1)
+    mix_got = mirrored(mix_send, 2)
+    key_keep, key_send = folded_message(place, key_keep, after(key_got, mix_keep), 0, rows, 8)
+    key_got = mirrored(key_send, 1)
+    (down_total,) = folded_last(place, down_keep, after(down_got, key_keep), 3, (hidden_width,), 0.5)
+    up_keep, up_send = folded(place, up_keep, after(up_got, down_total), 2, (), 0.5)
+    up_got = mirrored(up_send, 3)
+    key_keep, key_send = folded_message(place, key_keep, after(key_got, up_keep), 1, rows, 2)
+    key_got = mirrored(key_send, 2)
+    mix_keep, mix_send = folded(place, mix_keep, after(mix_got, key_keep), 2, (), 1)
+    mix_got = mirrored(mix_send, 3)
+    key_keep, key_send = folded_message(place, key_keep, after(key_got, mix_keep), 2, rows, 0.2)
+    key_got = mirrored(key_send, 3)
+    up_total, out_total = folded_last(place, up_keep, after(up_got, key_keep), 3, (hidden_width, width), 8)
+    key_got = after(key_got, up_total)
+    for at in range(3, len(strides_of(seqs)) - 1):
+        key_keep, key_send = folded_message(place, key_keep, key_got, at, rows, 0.2)
+        key_got = mirrored(key_send, at + 1)
+    k_total, taps_total, vectors = folded_message(
+        place, key_keep, key_got, len(strides_of(seqs)) - 1, rows, 8)
+    other_vectors = swapped(vectors)
+    q_total, v_total = folded_last(place, mix_keep, after(mix_got, vectors), 3, (width, width), 4)
+    gain1_grad, bias1_grad, gain2_grad, bias2_grad = run(
+        vector_kernel, (shape((full,), F32),) * 4, place, vectors, after(other_vectors, q_total), scalars=1, us=0.7)
     return (block_output, input_grad, gain1_grad, bias1_grad, q_total, k_total, v_total, taps_total, out_total,
             gain2_grad, bias2_grad, up_total, down_total)
 

time: 169 us -> 158 us (0.935)
  starting transfers between devices: 54.1 us -> 42.9 us
  waiting for transfers between devices: 27.4 us -> 23.9 us
  Pallas kernels: 83.8 us -> 86 us
    ppermute x18 -> x12, starting transfers between devices: 23.4 us -> 16.2 us  [turned(): return lax.ppermute(array, 'seq', pairs)]
    ppermute x18 -> x16, starting transfers between devices: 23.5 us -> 18.5 us  [mirrored(): return lax.ppermute(array, ('seq', 'head'), pairs)]
    ppermute x18 -> x12, waiting for transfers between devices: 8.89 us -> 4.31 us  [turned(): return lax.ppermute(array, 'seq', pairs)]
    pallas_call x34 -> x37, Pallas kernels: 83.8 us -> 86 us  [run(): pl.pallas_call(body, out_shape=outs, grid=grid, in_specs=[FEW] * scalars...]
    ppermute x18 -> x16, waiting for transfers between devices: 16.8 us -> 17.9 us  [mirrored(): return lax.ppermute(array, ('seq', 'head'), pairs)]
  transfers between devices with their start and end apart: 45 -> 38, of which waited for: 17 -> 13; matrix products, arithmetic and copies ran while one was open for 0% -> 1% of each run, Pallas kernels for 41% -> 49%
where the time goes in v2:
time: 158 us; the launch traced here: 156 us
  Pallas kernels  86 us (54%)
  starting transfers between devices  42.9 us (27%)
  waiting for transfers between devices  23.9 us (15%)
    pallas_call x37, Pallas kernels, run(): pl.pallas_call(body, out_shape=outs, grid=grid, in_specs=[FEW] * scalars...  86 us
    ppermute x16, starting transfers between devices, mirrored(): return lax.ppermute(array, ('seq', 'head'), pairs)  18.5 us
    ppermute x16, waiting for transfers between devices, mirrored(): return lax.ppermute(array, ('seq', 'head'), pairs)  17.9 us
    ppermute x12, starting transfers between devices, turned(): return lax.ppermute(array, 'seq', pairs)  16.2 us
    ppermute x2, starting transfers between devices, passed_along(): lax.ppermute(array, 'seq', [(i, i + by) for i in range(count) if 0 <= i +...  5.76 us
    ppermute x12, waiting for transfers between devices, turned(): return lax.ppermute(array, 'seq', pairs)  4.31 us
  transfers between devices with their start and end apart: 38, of which 13 were waited for; matrix products, arithmetic and copies ran while one was open for 1% of the time, Pallas kernels for 49%

profile of v2, /device:TPU:0, one launch (start us, length us, event | category | flops | bytes accessed | tf_op | source)
XLA Modules:
  0.0 156.3 jit_solution(10039700514147704132)
XLA Ops:
  1.7 0.7 negate_sqrt_fusion.beta_ref
  2.5 0.7 copy-done.1
  3.9 2.6 %shard_map.246 = (f32[24,512]{1,0:T(8,128)S(1)}, f32[1536,128]{1,0:T(8,128)S(1)}, f32[8,512]{1,0:T(8,128)S(1)}, f32[512,128]{1,0:T(8,128)S(1)}, f32[512,128]{1,0...) custom-call(s32[512]{0:T(512)S(1)} %copy-done.14, ...), custom_call_target="tpu_custom_call" | custom-call | flops 2700000000 | bytes 8100000 | tf_op jit(solution)/shard_map/pallas_call | solution.py:56
  6.6 3.6 %shard_map.247 = (bf16[512,768]{1,0:T(8,128)(2,1)S(1)}, bf16[512,384]{1,0:T(8,128)(2,1)S(1)}, bf16[512,384]{1,0:T(8,128)(2,1)S(1)}, bf16[512,384]{1,0:T(8,128)(2,1)S(1)}, bf16[64,384]{1,0:T(8,128)(2,1)S(1)}) custom-call(s32[2]{0:T(128)S(1)} %pad_add_fusion.place_ref, bf16[512,384]{1,0:T(8,128)(2,1)S(1)} %copy-done.9, ...), custom_call_target="tpu_custom_call" | custom-call | flops 3000000000 | bytes 9000000 | tf_op jit(solution)/shard_map/pallas_call | solution.py:56
  10.2 4.5 %collective-permute-start.1 = (bf16[64,384]{1,0:T(8,128)(2,1)S(1)}, bf16[64,384]{1,0:T(8,128)(2,1)S(1)}, u32[]{:S(2)}, u32[]{:S(2)}) collective-permute-start(bf16[64,384]{1,0:T(8,128)(2,1)S(1)} %get-tuple-element.159), channel_id=1, source_target_pairs={{0,2},{2,4},{4,6},{6,8},{8,10},{10,12},{12,14},{14,16},{16,18},{18... | collective-permute-start | bytes 147464 | tf_op jit(solution)/shard_map/ppermute | solution.py:106
  14.7 5.5 %shard_map.248.part_ref = bf16[512,384]{1,0:T(8,128)(2,1)S(1)} custom-call(bf16[512,384]{1,0:T(8,128)(2,1)S(1)} %get-tuple-element.156.k_ref, bf16[64,384]{1,0:T(8,128)(2,1)S(1)} %copy-done, f32[512,128]{1,0:T(8,128)S(1)} %get-tuple-element.157.dist_ref, f32[512,384]{1,0:T(8,128)S(1)} %get-tuple-element.158.beta_ref), custom_call_target="tpu_custom_call" | custom-call | flops 5400000000 | bytes 16200000 | tf_op jit(solution)/shard_map/pallas_call | solution.py:56
  20.2 1.1 shard_map.249
  21.3 2.5 %collective-permute-start.5 = (bf16[80,384]{1,0:T(8,128)(2,1)S(1)}, bf16[80,384]{1,0:T(8,128)(2,1)S(1)}, u32[]{:S(2)}, u32[]{:S(2)}) collective-permute-start(bf16[80,384]{1,0:T(8,128)(2,1)S(1)} %get-tuple-element.167.refs_0_), channel_id=1, source_target_pairs={{0,6},{2,0},{4,2},{6,4},{8,14},{10,8},{12,10},{14,12},{16,22},{18,... | collective-permute-start | bytes 184328 | tf_op jit(solution)/shard_map/ppermute | solution.py:88
  24.9 2.6 %shard_map.250 = (bf16[512,1536]{1,0:T(8,128)(2,1)S(1)}, bf16[512,768]{1,0:T(8,128)(2,1)S(1)}) custom-call(s32[2]{0:T(128)S(1)} %pad_add_fusion.place_ref, bf16[512,384]{1,0:T(8,128)(2,1)S(1)} %copy-done.8, bf16[512,384]{1,0:T(8,128)(2,1)S(1)} %collective-permute-done.2.other_ref, bf16[768,1536]{1,0:T(8,128)(2,1)S(1)} %copy-done.3), custom_call_target="tpu_custom_call" | custom-call | flops 2500000000 | bytes 7500000 | tf_op jit(solution)/shard_map/pallas_call | solution.py:56
  27.6 1.2 collective-permute-done.4.refs_2_
  28.7 0.7 collective-permute-done.3.refs_1_
  30.1 3.7 %collective-permute-start.8 = (bf16[80,384]{1,0:T(8,128)(2,1)S(1)}, bf16[80,384]{1,0:T(8,128)(2,1)S(1)}, u32[]{:S(2)}, u32[]{:S(2)}) collective-permute-start(bf16[80,384]{1,0:T(8,128)(2,1)S(1)} %get-tuple-element.178.refs_0_), channel_id=1, source_target_pairs={{0,24},{2,26},{4,28},{6,30},{8,0},{10,2},{12,4},{14,6},{16,8},{18,... | collective-permute-start | bytes 184328 | tf_op jit(solution)/shard_map/ppermute | solution.py:88
  33.8 1.0 collective-permute-start.6
  34.8 3.0 %shard_map.252.inside_ref = f32[512,384]{1,0:T(8,128)S(1)} custom-call(bf16[512,384]{1,0:T(8,128)(2,1)S(1)} %get-tuple-element.207.q_ref, bf16[512,384]{1,0:T(8,128)(2,1)S(1)} %get-tuple-element.173.k_ref, bf16[512,384]{1,0:T(8,128)(2,1)S(1)} %get-tuple-element.162.v_ref, f32[24,512]{1,0:T(8,128)S(1)} %get-tuple-element.174.lamr_ref, ...), custom_call_target="tpu_custom_call" | custom-call | flops 3500000000 | bytes 10500000 | tf_op jit(solution)/shard_map/pallas_call | solution.py:56
  37.8 1.1 collective-permute-done.7.refs_2_
  38.9 0.9 collective-permute-done.6.refs_1_
  39.8 0.8 shard_map.253
  40.7 1.7 %collective-permute-done.9.mix_other_ref = bf16[512,384]{1,0:T(8,128)(2,1)S(1)} collective-permute-done((bf16[512,384]{1,0:T(8,128)(2,1)S(1)}, bf16[512,384]{1,0:T(8,128)(2,1)S(1)}, u32[]{:S(2)}, u32[]{:S(2)}) %collective-permute-start.9) | collective-permute-done | bytes 393248 | tf_op jit(solution)/shard_map/ppermute | solution.py:101
  42.5 8.8 %shard_map.254 = (f32[512,768]{1,0:T(8,128)S(1)}, bf16[512,768]{1,0:T(8,128)(2,1)S(1)}, bf16[512,1536]{1,0:T(8,128)(2,1)S(1)}, bf16[512,1536]{1,0:T(8,128)(2,1)S(1)}, bf16[512,768]{1,0:T(8,128)(2,1)S(1)}) custom-call(s32[2]{0:T(128)S(1)} %pad_add_fusion.place_ref, bf16[512,384]{1,0:T(8,128)(2,1)S(1)} %copy-done.9, ...), custom_call_target="tpu_custom_call" | custom-call | flops 10800000000 | bytes 32400000 | tf_op jit(solution)/shard_map/pallas_call | solution.py:56
  51.4 3.9 %shard_map.255 = (bf16[8,48,1536]{2,1,0:T(8,128)(2,1)S(1)}, bf16[8,48,1536]{2,1,0:T(8,128)(2,1)S(1)}, f32[512,384]{1,0:T(8,128)S(1)}, bf16[512,384]{1,0:T(8,128)(2,1)S(1)}) custom-call(s32[2]{0:T(128)S(1)} %pad_add_fusion.place_ref, bf16[512,768]{1,0:T(8,128)(2,1)S(1)} %get-tuple-element.187.grad_ref, bf16[512,1536]{1,0:T(8,128)(2,1)S(1)} %get-tuple-element.188.hidden_ref, ...), custom_call_target="tpu_custom_call" | custom-call | flops 4100000000 | bytes 12299999 | tf_op jit(solution)/shard_map/pallas_call | solution.py:56
  55.5 1.0 collective-permute-start.12
  56.5 3.8 %shard_map.256 = (f32[512,384]{1,0:T(8,128)S(1)}, bf16[512,768]{1,0:T(8,128)(2,1)S(1)}, bf16[512,384]{1,0:T(8,128)(2,1)S(1)}, f32[8,768]{1,0:T(8,128)S(1)}, bf16[80,384]{1,0:T(8,128)(2,1)S(1)}) custom-call(s32[2]{0:T(128)S(1)} %pad_add_fusion.place_ref, bf16[512,768]{1,0:T(8,128)(2,1)S(1)} %get-tuple-element.186.part_ref, ...), custom_call_target="tpu_custom_call" | custom-call | flops 3900000000 | bytes 11700000 | tf_op jit(solution)/shard_map/pallas_call | solution.py:56
  60.3 1.0 collective-permute-start.16
  61.3 1.0 collective-permute-start.15
  62.3 2.1 %collective-permute-start.14 = (bf16[80,384]{1,0:T(8,128)(2,1)S(1)}, bf16[80,384]{1,0:T(8,128)(2,1)S(1)}, u32[]{:S(2)}, u32[]{:S(2)}) collective-permute-start(bf16[80,384]{1,0:T(8,128)(2,1)S(1)} %get-tuple-element.202.refs_0_), channel_id=1, source_target_pairs={{0,6},{2,0},{4,2},{6,4},{8,14},{10,8},{12,10},{14,12},{16,22},{18,... | collective-permute-start | bytes 184328 | tf_op jit(solution)/shard_map/ppermute | solution.py:88
  64.3 4.0 %shard_map.257 = (bf16[8,48,1920]{2,1,0:T(8,128)(2,1)S(1)}, bf16[8,48,1920]{2,1,0:T(8,128)(2,1)S(1)}, bf16[512,384]{1,0:T(8,128)(2,1)}) custom-call(s32[2]{0:T(128)S(1)} %pad_add_fusion.place_ref, bf16[512,768]{1,0:T(8,128)(2,1)S(1)} %get-tuple-element.193.refs_0_, bf16[512,768]{1,0:T(8,128)(2,1)S(1)} %get-tuple-element.194.refs_1_, ...), custom_call_target="tpu_custom_call" | custom-call | flops 3200000000 | bytes 9600000 | tf_op jit(solution)/shard_map/pallas_call | solution.py:56
  68.4 4.6 %collective-permute-done.13.got_ref = bf16[8,48,1536]{2,1,0:T(8,128)(2,1)S(1)} collective-permute-done((bf16[8,48,1536]{2,1,0:T(8,128)(2,1)S(1)}, bf16[8,48,1536]{2,1,0:T(8,128)(2,1)S(1)}, u32[]{:S(2)}, u32[]{:S(2)}) %collective-permute-start.13) | collective-permute-done | bytes 1179680 | tf_op jit(solution)/shard_map/ppermute | solution.py:125
  72.9 1.0 shard_map.258
  74.3 1.0 collective-permute-start.20
  76.3 1.0 collective-permute-start.18
  77.3 2.5 %collective-permute-start.17 = (bf16[80,384]{1,0:T(8,128)(2,1)S(1)}, bf16[80,384]{1,0:T(8,128)(2,1)S(1)}, u32[]{:S(2)}, u32[]{:S(2)}) collective-permute-start(bf16[80,384]{1,0:T(8,128)(2,1)S(1)} %get-tuple-element.213.refs_0_), channel_id=1, source_target_pairs={{0,24},{2,26},{4,28},{6,30},{8,0},{10,2},{12,4},{14,6},{16,8},{18,... | collective-permute-start | bytes 184328 | tf_op jit(solution)/shard_map/ppermute | solution.py:88
  79.8 0.9 collective-permute-start.24
  80.7 5.5 %shard_map.260 = (bf16[512,384]{1,0:T(8,128)(2,1)S(1)}, f32[512,384]{1,0:T(8,128)S(1)}, f32[512,384]{1,0:T(8,128)S(1)}) custom-call(bf16[512,384]{1,0:T(8,128)(2,1)S(1)} %get-tuple-element.207.q_ref, bf16[512,384]{1,0:T(8,128)(2,1)S(1)} %get-tuple-element.173.k_ref, bf16[512,384]{1,0:T(8,128)(2,1)S(1)} %get-tuple-element.162.v_ref, ...), custom_call_target="tpu_custom_call" | custom-call | flops 2140000000 | bytes 6420000 | tf_op jit(solution)/shard_map/pallas_call | solution.py:56
  86.2 2.6 %shard_map.261 = (bf16[512,384]{1,0:T(8,128)(2,1)S(1)}, f32[3,640,128]{2,1,0:T(8,128)S(1)}, bf16[64,384]{1,0:T(8,128)(2,1)S(1)}, f32[3,64,8,128]{3,2,1,0:T(8,128)S(1)}, f32[576,128]{1,0:T(8,128)S(1)}) custom-call(s32[2]{0:T(128)S(1)} %pad_add_fusion.place_ref, f32[512,384]{1,0:T(8,128)S(1)} %get-tuple-element.210.dk_ref, ...), custom_call_target="tpu_custom_call" | custom-call | flops 1000000000 | bytes 3000000 | tf_op jit(solution)/shard_map/pallas_call | solution.py:56
  88.8 1.3 collective-permute-start.21
  90.1 0.8 shard_map.262
  90.9 4.0 %collective-permute-start.23 = (bf16[2,48,1536]{2,1,0:T(8,128)(2,1)S(1)}, bf16[2,48,1536]{2,1,0:T(8,128)(2,1)S(1)}, u32[]{:S(2)}, u32[]{:S(2)}) collective-permute-start(bf16[2,48,1536]{2,1,0:T(8,128)(2,1)S(1)} %get-tuple-element.233), channel_id=1, source_target_pairs={{0,8},{1,17},{2,10},{3,19},{4,12},{5,21},{6,14},{7,23},{8,0},{9,25... | collective-permute-start | bytes 884744 | tf_op jit(solution)/shard_map/ppermute | solution.py:125
  94.9 1.8 %shard_map.263 = (bf16[8,48,768]{2,1,0:T(8,128)(2,1)S(1)}, bf16[8,48,768]{2,1,0:T(8,128)(2,1)S(1)}) custom-call(s32[2]{0:T(128)S(1)} %pad_add_fusion.place_ref, bf16[512,768]{1,0:T(8,128)(2,1)S(1)} %get-tuple-element.222.refs_0_.refs_1_.normed_ref, bf16[512,768]{1,0:T(8,128)(2,1)S(1)} %get-tuple-element.222.refs_0_.refs_1_.normed_ref, ...), custom_call_target="tpu_custom_call" | custom-call | flops 1900000000 | bytes 5700000 | tf_op jit(solution)/shard_map/pallas_call | solution.py:56
  96.7 11.6 %shard_map.264 = (f32[512,384]{1,0:T(8,128)S(1)}, f32[64,384]{1,0:T(8,128)S(1)}) custom-call(f32[3,640,128]{2,1,0:T(8,128)S(1)} %get-tuple-element.219.sg_ref, bf16[512,384]{1,0:T(8,128)(2,1)S(1)} %get-tuple-element.156.k_ref, f32[576,128]{1,0:T(8,128)S(1)} %get-tuple-element.220.ahead_ref, bf16[64,384]{1,0:T(8,128)(2,1)S(1)} %copy-done, ...), custom_call_target="tpu_custom_call" | custom-call | flops 4700000256 | bytes 14100000 | tf_op jit(solution)/shard_map/pallas_call | solution.py:56
  108.3 1.1 shard_map.265
  110.2 0.7 shard_map.267
  111.0 3.6 %shard_map.268 = (bf16[512,384]{1,0:T(8,128)(2,1)S(1)}, bf16[520,768]{1,0:T(8,128)(2,1)S(1)}) custom-call(s32[2]{0:T(128)S(1)} %pad_add_fusion.place_ref, f32[512,384]{1,0:T(8,128)S(1)} %get-tuple-element.231.grad_ref, bf16[64,384]{1,0:T(8,128)(2,1)S(1)} %collective-permute-done.21.edge_ref, f32[512,128]{1,0:T(8,128)S(1)} %get-tuple-element.153.docc_ref, ...), custom_call_target="tpu_custom_call" | custom-call | flops 3600000000 | bytes 10800000 | tf_op jit(solution)/shard_map/pallas_call | solution.py:56
  114.7 1.9 %collective-permute-start.31 = (bf16[1,48,1536]{2,1,0:T(8,128)(2,1)S(1)}, bf16[1,48,1536]{2,1,0:T(8,128)(2,1)S(1)}, u32[]{:S(2)}, u32[]{:S(2)}) collective-permute-start(bf16[1,48,1536]{2,1,0:T(8,128)(2,1)S(1)} %get-tuple-element.263), channel_id=1, source_target_pairs={{0,16},{1,9},{2,18},{3,11},{4,20},{5,13},{6,22},{7,15},{8,24},{9,1... | collective-permute-start | bytes 442376 | tf_op jit(solution)/shard_map/ppermute | solution.py:125
  116.5 2.0 %collective-permute-start.28 = (bf16[4,48,768]{2,1,0:T(8,128)(2,1)S(1)}, bf16[4,48,768]{2,1,0:T(8,128)(2,1)S(1)}, u32[]{:S(2)}, u32[]{:S(2)}) collective-permute-start(bf16[4,48,768]{2,1,0:T(8,128)(2,1)S(1)} %get-tuple-element.256), channel_id=1, source_target_pairs={{0,4},{1,3},{2,6},{3,1},{4,0},{5,7},{6,2},{7,5},{8,12},{9,11},{10,... | collective-permute-start | bytes 884744 | tf_op jit(solution)/shard_map/ppermute | solution.py:125
  118.6 2.4 %collective-permute-done.26.got_ref = bf16[4,48,1920]{2,1,0:T(8,128)(2,1)S(1)} collective-permute-done((bf16[4,48,1920]{2,1,0:T(8,128)(2,1)S(1)}, bf16[4,48,1920]{2,1,0:T(8,128)(2,1)S(1)}, u32[]{:S(2)}, u32[]{:S(2)}) %collective-permute-start.26) | collective-permute-done | bytes 737312 | tf_op jit(solution)/shard_map/ppermute | solution.py:125
  121.0 0.8 shard_map.269
  121.8 0.8 collective-permute-start.30
  122.6 1.3 shard_map.270
  123.9 1.4 collective-permute-start.27
  125.2 3.7 %shard_map.271 = bf16[512,384]{1,0:T(8,128)(2,1)} custom-call(s32[2]{0:T(128)S(1)} %pad_add_fusion.place_ref, bf16[520,768]{1,0:T(8,128)(2,1)S(1)} %get-tuple-element.244.part_ref, bf16[520,768]{1,0:T(8,128)(2,1)S(1)} %collective-permute-done.25.got_ref, bf16[512,384]{1,0:T(8,128)(2,1)S(1)} %copy-done.9, ...), custom_call_target="tpu_custom_call" | custom-call | flops 3700000000 | bytes 11100000 | tf_op jit(solution)/shard_map/pallas_call | solution.py:56
  129.6 1.6 %collective-permute-done.27.got_ref = bf16[456,384]{1,0:T(8,128)(2,1)S(1)} collective-permute-done((bf16[456,384]{1,0:T(8,128)(2,1)S(1)}, bf16[456,384]{1,0:T(8,128)(2,1)S(1)}, u32[]{:S(2)}, u32[]{:S(2)}) %collective-permute-start.27) | collective-permute-done | bytes 350240 | tf_op jit(solution)/shard_map/ppermute | solution.py:125
  131.9 1.1 collective-permute-start.29
  133.4 1.3 shard_map.274
  134.7 0.7 shard_map.275
  135.4 2.5 %collective-permute-start.35 = (bf16[1,48,1920]{2,1,0:T(8,128)(2,1)S(1)}, bf16[1,48,1920]{2,1,0:T(8,128)(2,1)S(1)}, u32[]{:S(2)}, u32[]{:S(2)}) collective-permute-start(bf16[1,48,1920]{2,1,0:T(8,128)(2,1)S(1)} %get-tuple-element.276), channel_id=1, source_target_pairs={{0,16},{1,9},{2,18},{3,11},{4,20},{5,13},{6,22},{7,15},{8,24},{9,1... | collective-permute-start | bytes 552968 | tf_op jit(solution)/shard_map/ppermute | solution.py:125
  138.5 1.3 collective-permute-start.32
  139.7 2.8 %collective-permute-done.33.got_ref = bf16[2,48,768]{2,1,0:T(8,128)(2,1)S(1)} collective-permute-done((bf16[2,48,768]{2,1,0:T(8,128)(2,1)S(1)}, bf16[2,48,768]{2,1,0:T(8,128)(2,1)S(1)}, u32[]{:S(2)}, u32[]{:S(2)}) %collective-permute-start.33) | collective-permute-done | bytes 147488 | tf_op jit(solution)/shard_map/ppermute | solution.py:125
  143.3 2.9 %collective-permute-done.32.got_ref = bf16[168,384]{1,0:T(8,128)(2,1)S(1)} collective-permute-done((bf16[168,384]{1,0:T(8,128)(2,1)S(1)}, bf16[168,384]{1,0:T(8,128)(2,1)S(1)}, u32[]{:S(2)}, u32[]{:S(2)}) %collective-permute-start.32) | collective-permute-done | bytes 129056 | tf_op jit(solution)/shard_map/ppermute | solution.py:125
  146.8 1.1 collective-permute-start.34
  147.9 1.3 shard_map.279
  149.2 3.5 %collective-permute-done.34.got_ref = bf16[120,384]{1,0:T(8,128)(2,1)S(1)} collective-permute-done((bf16[120,384]{1,0:T(8,128)(2,1)S(1)}, bf16[120,384]{1,0:T(8,128)(2,1)S(1)}, u32[]{:S(2)}, u32[]{:S(2)}) %collective-permute-start.34) | collective-permute-done | bytes 92192 | tf_op jit(solution)/shard_map/ppermute | solution.py:125
  152.7 1.2 shard_map.280
  153.9 1.2 shard_map.281
  155.1 1.1 shard_map.282
  (81 shorter events, 9.9 us)
Async XLA Ops:
  0.6 24.3 %collective-permute-start.2 = (bf16[512,384]{1,0:T(8,128)(2,1)}, bf16[512,384]{1,0:T(8,128)(2,1)S(1)}, u32[]{:S(2)}, u32[]{:S(2)}) collective-permute-start(bf16[512,384]{1,0:T(8,128)(2,1)} %own_ref.6), channel_id=1, source_target_pairs={{0,1},{1,0},{2,3},{3,2},{4,5},{5,4},{6,7},{7,6},{8,9},{9,8},{10,11... | collective-permute-start | bytes 1179656 | tf_op jit(solution)/shard_map/ppermute | solution.py:101
  1.2 5.3 %collective-permute-start = (bf16[512,384]{1,0:T(8,128)(2,1)}, bf16[512,384]{1,0:T(8,128)(2,1)S(1)}, u32[]{:S(2)}, u32[]{:S(2)}) collective-permute-start(bf16[512,384]{1,0:T(8,128)(2,1)} %own_ref.9), channel_id=1, source_target_pairs={{0,1},{1,0},{2,3},{3,2},{4,5},{5,4},{6,7},{7,6},{8,9},{9,8},{10,11... | collective-permute-start | bytes 1179656 | tf_op jit(solution)/shard_map/ppermute | solution.py:101
  1.2 39.5 %collective-permute-start.10 = (bf16[768,384]{1,0:T(8,128)(2,1)}, bf16[768,384]{1,0:T(8,128)(2,1)S(1)}, u32[]{:S(2)}, u32[]{:S(2)}) collective-permute-start(bf16[768,384]{1,0:T(8,128)(2,1)} %out_w_ref.1), channel_id=1, source_target_pairs={{0,1},{1,0},{2,3},{3,2},{4,5},{5,4},{6,7},{7,6},{8,9},{9,8},{10,11... | collective-permute-start | bytes 1769480 | tf_op jit(solution)/shard_map/ppermute | solution.py:101
  2.5 0.7 copy-start.1
  3.2 0.7 copy-start.14
  3.9 2.6 %copy-start.5 = (bf16[768,384]{1,0:T(8,128)(2,1)S(1)}, bf16[768,384]{1,0:T(8,128)(2,1)}, u32[]{:S(2)}) copy-start(bf16[768,384]{1,0:T(8,128)(2,1)} %wq_ref.3) | copy-start | bytes 1769476
  3.9 2.6 %copy-start.6 = (bf16[768,384]{1,0:T(8,128)(2,1)S(1)}, bf16[768,384]{1,0:T(8,128)(2,1)}, u32[]{:S(2)}) copy-start(bf16[768,384]{1,0:T(8,128)(2,1)} %wk_ref.3) | copy-start | bytes 1769476
  3.9 2.6 %copy-start.7 = (bf16[768,384]{1,0:T(8,128)(2,1)S(1)}, bf16[768,384]{1,0:T(8,128)(2,1)}, u32[]{:S(2)}) copy-start(bf16[768,384]{1,0:T(8,128)(2,1)} %wv_ref.3) | copy-start | bytes 1769476
  3.9 2.6 %copy-start.9 = (bf16[512,384]{1,0:T(8,128)(2,1)S(1)}, bf16[512,384]{1,0:T(8,128)(2,1)}, u32[]{:S(2)}) copy-start(bf16[512,384]{1,0:T(8,128)(2,1)} %own_ref.9) | copy-start | bytes 1179652
  3.9 2.6 %copy-start.10 = (f32[768]{0:T(1024)S(1)}, f32[768]{0:T(1024)}, u32[]{:S(2)}) copy-start(f32[768]{0:T(1024)} %bias_ref.2) | copy-start | bytes 9220
  3.9 2.6 %copy-start.13 = (f32[768]{0:T(1024)S(1)}, f32[768]{0:T(1024)}, u32[]{:S(2)}) copy-start(f32[768]{0:T(1024)} %gain_ref.7) | copy-start | bytes 9220
  6.6 8.1 %copy-start = (bf16[64,384]{1,0:T(8,128)(2,1)S(1)}, bf16[64,384]{1,0:T(8,128)(2,1)}, u32[]{:S(2)}) copy-start(bf16[64,384]{1,0:T(8,128)(2,1)} %taps_ref.7) | copy-start | bytes 147460
  10.2 9.9 %collective-permute-start.1 = (bf16[64,384]{1,0:T(8,128)(2,1)S(1)}, bf16[64,384]{1,0:T(8,128)(2,1)S(1)}, u32[]{:S(2)}, u32[]{:S(2)}) collective-permute-start(bf16[64,384]{1,0:T(8,128)(2,1)S(1)} %get-tuple-element.159), channel_id=1, source_target_pairs={{0,2},{2,4},{4,6},{6,8},{8,10},{10,12},{12,14},{14,16},{16,18},{18... | collective-permute-start | bytes 147464 | tf_op jit(solution)/shard_map/ppermute | solution.py:106
  20.2 4.8 %copy-start.3 = (bf16[768,1536]{1,0:T(8,128)(2,1)S(1)}, bf16[768,1536]{1,0:T(8,128)(2,1)}, u32[]{:S(2)}) copy-start(bf16[768,1536]{1,0:T(8,128)(2,1)} %down_ref.3) | copy-start | bytes 7077892
  20.2 4.8 %copy-start.8 = (bf16[512,384]{1,0:T(8,128)(2,1)S(1)}, bf16[512,384]{1,0:T(8,128)(2,1)}, u32[]{:S(2)}) copy-start(bf16[512,384]{1,0:T(8,128)(2,1)} %own_ref.6) | copy-start | bytes 1179652
  21.3 6.2 %collective-permute-start.5 = (bf16[80,384]{1,0:T(8,128)(2,1)S(1)}, bf16[80,384]{1,0:T(8,128)(2,1)S(1)}, u32[]{:S(2)}, u32[]{:S(2)}) collective-permute-start(bf16[80,384]{1,0:T(8,128)(2,1)S(1)} %get-tuple-element.167.refs_0_), channel_id=1, source_target_pairs={{0,6},{2,0},{4,2},{6,4},{8,14},{10,8},{12,10},{14,12},{16,22},{18,... | collective-permute-start | bytes 184328 | tf_op jit(solution)/shard_map/ppermute | solution.py:88
  23.8 4.9 %collective-permute-start.4 = (bf16[80,384]{1,0:T(8,128)(2,1)S(1)}, bf16[80,384]{1,0:T(8,128)(2,1)S(1)}, u32[]{:S(2)}, u32[]{:S(2)}) collective-permute-start(bf16[80,384]{1,0:T(8,128)(2,1)S(1)} %get-tuple-element.167.refs_0_), channel_id=1, source_target_pairs={{0,4},{2,6},{4,0},{6,2},{8,12},{10,14},{12,8},{14,10},{16,20},{18,... | collective-permute-start | bytes 184328 | tf_op jit(solution)/shard_map/ppermute | solution.py:88
  24.3 5.1 %collective-permute-start.3 = (bf16[80,384]{1,0:T(8,128)(2,1)S(1)}, bf16[80,384]{1,0:T(8,128)(2,1)S(1)}, u32[]{:S(2)}, u32[]{:S(2)}) collective-permute-start(bf16[80,384]{1,0:T(8,128)(2,1)S(1)} %get-tuple-element.167.refs_0_), channel_id=1, source_target_pairs={{0,2},{2,4},{4,6},{6,0},{8,10},{10,12},{12,14},{14,8},{16,18},{18,... | collective-permute-start | bytes 184328 | tf_op jit(solution)/shard_map/ppermute | solution.py:88
  30.1 7.6 %collective-permute-start.8 = (bf16[80,384]{1,0:T(8,128)(2,1)S(1)}, bf16[80,384]{1,0:T(8,128)(2,1)S(1)}, u32[]{:S(2)}, u32[]{:S(2)}) collective-permute-start(bf16[80,384]{1,0:T(8,128)(2,1)S(1)} %get-tuple-element.178.refs_0_), channel_id=1, source_target_pairs={{0,24},{2,26},{4,28},{6,30},{8,0},{10,2},{12,4},{14,6},{16,8},{18,... | collective-permute-start | bytes 184328 | tf_op jit(solution)/shard_map/ppermute | solution.py:88
  33.8 5.1 %collective-permute-start.7 = (bf16[80,384]{1,0:T(8,128)(2,1)S(1)}, bf16[80,384]{1,0:T(8,128)(2,1)S(1)}, u32[]{:S(2)}, u32[]{:S(2)}) collective-permute-start(bf16[80,384]{1,0:T(8,128)(2,1)S(1)} %get-tuple-element.178.refs_0_), channel_id=1, source_target_pairs={{0,16},{2,18},{4,20},{6,22},{8,24},{10,26},{12,28},{14,30},{16,0},... | collective-permute-start | bytes 184328 | tf_op jit(solution)/shard_map/ppermute | solution.py:88
  33.8 6.0 %collective-permute-start.6 = (bf16[80,384]{1,0:T(8,128)(2,1)S(1)}, bf16[80,384]{1,0:T(8,128)(2,1)S(1)}, u32[]{:S(2)}, u32[]{:S(2)}) collective-permute-start(bf16[80,384]{1,0:T(8,128)(2,1)S(1)} %get-tuple-element.178.refs_0_), channel_id=1, source_target_pairs={{0,8},{2,10},{4,12},{6,14},{8,16},{10,18},{12,20},{14,22},{16,24},... | collective-permute-start | bytes 184328 | tf_op jit(solution)/shard_map/ppermute | solution.py:88
  39.8 2.6 %copy-start.2 = (bf16[768,1536]{1,0:T(8,128)(2,1)S(1)}, bf16[768,1536]{1,0:T(8,128)(2,1)}, u32[]{:S(2)}) copy-start(bf16[768,1536]{1,0:T(8,128)(2,1)} %up_ref.1) | copy-start | bytes 7077892
  39.8 2.6 %copy-start.4 = (bf16[768,384]{1,0:T(8,128)(2,1)S(1)}, bf16[768,384]{1,0:T(8,128)(2,1)}, u32[]{:S(2)}) copy-start(bf16[768,384]{1,0:T(8,128)(2,1)} %out_w_ref.1) | copy-start | bytes 1769476
  39.8 2.6 %copy-start.11 = (f32[768]{0:T(1024)S(1)}, f32[768]{0:T(1024)}, u32[]{:S(2)}) copy-start(f32[768]{0:T(1024)} %bias_ref.3) | copy-start | bytes 9220
  39.8 2.6 %copy-start.12 = (f32[768]{0:T(1024)S(1)}, f32[768]{0:T(1024)}, u32[]{:S(2)}) copy-start(f32[768]{0:T(1024)} %gain_ref.6) | copy-start | bytes 9220
  40.6 1.8 %collective-permute-start.9 = (bf16[512,384]{1,0:T(8,128)(2,1)S(1)}, bf16[512,384]{1,0:T(8,128)(2,1)S(1)}, u32[]{:S(2)}, u32[]{:S(2)}) collective-permute-start(bf16[512,384]{1,0:T(8,128)(2,1)S(1)} %get-tuple-element.184.mix_own_ref.refs_3_), channel_id=1, source_target_pairs={{0,1},{1,0},{2,3},{3,2},{4,5},{5,4},{6,7},{7,6},{8,9},{9,8},{10,11... | collective-permute-start | bytes 1179656 | tf_op jit(solution)/shard_map/ppermute | solution.py:101
  51.2 5.3 %collective-permute-start.11 = (bf16[512,768]{1,0:T(8,128)(2,1)S(1)}, bf16[512,768]{1,0:T(8,128)(2,1)S(1)}, u32[]{:S(2)}, u32[]{:S(2)}) collective-permute-start(bf16[512,768]{1,0:T(8,128)(2,1)S(1)} %get-tuple-element.186.part_ref), channel_id=1, source_target_pairs={{0,1},{1,0},{2,3},{3,2},{4,5},{5,4},{6,7},{7,6},{8,9},{9,8},{10,11... | collective-permute-start | bytes 2359304 | tf_op jit(solution)/shard_map/ppermute | solution.py:101
  55.4 17.6 %collective-permute-start.13 = (bf16[8,48,1536]{2,1,0:T(8,128)(2,1)S(1)}, bf16[8,48,1536]{2,1,0:T(8,128)(2,1)S(1)}, u32[]{:S(2)}, u32[]{:S(2)}) collective-permute-start(bf16[8,48,1536]{2,1,0:T(8,128)(2,1)S(1)} %get-tuple-element.199), channel_id=1, source_target_pairs={{0,2},{1,5},{2,0},{3,7},{4,6},{5,1},{6,4},{7,3},{8,10},{9,13},{10,... | collective-permute-start | bytes 3538952 | tf_op jit(solution)/shard_map/ppermute | solution.py:125
  55.5 8.8 %collective-permute-start.12 = (bf16[512,384]{1,0:T(8,128)(2,1)S(1)}, bf16[512,384]{1,0:T(8,128)(2,1)S(1)}, u32[]{:S(2)}, u32[]{:S(2)}) collective-permute-start(bf16[512,384]{1,0:T(8,128)(2,1)S(1)} %get-tuple-element.196), channel_id=1, source_target_pairs={{0,1},{1,0},{2,3},{3,2},{4,5},{5,4},{6,7},{7,6},{8,9},{9,8},{10,11... | collective-permute-start | bytes 1179656 | tf_op jit(solution)/shard_map/ppermute | solution.py:101
  60.3 13.7 %collective-permute-start.16 = (bf16[80,384]{1,0:T(8,128)(2,1)S(1)}, bf16[80,384]{1,0:T(8,128)(2,1)S(1)}, u32[]{:S(2)}, u32[]{:S(2)}) collective-permute-start(bf16[80,384]{1,0:T(8,128)(2,1)S(1)} %get-tuple-element.202.refs_0_), channel_id=1, source_target_pairs={{0,2},{2,4},{4,6},{6,0},{8,10},{10,12},{12,14},{14,8},{16,18},{18,... | collective-permute-start | bytes 184328 | tf_op jit(solution)/shard_map/ppermute | solution.py:88
  61.3 12.7 %collective-permute-start.15 = (bf16[80,384]{1,0:T(8,128)(2,1)S(1)}, bf16[80,384]{1,0:T(8,128)(2,1)S(1)}, u32[]{:S(2)}, u32[]{:S(2)}) collective-permute-start(bf16[80,384]{1,0:T(8,128)(2,1)S(1)} %get-tuple-element.202.refs_0_), channel_id=1, source_target_pairs={{0,4},{2,6},{4,0},{6,2},{8,12},{10,14},{12,8},{14,10},{16,20},{18,... | collective-permute-start | bytes 184328 | tf_op jit(solution)/shard_map/ppermute | solution.py:88
  62.3 12.0 %collective-permute-start.14 = (bf16[80,384]{1,0:T(8,128)(2,1)S(1)}, bf16[80,384]{1,0:T(8,128)(2,1)S(1)}, u32[]{:S(2)}, u32[]{:S(2)}) collective-permute-start(bf16[80,384]{1,0:T(8,128)(2,1)S(1)} %get-tuple-element.202.refs_0_), channel_id=1, source_target_pairs={{0,6},{2,0},{4,2},{6,4},{8,14},{10,8},{12,10},{14,12},{16,22},{18,... | collective-permute-start | bytes 184328 | tf_op jit(solution)/shard_map/ppermute | solution.py:88
  74.3 15.9 %collective-permute-start.20 = (bf16[4,48,1536]{2,1,0:T(8,128)(2,1)S(1)}, bf16[4,48,1536]{2,1,0:T(8,128)(2,1)S(1)}, u32[]{:S(2)}, u32[]{:S(2)}) collective-permute-start(bf16[4,48,1536]{2,1,0:T(8,128)(2,1)S(1)} %get-tuple-element.224), channel_id=1, source_target_pairs={{0,4},{1,3},{2,6},{3,1},{4,0},{5,7},{6,2},{7,5},{8,12},{9,11},{10,... | collective-permute-start | bytes 1769480 | tf_op jit(solution)/shard_map/ppermute | solution.py:125
  75.9 10.3 %collective-permute-start.19 = (bf16[80,384]{1,0:T(8,128)(2,1)S(1)}, bf16[80,384]{1,0:T(8,128)(2,1)S(1)}, u32[]{:S(2)}, u32[]{:S(2)}) collective-permute-start(bf16[80,384]{1,0:T(8,128)(2,1)S(1)} %get-tuple-element.213.refs_0_), channel_id=1, source_target_pairs={{0,8},{2,10},{4,12},{6,14},{8,16},{10,18},{12,20},{14,22},{16,24},... | collective-permute-start | bytes 184328 | tf_op jit(solution)/shard_map/ppermute | solution.py:88
  76.3 9.9 %collective-permute-start.18 = (bf16[80,384]{1,0:T(8,128)(2,1)S(1)}, bf16[80,384]{1,0:T(8,128)(2,1)S(1)}, u32[]{:S(2)}, u32[]{:S(2)}) collective-permute-start(bf16[80,384]{1,0:T(8,128)(2,1)S(1)} %get-tuple-element.213.refs_0_), channel_id=1, source_target_pairs={{0,16},{2,18},{4,20},{6,22},{8,24},{10,26},{12,28},{14,30},{16,0},... | collective-permute-start | bytes 184328 | tf_op jit(solution)/shard_map/ppermute | solution.py:88
  77.3 8.9 %collective-permute-start.17 = (bf16[80,384]{1,0:T(8,128)(2,1)S(1)}, bf16[80,384]{1,0:T(8,128)(2,1)S(1)}, u32[]{:S(2)}, u32[]{:S(2)}) collective-permute-start(bf16[80,384]{1,0:T(8,128)(2,1)S(1)} %get-tuple-element.213.refs_0_), channel_id=1, source_target_pairs={{0,24},{2,26},{4,28},{6,30},{8,0},{10,2},{12,4},{14,6},{16,8},{18,... | collective-permute-start | bytes 184328 | tf_op jit(solution)/shard_map/ppermute | solution.py:88
  79.8 28.5 %collective-permute-start.24 = (bf16[8,48,1920]{2,1,0:T(8,128)(2,1)S(1)}, bf16[8,48,1920]{2,1,0:T(8,128)(2,1)S(1)}, u32[]{:S(2)}, u32[]{:S(2)}) collective-permute-start(bf16[8,48,1920]{2,1,0:T(8,128)(2,1)S(1)} %get-tuple-element.236), channel_id=1, source_target_pairs={{0,2},{1,5},{2,0},{3,7},{4,6},{5,1},{6,4},{7,3},{8,10},{9,13},{10,... | collective-permute-start | bytes 4423688 | tf_op jit(solution)/shard_map/ppermute | solution.py:125
  88.8 22.1 %collective-permute-start.21 = (bf16[64,384]{1,0:T(8,128)(2,1)S(1)}, bf16[64,384]{1,0:T(8,128)(2,1)S(1)}, u32[]{:S(2)}, u32[]{:S(2)}) collective-permute-start(bf16[64,384]{1,0:T(8,128)(2,1)S(1)} %get-tuple-element.225), channel_id=1, source_target_pairs={{2,0},{4,2},{6,4},{8,6},{10,8},{12,10},{14,12},{16,14},{18,16},{20... | collective-permute-start | bytes 147464 | tf_op jit(solution)/shard_map/ppermute | solution.py:106
  90.9 18.6 %collective-permute-start.23 = (bf16[2,48,1536]{2,1,0:T(8,128)(2,1)S(1)}, bf16[2,48,1536]{2,1,0:T(8,128)(2,1)S(1)}, u32[]{:S(2)}, u32[]{:S(2)}) collective-permute-start(bf16[2,48,1536]{2,1,0:T(8,128)(2,1)S(1)} %get-tuple-element.233), channel_id=1, source_target_pairs={{0,8},{1,17},{2,10},{3,19},{4,12},{5,21},{6,14},{7,23},{8,0},{9,25... | collective-permute-start | bytes 884744 | tf_op jit(solution)/shard_map/ppermute | solution.py:125
  96.6 13.6 %collective-permute-start.22 = (bf16[8,48,768]{2,1,0:T(8,128)(2,1)S(1)}, bf16[8,48,768]{2,1,0:T(8,128)(2,1)S(1)}, u32[]{:S(2)}, u32[]{:S(2)}) collective-permute-start(bf16[8,48,768]{2,1,0:T(8,128)(2,1)S(1)} %get-tuple-element.232), channel_id=1, source_target_pairs={{0,2},{1,5},{2,0},{3,7},{4,6},{5,1},{6,4},{7,3},{8,10},{9,13},{10,... | collective-permute-start | bytes 1769480 | tf_op jit(solution)/shard_map/ppermute | solution.py:125
  109.4 11.5 %collective-permute-start.26 = (bf16[4,48,1920]{2,1,0:T(8,128)(2,1)S(1)}, bf16[4,48,1920]{2,1,0:T(8,128)(2,1)S(1)}, u32[]{:S(2)}, u32[]{:S(2)}) collective-permute-start(bf16[4,48,1920]{2,1,0:T(8,128)(2,1)S(1)} %get-tuple-element.248), channel_id=1, source_target_pairs={{0,4},{1,3},{2,6},{3,1},{4,0},{5,7},{6,2},{7,5},{8,12},{9,11},{10,... | collective-permute-start | bytes 2211848 | tf_op jit(solution)/shard_map/ppermute | solution.py:125
  114.6 8.0 %collective-permute-start.25 = (bf16[520,768]{1,0:T(8,128)(2,1)S(1)}, bf16[520,768]{1,0:T(8,128)(2,1)S(1)}, u32[]{:S(2)}, u32[]{:S(2)}) collective-permute-start(bf16[520,768]{1,0:T(8,128)(2,1)S(1)} %get-tuple-element.244.part_ref), channel_id=1, source_target_pairs={{0,1},{1,0},{2,3},{3,2},{4,5},{5,4},{6,7},{7,6},{8,9},{9,8},{10,11... | collective-permute-start | bytes 2396168 | tf_op jit(solution)/shard_map/ppermute | solution.py:101
  114.7 18.7 %collective-permute-start.31 = (bf16[1,48,1536]{2,1,0:T(8,128)(2,1)S(1)}, bf16[1,48,1536]{2,1,0:T(8,128)(2,1)S(1)}, u32[]{:S(2)}, u32[]{:S(2)}) collective-permute-start(bf16[1,48,1536]{2,1,0:T(8,128)(2,1)S(1)} %get-tuple-element.263), channel_id=1, source_target_pairs={{0,16},{1,9},{2,18},{3,11},{4,20},{5,13},{6,22},{7,15},{8,24},{9,1... | collective-permute-start | bytes 442376 | tf_op jit(solution)/shard_map/ppermute | solution.py:125
  116.5 12.4 %collective-permute-start.28 = (bf16[4,48,768]{2,1,0:T(8,128)(2,1)S(1)}, bf16[4,48,768]{2,1,0:T(8,128)(2,1)S(1)}, u32[]{:S(2)}, u32[]{:S(2)}) collective-permute-start(bf16[4,48,768]{2,1,0:T(8,128)(2,1)S(1)} %get-tuple-element.256), channel_id=1, source_target_pairs={{0,4},{1,3},{2,6},{3,1},{4,0},{5,7},{6,2},{7,5},{8,12},{9,11},{10,... | collective-permute-start | bytes 884744 | tf_op jit(solution)/shard_map/ppermute | solution.py:125
  121.8 12.9 %collective-permute-start.30 = (bf16[2,48,1920]{2,1,0:T(8,128)(2,1)S(1)}, bf16[2,48,1920]{2,1,0:T(8,128)(2,1)S(1)}, u32[]{:S(2)}, u32[]{:S(2)}) collective-permute-start(bf16[2,48,1920]{2,1,0:T(8,128)(2,1)S(1)} %get-tuple-element.262), channel_id=1, source_target_pairs={{0,8},{1,17},{2,10},{3,19},{4,12},{5,21},{6,14},{7,23},{8,0},{9,25... | collective-permute-start | bytes 1105928 | tf_op jit(solution)/shard_map/ppermute | solution.py:125
  123.9 7.4 %collective-permute-start.27 = (bf16[456,384]{1,0:T(8,128)(2,1)S(1)}, bf16[456,384]{1,0:T(8,128)(2,1)S(1)}, u32[]{:S(2)}, u32[]{:S(2)}) collective-permute-start(bf16[456,384]{1,0:T(8,128)(2,1)S(1)} %get-tuple-element.255), channel_id=1, source_target_pairs={{0,2},{1,5},{2,0},{3,7},{4,6},{5,1},{6,4},{7,3},{8,10},{9,13},{10,... | collective-permute-start | bytes 1050632 | tf_op jit(solution)/shard_map/ppermute | solution.py:125
  131.9 5.9 %collective-permute-start.29 = (bf16[264,384]{1,0:T(8,128)(2,1)S(1)}, bf16[264,384]{1,0:T(8,128)(2,1)S(1)}, u32[]{:S(2)}, u32[]{:S(2)}) collective-permute-start(bf16[264,384]{1,0:T(8,128)(2,1)S(1)} %get-tuple-element.261), channel_id=1, source_target_pairs={{0,4},{1,3},{2,6},{3,1},{4,0},{5,7},{6,2},{7,5},{8,12},{9,11},{10,... | collective-permute-start | bytes 608264 | tf_op jit(solution)/shard_map/ppermute | solution.py:125
  133.1 9.5 %collective-permute-start.33 = (bf16[2,48,768]{2,1,0:T(8,128)(2,1)S(1)}, bf16[2,48,768]{2,1,0:T(8,128)(2,1)S(1)}, u32[]{:S(2)}, u32[]{:S(2)}) collective-permute-start(bf16[2,48,768]{2,1,0:T(8,128)(2,1)S(1)} %get-tuple-element.270), channel_id=1, source_target_pairs={{0,8},{1,17},{2,10},{3,19},{4,12},{5,21},{6,14},{7,23},{8,0},{9,25... | collective-permute-start | bytes 442376 | tf_op jit(solution)/shard_map/ppermute | solution.py:125
  135.4 11.4 %collective-permute-start.35 = (bf16[1,48,1920]{2,1,0:T(8,128)(2,1)S(1)}, bf16[1,48,1920]{2,1,0:T(8,128)(2,1)S(1)}, u32[]{:S(2)}, u32[]{:S(2)}) collective-permute-start(bf16[1,48,1920]{2,1,0:T(8,128)(2,1)S(1)} %get-tuple-element.276), channel_id=1, source_target_pairs={{0,16},{1,9},{2,18},{3,11},{4,20},{5,13},{6,22},{7,15},{8,24},{9,1... | collective-permute-start | bytes 552968 | tf_op jit(solution)/shard_map/ppermute | solution.py:125
  138.5 7.7 %collective-permute-start.32 = (bf16[168,384]{1,0:T(8,128)(2,1)S(1)}, bf16[168,384]{1,0:T(8,128)(2,1)S(1)}, u32[]{:S(2)}, u32[]{:S(2)}) collective-permute-start(bf16[168,384]{1,0:T(8,128)(2,1)S(1)} %get-tuple-element.269), channel_id=1, source_target_pairs={{0,8},{1,17},{2,10},{3,19},{4,12},{5,21},{6,14},{7,23},{8,0},{9,25... | collective-permute-start | bytes 387080 | tf_op jit(solution)/shard_map/ppermute | solution.py:125
  143.2 10.7 %collective-permute-start.37 = (bf16[1,48,768]{2,1,0:T(8,128)(2,1)S(1)}, bf16[1,48,768]{2,1,0:T(8,128)(2,1)S(1)}, u32[]{:S(2)}, u32[]{:S(2)}) collective-permute-start(bf16[1,48,768]{2,1,0:T(8,128)(2,1)S(1)} %get-tuple-element.281), channel_id=1, source_target_pairs={{0,16},{1,9},{2,18},{3,11},{4,20},{5,13},{6,22},{7,15},{8,24},{9,1... | collective-permute-start | bytes 221192 | tf_op jit(solution)/shard_map/ppermute | solution.py:125
  146.8 5.9 %collective-permute-start.34 = (bf16[120,384]{1,0:T(8,128)(2,1)S(1)}, bf16[120,384]{1,0:T(8,128)(2,1)S(1)}, u32[]{:S(2)}, u32[]{:S(2)}) collective-permute-start(bf16[120,384]{1,0:T(8,128)(2,1)S(1)} %get-tuple-element.275), channel_id=1, source_target_pairs={{0,16},{1,9},{2,18},{3,11},{4,20},{5,13},{6,22},{7,15},{8,24},{9,1... | collective-permute-start | bytes 276488 | tf_op jit(solution)/shard_map/ppermute | solution.py:125
  153.9 1.2 collective-permute-start.36

commit v3 on v2

--- a/solution.py
+++ b/solution.py
@@ -110,17 +110,20 @@
     return lax.rem(lax.div(place_ref[0], stride), radix)
 
 
-def strides_of(count):
+def strides_of(count, z_first=False):
     bits = [1 << k for k in range(count.bit_length() - 1)]
+    if z_first and len(bits) > 3:
+        x, y, low, high = bits[:4]
+        return [(low, high), (x, y), (y, x), (high, low)] + [(b, b) for b in bits[4:]]
     order = []
     for k in range(0, len(bits) - 1, 2):
         order += [(bits[k], bits[k + 1]), (bits[k + 1], bits[k])]
     return order + [(b, b) for b in bits[len(order) :]]
 
 
-def mirrored(array, at):
+def mirrored(array, at, z_first=False):
     count, cores = lax.axis_size("seq"), lax.axis_size("head")
-    strides = strides_of(count)[at]
+    strides = strides_of(count, z_first)[at]
     pairs = [(i * cores + h, (i ^ strides[h % 2]) * cores + h) for i in range(count) for h in range(cores)]
     return lax.ppermute(array, ("seq", "head"), pairs)
 
@@ -129,23 +132,23 @@
     return jnp.where(place_ref[1] == 0, first, second)
 
 
-def halved(place_ref, at, count):
-    pairs = strides_of(count)
-    left = count >> at
+def halved(place_ref, at, count, z_first=False):
+    pairs = strides_of(count, z_first)
+    lows = []
+    for h in range(2):
+        left = sorted(set(p[h] for p in pairs) - set(p[h] for p in pairs[:at]))
+        lows.append(1 << left.index(pairs[at][h]))
     bit = pick(place_ref, *(lax.rem(lax.div(place_ref[0], stride), 2) for stride in pairs[at]))
-    split = at % 2 == 0 and pairs[at][0] != pairs[at][1]
     places = []
-    for g in range(left // 2):
-        if split:
-            base, low = pick(place_ref, 2 * g, g // 2 * 4 + g % 2), pick(place_ref, 1, 2)
-        else:
-            base, low = 2 * g, 1
+    for g in range((count >> at) // 2):
+        bases = [g // low * 2 * low + g % low for low in lows]
+        base, low = pick(place_ref, *bases), pick(place_ref, *lows)
         places.append((base + bit * low, base + (1 - bit) * low))
     return places
 
 
-def put_halves(place_ref, at, count, total, keep, send):
-    for g, (mine, other) in enumerate(halved(place_ref, at, count)):
+def put_halves(place_ref, at, count, total, keep, send, z_first=False):
+    for g, (mine, other) in enumerate(halved(place_ref, at, count, z_first)):
         keep[g] = total[mine].astype(BF16)
         send[g] = total[other].astype(BF16)
 
@@ -153,7 +156,7 @@
 def put_rows(total, at, grad):
     rows = total.shape[1]
     for s in range(total.shape[0]):
-        total[s, :, at : at + grad.shape[1]] = grad[s * rows : (s + 1) * rows]
+        total[s, :, at : at + grad.shape[1]] = grad[s * rows : (s + 1) * rows].astype(total.dtype)
 
 
 def half_shapes(entries, rows, width):
@@ -179,15 +182,15 @@
     own_ref[...] = half_of(part, h, width)[...] + half_of(resid_ref, h, width)[...]
     send_ref[...] = half_of(part, 1 - h, width)[...].astype(BF16)
     put_rows(total, 0, mm(grad_ref[...], hidden_ref[...], TN))
-    put_halves(place_ref, 0, total.shape[0], total, keep, send)
-
-
-def fold_kernel(at, count, place_ref, keep_ref, got_ref, *refs):
+    put_halves(place_ref, 0, total.shape[0], total, keep, send, True)
+
+
+def fold_kernel(at, count, z_first, place_ref, keep_ref, got_ref, *refs):
     outs, total = refs[:-1], refs[-1]
     for g in range(total.shape[0]):
-        total[g] = keep_ref[g].astype(F32) + got_ref[g].astype(F32)
+        total[g] = (keep_ref[g].astype(F32) + got_ref[g].astype(F32)).astype(total.dtype)
     if total.shape[0] > 1:
-        put_halves(place_ref, at + 1, count, total, *outs)
+        put_halves(place_ref, at + 1, count, total, *outs, z_first)
         return
     begin = 0
     for out in outs:
@@ -195,19 +198,19 @@
         begin += out.shape[1]
 
 
-def folded(place, keep, got, at, widths, us):
+def folded(place, keep, got, at, widths, us, z_first=False):
     entries, rows, width = keep.shape
     outs = half_shapes(entries, rows, width) if entries > 1 else tuple(shape((rows, w), F32) for w in widths)
-    return run(functools.partial(fold_kernel, at, lax.axis_size("seq")), outs, place, keep, got, scalars=1,
-               scratch=[pltpu.VMEM((entries, rows, width), F32)], us=us)
-
-
-def folded_last(place, keep, got, at, widths, us):
+    return run(functools.partial(fold_kernel, at, lax.axis_size("seq"), z_first), outs, place, keep, got, scalars=1,
+               scratch=[pltpu.VMEM((entries, rows, width), BF16 if entries > 1 else F32)], us=us)
+
+
+def folded_last(place, keep, got, at, widths, us, z_first=False):
     while True:
-        res = folded(place, keep, got, at, widths, us)
+        res = folded(place, keep, got, at, widths, us, z_first)
         if keep.shape[0] == 1:
             return res
-        keep, got, at = res[0], mirrored(res[1], at + 1), at + 1
+        keep, got, at = res[0], mirrored(res[1], at + 1, z_first), at + 1
 
 
 def put_messages(place_ref, at, count, total, shared, keep, send):
@@ -322,7 +325,14 @@
     return parts
 
 
-def side_kernel(starts_ref, decay_ref, beta_ref, lamr_ref, lamc_ref, docr_ref, docc_ref, dist_ref,
+def one_less_exp(x):
+    acc = jnp.ones_like(x)
+    for k in range(7, 1, -1):
+        acc = 1.0 - x * (1.0 / k) * acc
+    return x * acc
+
+
+def side_kernel(starts_ref, decay_ref, lamr_ref, lamc_ref, docr_ref, docc_ref, dist_ref,
                 beta_out, first_out, last_out, gate_out, tri, same, wide):
     tok = starts_ref.shape[0]
     heads = decay_ref.shape[0]
@@ -362,7 +372,7 @@
     for ref, value in ((first_out, first), (last_out, last)):
         parts = split_parts(value, 2)
         ref[...] = mm(parts[0], spread) + mm(parts[1], spread)
-    wide[:heads] = beta_ref[...]
+    wide[:heads] = jnp.sqrt(one_less_exp(2.0 * jnp.minimum(decay_ref[...], RATE_CAP)))
     eye = (row == col).astype(F32).astype(BF16)
     beta_col = jnp.zeros((tok, LANES), F32)
     for part in split_parts(wide[...], 2):
@@ -391,7 +401,7 @@
                       - unit_rows * (jnp.sum(scaled * unit_rows, axis=1, keepdims=True) * scale))
 
 
-def by_rows(tok, body, size=64):
+def by_rows(tok, body, size=256):
     def step(i, carry):
         body(pl.ds(pl.multiple_of(i * size, size), size))
         return carry
@@ -753,13 +763,12 @@
     other_input = swapped(block_input)
     other_grad = swapped(out_grad)
     other_out = swapped(out_weight)
-    beta = jnp.sqrt(-jnp.expm1(-2.0 * jnp.minimum(decay_rate, RATE_CAP)))
     lamr, lamc, docr, docc, dist, beta_w, first_w, last_w, gate_w = run(
         side_kernel,
         (shape((8 * count, tok), F32), shape((count * tok, LANES), F32), shape((8, tok), F32),
          shape((tok, LANES), F32), shape((tok, LANES), F32),
          shape((tok, width), F32), shape((tok, width), F32), shape((tok, width), F32), shape((16, width), BF16)),
-        starts, decay_rate, beta,
+        starts, decay_rate, far=(0, 1),
         scratch=[vm((tok, tok), BF16), vm((tok, tok), BF16), vm((LANES, tok), F32)], us=2.7)
     other_input = after(other_input, docc)
     normed1, query, key, value, tail = run(
@@ -822,8 +831,7 @@
         down_kernel,
         half_shapes(seqs, rows, hidden_width) + (shape((tok, width), F32), shape((tok, width), BF16)),
         place, grad_full, hidden, down_weight, resid, scalars=1,
-        scratch=[vm((seqs, rows, hidden_width), F32), vm((tok, full), F32)], mib=24, us=4.1)
-    down_got = mirrored(down_send, 0)
+        scratch=[vm((seqs, rows, hidden_width), BF16), vm((tok, full), F32)], mib=24, us=2.46)
     ffn_other = swapped(ffn_send)
     got2 = after(got2, ffn_own)
     resid_grad, branch, g_low, sums2, message = run(
@@ -831,28 +839,27 @@
         (shape((tok, width), F32), shape((tok, full), BF16), shape((tok, width), BF16), shape((8, full), F32),
          shape((STEP + 16, width), BF16)),
         place, part2, got2, resid, grad_full, gain2, out_weight, query, first_w, gate_w,
-        scratch=[vm((tok, full), F32)], scalars=1, us=3.9)
+        scratch=[vm((tok, full), F32)], scalars=1, us=2.34)
     before = ()
     got = scan_send(message, 0, True)
     up_keep, up_send, block_output = run(
         functools.partial(up_kernel, (0, hidden_width)),
         half_shapes(seqs, rows, up_width) + (shape((tok, width), BF16),),
         place, after(normed2, message), branch, pre_grad, mixed, ffn_own, ffn_other, scalars=1,
-        scratch=[vm((seqs, rows, up_width), F32)], mib=24, us=3.2)
-    down_keep, down_send = folded(place, down_keep, after(down_got, block_output), 0, (), 4)
-    down_got = mirrored(down_send, 1)
-    got = [after(g, down_keep) for g in got]
+        scratch=[vm((seqs, rows, up_width), BF16)], mib=24, us=1.92)
+    got = [after(g, block_output) for g in got]
     for at in range(len(stages) - 1):
         before, message = scan_link(place, got, before, at, True)
         got = scan_send(message, at + 1, True)
     up_got = mirrored(after(up_send, message), 0)
+    down_got = mirrored(after(down_send, message), 0, True)
     query_late = after(query, message)
     query_grad, dk_part, dv_part = run(
         back_kernel, (shape((tok, width), BF16), shape((tok, width), F32), shape((tok, width), F32)),
         query_late, scaled, value, g_low, lamr, lamc, docr, docc, first_w, state,
         grid=(count,),
         in_specs=[pair_spec] * 4 + [lamr_spec, lamc_spec, None, None, pair_spec, state_spec],
-        out_specs=(pair_spec,) * 3, us=2.14)
+        out_specs=(pair_spec,) * 3, us=1.28)
     got = [after(g, query_grad) for g in got]
     value_grad, shifted_grad, edge, sums, ahead = run(
         functools.partial(carry_kernel, stages[-1]),
@@ -860,65 +867,67 @@
          shape((count, STEP, 8, LANES), F32), shape((tok + STEP, LANES), F32)),
         place, dk_part, dv_part, scaled, value, last_w, beta_w, docr, docc, shift_kernel, prev_tail,
         *got, *before, scalars=1,
-        scratch=[vm((count, STEP, LANES), F32), vm((count, STEP, LANES), F32)], us=1.0)
+        scratch=[vm((count, STEP, LANES), F32), vm((count, STEP, LANES), F32)], us=1.5)
     got_edge = passed_along(edge, -1)
-    down_keep, down_send = folded(place, down_keep, after(down_got, edge), 1, (), 8)
-    down_got = mirrored(down_send, 2)
     mix_keep, mix_send = run(
         functools.partial(grads_kernel, (0, width)), half_shapes(seqs, rows, 2 * width),
-        place, normed1, normed1, query_grad, after(value_grad, down_keep), scalars=1,
-        scratch=[vm((seqs, rows, 2 * width), F32)], us=1.9)
+        place, normed1, normed1, query_grad, after(value_grad, edge), scalars=1,
+        scratch=[vm((seqs, rows, 2 * width), BF16)], us=1.14)
     mix_got = mirrored(mix_send, 0)
+    up_keep, up_send = folded(place, up_keep, after(up_got, mix_keep), 0, (), 8)
+    up_got = mirrored(up_send, 1)
     key_rows, taps_grad = run(
         filter_back_kernel, (shape((tok, width), F32), shape((STEP, width), F32)),
-        shifted_grad, key, ahead, shift_kernel, after(sums, mix_keep),
+        shifted_grad, key, ahead, shift_kernel, after(sums, up_keep),
         scratch=[vm((count, tok + STEP, LANES), F32), vm((count, STEP, LANES), F32),
-                 vm((count, STEP, 8, LANES), F32)], us=4.7)
-    up_keep, up_send = folded(place, up_keep, after(up_got, key_rows), 0, (), 0.2)
-    up_got = mirrored(up_send, 1)
-    down_keep, down_send = folded(place, down_keep, after(down_got, up_keep), 2, (), 2)
-    down_got = mirrored(down_send, 3)
-    mix_keep, mix_send = folded(place, mix_keep, after(mix_got, down_keep), 0, (), 2)
-    mix_got = mirrored(mix_send, 1)
+                 vm((count, STEP, 8, LANES), F32)], us=7.05)
     key_grad, part1 = run(
         out_kernel, (shape((tok, width), BF16), shape((tok + 8, full), BF16)),
-        place, key_rows, after(got_edge, mix_keep), docc, query_grad, value_grad, q_weight, k_weight, v_weight,
+        place, key_rows, after(got_edge, key_rows), docc, query_grad, value_grad, q_weight, k_weight, v_weight,
         block_input, other_input,
-        scratch=[vm((tok, full), BF16), vm((tok, full), F32), vm((8, full), F32)], scalars=1, us=3.6)
+        scratch=[vm((tok, full), BF16), vm((tok, full), F32), vm((8, full), F32)], scalars=1, us=2.16)
     got1 = swapped(part1)
-    up_keep, up_send = folded(place, up_keep, after(up_got, key_grad), 1, (), 8)
+    up_keep, up_send = folded(place, up_keep, after(up_got, key_grad), 1, (), 0.5)
     up_got = mirrored(up_send, 2)
+    mix_keep, mix_send = folded(place, mix_keep, after(mix_got, up_keep), 0, (), 1)
+    mix_got = mirrored(mix_send, 1)
+    down_keep, down_send = folded(place, down_keep, after(down_got, mix_keep), 0, (), 1, True)
+    down_got = mirrored(down_send, 1, True)
     key_keep, key_send = run(
         key_grads_kernel, (shape((seqs // 2 * rows + STEP + 8, width), BF16),) * 2,
-        place, normed1, key_grad, taps_grad, sums2, part1, after(got1, up_keep), scalars=1,
-        scratch=[vm((seqs, rows, width), F32), vm((STEP + 8, width), F32)], us=1.3)
+        place, normed1, key_grad, taps_grad, sums2, part1, after(got1, down_keep), scalars=1,
+        scratch=[vm((seqs, rows, width), BF16), vm((STEP + 8, width), F32)], us=0.78)
     key_got = mirrored(key_send, 0)
     input_grad = run(
         input_kernel, shape((tok, width), BF16),
         place, part1, after(got1, key_keep), block_input, other_input, gain1, resid_grad, scalars=1,
-        scratch=[vm((tok, full), BF16), vm((tok, full), F32)], us=3.7)
-    mix_keep, mix_send = folded(place, mix_keep, after(mix_got, input_grad), 1, (), 1)
+        scratch=[vm((tok, full), BF16), vm((tok, full), F32)], us=0.89)
+    mix_keep, mix_send = folded(place, mix_keep, after(mix_got, input_grad), 1, (), 8)
     mix_got = mirrored(mix_send, 2)
-    key_keep, key_send = folded_message(place, key_keep, after(key_got, mix_keep), 0, rows, 8)
+    down_keep, down_send = folded(place, down_keep, after(down_got, mix_keep), 1, (), 1, True)
+    down_got = mirrored(down_send, 2, True)
+    up_keep, up_send = folded(place, up_keep, after(up_got, down_keep), 2, (), 0.2)
+    up_got = mirrored(up_send, 3)
+    key_keep, key_send = folded_message(place, key_keep, after(key_got, up_keep), 0, rows, 4)
     key_got = mirrored(key_send, 1)
-    (down_total,) = folded_last(place, down_keep, after(down_got, key_keep), 3, (hidden_width,), 0.5)
-    up_keep, up_send = folded(place, up_keep, after(up_got, down_total), 2, (), 0.5)
-    up_got = mirrored(up_send, 3)
-    key_keep, key_send = folded_message(place, key_keep, after(key_got, up_keep), 1, rows, 2)
+    down_keep, down_send = folded(place, down_keep, after(down_got, key_keep), 2, (), 4, True)
+    down_got = mirrored(down_send, 3, True)
+    mix_keep, mix_send = folded(place, mix_keep, after(mix_got, down_keep), 2, (), 4)
+    mix_got = mirrored(mix_send, 3)
+    key_keep, key_send = folded_message(place, key_keep, after(key_got, mix_keep), 1, rows, 2)
     key_got = mirrored(key_send, 2)
-    mix_keep, mix_send = folded(place, mix_keep, after(mix_got, key_keep), 2, (), 1)
-    mix_got = mirrored(mix_send, 3)
-    key_keep, key_send = folded_message(place, key_keep, after(key_got, mix_keep), 2, rows, 0.2)
+    up_total, out_total = folded_last(place, up_keep, after(up_got, key_keep), 3, (hidden_width, width), 1)
+    key_keep, key_send = folded_message(place, key_keep, after(key_got, up_total), 2, rows, 8)
     key_got = mirrored(key_send, 3)
-    up_total, out_total = folded_last(place, up_keep, after(up_got, key_keep), 3, (hidden_width, width), 8)
-    key_got = after(key_got, up_total)
+    (down_total,) = folded_last(place, down_keep, after(down_got, key_keep), 3, (hidden_width,), 0.2, True)
+    key_got = after(key_got, down_total)
     for at in range(3, len(strides_of(seqs)) - 1):
-        key_keep, key_send = folded_message(place, key_keep, key_got, at, rows, 0.2)
+        key_keep, key_send = folded_message(place, key_keep, key_got, at, rows, 8)
         key_got = mirrored(key_send, at + 1)
     k_total, taps_total, vectors = folded_message(
-        place, key_keep, key_got, len(strides_of(seqs)) - 1, rows, 8)
+        place, key_keep, key_got, len(strides_of(seqs)) - 1, rows, 0.5)
     other_vectors = swapped(vectors)
-    q_total, v_total = folded_last(place, mix_keep, after(mix_got, vectors), 3, (width, width), 4)
+    q_total, v_total = folded_last(place, mix_keep, after(mix_got, vectors), 3, (width, width), 0.5)
     gain1_grad, bias1_grad, gain2_grad, bias2_grad = run(
         vector_kernel, (shape((full,), F32),) * 4, place, vectors, after(other_vectors, q_total), scalars=1, us=0.7)
     return (block_output, input_grad, gain1_grad, bias1_grad, q_total, k_total, v_total, taps_total, out_total,

time: 158 us -> 151 us (0.956)
  starting transfers between devices: 42.9 us -> 52.3 us
  waiting for transfers between devices: 23.9 us -> 16.4 us
  Pallas kernels: 86 us -> 80.9 us
    ppermute x16, starting transfers between devices: 18.5 us -> 28.5 us  [mirrored(): return lax.ppermute(array, ('seq', 'head'), pairs)]
    ppermute x16, waiting for transfers between devices: 17.9 us -> 10.7 us  [mirrored(): return lax.ppermute(array, ('seq', 'head'), pairs)]
    pallas_call x37, Pallas kernels: 86 us -> 80.9 us  [run(): pl.pallas_call(body, out_shape=outs, grid=grid, in_specs=[FEW] * scalars...]
  transfers between devices with their start and end apart: 38 -> 38, of which waited for: 13 -> 13; matrix products, arithmetic and copies ran while one was open for 1% -> 0% of each run, Pallas kernels for 49% -> 47%
where the time goes in v3:
time: 151 us
  Pallas kernels  80.9 us (54%)
  starting transfers between devices  52.3 us (35%)
  waiting for transfers between devices  16.4 us (11%)
    pallas_call x37, Pallas kernels, run(): pl.pallas_call(body, out_shape=outs, grid=grid, in_specs=[FEW] * scalars...  80.9 us
    ppermute x16, starting transfers between devices, mirrored(): return lax.ppermute(array, ('seq', 'head'), pairs)  28.5 us
    ppermute x12, starting transfers between devices, turned(): return lax.ppermute(array, 'seq', pairs)  16.3 us
    ppermute x16, waiting for transfers between devices, mirrored(): return lax.ppermute(array, ('seq', 'head'), pairs)  10.7 us
    ppermute x2, starting transfers between devices, passed_along(): lax.ppermute(array, 'seq', [(i, i + by) for i in range(count) if 0 <= i +...  5.77 us
    ppermute x12, waiting for transfers between devices, turned(): return lax.ppermute(array, 'seq', pairs)  3.97 us
  transfers between devices with their start and end apart: 38, of which 13 were waited for; matrix products, arithmetic and copies ran while one was open for 0% of the time, Pallas kernels for 47%

profile of v3, /device:TPU:0, one launch (start us, length us, event | category | flops | bytes accessed | tf_op | source)
XLA Modules:
  0.0 150.8 jit_solution(1610027955022925479)
XLA Ops:
  1.8 3.4 %shard_map.246 = (f32[24,512]{1,0:T(8,128)S(1)}, f32[1536,128]{1,0:T(8,128)S(1)}, f32[8,512]{1,0:T(8,128)S(1)}, f32[512,128]{1,0:T(8,128)S(1)}, f32[512,128]{1,0...) custom-call(s32[512]{0:T(512)} %starts_ref.1, ...), custom_call_target="tpu_custom_call" | custom-call | flops 2700000000 | bytes 8100000 | tf_op jit(solution)/shard_map/pallas_call | solution.py:56
  5.3 2.6 %shard_map.247 = (bf16[512,768]{1,0:T(8,128)(2,1)S(1)}, bf16[512,384]{1,0:T(8,128)(2,1)S(1)}, bf16[512,384]{1,0:T(8,128)(2,1)S(1)}, bf16[512,384]{1,0:T(8,128)(2,1)S(1)}, bf16[64,384]{1,0:T(8,128)(2,1)S(1)}) custom-call(s32[2]{0:T(128)S(1)} %pad_add_fusion.place_ref, bf16[512,384]{1,0:T(8,128)(2,1)S(1)} %copy-done, ...), custom_call_target="tpu_custom_call" | custom-call | flops 3000000000 | bytes 9000000 | tf_op jit(solution)/shard_map/pallas_call | solution.py:56
  7.9 4.5 %collective-permute-start.1 = (bf16[64,384]{1,0:T(8,128)(2,1)S(1)}, bf16[64,384]{1,0:T(8,128)(2,1)S(1)}, u32[]{:S(2)}, u32[]{:S(2)}) collective-permute-start(bf16[64,384]{1,0:T(8,128)(2,1)S(1)} %get-tuple-element.160), channel_id=1, source_target_pairs={{0,2},{2,4},{4,6},{6,8},{8,10},{10,12},{12,14},{14,16},{16,18},{18... | collective-permute-start | bytes 147464 | tf_op jit(solution)/shard_map/ppermute | solution.py:106
  12.4 5.5 %shard_map.248.part_ref = bf16[512,384]{1,0:T(8,128)(2,1)S(1)} custom-call(bf16[512,384]{1,0:T(8,128)(2,1)S(1)} %get-tuple-element.157.k_ref, bf16[64,384]{1,0:T(8,128)(2,1)S(1)} %copy-done.9, f32[512,128]{1,0:T(8,128)S(1)} %get-tuple-element.158.dist_ref, f32[512,384]{1,0:T(8,128)S(1)} %get-tuple-element.159.beta_ref), custom_call_target="tpu_custom_call" | custom-call | flops 5400000000 | bytes 16200000 | tf_op jit(solution)/shard_map/pallas_call | solution.py:56
  17.9 1.1 shard_map.249
  19.0 2.5 %collective-permute-start.5 = (bf16[80,384]{1,0:T(8,128)(2,1)S(1)}, bf16[80,384]{1,0:T(8,128)(2,1)S(1)}, u32[]{:S(2)}, u32[]{:S(2)}) collective-permute-start(bf16[80,384]{1,0:T(8,128)(2,1)S(1)} %get-tuple-element.168.refs_0_), channel_id=1, source_target_pairs={{0,6},{2,0},{4,2},{6,4},{8,14},{10,8},{12,10},{14,12},{16,22},{18,... | collective-permute-start | bytes 184328 | tf_op jit(solution)/shard_map/ppermute | solution.py:88
  22.7 2.6 %shard_map.250 = (bf16[512,1536]{1,0:T(8,128)(2,1)S(1)}, bf16[512,768]{1,0:T(8,128)(2,1)S(1)}) custom-call(s32[2]{0:T(128)S(1)} %pad_add_fusion.place_ref, bf16[512,384]{1,0:T(8,128)(2,1)S(1)} %copy-done.8, bf16[512,384]{1,0:T(8,128)(2,1)S(1)} %collective-permute-done.2.other_ref, bf16[768,1536]{1,0:T(8,128)(2,1)S(1)} %copy-done.3), custom_call_target="tpu_custom_call" | custom-call | flops 2500000000 | bytes 7500000 | tf_op jit(solution)/shard_map/pallas_call | solution.py:56
  25.3 1.2 collective-permute-done.4.refs_2_
  26.4 0.7 collective-permute-done.3.refs_1_
  27.8 3.7 %collective-permute-start.8 = (bf16[80,384]{1,0:T(8,128)(2,1)S(1)}, bf16[80,384]{1,0:T(8,128)(2,1)S(1)}, u32[]{:S(2)}, u32[]{:S(2)}) collective-permute-start(bf16[80,384]{1,0:T(8,128)(2,1)S(1)} %get-tuple-element.179.refs_0_), channel_id=1, source_target_pairs={{0,24},{2,26},{4,28},{6,30},{8,0},{10,2},{12,4},{14,6},{16,8},{18,... | collective-permute-start | bytes 184328 | tf_op jit(solution)/shard_map/ppermute | solution.py:88
  31.5 1.0 collective-permute-start.6
  32.5 3.0 %shard_map.252.inside_ref = f32[512,384]{1,0:T(8,128)S(1)} custom-call(bf16[512,384]{1,0:T(8,128)(2,1)S(1)} %get-tuple-element.204.q_ref, bf16[512,384]{1,0:T(8,128)(2,1)S(1)} %get-tuple-element.174.k_ref, bf16[512,384]{1,0:T(8,128)(2,1)S(1)} %get-tuple-element.163.v_ref, f32[24,512]{1,0:T(8,128)S(1)} %get-tuple-element.175.lamr_ref, ...), custom_call_target="tpu_custom_call" | custom-call | flops 3500000000 | bytes 10500000 | tf_op jit(solution)/shard_map/pallas_call | solution.py:56
  35.5 1.1 collective-permute-done.7.refs_2_
  36.6 0.9 collective-permute-done.6.refs_1_
  37.5 0.8 shard_map.253
  38.5 1.7 %collective-permute-done.9.mix_other_ref = bf16[512,384]{1,0:T(8,128)(2,1)S(1)} collective-permute-done((bf16[512,384]{1,0:T(8,128)(2,1)S(1)}, bf16[512,384]{1,0:T(8,128)(2,1)S(1)}, u32[]{:S(2)}, u32[]{:S(2)}) %collective-permute-start.9) | collective-permute-done | bytes 393248 | tf_op jit(solution)/shard_map/ppermute | solution.py:101
  40.2 7.7 %shard_map.254 = (f32[512,768]{1,0:T(8,128)S(1)}, bf16[512,768]{1,0:T(8,128)(2,1)S(1)}, bf16[512,1536]{1,0:T(8,128)(2,1)S(1)}, bf16[512,1536]{1,0:T(8,128)(2,1)S(1)}, bf16[512,768]{1,0:T(8,128)(2,1)S(1)}) custom-call(s32[2]{0:T(128)S(1)} %pad_add_fusion.place_ref, bf16[512,384]{1,0:T(8,128)(2,1)S(1)} %copy-done, ...), custom_call_target="tpu_custom_call" | custom-call | flops 10800000000 | bytes 32400000 | tf_op jit(solution)/shard_map/pallas_call | solution.py:56
  48.1 3.7 %shard_map.255 = (bf16[8,48,1536]{2,1,0:T(8,128)(2,1)S(1)}, bf16[8,48,1536]{2,1,0:T(8,128)(2,1)S(1)}, f32[512,384]{1,0:T(8,128)S(1)}, bf16[512,384]{1,0:T(8,128)(2,1)S(1)}) custom-call(s32[2]{0:T(128)S(1)} %pad_add_fusion.place_ref, bf16[512,768]{1,0:T(8,128)(2,1)S(1)} %get-tuple-element.188.grad_ref, bf16[512,1536]{1,0:T(8,128)(2,1)S(1)} %get-tuple-element.189.hidden_ref, ...), custom_call_target="tpu_custom_call" | custom-call | flops 2460000000 | bytes 7380000 | tf_op jit(solution)/shard_map/pallas_call | solution.py:56
  52.2 2.7 %shard_map.256 = (f32[512,384]{1,0:T(8,128)S(1)}, bf16[512,768]{1,0:T(8,128)(2,1)S(1)}, bf16[512,384]{1,0:T(8,128)(2,1)S(1)}, f32[8,768]{1,0:T(8,128)S(1)}, bf16[80,384]{1,0:T(8,128)(2,1)S(1)}) custom-call(s32[2]{0:T(128)S(1)} %pad_add_fusion.place_ref, bf16[512,768]{1,0:T(8,128)(2,1)S(1)} %get-tuple-element.187.part_ref, ...), custom_call_target="tpu_custom_call" | custom-call | flops 2340000000 | bytes 7020000 | tf_op jit(solution)/shard_map/pallas_call | solution.py:56
  55.1 1.0 collective-permute-start.14
  56.1 2.8 %collective-permute-start.13 = (bf16[80,384]{1,0:T(8,128)(2,1)S(1)}, bf16[80,384]{1,0:T(8,128)(2,1)S(1)}, u32[]{:S(2)}, u32[]{:S(2)}) collective-permute-start(bf16[80,384]{1,0:T(8,128)(2,1)S(1)} %get-tuple-element.199.refs_0_), channel_id=1, source_target_pairs={{0,6},{2,0},{4,2},{6,4},{8,14},{10,8},{12,10},{14,12},{16,22},{18,... | collective-permute-start | bytes 184328 | tf_op jit(solution)/shard_map/ppermute | solution.py:88
  58.9 3.5 %shard_map.257 = (bf16[8,48,1920]{2,1,0:T(8,128)(2,1)S(1)}, bf16[8,48,1920]{2,1,0:T(8,128)(2,1)S(1)}, bf16[512,384]{1,0:T(8,128)(2,1)}) custom-call(s32[2]{0:T(128)S(1)} %pad_add_fusion.place_ref, bf16[512,768]{1,0:T(8,128)(2,1)S(1)} %get-tuple-element.194.refs_0_, bf16[512,768]{1,0:T(8,128)(2,1)S(1)} %get-tuple-element.195.refs_1_, ...), custom_call_target="tpu_custom_call" | custom-call | flops 1920000000 | bytes 5760000 | tf_op jit(solution)/shard_map/pallas_call | solution.py:56
  62.4 0.7 shard_map.258
  63.1 1.3 collective-permute-start.19
  64.9 1.0 collective-permute-start.17
  65.9 2.6 %collective-permute-start.16 = (bf16[80,384]{1,0:T(8,128)(2,1)S(1)}, bf16[80,384]{1,0:T(8,128)(2,1)S(1)}, u32[]{:S(2)}, u32[]{:S(2)}) collective-permute-start(bf16[80,384]{1,0:T(8,128)(2,1)S(1)} %get-tuple-element.210.refs_0_), channel_id=1, source_target_pairs={{0,24},{2,26},{4,28},{6,30},{8,0},{10,2},{12,4},{14,6},{16,8},{18,... | collective-permute-start | bytes 184328 | tf_op jit(solution)/shard_map/ppermute | solution.py:88
  68.4 5.5 %shard_map.259 = (bf16[512,384]{1,0:T(8,128)(2,1)S(1)}, f32[512,384]{1,0:T(8,128)S(1)}, f32[512,384]{1,0:T(8,128)S(1)}) custom-call(bf16[512,384]{1,0:T(8,128)(2,1)S(1)} %get-tuple-element.204.q_ref, bf16[512,384]{1,0:T(8,128)(2,1)S(1)} %get-tuple-element.174.k_ref, bf16[512,384]{1,0:T(8,128)(2,1)S(1)} %get-tuple-element.163.v_ref, ...), custom_call_target="tpu_custom_call" | custom-call | flops 1280000000 | bytes 3840000 | tf_op jit(solution)/shard_map/pallas_call | solution.py:56
  74.4 2.6 %shard_map.260 = (bf16[512,384]{1,0:T(8,128)(2,1)S(1)}, f32[3,640,128]{2,1,0:T(8,128)S(1)}, bf16[64,384]{1,0:T(8,128)(2,1)S(1)}, f32[3,64,8,128]{3,2,1,0:T(8,128)S(1)}, f32[576,128]{1,0:T(8,128)S(1)}) custom-call(s32[2]{0:T(128)S(1)} %pad_add_fusion.place_ref, f32[512,384]{1,0:T(8,128)S(1)} %get-tuple-element.207.dk_ref, ...), custom_call_target="tpu_custom_call" | custom-call | flops 1500000000 | bytes 4500000 | tf_op jit(solution)/shard_map/pallas_call | solution.py:56
  76.9 1.3 collective-permute-start.20
  78.2 1.7 %shard_map.261 = (bf16[8,48,768]{2,1,0:T(8,128)(2,1)S(1)}, bf16[8,48,768]{2,1,0:T(8,128)(2,1)S(1)}) custom-call(s32[2]{0:T(128)S(1)} %pad_add_fusion.place_ref, bf16[512,768]{1,0:T(8,128)(2,1)S(1)} %get-tuple-element.222.refs_0_.refs_1_.normed_ref, bf16[512,768]{1,0:T(8,128)(2,1)S(1)} %get-tuple-element.222.refs_0_.refs_1_.normed_ref, ...), custom_call_target="tpu_custom_call" | custom-call | flops 1140000000 | bytes 3419999 | tf_op jit(solution)/shard_map/pallas_call | solution.py:56
  79.9 2.7 %collective-permute-start.23 = (bf16[8,48,768]{2,1,0:T(8,128)(2,1)S(1)}, bf16[8,48,768]{2,1,0:T(8,128)(2,1)S(1)}, u32[]{:S(2)}, u32[]{:S(2)}) collective-permute-start(bf16[8,48,768]{2,1,0:T(8,128)(2,1)S(1)} %get-tuple-element.239), channel_id=1, source_target_pairs={{0,2},{1,5},{2,0},{3,7},{4,6},{5,1},{6,4},{7,3},{8,10},{9,13},{10,... | collective-permute-start | bytes 1769480 | tf_op jit(solution)/shard_map/ppermute | solution.py:128
  83.1 1.2 shard_map.262
  84.3 1.1 collective-permute-start.24
  85.4 11.6 %shard_map.263 = (f32[512,384]{1,0:T(8,128)S(1)}, f32[64,384]{1,0:T(8,128)S(1)}) custom-call(f32[3,640,128]{2,1,0:T(8,128)S(1)} %get-tuple-element.216.sg_ref, bf16[512,384]{1,0:T(8,128)(2,1)S(1)} %get-tuple-element.157.k_ref, f32[576,128]{1,0:T(8,128)S(1)} %get-tuple-element.217.ahead_ref, bf16[64,384]{1,0:T(8,128)(2,1)S(1)} %copy-done.9, ...), custom_call_target="tpu_custom_call" | custom-call | flops 7049999872 | bytes 21150000 | tf_op jit(solution)/shard_map/pallas_call | solution.py:56
  97.0 2.6 %shard_map.264 = (bf16[512,384]{1,0:T(8,128)(2,1)S(1)}, bf16[520,768]{1,0:T(8,128)(2,1)S(1)}) custom-call(s32[2]{0:T(128)S(1)} %pad_add_fusion.place_ref, f32[512,384]{1,0:T(8,128)S(1)} %get-tuple-element.230.grad_ref, bf16[64,384]{1,0:T(8,128)(2,1)S(1)} %collective-permute-done.20.edge_ref, f32[512,128]{1,0:T(8,128)S(1)} %get-tuple-element.154.docc_ref, ...), custom_call_target="tpu_custom_call" | custom-call | flops 2160000000 | bytes 6480000 | tf_op jit(solution)/shard_map/pallas_call | solution.py:56
  99.7 0.9 shard_map.265
  100.6 0.7 shard_map.266
  101.4 1.0 collective-permute-start.28
  102.4 0.9 collective-permute-done.22.got_ref
  103.3 4.6 %collective-permute-start.26 = (bf16[2,48,1920]{2,1,0:T(8,128)(2,1)S(1)}, bf16[2,48,1920]{2,1,0:T(8,128)(2,1)S(1)}, u32[]{:S(2)}, u32[]{:S(2)}) collective-permute-start(bf16[2,48,1920]{2,1,0:T(8,128)(2,1)S(1)} %get-tuple-element.252), channel_id=1, source_target_pairs={{0,8},{1,17},{2,10},{3,19},{4,12},{5,21},{6,14},{7,23},{8,0},{9,25... | collective-permute-start | bytes 1105928 | tf_op jit(solution)/shard_map/ppermute | solution.py:128
  107.8 1.0 shard_map.267
  108.9 3.4 %collective-permute-start.27 = (bf16[4,48,1536]{2,1,0:T(8,128)(2,1)S(1)}, bf16[4,48,1536]{2,1,0:T(8,128)(2,1)S(1)}, u32[]{:S(2)}, u32[]{:S(2)}) collective-permute-start(bf16[4,48,1536]{2,1,0:T(8,128)(2,1)S(1)} %get-tuple-element.253), channel_id=1, source_target_pairs={{0,2},{1,5},{2,0},{3,7},{4,6},{5,1},{6,4},{7,3},{8,10},{9,13},{10,... | collective-permute-start | bytes 1769480 | tf_op jit(solution)/shard_map/ppermute | solution.py:128
  112.2 1.2 shard_map.268
  113.6 2.5 %shard_map.269 = bf16[512,384]{1,0:T(8,128)(2,1)} custom-call(s32[2]{0:T(128)S(1)} %pad_add_fusion.place_ref, bf16[520,768]{1,0:T(8,128)(2,1)S(1)} %get-tuple-element.232.part_ref, bf16[520,768]{1,0:T(8,128)(2,1)S(1)} %collective-permute-done.21.got_ref, bf16[512,384]{1,0:T(8,128)(2,1)S(1)} %copy-done, bf16[512,384]{1,0:T(8,128)(2,1)S(1)} %collective-permute-done.other_ref, ...), custom_call_target="tpu_custom_call" | custom-call | flops 890000000 | bytes 2670000 | tf_op jit(solution)/shard_map/pallas_call | solution.py:56
  116.7 2.1 %collective-permute-start.30 = (bf16[2,48,768]{2,1,0:T(8,128)(2,1)S(1)}, bf16[2,48,768]{2,1,0:T(8,128)(2,1)S(1)}, u32[]{:S(2)}, u32[]{:S(2)}) collective-permute-start(bf16[2,48,768]{2,1,0:T(8,128)(2,1)S(1)} %get-tuple-element.264), channel_id=1, source_target_pairs={{0,8},{1,17},{2,10},{3,19},{4,12},{5,21},{6,14},{7,23},{8,0},{9,25... | collective-permute-start | bytes 442376 | tf_op jit(solution)/shard_map/ppermute | solution.py:128
  118.8 1.3 collective-permute-done.27.got_ref
  120.1 0.8 shard_map.271
  120.9 0.7 shard_map.272
  121.7 1.9 %collective-permute-start.31 = (bf16[2,48,1536]{2,1,0:T(8,128)(2,1)S(1)}, bf16[2,48,1536]{2,1,0:T(8,128)(2,1)S(1)}, u32[]{:S(2)}, u32[]{:S(2)}) collective-permute-start(bf16[2,48,1536]{2,1,0:T(8,128)(2,1)S(1)} %get-tuple-element.265), channel_id=1, source_target_pairs={{0,4},{1,3},{2,6},{3,1},{4,0},{5,7},{6,2},{7,5},{8,12},{9,11},{10,... | collective-permute-start | bytes 884744 | tf_op jit(solution)/shard_map/ppermute | solution.py:128
  124.5 1.9 %collective-permute-start.29 = (bf16[264,384]{1,0:T(8,128)(2,1)S(1)}, bf16[264,384]{1,0:T(8,128)(2,1)S(1)}, u32[]{:S(2)}, u32[]{:S(2)}) collective-permute-start(bf16[264,384]{1,0:T(8,128)(2,1)S(1)} %get-tuple-element.263), channel_id=1, source_target_pairs={{0,4},{1,3},{2,6},{3,1},{4,0},{5,7},{6,2},{7,5},{8,12},{9,11},{10,... | collective-permute-start | bytes 608264 | tf_op jit(solution)/shard_map/ppermute | solution.py:128
  126.4 2.0 %collective-permute-done.31.got_ref = bf16[2,48,1536]{2,1,0:T(8,128)(2,1)S(1)} collective-permute-done((bf16[2,48,1536]{2,1,0:T(8,128)(2,1)S(1)}, bf16[2,48,1536]{2,1,0:T(8,128)(2,1)S(1)}, u32[]{:S(2)}, u32[]{:S(2)}) %collective-permute-start.31) | collective-permute-done | bytes 294944 | tf_op jit(solution)/shard_map/ppermute | solution.py:128
  128.5 0.7 shard_map.274
  129.8 0.9 collective-permute-done.29.got_ref
  131.3 2.1 %collective-permute-start.32 = (bf16[168,384]{1,0:T(8,128)(2,1)S(1)}, bf16[168,384]{1,0:T(8,128)(2,1)S(1)}, u32[]{:S(2)}, u32[]{:S(2)}) collective-permute-start(bf16[168,384]{1,0:T(8,128)(2,1)S(1)} %get-tuple-element.272), channel_id=1, source_target_pairs={{0,8},{1,17},{2,10},{3,19},{4,12},{5,21},{6,14},{7,23},{8,0},{9,25... | collective-permute-start | bytes 387080 | tf_op jit(solution)/shard_map/ppermute | solution.py:128
  133.4 2.8 %collective-permute-start.35 = (bf16[1,48,1536]{2,1,0:T(8,128)(2,1)S(1)}, bf16[1,48,1536]{2,1,0:T(8,128)(2,1)S(1)}, u32[]{:S(2)}, u32[]{:S(2)}) collective-permute-start(bf16[1,48,1536]{2,1,0:T(8,128)(2,1)S(1)} %get-tuple-element.279), channel_id=1, source_target_pairs={{0,16},{1,9},{2,18},{3,11},{4,20},{5,13},{6,22},{7,15},{8,24},{9,1... | collective-permute-start | bytes 442376 | tf_op jit(solution)/shard_map/ppermute | solution.py:128
  136.2 1.3 shard_map.277
  137.5 2.6 %collective-permute-done.32.got_ref = bf16[168,384]{1,0:T(8,128)(2,1)S(1)} collective-permute-done((bf16[168,384]{1,0:T(8,128)(2,1)S(1)}, bf16[168,384]{1,0:T(8,128)(2,1)S(1)}, u32[]{:S(2)}, u32[]{:S(2)}) %collective-permute-start.32) | collective-permute-done | bytes 129056 | tf_op jit(solution)/shard_map/ppermute | solution.py:128
  140.7 1.2 collective-permute-start.34
  142.0 1.8 %collective-permute-start.37 = (bf16[1,48,768]{2,1,0:T(8,128)(2,1)S(1)}, bf16[1,48,768]{2,1,0:T(8,128)(2,1)S(1)}, u32[]{:S(2)}, u32[]{:S(2)}) collective-permute-start(bf16[1,48,768]{2,1,0:T(8,128)(2,1)S(1)} %get-tuple-element.283), channel_id=1, source_target_pairs={{0,16},{1,9},{2,18},{3,11},{4,20},{5,13},{6,22},{7,15},{8,24},{9,1... | collective-permute-start | bytes 221192 | tf_op jit(solution)/shard_map/ppermute | solution.py:128
  143.7 1.3 shard_map.279
  145.0 2.2 %collective-permute-done.34.got_ref = bf16[120,384]{1,0:T(8,128)(2,1)S(1)} collective-permute-done((bf16[120,384]{1,0:T(8,128)(2,1)S(1)}, bf16[120,384]{1,0:T(8,128)(2,1)S(1)}, u32[]{:S(2)}, u32[]{:S(2)}) %collective-permute-start.34) | collective-permute-done | bytes 92192 | tf_op jit(solution)/shard_map/ppermute | solution.py:128
  147.2 1.2 shard_map.280
  148.5 1.2 shard_map.281
  149.7 1.1 shard_map.282
  (76 shorter events, 8.7 us)
Async XLA Ops:
  0.6 4.6 %collective-permute-start = (bf16[512,384]{1,0:T(8,128)(2,1)}, bf16[512,384]{1,0:T(8,128)(2,1)S(1)}, u32[]{:S(2)}, u32[]{:S(2)}) collective-permute-start(bf16[512,384]{1,0:T(8,128)(2,1)} %own_ref.9), channel_id=1, source_target_pairs={{0,1},{1,0},{2,3},{3,2},{4,5},{5,4},{6,7},{7,6},{8,9},{9,8},{10,11... | collective-permute-start | bytes 1179656 | tf_op jit(solution)/shard_map/ppermute | solution.py:101
  1.2 21.5 %collective-permute-start.2 = (bf16[512,384]{1,0:T(8,128)(2,1)}, bf16[512,384]{1,0:T(8,128)(2,1)S(1)}, u32[]{:S(2)}, u32[]{:S(2)}) collective-permute-start(bf16[512,384]{1,0:T(8,128)(2,1)} %own_ref.6), channel_id=1, source_target_pairs={{0,1},{1,0},{2,3},{3,2},{4,5},{5,4},{6,7},{7,6},{8,9},{9,8},{10,11... | collective-permute-start | bytes 1179656 | tf_op jit(solution)/shard_map/ppermute | solution.py:101
  1.2 37.2 %collective-permute-start.10 = (bf16[768,384]{1,0:T(8,128)(2,1)}, bf16[768,384]{1,0:T(8,128)(2,1)S(1)}, u32[]{:S(2)}, u32[]{:S(2)}) collective-permute-start(bf16[768,384]{1,0:T(8,128)(2,1)} %out_w_ref.1), channel_id=1, source_target_pairs={{0,1},{1,0},{2,3},{3,2},{4,5},{5,4},{6,7},{7,6},{8,9},{9,8},{10,11... | collective-permute-start | bytes 1769480 | tf_op jit(solution)/shard_map/ppermute | solution.py:101
  1.7 3.5 %copy-start = (bf16[512,384]{1,0:T(8,128)(2,1)S(1)}, bf16[512,384]{1,0:T(8,128)(2,1)}, u32[]{:S(2)}) copy-start(bf16[512,384]{1,0:T(8,128)(2,1)} %own_ref.9) | copy-start | bytes 1179652
  1.8 3.5 %copy-start.1 = (f32[768]{0:T(1024)S(1)}, f32[768]{0:T(1024)}, u32[]{:S(2)}) copy-start(f32[768]{0:T(1024)} %gain_ref.7) | copy-start | bytes 9220
  1.8 3.5 %copy-start.5 = (bf16[768,384]{1,0:T(8,128)(2,1)S(1)}, bf16[768,384]{1,0:T(8,128)(2,1)}, u32[]{:S(2)}) copy-start(bf16[768,384]{1,0:T(8,128)(2,1)} %wq_ref.3) | copy-start | bytes 1769476
  1.8 3.5 %copy-start.6 = (bf16[768,384]{1,0:T(8,128)(2,1)S(1)}, bf16[768,384]{1,0:T(8,128)(2,1)}, u32[]{:S(2)}) copy-start(bf16[768,384]{1,0:T(8,128)(2,1)} %wk_ref.3) | copy-start | bytes 1769476
  1.8 3.5 %copy-start.7 = (bf16[768,384]{1,0:T(8,128)(2,1)S(1)}, bf16[768,384]{1,0:T(8,128)(2,1)}, u32[]{:S(2)}) copy-start(bf16[768,384]{1,0:T(8,128)(2,1)} %wv_ref.3) | copy-start | bytes 1769476
  1.8 3.5 %copy-start.10 = (f32[768]{0:T(1024)S(1)}, f32[768]{0:T(1024)}, u32[]{:S(2)}) copy-start(f32[768]{0:T(1024)} %bias_ref.2) | copy-start | bytes 9220
  5.3 7.1 %copy-start.9 = (bf16[64,384]{1,0:T(8,128)(2,1)S(1)}, bf16[64,384]{1,0:T(8,128)(2,1)}, u32[]{:S(2)}) copy-start(bf16[64,384]{1,0:T(8,128)(2,1)} %taps_ref.7) | copy-start | bytes 147460
  7.9 10.0 %collective-permute-start.1 = (bf16[64,384]{1,0:T(8,128)(2,1)S(1)}, bf16[64,384]{1,0:T(8,128)(2,1)S(1)}, u32[]{:S(2)}, u32[]{:S(2)}) collective-permute-start(bf16[64,384]{1,0:T(8,128)(2,1)S(1)} %get-tuple-element.160), channel_id=1, source_target_pairs={{0,2},{2,4},{4,6},{6,8},{8,10},{10,12},{12,14},{14,16},{16,18},{18... | collective-permute-start | bytes 147464 | tf_op jit(solution)/shard_map/ppermute | solution.py:106
  17.9 4.8 %copy-start.3 = (bf16[768,1536]{1,0:T(8,128)(2,1)S(1)}, bf16[768,1536]{1,0:T(8,128)(2,1)}, u32[]{:S(2)}) copy-start(bf16[768,1536]{1,0:T(8,128)(2,1)} %down_ref.3) | copy-start | bytes 7077892
  17.9 4.8 %copy-start.8 = (bf16[512,384]{1,0:T(8,128)(2,1)S(1)}, bf16[512,384]{1,0:T(8,128)(2,1)}, u32[]{:S(2)}) copy-start(bf16[512,384]{1,0:T(8,128)(2,1)} %own_ref.6) | copy-start | bytes 1179652
  19.0 6.2 %collective-permute-start.5 = (bf16[80,384]{1,0:T(8,128)(2,1)S(1)}, bf16[80,384]{1,0:T(8,128)(2,1)S(1)}, u32[]{:S(2)}, u32[]{:S(2)}) collective-permute-start(bf16[80,384]{1,0:T(8,128)(2,1)S(1)} %get-tuple-element.168.refs_0_), channel_id=1, source_target_pairs={{0,6},{2,0},{4,2},{6,4},{8,14},{10,8},{12,10},{14,12},{16,22},{18,... | collective-permute-start | bytes 184328 | tf_op jit(solution)/shard_map/ppermute | solution.py:88
  21.5 4.9 %collective-permute-start.4 = (bf16[80,384]{1,0:T(8,128)(2,1)S(1)}, bf16[80,384]{1,0:T(8,128)(2,1)S(1)}, u32[]{:S(2)}, u32[]{:S(2)}) collective-permute-start(bf16[80,384]{1,0:T(8,128)(2,1)S(1)} %get-tuple-element.168.refs_0_), channel_id=1, source_target_pairs={{0,4},{2,6},{4,0},{6,2},{8,12},{10,14},{12,8},{14,10},{16,20},{18,... | collective-permute-start | bytes 184328 | tf_op jit(solution)/shard_map/ppermute | solution.py:88
  22.1 5.1 %collective-permute-start.3 = (bf16[80,384]{1,0:T(8,128)(2,1)S(1)}, bf16[80,384]{1,0:T(8,128)(2,1)S(1)}, u32[]{:S(2)}, u32[]{:S(2)}) collective-permute-start(bf16[80,384]{1,0:T(8,128)(2,1)S(1)} %get-tuple-element.168.refs_0_), channel_id=1, source_target_pairs={{0,2},{2,4},{4,6},{6,0},{8,10},{10,12},{12,14},{14,8},{16,18},{18,... | collective-permute-start | bytes 184328 | tf_op jit(solution)/shard_map/ppermute | solution.py:88
  27.8 7.6 %collective-permute-start.8 = (bf16[80,384]{1,0:T(8,128)(2,1)S(1)}, bf16[80,384]{1,0:T(8,128)(2,1)S(1)}, u32[]{:S(2)}, u32[]{:S(2)}) collective-permute-start(bf16[80,384]{1,0:T(8,128)(2,1)S(1)} %get-tuple-element.179.refs_0_), channel_id=1, source_target_pairs={{0,24},{2,26},{4,28},{6,30},{8,0},{10,2},{12,4},{14,6},{16,8},{18,... | collective-permute-start | bytes 184328 | tf_op jit(solution)/shard_map/ppermute | solution.py:88
  31.5 5.1 %collective-permute-start.7 = (bf16[80,384]{1,0:T(8,128)(2,1)S(1)}, bf16[80,384]{1,0:T(8,128)(2,1)S(1)}, u32[]{:S(2)}, u32[]{:S(2)}) collective-permute-start(bf16[80,384]{1,0:T(8,128)(2,1)S(1)} %get-tuple-element.179.refs_0_), channel_id=1, source_target_pairs={{0,16},{2,18},{4,20},{6,22},{8,24},{10,26},{12,28},{14,30},{16,0},... | collective-permute-start | bytes 184328 | tf_op jit(solution)/shard_map/ppermute | solution.py:88
  31.5 6.0 %collective-permute-start.6 = (bf16[80,384]{1,0:T(8,128)(2,1)S(1)}, bf16[80,384]{1,0:T(8,128)(2,1)S(1)}, u32[]{:S(2)}, u32[]{:S(2)}) collective-permute-start(bf16[80,384]{1,0:T(8,128)(2,1)S(1)} %get-tuple-element.179.refs_0_), channel_id=1, source_target_pairs={{0,8},{2,10},{4,12},{6,14},{8,16},{10,18},{12,20},{14,22},{16,24},... | collective-permute-start | bytes 184328 | tf_op jit(solution)/shard_map/ppermute | solution.py:88
  37.5 2.6 %copy-start.2 = (bf16[768,1536]{1,0:T(8,128)(2,1)S(1)}, bf16[768,1536]{1,0:T(8,128)(2,1)}, u32[]{:S(2)}) copy-start(bf16[768,1536]{1,0:T(8,128)(2,1)} %up_ref.1) | copy-start | bytes 7077892
  37.5 2.6 %copy-start.4 = (bf16[768,384]{1,0:T(8,128)(2,1)S(1)}, bf16[768,384]{1,0:T(8,128)(2,1)}, u32[]{:S(2)}) copy-start(bf16[768,384]{1,0:T(8,128)(2,1)} %out_w_ref.1) | copy-start | bytes 1769476
  37.5 2.6 %copy-start.11 = (f32[768]{0:T(1024)S(1)}, f32[768]{0:T(1024)}, u32[]{:S(2)}) copy-start(f32[768]{0:T(1024)} %bias_ref.3) | copy-start | bytes 9220
  37.5 2.6 %copy-start.12 = (f32[768]{0:T(1024)S(1)}, f32[768]{0:T(1024)}, u32[]{:S(2)}) copy-start(f32[768]{0:T(1024)} %gain_ref.6) | copy-start | bytes 9220
  38.4 1.8 %collective-permute-start.9 = (bf16[512,384]{1,0:T(8,128)(2,1)S(1)}, bf16[512,384]{1,0:T(8,128)(2,1)S(1)}, u32[]{:S(2)}, u32[]{:S(2)}) collective-permute-start(bf16[512,384]{1,0:T(8,128)(2,1)S(1)} %get-tuple-element.185.mix_own_ref.refs_3_), channel_id=1, source_target_pairs={{0,1},{1,0},{2,3},{3,2},{4,5},{5,4},{6,7},{7,6},{8,9},{9,8},{10,11... | collective-permute-start | bytes 1179656 | tf_op jit(solution)/shard_map/ppermute | solution.py:101
  47.9 4.4 %collective-permute-start.11 = (bf16[512,768]{1,0:T(8,128)(2,1)S(1)}, bf16[512,768]{1,0:T(8,128)(2,1)S(1)}, u32[]{:S(2)}, u32[]{:S(2)}) collective-permute-start(bf16[512,768]{1,0:T(8,128)(2,1)S(1)} %get-tuple-element.187.part_ref), channel_id=1, source_target_pairs={{0,1},{1,0},{2,3},{3,2},{4,5},{5,4},{6,7},{7,6},{8,9},{9,8},{10,11... | collective-permute-start | bytes 2359304 | tf_op jit(solution)/shard_map/ppermute | solution.py:101
  51.8 7.1 %collective-permute-start.12 = (bf16[512,384]{1,0:T(8,128)(2,1)S(1)}, bf16[512,384]{1,0:T(8,128)(2,1)S(1)}, u32[]{:S(2)}, u32[]{:S(2)}) collective-permute-start(bf16[512,384]{1,0:T(8,128)(2,1)S(1)} %get-tuple-element.197), channel_id=1, source_target_pairs={{0,1},{1,0},{2,3},{3,2},{4,5},{5,4},{6,7},{7,6},{8,9},{9,8},{10,11... | collective-permute-start | bytes 1179656 | tf_op jit(solution)/shard_map/ppermute | solution.py:101
  55.0 7.4 %collective-permute-start.15 = (bf16[80,384]{1,0:T(8,128)(2,1)S(1)}, bf16[80,384]{1,0:T(8,128)(2,1)S(1)}, u32[]{:S(2)}, u32[]{:S(2)}) collective-permute-start(bf16[80,384]{1,0:T(8,128)(2,1)S(1)} %get-tuple-element.199.refs_0_), channel_id=1, source_target_pairs={{0,2},{2,4},{4,6},{6,0},{8,10},{10,12},{12,14},{14,8},{16,18},{18,... | collective-permute-start | bytes 184328 | tf_op jit(solution)/shard_map/ppermute | solution.py:88
  55.1 7.3 %collective-permute-start.14 = (bf16[80,384]{1,0:T(8,128)(2,1)S(1)}, bf16[80,384]{1,0:T(8,128)(2,1)S(1)}, u32[]{:S(2)}, u32[]{:S(2)}) collective-permute-start(bf16[80,384]{1,0:T(8,128)(2,1)S(1)} %get-tuple-element.199.refs_0_), channel_id=1, source_target_pairs={{0,4},{2,6},{4,0},{6,2},{8,12},{10,14},{12,8},{14,10},{16,20},{18,... | collective-permute-start | bytes 184328 | tf_op jit(solution)/shard_map/ppermute | solution.py:88
  56.1 6.4 %collective-permute-start.13 = (bf16[80,384]{1,0:T(8,128)(2,1)S(1)}, bf16[80,384]{1,0:T(8,128)(2,1)S(1)}, u32[]{:S(2)}, u32[]{:S(2)}) collective-permute-start(bf16[80,384]{1,0:T(8,128)(2,1)S(1)} %get-tuple-element.199.refs_0_), channel_id=1, source_target_pairs={{0,6},{2,0},{4,2},{6,4},{8,14},{10,8},{12,10},{14,12},{16,22},{18,... | collective-permute-start | bytes 184328 | tf_op jit(solution)/shard_map/ppermute | solution.py:88
  63.1 20.0 %collective-permute-start.19 = (bf16[8,48,1920]{2,1,0:T(8,128)(2,1)S(1)}, bf16[8,48,1920]{2,1,0:T(8,128)(2,1)S(1)}, u32[]{:S(2)}, u32[]{:S(2)}) collective-permute-start(bf16[8,48,1920]{2,1,0:T(8,128)(2,1)S(1)} %get-tuple-element.221), channel_id=1, source_target_pairs={{0,2},{1,5},{2,0},{3,7},{4,6},{5,1},{6,4},{7,3},{8,10},{9,13},{10,... | collective-permute-start | bytes 4423688 | tf_op jit(solution)/shard_map/ppermute | solution.py:128
  64.4 10.0 %collective-permute-start.18 = (bf16[80,384]{1,0:T(8,128)(2,1)S(1)}, bf16[80,384]{1,0:T(8,128)(2,1)S(1)}, u32[]{:S(2)}, u32[]{:S(2)}) collective-permute-start(bf16[80,384]{1,0:T(8,128)(2,1)S(1)} %get-tuple-element.210.refs_0_), channel_id=1, source_target_pairs={{0,8},{2,10},{4,12},{6,14},{8,16},{10,18},{12,20},{14,22},{16,24},... | collective-permute-start | bytes 184328 | tf_op jit(solution)/shard_map/ppermute | solution.py:88
  64.9 9.5 %collective-permute-start.17 = (bf16[80,384]{1,0:T(8,128)(2,1)S(1)}, bf16[80,384]{1,0:T(8,128)(2,1)S(1)}, u32[]{:S(2)}, u32[]{:S(2)}) collective-permute-start(bf16[80,384]{1,0:T(8,128)(2,1)S(1)} %get-tuple-element.210.refs_0_), channel_id=1, source_target_pairs={{0,16},{2,18},{4,20},{6,22},{8,24},{10,26},{12,28},{14,30},{16,0},... | collective-permute-start | bytes 184328 | tf_op jit(solution)/shard_map/ppermute | solution.py:88
  65.9 8.5 %collective-permute-start.16 = (bf16[80,384]{1,0:T(8,128)(2,1)S(1)}, bf16[80,384]{1,0:T(8,128)(2,1)S(1)}, u32[]{:S(2)}, u32[]{:S(2)}) collective-permute-start(bf16[80,384]{1,0:T(8,128)(2,1)S(1)} %get-tuple-element.210.refs_0_), channel_id=1, source_target_pairs={{0,24},{2,26},{4,28},{6,30},{8,0},{10,2},{12,4},{14,6},{16,8},{18,... | collective-permute-start | bytes 184328 | tf_op jit(solution)/shard_map/ppermute | solution.py:88
  73.9 29.3 %collective-permute-start.22 = (bf16[8,48,1536]{2,1,0:T(8,128)(2,1)S(1)}, bf16[8,48,1536]{2,1,0:T(8,128)(2,1)S(1)}, u32[]{:S(2)}, u32[]{:S(2)}) collective-permute-start(bf16[8,48,1536]{2,1,0:T(8,128)(2,1)S(1)} %get-tuple-element.238), channel_id=1, source_target_pairs={{0,8},{1,17},{2,10},{3,19},{4,12},{5,21},{6,14},{7,23},{8,0},{9,25... | collective-permute-start | bytes 3538952 | tf_op jit(solution)/shard_map/ppermute | solution.py:128
  76.9 20.1 %collective-permute-start.20 = (bf16[64,384]{1,0:T(8,128)(2,1)S(1)}, bf16[64,384]{1,0:T(8,128)(2,1)S(1)}, u32[]{:S(2)}, u32[]{:S(2)}) collective-permute-start(bf16[64,384]{1,0:T(8,128)(2,1)S(1)} %get-tuple-element.224), channel_id=1, source_target_pairs={{2,0},{4,2},{6,4},{8,6},{10,8},{12,10},{14,12},{16,14},{18,16},{20... | collective-permute-start | bytes 147464 | tf_op jit(solution)/shard_map/ppermute | solution.py:106
  79.9 20.7 %collective-permute-start.23 = (bf16[8,48,768]{2,1,0:T(8,128)(2,1)S(1)}, bf16[8,48,768]{2,1,0:T(8,128)(2,1)S(1)}, u32[]{:S(2)}, u32[]{:S(2)}) collective-permute-start(bf16[8,48,768]{2,1,0:T(8,128)(2,1)S(1)} %get-tuple-element.239), channel_id=1, source_target_pairs={{0,2},{1,5},{2,0},{3,7},{4,6},{5,1},{6,4},{7,3},{8,10},{9,13},{10,... | collective-permute-start | bytes 1769480 | tf_op jit(solution)/shard_map/ppermute | solution.py:128
  84.3 15.5 %collective-permute-start.24 = (bf16[4,48,1920]{2,1,0:T(8,128)(2,1)S(1)}, bf16[4,48,1920]{2,1,0:T(8,128)(2,1)S(1)}, u32[]{:S(2)}, u32[]{:S(2)}) collective-permute-start(bf16[4,48,1920]{2,1,0:T(8,128)(2,1)S(1)} %get-tuple-element.240), channel_id=1, source_target_pairs={{0,4},{1,3},{2,6},{3,1},{4,0},{5,7},{6,2},{7,5},{8,12},{9,11},{10,... | collective-permute-start | bytes 2211848 | tf_op jit(solution)/shard_map/ppermute | solution.py:128
  99.6 12.6 %collective-permute-start.21 = (bf16[520,768]{1,0:T(8,128)(2,1)S(1)}, bf16[520,768]{1,0:T(8,128)(2,1)S(1)}, u32[]{:S(2)}, u32[]{:S(2)}) collective-permute-start(bf16[520,768]{1,0:T(8,128)(2,1)S(1)} %get-tuple-element.232.part_ref), channel_id=1, source_target_pairs={{0,1},{1,0},{2,3},{3,2},{4,5},{5,4},{6,7},{7,6},{8,9},{9,8},{10,11... | collective-permute-start | bytes 2396168 | tf_op jit(solution)/shard_map/ppermute | solution.py:101
  101.4 14.7 %collective-permute-start.28 = (bf16[4,48,768]{2,1,0:T(8,128)(2,1)S(1)}, bf16[4,48,768]{2,1,0:T(8,128)(2,1)S(1)}, u32[]{:S(2)}, u32[]{:S(2)}) collective-permute-start(bf16[4,48,768]{2,1,0:T(8,128)(2,1)S(1)} %get-tuple-element.254), channel_id=1, source_target_pairs={{0,4},{1,3},{2,6},{3,1},{4,0},{5,7},{6,2},{7,5},{8,12},{9,11},{10,... | collective-permute-start | bytes 884744 | tf_op jit(solution)/shard_map/ppermute | solution.py:128
  103.3 17.6 %collective-permute-start.26 = (bf16[2,48,1920]{2,1,0:T(8,128)(2,1)S(1)}, bf16[2,48,1920]{2,1,0:T(8,128)(2,1)S(1)}, u32[]{:S(2)}, u32[]{:S(2)}) collective-permute-start(bf16[2,48,1920]{2,1,0:T(8,128)(2,1)S(1)} %get-tuple-element.252), channel_id=1, source_target_pairs={{0,8},{1,17},{2,10},{3,19},{4,12},{5,21},{6,14},{7,23},{8,0},{9,25... | collective-permute-start | bytes 1105928 | tf_op jit(solution)/shard_map/ppermute | solution.py:128
  108.9 11.2 %collective-permute-start.27 = (bf16[4,48,1536]{2,1,0:T(8,128)(2,1)S(1)}, bf16[4,48,1536]{2,1,0:T(8,128)(2,1)S(1)}, u32[]{:S(2)}, u32[]{:S(2)}) collective-permute-start(bf16[4,48,1536]{2,1,0:T(8,128)(2,1)S(1)} %get-tuple-element.253), channel_id=1, source_target_pairs={{0,2},{1,5},{2,0},{3,7},{4,6},{5,1},{6,4},{7,3},{8,10},{9,13},{10,... | collective-permute-start | bytes 1769480 | tf_op jit(solution)/shard_map/ppermute | solution.py:128
  113.5 10.4 %collective-permute-start.25 = (bf16[456,384]{1,0:T(8,128)(2,1)S(1)}, bf16[456,384]{1,0:T(8,128)(2,1)S(1)}, u32[]{:S(2)}, u32[]{:S(2)}) collective-permute-start(bf16[456,384]{1,0:T(8,128)(2,1)S(1)} %get-tuple-element.251), channel_id=1, source_target_pairs={{0,2},{1,5},{2,0},{3,7},{4,6},{5,1},{6,4},{7,3},{8,10},{9,13},{10,... | collective-permute-start | bytes 1050632 | tf_op jit(solution)/shard_map/ppermute | solution.py:128
  116.7 12.5 %collective-permute-start.30 = (bf16[2,48,768]{2,1,0:T(8,128)(2,1)S(1)}, bf16[2,48,768]{2,1,0:T(8,128)(2,1)S(1)}, u32[]{:S(2)}, u32[]{:S(2)}) collective-permute-start(bf16[2,48,768]{2,1,0:T(8,128)(2,1)S(1)} %get-tuple-element.264), channel_id=1, source_target_pairs={{0,8},{1,17},{2,10},{3,19},{4,12},{5,21},{6,14},{7,23},{8,0},{9,25... | collective-permute-start | bytes 442376 | tf_op jit(solution)/shard_map/ppermute | solution.py:128
  121.6 14.6 %collective-permute-start.33 = (bf16[1,48,1920]{2,1,0:T(8,128)(2,1)S(1)}, bf16[1,48,1920]{2,1,0:T(8,128)(2,1)S(1)}, u32[]{:S(2)}, u32[]{:S(2)}) collective-permute-start(bf16[1,48,1920]{2,1,0:T(8,128)(2,1)S(1)} %get-tuple-element.273), channel_id=1, source_target_pairs={{0,16},{1,9},{2,18},{3,11},{4,20},{5,13},{6,22},{7,15},{8,24},{9,1... | collective-permute-start | bytes 552968 | tf_op jit(solution)/shard_map/ppermute | solution.py:128
  121.7 6.8 %collective-permute-start.31 = (bf16[2,48,1536]{2,1,0:T(8,128)(2,1)S(1)}, bf16[2,48,1536]{2,1,0:T(8,128)(2,1)S(1)}, u32[]{:S(2)}, u32[]{:S(2)}) collective-permute-start(bf16[2,48,1536]{2,1,0:T(8,128)(2,1)S(1)} %get-tuple-element.265), channel_id=1, source_target_pairs={{0,4},{1,3},{2,6},{3,1},{4,0},{5,7},{6,2},{7,5},{8,12},{9,11},{10,... | collective-permute-start | bytes 884744 | tf_op jit(solution)/shard_map/ppermute | solution.py:128
  124.5 6.1 %collective-permute-start.29 = (bf16[264,384]{1,0:T(8,128)(2,1)S(1)}, bf16[264,384]{1,0:T(8,128)(2,1)S(1)}, u32[]{:S(2)}, u32[]{:S(2)}) collective-permute-start(bf16[264,384]{1,0:T(8,128)(2,1)S(1)} %get-tuple-element.263), channel_id=1, source_target_pairs={{0,4},{1,3},{2,6},{3,1},{4,0},{5,7},{6,2},{7,5},{8,12},{9,11},{10,... | collective-permute-start | bytes 608264 | tf_op jit(solution)/shard_map/ppermute | solution.py:128
  131.3 8.9 %collective-permute-start.32 = (bf16[168,384]{1,0:T(8,128)(2,1)S(1)}, bf16[168,384]{1,0:T(8,128)(2,1)S(1)}, u32[]{:S(2)}, u32[]{:S(2)}) collective-permute-start(bf16[168,384]{1,0:T(8,128)(2,1)S(1)} %get-tuple-element.272), channel_id=1, source_target_pairs={{0,8},{1,17},{2,10},{3,19},{4,12},{5,21},{6,14},{7,23},{8,0},{9,25... | collective-permute-start | bytes 387080 | tf_op jit(solution)/shard_map/ppermute | solution.py:128
  133.4 10.4 %collective-permute-start.35 = (bf16[1,48,1536]{2,1,0:T(8,128)(2,1)S(1)}, bf16[1,48,1536]{2,1,0:T(8,128)(2,1)S(1)}, u32[]{:S(2)}, u32[]{:S(2)}) collective-permute-start(bf16[1,48,1536]{2,1,0:T(8,128)(2,1)S(1)} %get-tuple-element.279), channel_id=1, source_target_pairs={{0,16},{1,9},{2,18},{3,11},{4,20},{5,13},{6,22},{7,15},{8,24},{9,1... | collective-permute-start | bytes 442376 | tf_op jit(solution)/shard_map/ppermute | solution.py:128
  140.7 6.5 %collective-permute-start.34 = (bf16[120,384]{1,0:T(8,128)(2,1)S(1)}, bf16[120,384]{1,0:T(8,128)(2,1)S(1)}, u32[]{:S(2)}, u32[]{:S(2)}) collective-permute-start(bf16[120,384]{1,0:T(8,128)(2,1)S(1)} %get-tuple-element.278), channel_id=1, source_target_pairs={{0,16},{1,9},{2,18},{3,11},{4,20},{5,13},{6,22},{7,15},{8,24},{9,1... | collective-permute-start | bytes 276488 | tf_op jit(solution)/shard_map/ppermute | solution.py:128
  142.0 6.5 %collective-permute-start.37 = (bf16[1,48,768]{2,1,0:T(8,128)(2,1)S(1)}, bf16[1,48,768]{2,1,0:T(8,128)(2,1)S(1)}, u32[]{:S(2)}, u32[]{:S(2)}) collective-permute-start(bf16[1,48,768]{2,1,0:T(8,128)(2,1)S(1)} %get-tuple-element.283), channel_id=1, source_target_pairs={{0,16},{1,9},{2,18},{3,11},{4,20},{5,13},{6,22},{7,15},{8,24},{9,1... | collective-permute-start | bytes 221192 | tf_op jit(solution)/shard_map/ppermute | solution.py:128
  148.5 1.2 collective-permute-start.36

commit v4 on v3

--- a/solution.py
+++ b/solution.py
@@ -11,6 +11,7 @@
 RATE_CAP = 0.05
 LANES = 128
 STEP = 64
+SPAN = 32
 FAR = float(1 << 20)
 GELU_SCALE = 0.7978845608028654
 GELU_CUBE = 0.044715
@@ -401,7 +402,7 @@
                       - unit_rows * (jnp.sum(scaled * unit_rows, axis=1, keepdims=True) * scale))
 
 
-def by_rows(tok, body, size=256):
+def by_rows(tok, body, size=512):
     def step(i, carry):
         body(pl.ds(pl.multiple_of(i * size, size), size))
         return carry
@@ -434,15 +435,15 @@
 def filter_chunk(keys, taps, dist, count, t0):
     def group(a, acc):
         acc = list(acc)
-        for b in range(8):
-            j = a * 8 + b
+        for b in range(32):
+            j = a * 32 + b
             keep = dist >= j.astype(F32)
             for l in range(count):
-                x = keys[l, pl.ds(STEP + t0 - a * 8 - b, STEP), :]
+                x = keys[l, pl.ds(STEP + t0 - a * 32 - b, STEP), :]
                 acc[l] = acc[l] + jnp.where(keep, x * taps[l, pl.ds(j, 1), :], 0.0)
         return tuple(acc)
 
-    return lax.fori_loop(0, 8, group, tuple(jnp.zeros((STEP, LANES), F32) for _ in range(count)))
+    return lax.fori_loop(0, STEP // 32, group, tuple(jnp.zeros((STEP, LANES), F32) for _ in range(count)))
 
 
 def filter_kernel(k_ref, taps_ref, dist_ref, beta_ref, out_ref, keys, taps):
@@ -623,20 +624,20 @@
 
 
 def filter_back_chunk(sg, keys, taps, ahead, sums, count, s0):
-    held = [keys[l, pl.ds(s0, STEP), :] for l in range(count)]
+    held = [keys[l, pl.ds(s0, SPAN), :] for l in range(count)]
 
     def group(a, acc):
         acc = list(acc)
-        for b in range(8):
-            j = a * 8 + b
+        for b in range(16):
+            j = a * 16 + b
             keep = ahead > j.astype(F32)
             for l in range(count):
-                u = jnp.where(keep, sg[l, pl.ds(s0 + a * 8 + b, STEP), :], 0.0)
+                u = jnp.where(keep, sg[l, pl.ds(s0 + a * 16 + b, SPAN), :], 0.0)
                 acc[l] = acc[l] + u * taps[l, pl.ds(j, 1), :]
-                sums[l, j] += jnp.sum((held[l] * u).reshape(STEP // 8, 8, LANES), axis=0)
+                sums[l, j] += jnp.sum((held[l] * u).reshape(SPAN // 8, 8, LANES), axis=0)
         return tuple(acc)
 
-    return lax.fori_loop(0, 8, group, tuple(jnp.zeros((STEP, LANES), F32) for _ in range(count)))
+    return lax.fori_loop(0, STEP // 16, group, tuple(jnp.zeros((SPAN, LANES), F32) for _ in range(count)))
 
 
 def reach(docr_ref, docc_ref, ahead_ref):
@@ -669,9 +670,11 @@
         keys[l] = tail_ref[:, span].astype(F32)
         taps[l] = taps_ref[:, span].astype(F32)
     sums[...] = jnp.zeros_like(sums)
-    acc = filter_back_chunk(sg_ref, keys, taps, ahead_ref[:STEP], sums, count, 0)
-    for l in range(count):
-        edge_ref[:, l * LANES : (l + 1) * LANES] = acc[l].astype(BF16)
+    for s0 in range(0, STEP, SPAN):
+        at = slice(s0, s0 + SPAN)
+        acc = filter_back_chunk(sg_ref, keys, taps, ahead_ref[at], sums, count, s0)
+        for l in range(count):
+            edge_ref[at, l * LANES : (l + 1) * LANES] = acc[l].astype(BF16)
 
 
 def filter_back_kernel(sg_ref, k_ref, ahead_ref, taps_ref, sums_in, grad_ref, taps_grad_ref, keys, taps, sums):
@@ -684,13 +687,13 @@
     sums[...] = sums_in[...]
 
     def chunk(c, carry):
-        s0 = pl.multiple_of(c * STEP, STEP)
-        acc = filter_back_chunk(sg_ref, keys, taps, ahead_ref[pl.ds(s0, STEP)], sums, count, s0)
+        s0 = pl.multiple_of(c * SPAN, SPAN)
+        acc = filter_back_chunk(sg_ref, keys, taps, ahead_ref[pl.ds(s0, SPAN)], sums, count, s0)
         for l in range(count):
-            grad_ref[pl.ds(s0 - STEP, STEP), l * LANES : (l + 1) * LANES] = acc[l]
+            grad_ref[pl.ds(s0 - STEP, SPAN), l * LANES : (l + 1) * LANES] = acc[l]
         return carry
 
-    lax.fori_loop(1, tok // STEP + 1, chunk, 0)
+    lax.fori_loop(STEP // SPAN, (tok + STEP) // SPAN, chunk, 0)
     for l in range(count):
         taps_grad_ref[:, l * LANES : (l + 1) * LANES] = jnp.sum(sums[l], axis=1)
 

time: 151 us -> 150 us (level)
  Pallas kernels: 80.9 us -> 77.4 us
  waiting for transfers between devices: 16.4 us -> 18.8 us
    pallas_call x37, Pallas kernels: 80.9 us -> 77.4 us  [run(): pl.pallas_call(body, out_shape=outs, grid=grid, in_specs=[FEW] * scalars...]
    ppermute x16, waiting for transfers between devices: 10.7 us -> 13.1 us  [mirrored(): return lax.ppermute(array, ('seq', 'head'), pairs)]
  transfers between devices with their start and end apart: 38 -> 38, of which waited for: 13 -> 13; matrix products, arithmetic and copies ran while one was open for 0% -> 0% of each run, Pallas kernels for 47% -> 46%
where the time goes in v4:
time: 150 us; the launch traced here: 149 us
  Pallas kernels  77.4 us (52%)
  starting transfers between devices  52 us (35%)
  waiting for transfers between devices  18.8 us (13%)
    pallas_call x37, Pallas kernels, run(): pl.pallas_call(body, out_shape=outs, grid=grid, in_specs=[FEW] * scalars...  77.4 us
    ppermute x16, starting transfers between devices, mirrored(): return lax.ppermute(array, ('seq', 'head'), pairs)  28.2 us
    ppermute x12, starting transfers between devices, turned(): return lax.ppermute(array, 'seq', pairs)  16.3 us
    ppermute x16, waiting for transfers between devices, mirrored(): return lax.ppermute(array, ('seq', 'head'), pairs)  13.1 us
    ppermute x2, starting transfers between devices, passed_along(): lax.ppermute(array, 'seq', [(i, i + by) for i in range(count) if 0 <= i +...  5.77 us
    ppermute x12, waiting for transfers between devices, turned(): return lax.ppermute(array, 'seq', pairs)  3.98 us
  transfers between devices with their start and end apart: 38, of which 13 were waited for; matrix products, arithmetic and copies ran while one was open for 0% of the time, Pallas kernels for 46%

profile of v4, /device:TPU:0, one launch (start us, length us, event | category | flops | bytes accessed | tf_op | source)
XLA Modules:
  0.0 149.4 jit_solution(5531435730790171664)
XLA Ops:
  1.8 3.4 %shard_map.246 = (f32[24,512]{1,0:T(8,128)S(1)}, f32[1536,128]{1,0:T(8,128)S(1)}, f32[8,512]{1,0:T(8,128)S(1)}, f32[512,128]{1,0:T(8,128)S(1)}, f32[512,128]{1,0...) custom-call(s32[512]{0:T(512)} %starts_ref.1, ...), custom_call_target="tpu_custom_call" | custom-call | flops 2700000000 | bytes 8100000 | tf_op jit(solution)/shard_map/pallas_call | solution.py:57
  5.3 2.3 %shard_map.247 = (bf16[512,768]{1,0:T(8,128)(2,1)S(1)}, bf16[512,384]{1,0:T(8,128)(2,1)S(1)}, bf16[512,384]{1,0:T(8,128)(2,1)S(1)}, bf16[512,384]{1,0:T(8,128)(2,1)S(1)}, bf16[64,384]{1,0:T(8,128)(2,1)S(1)}) custom-call(s32[2]{0:T(128)S(1)} %pad_add_fusion.place_ref, bf16[512,384]{1,0:T(8,128)(2,1)S(1)} %copy-done, ...), custom_call_target="tpu_custom_call" | custom-call | flops 3000000000 | bytes 9000000 | tf_op jit(solution)/shard_map/pallas_call | solution.py:57
  7.7 4.5 %collective-permute-start.1 = (bf16[64,384]{1,0:T(8,128)(2,1)S(1)}, bf16[64,384]{1,0:T(8,128)(2,1)S(1)}, u32[]{:S(2)}, u32[]{:S(2)}) collective-permute-start(bf16[64,384]{1,0:T(8,128)(2,1)S(1)} %get-tuple-element.160), channel_id=1, source_target_pairs={{0,2},{2,4},{4,6},{6,8},{8,10},{10,12},{12,14},{14,16},{16,18},{18... | collective-permute-start | bytes 147464 | tf_op jit(solution)/shard_map/ppermute | solution.py:107
  12.1 5.1 %shard_map.248.part_ref = bf16[512,384]{1,0:T(8,128)(2,1)S(1)} custom-call(bf16[512,384]{1,0:T(8,128)(2,1)S(1)} %get-tuple-element.157.k_ref, bf16[64,384]{1,0:T(8,128)(2,1)S(1)} %copy-done.9, f32[512,128]{1,0:T(8,128)S(1)} %get-tuple-element.158.dist_ref, f32[512,384]{1,0:T(8,128)S(1)} %get-tuple-element.159.beta_ref), custom_call_target="tpu_custom_call" | custom-call | flops 5400000000 | bytes 16200000 | tf_op jit(solution)/shard_map/pallas_call | solution.py:57
  17.2 1.1 shard_map.249
  18.3 2.5 %collective-permute-start.5 = (bf16[80,384]{1,0:T(8,128)(2,1)S(1)}, bf16[80,384]{1,0:T(8,128)(2,1)S(1)}, u32[]{:S(2)}, u32[]{:S(2)}) collective-permute-start(bf16[80,384]{1,0:T(8,128)(2,1)S(1)} %get-tuple-element.168.refs_0_), channel_id=1, source_target_pairs={{0,6},{2,0},{4,2},{6,4},{8,14},{10,8},{12,10},{14,12},{16,22},{18,... | collective-permute-start | bytes 184328 | tf_op jit(solution)/shard_map/ppermute | solution.py:89
  21.9 2.6 %shard_map.250 = (bf16[512,1536]{1,0:T(8,128)(2,1)S(1)}, bf16[512,768]{1,0:T(8,128)(2,1)S(1)}) custom-call(s32[2]{0:T(128)S(1)} %pad_add_fusion.place_ref, bf16[512,384]{1,0:T(8,128)(2,1)S(1)} %copy-done.8, bf16[512,384]{1,0:T(8,128)(2,1)S(1)} %collective-permute-done.2.other_ref, bf16[768,1536]{1,0:T(8,128)(2,1)S(1)} %copy-done.3), custom_call_target="tpu_custom_call" | custom-call | flops 2500000000 | bytes 7500000 | tf_op jit(solution)/shard_map/pallas_call | solution.py:57
  24.6 1.2 collective-permute-done.4.refs_2_
  25.7 0.7 collective-permute-done.3.refs_1_
  27.1 3.7 %collective-permute-start.8 = (bf16[80,384]{1,0:T(8,128)(2,1)S(1)}, bf16[80,384]{1,0:T(8,128)(2,1)S(1)}, u32[]{:S(2)}, u32[]{:S(2)}) collective-permute-start(bf16[80,384]{1,0:T(8,128)(2,1)S(1)} %get-tuple-element.179.refs_0_), channel_id=1, source_target_pairs={{0,24},{2,26},{4,28},{6,30},{8,0},{10,2},{12,4},{14,6},{16,8},{18,... | collective-permute-start | bytes 184328 | tf_op jit(solution)/shard_map/ppermute | solution.py:89
  30.8 1.0 collective-permute-start.6
  31.8 2.9 %shard_map.252.inside_ref = f32[512,384]{1,0:T(8,128)S(1)} custom-call(bf16[512,384]{1,0:T(8,128)(2,1)S(1)} %get-tuple-element.204.q_ref, bf16[512,384]{1,0:T(8,128)(2,1)S(1)} %get-tuple-element.174.k_ref, bf16[512,384]{1,0:T(8,128)(2,1)S(1)} %get-tuple-element.163.v_ref, f32[24,512]{1,0:T(8,128)S(1)} %get-tuple-element.175.lamr_ref, ...), custom_call_target="tpu_custom_call" | custom-call | flops 3500000000 | bytes 10500000 | tf_op jit(solution)/shard_map/pallas_call | solution.py:57
  34.8 1.1 collective-permute-done.7.refs_2_
  35.9 0.9 collective-permute-done.6.refs_1_
  36.8 0.8 shard_map.253
  37.8 1.7 %collective-permute-done.9.mix_other_ref = bf16[512,384]{1,0:T(8,128)(2,1)S(1)} collective-permute-done((bf16[512,384]{1,0:T(8,128)(2,1)S(1)}, bf16[512,384]{1,0:T(8,128)(2,1)S(1)}, u32[]{:S(2)}, u32[]{:S(2)}) %collective-permute-start.9) | collective-permute-done | bytes 393248 | tf_op jit(solution)/shard_map/ppermute | solution.py:102
  39.5 7.5 %shard_map.254 = (f32[512,768]{1,0:T(8,128)S(1)}, bf16[512,768]{1,0:T(8,128)(2,1)S(1)}, bf16[512,1536]{1,0:T(8,128)(2,1)S(1)}, bf16[512,1536]{1,0:T(8,128)(2,1)S(1)}, bf16[512,768]{1,0:T(8,128)(2,1)S(1)}) custom-call(s32[2]{0:T(128)S(1)} %pad_add_fusion.place_ref, bf16[512,384]{1,0:T(8,128)(2,1)S(1)} %copy-done, ...), custom_call_target="tpu_custom_call" | custom-call | flops 10800000000 | bytes 32400000 | tf_op jit(solution)/shard_map/pallas_call | solution.py:57
  47.1 3.7 %shard_map.255 = (bf16[8,48,1536]{2,1,0:T(8,128)(2,1)S(1)}, bf16[8,48,1536]{2,1,0:T(8,128)(2,1)S(1)}, f32[512,384]{1,0:T(8,128)S(1)}, bf16[512,384]{1,0:T(8,128)(2,1)S(1)}) custom-call(s32[2]{0:T(128)S(1)} %pad_add_fusion.place_ref, bf16[512,768]{1,0:T(8,128)(2,1)S(1)} %get-tuple-element.188.grad_ref, bf16[512,1536]{1,0:T(8,128)(2,1)S(1)} %get-tuple-element.189.hidden_ref, ...), custom_call_target="tpu_custom_call" | custom-call | flops 2460000000 | bytes 7380000 | tf_op jit(solution)/shard_map/pallas_call | solution.py:57
  51.3 2.6 %shard_map.256 = (f32[512,384]{1,0:T(8,128)S(1)}, bf16[512,768]{1,0:T(8,128)(2,1)S(1)}, bf16[512,384]{1,0:T(8,128)(2,1)S(1)}, f32[8,768]{1,0:T(8,128)S(1)}, bf16[80,384]{1,0:T(8,128)(2,1)S(1)}) custom-call(s32[2]{0:T(128)S(1)} %pad_add_fusion.place_ref, bf16[512,768]{1,0:T(8,128)(2,1)S(1)} %get-tuple-element.187.part_ref, ...), custom_call_target="tpu_custom_call" | custom-call | flops 2340000000 | bytes 7020000 | tf_op jit(solution)/shard_map/pallas_call | solution.py:57
  54.0 1.0 collective-permute-start.14
  55.0 2.8 %collective-permute-start.13 = (bf16[80,384]{1,0:T(8,128)(2,1)S(1)}, bf16[80,384]{1,0:T(8,128)(2,1)S(1)}, u32[]{:S(2)}, u32[]{:S(2)}) collective-permute-start(bf16[80,384]{1,0:T(8,128)(2,1)S(1)} %get-tuple-element.199.refs_0_), channel_id=1, source_target_pairs={{0,6},{2,0},{4,2},{6,4},{8,14},{10,8},{12,10},{14,12},{16,22},{18,... | collective-permute-start | bytes 184328 | tf_op jit(solution)/shard_map/ppermute | solution.py:89
  57.8 3.5 %shard_map.257 = (bf16[8,48,1920]{2,1,0:T(8,128)(2,1)S(1)}, bf16[8,48,1920]{2,1,0:T(8,128)(2,1)S(1)}, bf16[512,384]{1,0:T(8,128)(2,1)}) custom-call(s32[2]{0:T(128)S(1)} %pad_add_fusion.place_ref, bf16[512,768]{1,0:T(8,128)(2,1)S(1)} %get-tuple-element.194.refs_0_, bf16[512,768]{1,0:T(8,128)(2,1)S(1)} %get-tuple-element.195.refs_1_, ...), custom_call_target="tpu_custom_call" | custom-call | flops 1920000000 | bytes 5760000 | tf_op jit(solution)/shard_map/pallas_call | solution.py:57
  61.3 0.7 shard_map.258
  62.0 1.3 collective-permute-start.19
  63.8 1.0 collective-permute-start.17
  64.8 2.6 %collective-permute-start.16 = (bf16[80,384]{1,0:T(8,128)(2,1)S(1)}, bf16[80,384]{1,0:T(8,128)(2,1)S(1)}, u32[]{:S(2)}, u32[]{:S(2)}) collective-permute-start(bf16[80,384]{1,0:T(8,128)(2,1)S(1)} %get-tuple-element.210.refs_0_), channel_id=1, source_target_pairs={{0,24},{2,26},{4,28},{6,30},{8,0},{10,2},{12,4},{14,6},{16,8},{18,... | collective-permute-start | bytes 184328 | tf_op jit(solution)/shard_map/ppermute | solution.py:89
  67.3 5.5 %shard_map.259 = (bf16[512,384]{1,0:T(8,128)(2,1)S(1)}, f32[512,384]{1,0:T(8,128)S(1)}, f32[512,384]{1,0:T(8,128)S(1)}) custom-call(bf16[512,384]{1,0:T(8,128)(2,1)S(1)} %get-tuple-element.204.q_ref, bf16[512,384]{1,0:T(8,128)(2,1)S(1)} %get-tuple-element.174.k_ref, bf16[512,384]{1,0:T(8,128)(2,1)S(1)} %get-tuple-element.163.v_ref, ...), custom_call_target="tpu_custom_call" | custom-call | flops 1280000000 | bytes 3840000 | tf_op jit(solution)/shard_map/pallas_call | solution.py:57
  73.3 2.4 %shard_map.260 = (bf16[512,384]{1,0:T(8,128)(2,1)S(1)}, f32[3,640,128]{2,1,0:T(8,128)S(1)}, bf16[64,384]{1,0:T(8,128)(2,1)S(1)}, f32[3,64,8,128]{3,2,1,0:T(8,128)S(1)}, f32[576,128]{1,0:T(8,128)S(1)}) custom-call(s32[2]{0:T(128)S(1)} %pad_add_fusion.place_ref, f32[512,384]{1,0:T(8,128)S(1)} %get-tuple-element.207.dk_ref, ...), custom_call_target="tpu_custom_call" | custom-call | flops 1500000000 | bytes 4500000 | tf_op jit(solution)/shard_map/pallas_call | solution.py:57
  75.6 1.3 collective-permute-start.20
  76.9 1.7 %shard_map.261 = (bf16[8,48,768]{2,1,0:T(8,128)(2,1)S(1)}, bf16[8,48,768]{2,1,0:T(8,128)(2,1)S(1)}) custom-call(s32[2]{0:T(128)S(1)} %pad_add_fusion.place_ref, bf16[512,768]{1,0:T(8,128)(2,1)S(1)} %get-tuple-element.222.refs_0_.refs_1_.normed_ref, bf16[512,768]{1,0:T(8,128)(2,1)S(1)} %get-tuple-element.222.refs_0_.refs_1_.normed_ref, ...), custom_call_target="tpu_custom_call" | custom-call | flops 1140000000 | bytes 3419999 | tf_op jit(solution)/shard_map/pallas_call | solution.py:57
  78.6 2.7 %collective-permute-start.23 = (bf16[8,48,768]{2,1,0:T(8,128)(2,1)S(1)}, bf16[8,48,768]{2,1,0:T(8,128)(2,1)S(1)}, u32[]{:S(2)}, u32[]{:S(2)}) collective-permute-start(bf16[8,48,768]{2,1,0:T(8,128)(2,1)S(1)} %get-tuple-element.239), channel_id=1, source_target_pairs={{0,2},{1,5},{2,0},{3,7},{4,6},{5,1},{6,4},{7,3},{8,10},{9,13},{10,... | collective-permute-start | bytes 1769480 | tf_op jit(solution)/shard_map/ppermute | solution.py:129
  82.0 1.2 shard_map.262
  83.1 1.2 collective-permute-start.24
  84.3 9.8 %shard_map.263 = (f32[512,384]{1,0:T(8,128)S(1)}, f32[64,384]{1,0:T(8,128)S(1)}) custom-call(f32[3,640,128]{2,1,0:T(8,128)S(1)} %get-tuple-element.216.sg_ref, bf16[512,384]{1,0:T(8,128)(2,1)S(1)} %get-tuple-element.157.k_ref, f32[576,128]{1,0:T(8,128)S(1)} %get-tuple-element.217.ahead_ref, bf16[64,384]{1,0:T(8,128)(2,1)S(1)} %copy-done.9, ...), custom_call_target="tpu_custom_call" | custom-call | flops 7049999872 | bytes 21150000 | tf_op jit(solution)/shard_map/pallas_call | solution.py:57
  94.1 2.2 %shard_map.264 = (bf16[512,384]{1,0:T(8,128)(2,1)S(1)}, bf16[520,768]{1,0:T(8,128)(2,1)S(1)}) custom-call(s32[2]{0:T(128)S(1)} %pad_add_fusion.place_ref, f32[512,384]{1,0:T(8,128)S(1)} %get-tuple-element.230.grad_ref, bf16[64,384]{1,0:T(8,128)(2,1)S(1)} %collective-permute-done.20.edge_ref, f32[512,128]{1,0:T(8,128)S(1)} %get-tuple-element.154.docc_ref, ...), custom_call_target="tpu_custom_call" | custom-call | flops 2160000000 | bytes 6480000 | tf_op jit(solution)/shard_map/pallas_call | solution.py:57
  96.4 0.9 shard_map.265
  97.3 0.7 shard_map.266
  98.1 1.0 collective-permute-start.28
  99.1 3.1 %collective-permute-done.22.got_ref = bf16[8,48,1536]{2,1,0:T(8,128)(2,1)S(1)} collective-permute-done((bf16[8,48,1536]{2,1,0:T(8,128)(2,1)S(1)}, bf16[8,48,1536]{2,1,0:T(8,128)(2,1)S(1)}, u32[]{:S(2)}, u32[]{:S(2)}) %collective-permute-start.22) | collective-permute-done | bytes 1179680 | tf_op jit(solution)/shard_map/ppermute | solution.py:129
  102.2 4.2 %collective-permute-start.26 = (bf16[2,48,1920]{2,1,0:T(8,128)(2,1)S(1)}, bf16[2,48,1920]{2,1,0:T(8,128)(2,1)S(1)}, u32[]{:S(2)}, u32[]{:S(2)}) collective-permute-start(bf16[2,48,1920]{2,1,0:T(8,128)(2,1)S(1)} %get-tuple-element.252), channel_id=1, source_target_pairs={{0,8},{1,17},{2,10},{3,19},{4,12},{5,21},{6,14},{7,23},{8,0},{9,25... | collective-permute-start | bytes 1105928 | tf_op jit(solution)/shard_map/ppermute | solution.py:129
  106.4 1.0 shard_map.267
  107.4 3.5 %collective-permute-start.27 = (bf16[4,48,1536]{2,1,0:T(8,128)(2,1)S(1)}, bf16[4,48,1536]{2,1,0:T(8,128)(2,1)S(1)}, u32[]{:S(2)}, u32[]{:S(2)}) collective-permute-start(bf16[4,48,1536]{2,1,0:T(8,128)(2,1)S(1)} %get-tuple-element.253), channel_id=1, source_target_pairs={{0,2},{1,5},{2,0},{3,7},{4,6},{5,1},{6,4},{7,3},{8,10},{9,13},{10,... | collective-permute-start | bytes 1769480 | tf_op jit(solution)/shard_map/ppermute | solution.py:129
  110.9 1.2 shard_map.268
  112.2 2.5 %shard_map.269 = bf16[512,384]{1,0:T(8,128)(2,1)} custom-call(s32[2]{0:T(128)S(1)} %pad_add_fusion.place_ref, bf16[520,768]{1,0:T(8,128)(2,1)S(1)} %get-tuple-element.232.part_ref, bf16[520,768]{1,0:T(8,128)(2,1)S(1)} %collective-permute-done.21.got_ref, bf16[512,384]{1,0:T(8,128)(2,1)S(1)} %copy-done, bf16[512,384]{1,0:T(8,128)(2,1)S(1)} %collective-permute-done.other_ref, ...), custom_call_target="tpu_custom_call" | custom-call | flops 890000000 | bytes 2670000 | tf_op jit(solution)/shard_map/pallas_call | solution.py:57
  115.3 2.1 %collective-permute-start.30 = (bf16[2,48,768]{2,1,0:T(8,128)(2,1)S(1)}, bf16[2,48,768]{2,1,0:T(8,128)(2,1)S(1)}, u32[]{:S(2)}, u32[]{:S(2)}) collective-permute-start(bf16[2,48,768]{2,1,0:T(8,128)(2,1)S(1)} %get-tuple-element.264), channel_id=1, source_target_pairs={{0,8},{1,17},{2,10},{3,19},{4,12},{5,21},{6,14},{7,23},{8,0},{9,25... | collective-permute-start | bytes 442376 | tf_op jit(solution)/shard_map/ppermute | solution.py:129
  117.4 1.3 collective-permute-done.27.got_ref
  118.7 0.8 shard_map.271
  119.5 0.7 shard_map.272
  120.3 1.9 %collective-permute-start.31 = (bf16[2,48,1536]{2,1,0:T(8,128)(2,1)S(1)}, bf16[2,48,1536]{2,1,0:T(8,128)(2,1)S(1)}, u32[]{:S(2)}, u32[]{:S(2)}) collective-permute-start(bf16[2,48,1536]{2,1,0:T(8,128)(2,1)S(1)} %get-tuple-element.265), channel_id=1, source_target_pairs={{0,4},{1,3},{2,6},{3,1},{4,0},{5,7},{6,2},{7,5},{8,12},{9,11},{10,... | collective-permute-start | bytes 884744 | tf_op jit(solution)/shard_map/ppermute | solution.py:129
  123.1 1.9 %collective-permute-start.29 = (bf16[264,384]{1,0:T(8,128)(2,1)S(1)}, bf16[264,384]{1,0:T(8,128)(2,1)S(1)}, u32[]{:S(2)}, u32[]{:S(2)}) collective-permute-start(bf16[264,384]{1,0:T(8,128)(2,1)S(1)} %get-tuple-element.263), channel_id=1, source_target_pairs={{0,4},{1,3},{2,6},{3,1},{4,0},{5,7},{6,2},{7,5},{8,12},{9,11},{10,... | collective-permute-start | bytes 608264 | tf_op jit(solution)/shard_map/ppermute | solution.py:129
  125.1 2.0 %collective-permute-done.31.got_ref = bf16[2,48,1536]{2,1,0:T(8,128)(2,1)S(1)} collective-permute-done((bf16[2,48,1536]{2,1,0:T(8,128)(2,1)S(1)}, bf16[2,48,1536]{2,1,0:T(8,128)(2,1)S(1)}, u32[]{:S(2)}, u32[]{:S(2)}) %collective-permute-start.31) | collective-permute-done | bytes 294944 | tf_op jit(solution)/shard_map/ppermute | solution.py:129
  127.1 0.7 shard_map.274
  128.4 0.9 collective-permute-done.29.got_ref
  129.9 2.1 %collective-permute-start.32 = (bf16[168,384]{1,0:T(8,128)(2,1)S(1)}, bf16[168,384]{1,0:T(8,128)(2,1)S(1)}, u32[]{:S(2)}, u32[]{:S(2)}) collective-permute-start(bf16[168,384]{1,0:T(8,128)(2,1)S(1)} %get-tuple-element.272), channel_id=1, source_target_pairs={{0,8},{1,17},{2,10},{3,19},{4,12},{5,21},{6,14},{7,23},{8,0},{9,25... | collective-permute-start | bytes 387080 | tf_op jit(solution)/shard_map/ppermute | solution.py:129
  132.0 2.8 %collective-permute-start.35 = (bf16[1,48,1536]{2,1,0:T(8,128)(2,1)S(1)}, bf16[1,48,1536]{2,1,0:T(8,128)(2,1)S(1)}, u32[]{:S(2)}, u32[]{:S(2)}) collective-permute-start(bf16[1,48,1536]{2,1,0:T(8,128)(2,1)S(1)} %get-tuple-element.279), channel_id=1, source_target_pairs={{0,16},{1,9},{2,18},{3,11},{4,20},{5,13},{6,22},{7,15},{8,24},{9,1... | collective-permute-start | bytes 442376 | tf_op jit(solution)/shard_map/ppermute | solution.py:129
  134.8 1.3 shard_map.277
  136.1 2.6 %collective-permute-done.32.got_ref = bf16[168,384]{1,0:T(8,128)(2,1)S(1)} collective-permute-done((bf16[168,384]{1,0:T(8,128)(2,1)S(1)}, bf16[168,384]{1,0:T(8,128)(2,1)S(1)}, u32[]{:S(2)}, u32[]{:S(2)}) %collective-permute-start.32) | collective-permute-done | bytes 129056 | tf_op jit(solution)/shard_map/ppermute | solution.py:129
  139.3 1.2 collective-permute-start.34
  140.6 1.7 %collective-permute-start.37 = (bf16[1,48,768]{2,1,0:T(8,128)(2,1)S(1)}, bf16[1,48,768]{2,1,0:T(8,128)(2,1)S(1)}, u32[]{:S(2)}, u32[]{:S(2)}) collective-permute-start(bf16[1,48,768]{2,1,0:T(8,128)(2,1)S(1)} %get-tuple-element.283), channel_id=1, source_target_pairs={{0,16},{1,9},{2,18},{3,11},{4,20},{5,13},{6,22},{7,15},{8,24},{9,1... | collective-permute-start | bytes 221192 | tf_op jit(solution)/shard_map/ppermute | solution.py:129
  142.3 1.3 shard_map.279
  143.6 2.2 %collective-permute-done.34.got_ref = bf16[120,384]{1,0:T(8,128)(2,1)S(1)} collective-permute-done((bf16[120,384]{1,0:T(8,128)(2,1)S(1)}, bf16[120,384]{1,0:T(8,128)(2,1)S(1)}, u32[]{:S(2)}, u32[]{:S(2)}) %collective-permute-start.34) | collective-permute-done | bytes 92192 | tf_op jit(solution)/shard_map/ppermute | solution.py:129
  145.8 1.2 shard_map.280
  147.1 1.2 shard_map.281
  148.3 1.1 shard_map.282
  (76 shorter events, 8.9 us)
Async XLA Ops:
  0.6 4.6 %collective-permute-start = (bf16[512,384]{1,0:T(8,128)(2,1)}, bf16[512,384]{1,0:T(8,128)(2,1)S(1)}, u32[]{:S(2)}, u32[]{:S(2)}) collective-permute-start(bf16[512,384]{1,0:T(8,128)(2,1)} %own_ref.9), channel_id=1, source_target_pairs={{0,1},{1,0},{2,3},{3,2},{4,5},{5,4},{6,7},{7,6},{8,9},{9,8},{10,11... | collective-permute-start | bytes 1179656 | tf_op jit(solution)/shard_map/ppermute | solution.py:102
  1.2 20.8 %collective-permute-start.2 = (bf16[512,384]{1,0:T(8,128)(2,1)}, bf16[512,384]{1,0:T(8,128)(2,1)S(1)}, u32[]{:S(2)}, u32[]{:S(2)}) collective-permute-start(bf16[512,384]{1,0:T(8,128)(2,1)} %own_ref.6), channel_id=1, source_target_pairs={{0,1},{1,0},{2,3},{3,2},{4,5},{5,4},{6,7},{7,6},{8,9},{9,8},{10,11... | collective-permute-start | bytes 1179656 | tf_op jit(solution)/shard_map/ppermute | solution.py:102
  1.2 36.5 %collective-permute-start.10 = (bf16[768,384]{1,0:T(8,128)(2,1)}, bf16[768,384]{1,0:T(8,128)(2,1)S(1)}, u32[]{:S(2)}, u32[]{:S(2)}) collective-permute-start(bf16[768,384]{1,0:T(8,128)(2,1)} %out_w_ref.1), channel_id=1, source_target_pairs={{0,1},{1,0},{2,3},{3,2},{4,5},{5,4},{6,7},{7,6},{8,9},{9,8},{10,11... | collective-permute-start | bytes 1769480 | tf_op jit(solution)/shard_map/ppermute | solution.py:102
  1.7 3.5 %copy-start = (bf16[512,384]{1,0:T(8,128)(2,1)S(1)}, bf16[512,384]{1,0:T(8,128)(2,1)}, u32[]{:S(2)}) copy-start(bf16[512,384]{1,0:T(8,128)(2,1)} %own_ref.9) | copy-start | bytes 1179652
  1.8 3.5 %copy-start.1 = (f32[768]{0:T(1024)S(1)}, f32[768]{0:T(1024)}, u32[]{:S(2)}) copy-start(f32[768]{0:T(1024)} %gain_ref.7) | copy-start | bytes 9220
  1.8 3.5 %copy-start.5 = (bf16[768,384]{1,0:T(8,128)(2,1)S(1)}, bf16[768,384]{1,0:T(8,128)(2,1)}, u32[]{:S(2)}) copy-start(bf16[768,384]{1,0:T(8,128)(2,1)} %wq_ref.3) | copy-start | bytes 1769476
  1.8 3.5 %copy-start.6 = (bf16[768,384]{1,0:T(8,128)(2,1)S(1)}, bf16[768,384]{1,0:T(8,128)(2,1)}, u32[]{:S(2)}) copy-start(bf16[768,384]{1,0:T(8,128)(2,1)} %wk_ref.3) | copy-start | bytes 1769476
  1.8 3.5 %copy-start.7 = (bf16[768,384]{1,0:T(8,128)(2,1)S(1)}, bf16[768,384]{1,0:T(8,128)(2,1)}, u32[]{:S(2)}) copy-start(bf16[768,384]{1,0:T(8,128)(2,1)} %wv_ref.3) | copy-start | bytes 1769476
  1.8 3.5 %copy-start.10 = (f32[768]{0:T(1024)S(1)}, f32[768]{0:T(1024)}, u32[]{:S(2)}) copy-start(f32[768]{0:T(1024)} %bias_ref.2) | copy-start | bytes 9220
  5.3 6.8 %copy-start.9 = (bf16[64,384]{1,0:T(8,128)(2,1)S(1)}, bf16[64,384]{1,0:T(8,128)(2,1)}, u32[]{:S(2)}) copy-start(bf16[64,384]{1,0:T(8,128)(2,1)} %taps_ref.7) | copy-start | bytes 147460
  7.7 9.6 %collective-permute-start.1 = (bf16[64,384]{1,0:T(8,128)(2,1)S(1)}, bf16[64,384]{1,0:T(8,128)(2,1)S(1)}, u32[]{:S(2)}, u32[]{:S(2)}) collective-permute-start(bf16[64,384]{1,0:T(8,128)(2,1)S(1)} %get-tuple-element.160), channel_id=1, source_target_pairs={{0,2},{2,4},{4,6},{6,8},{8,10},{10,12},{12,14},{14,16},{16,18},{18... | collective-permute-start | bytes 147464 | tf_op jit(solution)/shard_map/ppermute | solution.py:107
  17.2 4.7 %copy-start.3 = (bf16[768,1536]{1,0:T(8,128)(2,1)S(1)}, bf16[768,1536]{1,0:T(8,128)(2,1)}, u32[]{:S(2)}) copy-start(bf16[768,1536]{1,0:T(8,128)(2,1)} %down_ref.3) | copy-start | bytes 7077892
  17.2 4.7 %copy-start.8 = (bf16[512,384]{1,0:T(8,128)(2,1)S(1)}, bf16[512,384]{1,0:T(8,128)(2,1)}, u32[]{:S(2)}) copy-start(bf16[512,384]{1,0:T(8,128)(2,1)} %own_ref.6) | copy-start | bytes 1179652
  18.3 6.2 %collective-permute-start.5 = (bf16[80,384]{1,0:T(8,128)(2,1)S(1)}, bf16[80,384]{1,0:T(8,128)(2,1)S(1)}, u32[]{:S(2)}, u32[]{:S(2)}) collective-permute-start(bf16[80,384]{1,0:T(8,128)(2,1)S(1)} %get-tuple-element.168.refs_0_), channel_id=1, source_target_pairs={{0,6},{2,0},{4,2},{6,4},{8,14},{10,8},{12,10},{14,12},{16,22},{18,... | collective-permute-start | bytes 184328 | tf_op jit(solution)/shard_map/ppermute | solution.py:89
  20.8 4.9 %collective-permute-start.4 = (bf16[80,384]{1,0:T(8,128)(2,1)S(1)}, bf16[80,384]{1,0:T(8,128)(2,1)S(1)}, u32[]{:S(2)}, u32[]{:S(2)}) collective-permute-start(bf16[80,384]{1,0:T(8,128)(2,1)S(1)} %get-tuple-element.168.refs_0_), channel_id=1, source_target_pairs={{0,4},{2,6},{4,0},{6,2},{8,12},{10,14},{12,8},{14,10},{16,20},{18,... | collective-permute-start | bytes 184328 | tf_op jit(solution)/shard_map/ppermute | solution.py:89
  21.3 5.1 %collective-permute-start.3 = (bf16[80,384]{1,0:T(8,128)(2,1)S(1)}, bf16[80,384]{1,0:T(8,128)(2,1)S(1)}, u32[]{:S(2)}, u32[]{:S(2)}) collective-permute-start(bf16[80,384]{1,0:T(8,128)(2,1)S(1)} %get-tuple-element.168.refs_0_), channel_id=1, source_target_pairs={{0,2},{2,4},{4,6},{6,0},{8,10},{10,12},{12,14},{14,8},{16,18},{18,... | collective-permute-start | bytes 184328 | tf_op jit(solution)/shard_map/ppermute | solution.py:89
  27.1 7.6 %collective-permute-start.8 = (bf16[80,384]{1,0:T(8,128)(2,1)S(1)}, bf16[80,384]{1,0:T(8,128)(2,1)S(1)}, u32[]{:S(2)}, u32[]{:S(2)}) collective-permute-start(bf16[80,384]{1,0:T(8,128)(2,1)S(1)} %get-tuple-element.179.refs_0_), channel_id=1, source_target_pairs={{0,24},{2,26},{4,28},{6,30},{8,0},{10,2},{12,4},{14,6},{16,8},{18,... | collective-permute-start | bytes 184328 | tf_op jit(solution)/shard_map/ppermute | solution.py:89
  30.8 5.1 %collective-permute-start.7 = (bf16[80,384]{1,0:T(8,128)(2,1)S(1)}, bf16[80,384]{1,0:T(8,128)(2,1)S(1)}, u32[]{:S(2)}, u32[]{:S(2)}) collective-permute-start(bf16[80,384]{1,0:T(8,128)(2,1)S(1)} %get-tuple-element.179.refs_0_), channel_id=1, source_target_pairs={{0,16},{2,18},{4,20},{6,22},{8,24},{10,26},{12,28},{14,30},{16,0},... | collective-permute-start | bytes 184328 | tf_op jit(solution)/shard_map/ppermute | solution.py:89
  30.8 6.0 %collective-permute-start.6 = (bf16[80,384]{1,0:T(8,128)(2,1)S(1)}, bf16[80,384]{1,0:T(8,128)(2,1)S(1)}, u32[]{:S(2)}, u32[]{:S(2)}) collective-permute-start(bf16[80,384]{1,0:T(8,128)(2,1)S(1)} %get-tuple-element.179.refs_0_), channel_id=1, source_target_pairs={{0,8},{2,10},{4,12},{6,14},{8,16},{10,18},{12,20},{14,22},{16,24},... | collective-permute-start | bytes 184328 | tf_op jit(solution)/shard_map/ppermute | solution.py:89
  36.8 2.6 %copy-start.2 = (bf16[768,1536]{1,0:T(8,128)(2,1)S(1)}, bf16[768,1536]{1,0:T(8,128)(2,1)}, u32[]{:S(2)}) copy-start(bf16[768,1536]{1,0:T(8,128)(2,1)} %up_ref.1) | copy-start | bytes 7077892
  36.8 2.6 %copy-start.4 = (bf16[768,384]{1,0:T(8,128)(2,1)S(1)}, bf16[768,384]{1,0:T(8,128)(2,1)}, u32[]{:S(2)}) copy-start(bf16[768,384]{1,0:T(8,128)(2,1)} %out_w_ref.1) | copy-start | bytes 1769476
  36.8 2.6 %copy-start.11 = (f32[768]{0:T(1024)S(1)}, f32[768]{0:T(1024)}, u32[]{:S(2)}) copy-start(f32[768]{0:T(1024)} %bias_ref.3) | copy-start | bytes 9220
  36.8 2.6 %copy-start.12 = (f32[768]{0:T(1024)S(1)}, f32[768]{0:T(1024)}, u32[]{:S(2)}) copy-start(f32[768]{0:T(1024)} %gain_ref.6) | copy-start | bytes 9220
  37.7 1.8 %collective-permute-start.9 = (bf16[512,384]{1,0:T(8,128)(2,1)S(1)}, bf16[512,384]{1,0:T(8,128)(2,1)S(1)}, u32[]{:S(2)}, u32[]{:S(2)}) collective-permute-start(bf16[512,384]{1,0:T(8,128)(2,1)S(1)} %get-tuple-element.185.mix_own_ref.refs_3_), channel_id=1, source_target_pairs={{0,1},{1,0},{2,3},{3,2},{4,5},{5,4},{6,7},{7,6},{8,9},{9,8},{10,11... | collective-permute-start | bytes 1179656 | tf_op jit(solution)/shard_map/ppermute | solution.py:102
  46.9 4.4 %collective-permute-start.11 = (bf16[512,768]{1,0:T(8,128)(2,1)S(1)}, bf16[512,768]{1,0:T(8,128)(2,1)S(1)}, u32[]{:S(2)}, u32[]{:S(2)}) collective-permute-start(bf16[512,768]{1,0:T(8,128)(2,1)S(1)} %get-tuple-element.187.part_ref), channel_id=1, source_target_pairs={{0,1},{1,0},{2,3},{3,2},{4,5},{5,4},{6,7},{7,6},{8,9},{9,8},{10,11... | collective-permute-start | bytes 2359304 | tf_op jit(solution)/shard_map/ppermute | solution.py:102
  50.9 7.0 %collective-permute-start.12 = (bf16[512,384]{1,0:T(8,128)(2,1)S(1)}, bf16[512,384]{1,0:T(8,128)(2,1)S(1)}, u32[]{:S(2)}, u32[]{:S(2)}) collective-permute-start(bf16[512,384]{1,0:T(8,128)(2,1)S(1)} %get-tuple-element.197), channel_id=1, source_target_pairs={{0,1},{1,0},{2,3},{3,2},{4,5},{5,4},{6,7},{7,6},{8,9},{9,8},{10,11... | collective-permute-start | bytes 1179656 | tf_op jit(solution)/shard_map/ppermute | solution.py:102
  53.9 7.4 %collective-permute-start.15 = (bf16[80,384]{1,0:T(8,128)(2,1)S(1)}, bf16[80,384]{1,0:T(8,128)(2,1)S(1)}, u32[]{:S(2)}, u32[]{:S(2)}) collective-permute-start(bf16[80,384]{1,0:T(8,128)(2,1)S(1)} %get-tuple-element.199.refs_0_), channel_id=1, source_target_pairs={{0,2},{2,4},{4,6},{6,0},{8,10},{10,12},{12,14},{14,8},{16,18},{18,... | collective-permute-start | bytes 184328 | tf_op jit(solution)/shard_map/ppermute | solution.py:89
  54.0 7.3 %collective-permute-start.14 = (bf16[80,384]{1,0:T(8,128)(2,1)S(1)}, bf16[80,384]{1,0:T(8,128)(2,1)S(1)}, u32[]{:S(2)}, u32[]{:S(2)}) collective-permute-start(bf16[80,384]{1,0:T(8,128)(2,1)S(1)} %get-tuple-element.199.refs_0_), channel_id=1, source_target_pairs={{0,4},{2,6},{4,0},{6,2},{8,12},{10,14},{12,8},{14,10},{16,20},{18,... | collective-permute-start | bytes 184328 | tf_op jit(solution)/shard_map/ppermute | solution.py:89
  55.0 6.4 %collective-permute-start.13 = (bf16[80,384]{1,0:T(8,128)(2,1)S(1)}, bf16[80,384]{1,0:T(8,128)(2,1)S(1)}, u32[]{:S(2)}, u32[]{:S(2)}) collective-permute-start(bf16[80,384]{1,0:T(8,128)(2,1)S(1)} %get-tuple-element.199.refs_0_), channel_id=1, source_target_pairs={{0,6},{2,0},{4,2},{6,4},{8,14},{10,8},{12,10},{14,12},{16,22},{18,... | collective-permute-start | bytes 184328 | tf_op jit(solution)/shard_map/ppermute | solution.py:89
  62.0 20.0 %collective-permute-start.19 = (bf16[8,48,1920]{2,1,0:T(8,128)(2,1)S(1)}, bf16[8,48,1920]{2,1,0:T(8,128)(2,1)S(1)}, u32[]{:S(2)}, u32[]{:S(2)}) collective-permute-start(bf16[8,48,1920]{2,1,0:T(8,128)(2,1)S(1)} %get-tuple-element.221), channel_id=1, source_target_pairs={{0,2},{1,5},{2,0},{3,7},{4,6},{5,1},{6,4},{7,3},{8,10},{9,13},{10,... | collective-permute-start | bytes 4423688 | tf_op jit(solution)/shard_map/ppermute | solution.py:129
  63.3 10.0 %collective-permute-start.18 = (bf16[80,384]{1,0:T(8,128)(2,1)S(1)}, bf16[80,384]{1,0:T(8,128)(2,1)S(1)}, u32[]{:S(2)}, u32[]{:S(2)}) collective-permute-start(bf16[80,384]{1,0:T(8,128)(2,1)S(1)} %get-tuple-element.210.refs_0_), channel_id=1, source_target_pairs={{0,8},{2,10},{4,12},{6,14},{8,16},{10,18},{12,20},{14,22},{16,24},... | collective-permute-start | bytes 184328 | tf_op jit(solution)/shard_map/ppermute | solution.py:89
  63.8 9.5 %collective-permute-start.17 = (bf16[80,384]{1,0:T(8,128)(2,1)S(1)}, bf16[80,384]{1,0:T(8,128)(2,1)S(1)}, u32[]{:S(2)}, u32[]{:S(2)}) collective-permute-start(bf16[80,384]{1,0:T(8,128)(2,1)S(1)} %get-tuple-element.210.refs_0_), channel_id=1, source_target_pairs={{0,16},{2,18},{4,20},{6,22},{8,24},{10,26},{12,28},{14,30},{16,0},... | collective-permute-start | bytes 184328 | tf_op jit(solution)/shard_map/ppermute | solution.py:89
  64.8 8.5 %collective-permute-start.16 = (bf16[80,384]{1,0:T(8,128)(2,1)S(1)}, bf16[80,384]{1,0:T(8,128)(2,1)S(1)}, u32[]{:S(2)}, u32[]{:S(2)}) collective-permute-start(bf16[80,384]{1,0:T(8,128)(2,1)S(1)} %get-tuple-element.210.refs_0_), channel_id=1, source_target_pairs={{0,24},{2,26},{4,28},{6,30},{8,0},{10,2},{12,4},{14,6},{16,8},{18,... | collective-permute-start | bytes 184328 | tf_op jit(solution)/shard_map/ppermute | solution.py:89
  72.8 29.3 %collective-permute-start.22 = (bf16[8,48,1536]{2,1,0:T(8,128)(2,1)S(1)}, bf16[8,48,1536]{2,1,0:T(8,128)(2,1)S(1)}, u32[]{:S(2)}, u32[]{:S(2)}) collective-permute-start(bf16[8,48,1536]{2,1,0:T(8,128)(2,1)S(1)} %get-tuple-element.238), channel_id=1, source_target_pairs={{0,8},{1,17},{2,10},{3,19},{4,12},{5,21},{6,14},{7,23},{8,0},{9,25... | collective-permute-start | bytes 3538952 | tf_op jit(solution)/shard_map/ppermute | solution.py:129
  75.6 18.5 %collective-permute-start.20 = (bf16[64,384]{1,0:T(8,128)(2,1)S(1)}, bf16[64,384]{1,0:T(8,128)(2,1)S(1)}, u32[]{:S(2)}, u32[]{:S(2)}) collective-permute-start(bf16[64,384]{1,0:T(8,128)(2,1)S(1)} %get-tuple-element.224), channel_id=1, source_target_pairs={{2,0},{4,2},{6,4},{8,6},{10,8},{12,10},{14,12},{16,14},{18,16},{20... | collective-permute-start | bytes 147464 | tf_op jit(solution)/shard_map/ppermute | solution.py:107
  78.6 18.7 %collective-permute-start.23 = (bf16[8,48,768]{2,1,0:T(8,128)(2,1)S(1)}, bf16[8,48,768]{2,1,0:T(8,128)(2,1)S(1)}, u32[]{:S(2)}, u32[]{:S(2)}) collective-permute-start(bf16[8,48,768]{2,1,0:T(8,128)(2,1)S(1)} %get-tuple-element.239), channel_id=1, source_target_pairs={{0,2},{1,5},{2,0},{3,7},{4,6},{5,1},{6,4},{7,3},{8,10},{9,13},{10,... | collective-permute-start | bytes 1769480 | tf_op jit(solution)/shard_map/ppermute | solution.py:129
  83.1 13.3 %collective-permute-start.24 = (bf16[4,48,1920]{2,1,0:T(8,128)(2,1)S(1)}, bf16[4,48,1920]{2,1,0:T(8,128)(2,1)S(1)}, u32[]{:S(2)}, u32[]{:S(2)}) collective-permute-start(bf16[4,48,1920]{2,1,0:T(8,128)(2,1)S(1)} %get-tuple-element.240), channel_id=1, source_target_pairs={{0,4},{1,3},{2,6},{3,1},{4,0},{5,7},{6,2},{7,5},{8,12},{9,11},{10,... | collective-permute-start | bytes 2211848 | tf_op jit(solution)/shard_map/ppermute | solution.py:129
  96.4 14.5 %collective-permute-start.21 = (bf16[520,768]{1,0:T(8,128)(2,1)S(1)}, bf16[520,768]{1,0:T(8,128)(2,1)S(1)}, u32[]{:S(2)}, u32[]{:S(2)}) collective-permute-start(bf16[520,768]{1,0:T(8,128)(2,1)S(1)} %get-tuple-element.232.part_ref), channel_id=1, source_target_pairs={{0,1},{1,0},{2,3},{3,2},{4,5},{5,4},{6,7},{7,6},{8,9},{9,8},{10,11... | collective-permute-start | bytes 2396168 | tf_op jit(solution)/shard_map/ppermute | solution.py:102
  98.1 16.6 %collective-permute-start.28 = (bf16[4,48,768]{2,1,0:T(8,128)(2,1)S(1)}, bf16[4,48,768]{2,1,0:T(8,128)(2,1)S(1)}, u32[]{:S(2)}, u32[]{:S(2)}) collective-permute-start(bf16[4,48,768]{2,1,0:T(8,128)(2,1)S(1)} %get-tuple-element.254), channel_id=1, source_target_pairs={{0,4},{1,3},{2,6},{3,1},{4,0},{5,7},{6,2},{7,5},{8,12},{9,11},{10,... | collective-permute-start | bytes 884744 | tf_op jit(solution)/shard_map/ppermute | solution.py:129
  102.2 17.3 %collective-permute-start.26 = (bf16[2,48,1920]{2,1,0:T(8,128)(2,1)S(1)}, bf16[2,48,1920]{2,1,0:T(8,128)(2,1)S(1)}, u32[]{:S(2)}, u32[]{:S(2)}) collective-permute-start(bf16[2,48,1920]{2,1,0:T(8,128)(2,1)S(1)} %get-tuple-element.252), channel_id=1, source_target_pairs={{0,8},{1,17},{2,10},{3,19},{4,12},{5,21},{6,14},{7,23},{8,0},{9,25... | collective-permute-start | bytes 1105928 | tf_op jit(solution)/shard_map/ppermute | solution.py:129
  107.4 11.3 %collective-permute-start.27 = (bf16[4,48,1536]{2,1,0:T(8,128)(2,1)S(1)}, bf16[4,48,1536]{2,1,0:T(8,128)(2,1)S(1)}, u32[]{:S(2)}, u32[]{:S(2)}) collective-permute-start(bf16[4,48,1536]{2,1,0:T(8,128)(2,1)S(1)} %get-tuple-element.253), channel_id=1, source_target_pairs={{0,2},{1,5},{2,0},{3,7},{4,6},{5,1},{6,4},{7,3},{8,10},{9,13},{10,... | collective-permute-start | bytes 1769480 | tf_op jit(solution)/shard_map/ppermute | solution.py:129
  112.1 10.4 %collective-permute-start.25 = (bf16[456,384]{1,0:T(8,128)(2,1)S(1)}, bf16[456,384]{1,0:T(8,128)(2,1)S(1)}, u32[]{:S(2)}, u32[]{:S(2)}) collective-permute-start(bf16[456,384]{1,0:T(8,128)(2,1)S(1)} %get-tuple-element.251), channel_id=1, source_target_pairs={{0,2},{1,5},{2,0},{3,7},{4,6},{5,1},{6,4},{7,3},{8,10},{9,13},{10,... | collective-permute-start | bytes 1050632 | tf_op jit(solution)/shard_map/ppermute | solution.py:129
  115.3 12.5 %collective-permute-start.30 = (bf16[2,48,768]{2,1,0:T(8,128)(2,1)S(1)}, bf16[2,48,768]{2,1,0:T(8,128)(2,1)S(1)}, u32[]{:S(2)}, u32[]{:S(2)}) collective-permute-start(bf16[2,48,768]{2,1,0:T(8,128)(2,1)S(1)} %get-tuple-element.264), channel_id=1, source_target_pairs={{0,8},{1,17},{2,10},{3,19},{4,12},{5,21},{6,14},{7,23},{8,0},{9,25... | collective-permute-start | bytes 442376 | tf_op jit(solution)/shard_map/ppermute | solution.py:129
  120.2 14.6 %collective-permute-start.33 = (bf16[1,48,1920]{2,1,0:T(8,128)(2,1)S(1)}, bf16[1,48,1920]{2,1,0:T(8,128)(2,1)S(1)}, u32[]{:S(2)}, u32[]{:S(2)}) collective-permute-start(bf16[1,48,1920]{2,1,0:T(8,128)(2,1)S(1)} %get-tuple-element.273), channel_id=1, source_target_pairs={{0,16},{1,9},{2,18},{3,11},{4,20},{5,13},{6,22},{7,15},{8,24},{9,1... | collective-permute-start | bytes 552968 | tf_op jit(solution)/shard_map/ppermute | solution.py:129
  120.3 6.8 %collective-permute-start.31 = (bf16[2,48,1536]{2,1,0:T(8,128)(2,1)S(1)}, bf16[2,48,1536]{2,1,0:T(8,128)(2,1)S(1)}, u32[]{:S(2)}, u32[]{:S(2)}) collective-permute-start(bf16[2,48,1536]{2,1,0:T(8,128)(2,1)S(1)} %get-tuple-element.265), channel_id=1, source_target_pairs={{0,4},{1,3},{2,6},{3,1},{4,0},{5,7},{6,2},{7,5},{8,12},{9,11},{10,... | collective-permute-start | bytes 884744 | tf_op jit(solution)/shard_map/ppermute | solution.py:129
  123.1 6.1 %collective-permute-start.29 = (bf16[264,384]{1,0:T(8,128)(2,1)S(1)}, bf16[264,384]{1,0:T(8,128)(2,1)S(1)}, u32[]{:S(2)}, u32[]{:S(2)}) collective-permute-start(bf16[264,384]{1,0:T(8,128)(2,1)S(1)} %get-tuple-element.263), channel_id=1, source_target_pairs={{0,4},{1,3},{2,6},{3,1},{4,0},{5,7},{6,2},{7,5},{8,12},{9,11},{10,... | collective-permute-start | bytes 608264 | tf_op jit(solution)/shard_map/ppermute | solution.py:129
  129.9 8.9 %collective-permute-start.32 = (bf16[168,384]{1,0:T(8,128)(2,1)S(1)}, bf16[168,384]{1,0:T(8,128)(2,1)S(1)}, u32[]{:S(2)}, u32[]{:S(2)}) collective-permute-start(bf16[168,384]{1,0:T(8,128)(2,1)S(1)} %get-tuple-element.272), channel_id=1, source_target_pairs={{0,8},{1,17},{2,10},{3,19},{4,12},{5,21},{6,14},{7,23},{8,0},{9,25... | collective-permute-start | bytes 387080 | tf_op jit(solution)/shard_map/ppermute | solution.py:129
  132.0 10.3 %collective-permute-start.35 = (bf16[1,48,1536]{2,1,0:T(8,128)(2,1)S(1)}, bf16[1,48,1536]{2,1,0:T(8,128)(2,1)S(1)}, u32[]{:S(2)}, u32[]{:S(2)}) collective-permute-start(bf16[1,48,1536]{2,1,0:T(8,128)(2,1)S(1)} %get-tuple-element.279), channel_id=1, source_target_pairs={{0,16},{1,9},{2,18},{3,11},{4,20},{5,13},{6,22},{7,15},{8,24},{9,1... | collective-permute-start | bytes 442376 | tf_op jit(solution)/shard_map/ppermute | solution.py:129
  139.3 6.5 %collective-permute-start.34 = (bf16[120,384]{1,0:T(8,128)(2,1)S(1)}, bf16[120,384]{1,0:T(8,128)(2,1)S(1)}, u32[]{:S(2)}, u32[]{:S(2)}) collective-permute-start(bf16[120,384]{1,0:T(8,128)(2,1)S(1)} %get-tuple-element.278), channel_id=1, source_target_pairs={{0,16},{1,9},{2,18},{3,11},{4,20},{5,13},{6,22},{7,15},{8,24},{9,1... | collective-permute-start | bytes 276488 | tf_op jit(solution)/shard_map/ppermute | solution.py:129
  140.6 6.5 %collective-permute-start.37 = (bf16[1,48,768]{2,1,0:T(8,128)(2,1)S(1)}, bf16[1,48,768]{2,1,0:T(8,128)(2,1)S(1)}, u32[]{:S(2)}, u32[]{:S(2)}) collective-permute-start(bf16[1,48,768]{2,1,0:T(8,128)(2,1)S(1)} %get-tuple-element.283), channel_id=1, source_target_pairs={{0,16},{1,9},{2,18},{3,11},{4,20},{5,13},{6,22},{7,15},{8,24},{9,1... | collective-permute-start | bytes 221192 | tf_op jit(solution)/shard_map/ppermute | solution.py:129
  147.1 1.2 collective-permute-start.36

commit v5 on v4

--- a/solution.py
+++ b/solution.py
@@ -252,11 +252,16 @@
                scratch=[pltpu.VMEM((entries, rows, width), F32)], us=us)
 
 
-def vector_kernel(place_ref, own_ref, other_ref, *outs):
+def end_kernel(widths, place_ref, keep_ref, got_ref, own_ref, other_ref, *outs):
+    begin = 0
+    for out, width in zip(outs, widths):
+        span = slice(begin, begin + width)
+        out[...] = keep_ref[0, :, span].astype(F32) + got_ref[0, :, span].astype(F32)
+        begin += width
     h = place_ref[1]
-    width = own_ref.shape[1]
     own, other = own_ref[...], other_ref[...]
-    for k, out in enumerate(outs):
+    width = own.shape[1]
+    for k, out in enumerate(outs[len(widths) :]):
         out[:width] = jnp.where(h == 0, own[k], other[k])
         out[width:] = jnp.where(h == 0, other[k], own[k])
 
@@ -351,7 +356,7 @@
     wide[:heads] = decay_ref[...]
     lam_col = jnp.zeros((tok, LANES), F32)
     lam_row = jnp.zeros((16, tok), F32)
-    for part in split_parts(wide[...], 3):
+    for part in split_parts(wide[...], 2):
         lam_col = lam_col + mm(tri[...], part, NT)
         lam_row = lam_row + mm(part[:16], tri[...], NT)
     lamr_ref[...] = jnp.zeros_like(lamr_ref)
@@ -792,7 +797,7 @@
     lamr_spec = pl.BlockSpec((8, tok), lambda p: (p, 0))
     lamc_spec = pl.BlockSpec((tok, LANES), lambda p: (p, 0))
     state_spec = pl.BlockSpec((STEP, LANES), lambda p: (0, p))
-    tile = 512
+    tile = 768
 
     before = ()
     got = scan_send(message, 0, False)
@@ -930,9 +935,13 @@
     k_total, taps_total, vectors = folded_message(
         place, key_keep, key_got, len(strides_of(seqs)) - 1, rows, 0.5)
     other_vectors = swapped(vectors)
-    q_total, v_total = folded_last(place, mix_keep, after(mix_got, vectors), 3, (width, width), 0.5)
-    gain1_grad, bias1_grad, gain2_grad, bias2_grad = run(
-        vector_kernel, (shape((full,), F32),) * 4, place, vectors, after(other_vectors, q_total), scalars=1, us=0.7)
+    mix_got = after(mix_got, vectors)
+    for at in range(3, len(strides_of(seqs)) - 1):
+        mix_keep, mix_send = folded(place, mix_keep, mix_got, at, (), 0.5)
+        mix_got = mirrored(mix_send, at + 1)
+    q_total, v_total, gain1_grad, bias1_grad, gain2_grad, bias2_grad = run(
+        functools.partial(end_kernel, (width, width)), (shape((rows, width), F32),) * 2 + (shape((full,), F32),) * 4,
+        place, mix_keep, mix_got, vectors, other_vectors, scalars=1, us=0.5)
     return (block_output, input_grad, gain1_grad, bias1_grad, q_total, k_total, v_total, taps_total, out_total,
             gain2_grad, bias2_grad, up_total, down_total)
 

time: 150 us -> 149 us (level)
  Pallas kernels: 77.4 us -> 75.5 us
    pallas_call x37 -> x36, Pallas kernels: 77.4 us -> 75.5 us  [run(): pl.pallas_call(body, out_shape=outs, grid=grid, in_specs=[FEW] * scalars...]
  transfers between devices with their start and end apart: 38 -> 38, of which waited for: 13 -> 14; matrix products, arithmetic and copies ran while one was open for 0% -> 0% of each run, Pallas kernels for 46% -> 45%
where the time goes in v5:
time: 149 us
  Pallas kernels  75.5 us (51%)
  starting transfers between devices  52 us (35%)
  waiting for transfers between devices  20.2 us (14%)
    pallas_call x36, Pallas kernels, run(): pl.pallas_call(body, out_shape=outs, grid=grid, in_specs=[FEW] * scalars...  75.5 us
    ppermute x16, starting transfers between devices, mirrored(): return lax.ppermute(array, ('seq', 'head'), pairs)  28.2 us
    ppermute x12, starting transfers between devices, turned(): return lax.ppermute(array, 'seq', pairs)  16.3 us
    ppermute x16, waiting for transfers between devices, mirrored(): return lax.ppermute(array, ('seq', 'head'), pairs)  13.1 us
    ppermute x2, starting transfers between devices, passed_along(): lax.ppermute(array, 'seq', [(i, i + by) for i in range(count) if 0 <= i +...  5.76 us
    ppermute x12, waiting for transfers between devices, turned(): return lax.ppermute(array, 'seq', pairs)  4.16 us
  transfers between devices with their start and end apart: 38, of which 14 were waited for; matrix products, arithmetic and copies ran while one was open for 0% of the time, Pallas kernels for 45%

profile of v5, /device:TPU:0, one launch (start us, length us, event | category | flops | bytes accessed | tf_op | source)
XLA Modules:
  0.0 149.0 jit_solution(4176926963227907751)
XLA Ops:
  1.8 3.2 %shard_map.246 = (f32[24,512]{1,0:T(8,128)S(1)}, f32[1536,128]{1,0:T(8,128)S(1)}, f32[8,512]{1,0:T(8,128)S(1)}, f32[512,128]{1,0:T(8,128)S(1)}, f32[512,128]{1,0...) custom-call(s32[512]{0:T(512)} %starts_ref.1, ...), custom_call_target="tpu_custom_call" | custom-call | flops 2700000000 | bytes 8100000 | tf_op jit(solution)/shard_map/pallas_call | solution.py:57
  5.1 2.3 %shard_map.247 = (bf16[512,768]{1,0:T(8,128)(2,1)S(1)}, bf16[512,384]{1,0:T(8,128)(2,1)S(1)}, bf16[512,384]{1,0:T(8,128)(2,1)S(1)}, bf16[512,384]{1,0:T(8,128)(2,1)S(1)}, bf16[64,384]{1,0:T(8,128)(2,1)S(1)}) custom-call(s32[2]{0:T(128)S(1)} %pad_add_fusion.place_ref, bf16[512,384]{1,0:T(8,128)(2,1)S(1)} %copy-done, ...), custom_call_target="tpu_custom_call" | custom-call | flops 3000000000 | bytes 9000000 | tf_op jit(solution)/shard_map/pallas_call | solution.py:57
  7.4 4.5 %collective-permute-start.1 = (bf16[64,384]{1,0:T(8,128)(2,1)S(1)}, bf16[64,384]{1,0:T(8,128)(2,1)S(1)}, u32[]{:S(2)}, u32[]{:S(2)}) collective-permute-start(bf16[64,384]{1,0:T(8,128)(2,1)S(1)} %get-tuple-element.159), channel_id=1, source_target_pairs={{0,2},{2,4},{4,6},{6,8},{8,10},{10,12},{12,14},{14,16},{16,18},{18... | collective-permute-start | bytes 147464 | tf_op jit(solution)/shard_map/ppermute | solution.py:107
  11.9 5.1 %shard_map.248.part_ref = bf16[512,384]{1,0:T(8,128)(2,1)S(1)} custom-call(bf16[512,384]{1,0:T(8,128)(2,1)S(1)} %get-tuple-element.156.k_ref, bf16[64,384]{1,0:T(8,128)(2,1)S(1)} %copy-done.9, f32[512,128]{1,0:T(8,128)S(1)} %get-tuple-element.157.dist_ref, f32[512,384]{1,0:T(8,128)S(1)} %get-tuple-element.158.beta_ref), custom_call_target="tpu_custom_call" | custom-call | flops 5400000000 | bytes 16200000 | tf_op jit(solution)/shard_map/pallas_call | solution.py:57
  17.0 1.1 shard_map.249
  18.1 2.5 %collective-permute-start.5 = (bf16[80,384]{1,0:T(8,128)(2,1)S(1)}, bf16[80,384]{1,0:T(8,128)(2,1)S(1)}, u32[]{:S(2)}, u32[]{:S(2)}) collective-permute-start(bf16[80,384]{1,0:T(8,128)(2,1)S(1)} %get-tuple-element.167.refs_0_), channel_id=1, source_target_pairs={{0,6},{2,0},{4,2},{6,4},{8,14},{10,8},{12,10},{14,12},{16,22},{18,... | collective-permute-start | bytes 184328 | tf_op jit(solution)/shard_map/ppermute | solution.py:89
  21.7 2.4 %shard_map.250 = (bf16[512,1536]{1,0:T(8,128)(2,1)S(1)}, bf16[512,768]{1,0:T(8,128)(2,1)S(1)}) custom-call(s32[2]{0:T(128)S(1)} %pad_add_fusion.place_ref, bf16[512,384]{1,0:T(8,128)(2,1)S(1)} %copy-done.8, bf16[512,384]{1,0:T(8,128)(2,1)S(1)} %collective-permute-done.2.other_ref, bf16[768,1536]{1,0:T(8,128)(2,1)S(1)} %copy-done.3), custom_call_target="tpu_custom_call" | custom-call | flops 2500000000 | bytes 7500000 | tf_op jit(solution)/shard_map/pallas_call | solution.py:57
  24.1 1.3 collective-permute-done.4.refs_2_
  25.5 0.7 collective-permute-done.3.refs_1_
  26.9 3.7 %collective-permute-start.8 = (bf16[80,384]{1,0:T(8,128)(2,1)S(1)}, bf16[80,384]{1,0:T(8,128)(2,1)S(1)}, u32[]{:S(2)}, u32[]{:S(2)}) collective-permute-start(bf16[80,384]{1,0:T(8,128)(2,1)S(1)} %get-tuple-element.178.refs_0_), channel_id=1, source_target_pairs={{0,24},{2,26},{4,28},{6,30},{8,0},{10,2},{12,4},{14,6},{16,8},{18,... | collective-permute-start | bytes 184328 | tf_op jit(solution)/shard_map/ppermute | solution.py:89
  30.5 1.0 collective-permute-start.6
  31.5 2.9 %shard_map.252.inside_ref = f32[512,384]{1,0:T(8,128)S(1)} custom-call(bf16[512,384]{1,0:T(8,128)(2,1)S(1)} %get-tuple-element.203.q_ref, bf16[512,384]{1,0:T(8,128)(2,1)S(1)} %get-tuple-element.173.k_ref, bf16[512,384]{1,0:T(8,128)(2,1)S(1)} %get-tuple-element.162.v_ref, f32[24,512]{1,0:T(8,128)S(1)} %get-tuple-element.174.lamr_ref, ...), custom_call_target="tpu_custom_call" | custom-call | flops 3500000000 | bytes 10500000 | tf_op jit(solution)/shard_map/pallas_call | solution.py:57
  34.5 1.1 collective-permute-done.7.refs_2_
  35.7 0.9 collective-permute-done.6.refs_1_
  36.6 0.8 shard_map.253
  37.5 1.7 %collective-permute-done.9.mix_other_ref = bf16[512,384]{1,0:T(8,128)(2,1)S(1)} collective-permute-done((bf16[512,384]{1,0:T(8,128)(2,1)S(1)}, bf16[512,384]{1,0:T(8,128)(2,1)S(1)}, u32[]{:S(2)}, u32[]{:S(2)}) %collective-permute-start.9) | collective-permute-done | bytes 393248 | tf_op jit(solution)/shard_map/ppermute | solution.py:102
  39.2 7.2 %shard_map.254 = (f32[512,768]{1,0:T(8,128)S(1)}, bf16[512,768]{1,0:T(8,128)(2,1)S(1)}, bf16[512,1536]{1,0:T(8,128)(2,1)S(1)}, bf16[512,1536]{1,0:T(8,128)(2,1)S(1)}, bf16[512,768]{1,0:T(8,128)(2,1)S(1)}) custom-call(s32[2]{0:T(128)S(1)} %pad_add_fusion.place_ref, bf16[512,384]{1,0:T(8,128)(2,1)S(1)} %copy-done, ...), custom_call_target="tpu_custom_call" | custom-call | flops 10800000000 | bytes 32400000 | tf_op jit(solution)/shard_map/pallas_call | solution.py:57
  46.6 3.7 %shard_map.255 = (bf16[8,48,1536]{2,1,0:T(8,128)(2,1)S(1)}, bf16[8,48,1536]{2,1,0:T(8,128)(2,1)S(1)}, f32[512,384]{1,0:T(8,128)S(1)}, bf16[512,384]{1,0:T(8,128)(2,1)S(1)}) custom-call(s32[2]{0:T(128)S(1)} %pad_add_fusion.place_ref, bf16[512,768]{1,0:T(8,128)(2,1)S(1)} %get-tuple-element.187.grad_ref, bf16[512,1536]{1,0:T(8,128)(2,1)S(1)} %get-tuple-element.188.hidden_ref, ...), custom_call_target="tpu_custom_call" | custom-call | flops 2460000000 | bytes 7380000 | tf_op jit(solution)/shard_map/pallas_call | solution.py:57
  50.8 2.6 %shard_map.256 = (f32[512,384]{1,0:T(8,128)S(1)}, bf16[512,768]{1,0:T(8,128)(2,1)S(1)}, bf16[512,384]{1,0:T(8,128)(2,1)S(1)}, f32[8,768]{1,0:T(8,128)S(1)}, bf16[80,384]{1,0:T(8,128)(2,1)S(1)}) custom-call(s32[2]{0:T(128)S(1)} %pad_add_fusion.place_ref, bf16[512,768]{1,0:T(8,128)(2,1)S(1)} %get-tuple-element.186.part_ref, ...), custom_call_target="tpu_custom_call" | custom-call | flops 2340000000 | bytes 7020000 | tf_op jit(solution)/shard_map/pallas_call | solution.py:57
  53.5 1.0 collective-permute-start.14
  54.5 2.8 %collective-permute-start.13 = (bf16[80,384]{1,0:T(8,128)(2,1)S(1)}, bf16[80,384]{1,0:T(8,128)(2,1)S(1)}, u32[]{:S(2)}, u32[]{:S(2)}) collective-permute-start(bf16[80,384]{1,0:T(8,128)(2,1)S(1)} %get-tuple-element.198.refs_0_), channel_id=1, source_target_pairs={{0,6},{2,0},{4,2},{6,4},{8,14},{10,8},{12,10},{14,12},{16,22},{18,... | collective-permute-start | bytes 184328 | tf_op jit(solution)/shard_map/ppermute | solution.py:89
  57.3 3.5 %shard_map.257 = (bf16[8,48,1920]{2,1,0:T(8,128)(2,1)S(1)}, bf16[8,48,1920]{2,1,0:T(8,128)(2,1)S(1)}, bf16[512,384]{1,0:T(8,128)(2,1)}) custom-call(s32[2]{0:T(128)S(1)} %pad_add_fusion.place_ref, bf16[512,768]{1,0:T(8,128)(2,1)S(1)} %get-tuple-element.193.refs_0_, bf16[512,768]{1,0:T(8,128)(2,1)S(1)} %get-tuple-element.194.refs_1_, ...), custom_call_target="tpu_custom_call" | custom-call | flops 1920000000 | bytes 5760000 | tf_op jit(solution)/shard_map/pallas_call | solution.py:57
  60.8 0.7 shard_map.258
  61.5 1.3 collective-permute-start.19
  63.3 1.0 collective-permute-start.17
  64.3 2.6 %collective-permute-start.16 = (bf16[80,384]{1,0:T(8,128)(2,1)S(1)}, bf16[80,384]{1,0:T(8,128)(2,1)S(1)}, u32[]{:S(2)}, u32[]{:S(2)}) collective-permute-start(bf16[80,384]{1,0:T(8,128)(2,1)S(1)} %get-tuple-element.209.refs_0_), channel_id=1, source_target_pairs={{0,24},{2,26},{4,28},{6,30},{8,0},{10,2},{12,4},{14,6},{16,8},{18,... | collective-permute-start | bytes 184328 | tf_op jit(solution)/shard_map/ppermute | solution.py:89
  66.9 5.5 %shard_map.259 = (bf16[512,384]{1,0:T(8,128)(2,1)S(1)}, f32[512,384]{1,0:T(8,128)S(1)}, f32[512,384]{1,0:T(8,128)S(1)}) custom-call(bf16[512,384]{1,0:T(8,128)(2,1)S(1)} %get-tuple-element.203.q_ref, bf16[512,384]{1,0:T(8,128)(2,1)S(1)} %get-tuple-element.173.k_ref, bf16[512,384]{1,0:T(8,128)(2,1)S(1)} %get-tuple-element.162.v_ref, ...), custom_call_target="tpu_custom_call" | custom-call | flops 1280000000 | bytes 3840000 | tf_op jit(solution)/shard_map/pallas_call | solution.py:57
  72.8 2.4 %shard_map.260 = (bf16[512,384]{1,0:T(8,128)(2,1)S(1)}, f32[3,640,128]{2,1,0:T(8,128)S(1)}, bf16[64,384]{1,0:T(8,128)(2,1)S(1)}, f32[3,64,8,128]{3,2,1,0:T(8,128)S(1)}, f32[576,128]{1,0:T(8,128)S(1)}) custom-call(s32[2]{0:T(128)S(1)} %pad_add_fusion.place_ref, f32[512,384]{1,0:T(8,128)S(1)} %get-tuple-element.206.dk_ref, ...), custom_call_target="tpu_custom_call" | custom-call | flops 1500000000 | bytes 4500000 | tf_op jit(solution)/shard_map/pallas_call | solution.py:57
  75.1 1.3 collective-permute-start.20
  76.4 1.7 %shard_map.261 = (bf16[8,48,768]{2,1,0:T(8,128)(2,1)S(1)}, bf16[8,48,768]{2,1,0:T(8,128)(2,1)S(1)}) custom-call(s32[2]{0:T(128)S(1)} %pad_add_fusion.place_ref, bf16[512,768]{1,0:T(8,128)(2,1)S(1)} %get-tuple-element.221.refs_0_.refs_1_.normed_ref, bf16[512,768]{1,0:T(8,128)(2,1)S(1)} %get-tuple-element.221.refs_0_.refs_1_.normed_ref, ...), custom_call_target="tpu_custom_call" | custom-call | flops 1140000000 | bytes 3419999 | tf_op jit(solution)/shard_map/pallas_call | solution.py:57
  78.1 2.7 %collective-permute-start.23 = (bf16[8,48,768]{2,1,0:T(8,128)(2,1)S(1)}, bf16[8,48,768]{2,1,0:T(8,128)(2,1)S(1)}, u32[]{:S(2)}, u32[]{:S(2)}) collective-permute-start(bf16[8,48,768]{2,1,0:T(8,128)(2,1)S(1)} %get-tuple-element.238), channel_id=1, source_target_pairs={{0,2},{1,5},{2,0},{3,7},{4,6},{5,1},{6,4},{7,3},{8,10},{9,13},{10,... | collective-permute-start | bytes 1769480 | tf_op jit(solution)/shard_map/ppermute | solution.py:129
  81.5 1.2 shard_map.262
  82.7 1.1 collective-permute-start.24
  83.8 9.8 %shard_map.263 = (f32[512,384]{1,0:T(8,128)S(1)}, f32[64,384]{1,0:T(8,128)S(1)}) custom-call(f32[3,640,128]{2,1,0:T(8,128)S(1)} %get-tuple-element.215.sg_ref, bf16[512,384]{1,0:T(8,128)(2,1)S(1)} %get-tuple-element.156.k_ref, f32[576,128]{1,0:T(8,128)S(1)} %get-tuple-element.216.ahead_ref, bf16[64,384]{1,0:T(8,128)(2,1)S(1)} %copy-done.9, ...), custom_call_target="tpu_custom_call" | custom-call | flops 7049999872 | bytes 21150000 | tf_op jit(solution)/shard_map/pallas_call | solution.py:57
  93.6 2.2 %shard_map.264 = (bf16[512,384]{1,0:T(8,128)(2,1)S(1)}, bf16[520,768]{1,0:T(8,128)(2,1)S(1)}) custom-call(s32[2]{0:T(128)S(1)} %pad_add_fusion.place_ref, f32[512,384]{1,0:T(8,128)S(1)} %get-tuple-element.229.grad_ref, bf16[64,384]{1,0:T(8,128)(2,1)S(1)} %collective-permute-done.20.edge_ref, f32[512,128]{1,0:T(8,128)S(1)} %get-tuple-element.153.docc_ref, ...), custom_call_target="tpu_custom_call" | custom-call | flops 2160000000 | bytes 6480000 | tf_op jit(solution)/shard_map/pallas_call | solution.py:57
  95.9 0.9 shard_map.265
  96.8 0.7 shard_map.266
  97.6 1.0 collective-permute-start.25
  98.6 3.1 %collective-permute-done.22.got_ref = bf16[8,48,1536]{2,1,0:T(8,128)(2,1)S(1)} collective-permute-done((bf16[8,48,1536]{2,1,0:T(8,128)(2,1)S(1)}, bf16[8,48,1536]{2,1,0:T(8,128)(2,1)S(1)}, u32[]{:S(2)}, u32[]{:S(2)}) %collective-permute-start.22) | collective-permute-done | bytes 1179680 | tf_op jit(solution)/shard_map/ppermute | solution.py:129
  101.7 4.2 %collective-permute-start.30 = (bf16[2,48,1920]{2,1,0:T(8,128)(2,1)S(1)}, bf16[2,48,1920]{2,1,0:T(8,128)(2,1)S(1)}, u32[]{:S(2)}, u32[]{:S(2)}) collective-permute-start(bf16[2,48,1920]{2,1,0:T(8,128)(2,1)S(1)} %get-tuple-element.259), channel_id=1, source_target_pairs={{0,8},{1,17},{2,10},{3,19},{4,12},{5,21},{6,14},{7,23},{8,0},{9,25... | collective-permute-start | bytes 1105928 | tf_op jit(solution)/shard_map/ppermute | solution.py:129
  105.9 1.0 shard_map.267
  106.9 3.5 %collective-permute-start.27 = (bf16[4,48,1536]{2,1,0:T(8,128)(2,1)S(1)}, bf16[4,48,1536]{2,1,0:T(8,128)(2,1)S(1)}, u32[]{:S(2)}, u32[]{:S(2)}) collective-permute-start(bf16[4,48,1536]{2,1,0:T(8,128)(2,1)S(1)} %get-tuple-element.254), channel_id=1, source_target_pairs={{0,2},{1,5},{2,0},{3,7},{4,6},{5,1},{6,4},{7,3},{8,10},{9,13},{10,... | collective-permute-start | bytes 1769480 | tf_op jit(solution)/shard_map/ppermute | solution.py:129
  110.4 1.2 shard_map.268
  111.7 2.5 %shard_map.269 = bf16[512,384]{1,0:T(8,128)(2,1)} custom-call(s32[2]{0:T(128)S(1)} %pad_add_fusion.place_ref, bf16[520,768]{1,0:T(8,128)(2,1)S(1)} %get-tuple-element.231.part_ref, bf16[520,768]{1,0:T(8,128)(2,1)S(1)} %collective-permute-done.21.got_ref, bf16[512,384]{1,0:T(8,128)(2,1)S(1)} %copy-done, bf16[512,384]{1,0:T(8,128)(2,1)S(1)} %collective-permute-done.other_ref, ...), custom_call_target="tpu_custom_call" | custom-call | flops 890000000 | bytes 2670000 | tf_op jit(solution)/shard_map/pallas_call | solution.py:57
  114.8 2.1 %collective-permute-start.26 = (bf16[2,48,768]{2,1,0:T(8,128)(2,1)S(1)}, bf16[2,48,768]{2,1,0:T(8,128)(2,1)S(1)}, u32[]{:S(2)}, u32[]{:S(2)}) collective-permute-start(bf16[2,48,768]{2,1,0:T(8,128)(2,1)S(1)} %get-tuple-element.253), channel_id=1, source_target_pairs={{0,8},{1,17},{2,10},{3,19},{4,12},{5,21},{6,14},{7,23},{8,0},{9,25... | collective-permute-start | bytes 442376 | tf_op jit(solution)/shard_map/ppermute | solution.py:129
  116.9 1.3 collective-permute-done.27.got_ref
  118.2 0.8 shard_map.271
  119.0 0.7 shard_map.272
  119.8 1.9 %collective-permute-start.28 = (bf16[2,48,1536]{2,1,0:T(8,128)(2,1)S(1)}, bf16[2,48,1536]{2,1,0:T(8,128)(2,1)S(1)}, u32[]{:S(2)}, u32[]{:S(2)}) collective-permute-start(bf16[2,48,1536]{2,1,0:T(8,128)(2,1)S(1)} %get-tuple-element.257), channel_id=1, source_target_pairs={{0,4},{1,3},{2,6},{3,1},{4,0},{5,7},{6,2},{7,5},{8,12},{9,11},{10,... | collective-permute-start | bytes 884744 | tf_op jit(solution)/shard_map/ppermute | solution.py:129
  122.6 1.9 %collective-permute-start.32 = (bf16[264,384]{1,0:T(8,128)(2,1)S(1)}, bf16[264,384]{1,0:T(8,128)(2,1)S(1)}, u32[]{:S(2)}, u32[]{:S(2)}) collective-permute-start(bf16[264,384]{1,0:T(8,128)(2,1)S(1)} %get-tuple-element.269), channel_id=1, source_target_pairs={{0,4},{1,3},{2,6},{3,1},{4,0},{5,7},{6,2},{7,5},{8,12},{9,11},{10,... | collective-permute-start | bytes 608264 | tf_op jit(solution)/shard_map/ppermute | solution.py:129
  124.6 2.0 %collective-permute-done.28.got_ref = bf16[2,48,1536]{2,1,0:T(8,128)(2,1)S(1)} collective-permute-done((bf16[2,48,1536]{2,1,0:T(8,128)(2,1)S(1)}, bf16[2,48,1536]{2,1,0:T(8,128)(2,1)S(1)}, u32[]{:S(2)}, u32[]{:S(2)}) %collective-permute-start.28) | collective-permute-done | bytes 294944 | tf_op jit(solution)/shard_map/ppermute | solution.py:129
  126.6 0.7 shard_map.274
  127.9 0.9 collective-permute-done.32.got_ref
  129.4 2.1 %collective-permute-start.33 = (bf16[168,384]{1,0:T(8,128)(2,1)S(1)}, bf16[168,384]{1,0:T(8,128)(2,1)S(1)}, u32[]{:S(2)}, u32[]{:S(2)}) collective-permute-start(bf16[168,384]{1,0:T(8,128)(2,1)S(1)} %get-tuple-element.272), channel_id=1, source_target_pairs={{0,8},{1,17},{2,10},{3,19},{4,12},{5,21},{6,14},{7,23},{8,0},{9,25... | collective-permute-start | bytes 387080 | tf_op jit(solution)/shard_map/ppermute | solution.py:129
  131.5 2.8 %collective-permute-start.36 = (bf16[1,48,1536]{2,1,0:T(8,128)(2,1)S(1)}, bf16[1,48,1536]{2,1,0:T(8,128)(2,1)S(1)}, u32[]{:S(2)}, u32[]{:S(2)}) collective-permute-start(bf16[1,48,1536]{2,1,0:T(8,128)(2,1)S(1)} %get-tuple-element.279), channel_id=1, source_target_pairs={{0,16},{1,9},{2,18},{3,11},{4,20},{5,13},{6,22},{7,15},{8,24},{9,1... | collective-permute-start | bytes 442376 | tf_op jit(solution)/shard_map/ppermute | solution.py:129
  134.3 1.3 shard_map.277
  135.6 2.6 %collective-permute-done.33.got_ref = bf16[168,384]{1,0:T(8,128)(2,1)S(1)} collective-permute-done((bf16[168,384]{1,0:T(8,128)(2,1)S(1)}, bf16[168,384]{1,0:T(8,128)(2,1)S(1)}, u32[]{:S(2)}, u32[]{:S(2)}) %collective-permute-start.33) | collective-permute-done | bytes 129056 | tf_op jit(solution)/shard_map/ppermute | solution.py:129
  138.8 1.2 collective-permute-start.35
  140.1 1.7 %collective-permute-start.31 = (bf16[1,48,768]{2,1,0:T(8,128)(2,1)S(1)}, bf16[1,48,768]{2,1,0:T(8,128)(2,1)S(1)}, u32[]{:S(2)}, u32[]{:S(2)}) collective-permute-start(bf16[1,48,768]{2,1,0:T(8,128)(2,1)S(1)} %get-tuple-element.268), channel_id=1, source_target_pairs={{0,16},{1,9},{2,18},{3,11},{4,20},{5,13},{6,22},{7,15},{8,24},{9,1... | collective-permute-start | bytes 221192 | tf_op jit(solution)/shard_map/ppermute | solution.py:129
  141.8 1.3 shard_map.279
  143.1 2.2 %collective-permute-done.35.got_ref = bf16[120,384]{1,0:T(8,128)(2,1)S(1)} collective-permute-done((bf16[120,384]{1,0:T(8,128)(2,1)S(1)}, bf16[120,384]{1,0:T(8,128)(2,1)S(1)}, u32[]{:S(2)}, u32[]{:S(2)}) %collective-permute-start.35) | collective-permute-done | bytes 92192 | tf_op jit(solution)/shard_map/ppermute | solution.py:129
  145.3 1.2 shard_map.280
  146.6 1.2 collective-permute-done.37.other_ref
  147.7 1.2 shard_map.281
  (75 shorter events, 8.8 us)
Async XLA Ops:
  0.6 4.3 %collective-permute-start = (bf16[512,384]{1,0:T(8,128)(2,1)}, bf16[512,384]{1,0:T(8,128)(2,1)S(1)}, u32[]{:S(2)}, u32[]{:S(2)}) collective-permute-start(bf16[512,384]{1,0:T(8,128)(2,1)} %own_ref.9), channel_id=1, source_target_pairs={{0,1},{1,0},{2,3},{3,2},{4,5},{5,4},{6,7},{7,6},{8,9},{9,8},{10,11... | collective-permute-start | bytes 1179656 | tf_op jit(solution)/shard_map/ppermute | solution.py:102
  1.2 20.5 %collective-permute-start.2 = (bf16[512,384]{1,0:T(8,128)(2,1)}, bf16[512,384]{1,0:T(8,128)(2,1)S(1)}, u32[]{:S(2)}, u32[]{:S(2)}) collective-permute-start(bf16[512,384]{1,0:T(8,128)(2,1)} %own_ref.6), channel_id=1, source_target_pairs={{0,1},{1,0},{2,3},{3,2},{4,5},{5,4},{6,7},{7,6},{8,9},{9,8},{10,11... | collective-permute-start | bytes 1179656 | tf_op jit(solution)/shard_map/ppermute | solution.py:102
  1.2 36.3 %collective-permute-start.10 = (bf16[768,384]{1,0:T(8,128)(2,1)}, bf16[768,384]{1,0:T(8,128)(2,1)S(1)}, u32[]{:S(2)}, u32[]{:S(2)}) collective-permute-start(bf16[768,384]{1,0:T(8,128)(2,1)} %out_w_ref.1), channel_id=1, source_target_pairs={{0,1},{1,0},{2,3},{3,2},{4,5},{5,4},{6,7},{7,6},{8,9},{9,8},{10,11... | collective-permute-start | bytes 1769480 | tf_op jit(solution)/shard_map/ppermute | solution.py:102
  1.7 3.2 %copy-start = (bf16[512,384]{1,0:T(8,128)(2,1)S(1)}, bf16[512,384]{1,0:T(8,128)(2,1)}, u32[]{:S(2)}) copy-start(bf16[512,384]{1,0:T(8,128)(2,1)} %own_ref.9) | copy-start | bytes 1179652
  1.7 3.2 %copy-start.1 = (f32[768]{0:T(1024)S(1)}, f32[768]{0:T(1024)}, u32[]{:S(2)}) copy-start(f32[768]{0:T(1024)} %gain_ref.7) | copy-start | bytes 9220
  1.8 3.3 %copy-start.5 = (bf16[768,384]{1,0:T(8,128)(2,1)S(1)}, bf16[768,384]{1,0:T(8,128)(2,1)}, u32[]{:S(2)}) copy-start(bf16[768,384]{1,0:T(8,128)(2,1)} %wq_ref.3) | copy-start | bytes 1769476
  1.8 3.3 %copy-start.6 = (bf16[768,384]{1,0:T(8,128)(2,1)S(1)}, bf16[768,384]{1,0:T(8,128)(2,1)}, u32[]{:S(2)}) copy-start(bf16[768,384]{1,0:T(8,128)(2,1)} %wk_ref.3) | copy-start | bytes 1769476
  1.8 3.3 %copy-start.7 = (bf16[768,384]{1,0:T(8,128)(2,1)S(1)}, bf16[768,384]{1,0:T(8,128)(2,1)}, u32[]{:S(2)}) copy-start(bf16[768,384]{1,0:T(8,128)(2,1)} %wv_ref.3) | copy-start | bytes 1769476
  1.8 3.3 %copy-start.10 = (f32[768]{0:T(1024)S(1)}, f32[768]{0:T(1024)}, u32[]{:S(2)}) copy-start(f32[768]{0:T(1024)} %bias_ref.2) | copy-start | bytes 9220
  5.0 6.8 %copy-start.9 = (bf16[64,384]{1,0:T(8,128)(2,1)S(1)}, bf16[64,384]{1,0:T(8,128)(2,1)}, u32[]{:S(2)}) copy-start(bf16[64,384]{1,0:T(8,128)(2,1)} %taps_ref.7) | copy-start | bytes 147460
  7.4 9.6 %collective-permute-start.1 = (bf16[64,384]{1,0:T(8,128)(2,1)S(1)}, bf16[64,384]{1,0:T(8,128)(2,1)S(1)}, u32[]{:S(2)}, u32[]{:S(2)}) collective-permute-start(bf16[64,384]{1,0:T(8,128)(2,1)S(1)} %get-tuple-element.159), channel_id=1, source_target_pairs={{0,2},{2,4},{4,6},{6,8},{8,10},{10,12},{12,14},{14,16},{16,18},{18... | collective-permute-start | bytes 147464 | tf_op jit(solution)/shard_map/ppermute | solution.py:107
  17.0 4.7 %copy-start.3 = (bf16[768,1536]{1,0:T(8,128)(2,1)S(1)}, bf16[768,1536]{1,0:T(8,128)(2,1)}, u32[]{:S(2)}) copy-start(bf16[768,1536]{1,0:T(8,128)(2,1)} %down_ref.3) | copy-start | bytes 7077892
  17.0 4.7 %copy-start.8 = (bf16[512,384]{1,0:T(8,128)(2,1)S(1)}, bf16[512,384]{1,0:T(8,128)(2,1)}, u32[]{:S(2)}) copy-start(bf16[512,384]{1,0:T(8,128)(2,1)} %own_ref.6) | copy-start | bytes 1179652
  18.1 6.0 %collective-permute-start.5 = (bf16[80,384]{1,0:T(8,128)(2,1)S(1)}, bf16[80,384]{1,0:T(8,128)(2,1)S(1)}, u32[]{:S(2)}, u32[]{:S(2)}) collective-permute-start(bf16[80,384]{1,0:T(8,128)(2,1)S(1)} %get-tuple-element.167.refs_0_), channel_id=1, source_target_pairs={{0,6},{2,0},{4,2},{6,4},{8,14},{10,8},{12,10},{14,12},{16,22},{18,... | collective-permute-start | bytes 184328 | tf_op jit(solution)/shard_map/ppermute | solution.py:89
  20.6 4.9 %collective-permute-start.4 = (bf16[80,384]{1,0:T(8,128)(2,1)S(1)}, bf16[80,384]{1,0:T(8,128)(2,1)S(1)}, u32[]{:S(2)}, u32[]{:S(2)}) collective-permute-start(bf16[80,384]{1,0:T(8,128)(2,1)S(1)} %get-tuple-element.167.refs_0_), channel_id=1, source_target_pairs={{0,4},{2,6},{4,0},{6,2},{8,12},{10,14},{12,8},{14,10},{16,20},{18,... | collective-permute-start | bytes 184328 | tf_op jit(solution)/shard_map/ppermute | solution.py:89
  21.1 5.1 %collective-permute-start.3 = (bf16[80,384]{1,0:T(8,128)(2,1)S(1)}, bf16[80,384]{1,0:T(8,128)(2,1)S(1)}, u32[]{:S(2)}, u32[]{:S(2)}) collective-permute-start(bf16[80,384]{1,0:T(8,128)(2,1)S(1)} %get-tuple-element.167.refs_0_), channel_id=1, source_target_pairs={{0,2},{2,4},{4,6},{6,0},{8,10},{10,12},{12,14},{14,8},{16,18},{18,... | collective-permute-start | bytes 184328 | tf_op jit(solution)/shard_map/ppermute | solution.py:89
  26.9 7.6 %collective-permute-start.8 = (bf16[80,384]{1,0:T(8,128)(2,1)S(1)}, bf16[80,384]{1,0:T(8,128)(2,1)S(1)}, u32[]{:S(2)}, u32[]{:S(2)}) collective-permute-start(bf16[80,384]{1,0:T(8,128)(2,1)S(1)} %get-tuple-element.178.refs_0_), channel_id=1, source_target_pairs={{0,24},{2,26},{4,28},{6,30},{8,0},{10,2},{12,4},{14,6},{16,8},{18,... | collective-permute-start | bytes 184328 | tf_op jit(solution)/shard_map/ppermute | solution.py:89
  30.5 5.1 %collective-permute-start.7 = (bf16[80,384]{1,0:T(8,128)(2,1)S(1)}, bf16[80,384]{1,0:T(8,128)(2,1)S(1)}, u32[]{:S(2)}, u32[]{:S(2)}) collective-permute-start(bf16[80,384]{1,0:T(8,128)(2,1)S(1)} %get-tuple-element.178.refs_0_), channel_id=1, source_target_pairs={{0,16},{2,18},{4,20},{6,22},{8,24},{10,26},{12,28},{14,30},{16,0},... | collective-permute-start | bytes 184328 | tf_op jit(solution)/shard_map/ppermute | solution.py:89
  30.5 6.0 %collective-permute-start.6 = (bf16[80,384]{1,0:T(8,128)(2,1)S(1)}, bf16[80,384]{1,0:T(8,128)(2,1)S(1)}, u32[]{:S(2)}, u32[]{:S(2)}) collective-permute-start(bf16[80,384]{1,0:T(8,128)(2,1)S(1)} %get-tuple-element.178.refs_0_), channel_id=1, source_target_pairs={{0,8},{2,10},{4,12},{6,14},{8,16},{10,18},{12,20},{14,22},{16,24},... | collective-permute-start | bytes 184328 | tf_op jit(solution)/shard_map/ppermute | solution.py:89
  36.6 2.6 %copy-start.2 = (bf16[768,1536]{1,0:T(8,128)(2,1)S(1)}, bf16[768,1536]{1,0:T(8,128)(2,1)}, u32[]{:S(2)}) copy-start(bf16[768,1536]{1,0:T(8,128)(2,1)} %up_ref.1) | copy-start | bytes 7077892
  36.6 2.6 %copy-start.4 = (bf16[768,384]{1,0:T(8,128)(2,1)S(1)}, bf16[768,384]{1,0:T(8,128)(2,1)}, u32[]{:S(2)}) copy-start(bf16[768,384]{1,0:T(8,128)(2,1)} %out_w_ref.1) | copy-start | bytes 1769476
  36.6 2.6 %copy-start.11 = (f32[768]{0:T(1024)S(1)}, f32[768]{0:T(1024)}, u32[]{:S(2)}) copy-start(f32[768]{0:T(1024)} %bias_ref.3) | copy-start | bytes 9220
  36.6 2.6 %copy-start.12 = (f32[768]{0:T(1024)S(1)}, f32[768]{0:T(1024)}, u32[]{:S(2)}) copy-start(f32[768]{0:T(1024)} %gain_ref.6) | copy-start | bytes 9220
  37.4 1.8 %collective-permute-start.9 = (bf16[512,384]{1,0:T(8,128)(2,1)S(1)}, bf16[512,384]{1,0:T(8,128)(2,1)S(1)}, u32[]{:S(2)}, u32[]{:S(2)}) collective-permute-start(bf16[512,384]{1,0:T(8,128)(2,1)S(1)} %get-tuple-element.184.mix_own_ref.refs_3_), channel_id=1, source_target_pairs={{0,1},{1,0},{2,3},{3,2},{4,5},{5,4},{6,7},{7,6},{8,9},{9,8},{10,11... | collective-permute-start | bytes 1179656 | tf_op jit(solution)/shard_map/ppermute | solution.py:102
  46.5 4.3 %collective-permute-start.11 = (bf16[512,768]{1,0:T(8,128)(2,1)S(1)}, bf16[512,768]{1,0:T(8,128)(2,1)S(1)}, u32[]{:S(2)}, u32[]{:S(2)}) collective-permute-start(bf16[512,768]{1,0:T(8,128)(2,1)S(1)} %get-tuple-element.186.part_ref), channel_id=1, source_target_pairs={{0,1},{1,0},{2,3},{3,2},{4,5},{5,4},{6,7},{7,6},{8,9},{9,8},{10,11... | collective-permute-start | bytes 2359304 | tf_op jit(solution)/shard_map/ppermute | solution.py:102
  50.4 7.0 %collective-permute-start.12 = (bf16[512,384]{1,0:T(8,128)(2,1)S(1)}, bf16[512,384]{1,0:T(8,128)(2,1)S(1)}, u32[]{:S(2)}, u32[]{:S(2)}) collective-permute-start(bf16[512,384]{1,0:T(8,128)(2,1)S(1)} %get-tuple-element.196), channel_id=1, source_target_pairs={{0,1},{1,0},{2,3},{3,2},{4,5},{5,4},{6,7},{7,6},{8,9},{9,8},{10,11... | collective-permute-start | bytes 1179656 | tf_op jit(solution)/shard_map/ppermute | solution.py:102
  53.4 7.4 %collective-permute-start.15 = (bf16[80,384]{1,0:T(8,128)(2,1)S(1)}, bf16[80,384]{1,0:T(8,128)(2,1)S(1)}, u32[]{:S(2)}, u32[]{:S(2)}) collective-permute-start(bf16[80,384]{1,0:T(8,128)(2,1)S(1)} %get-tuple-element.198.refs_0_), channel_id=1, source_target_pairs={{0,2},{2,4},{4,6},{6,0},{8,10},{10,12},{12,14},{14,8},{16,18},{18,... | collective-permute-start | bytes 184328 | tf_op jit(solution)/shard_map/ppermute | solution.py:89
  53.5 7.4 %collective-permute-start.14 = (bf16[80,384]{1,0:T(8,128)(2,1)S(1)}, bf16[80,384]{1,0:T(8,128)(2,1)S(1)}, u32[]{:S(2)}, u32[]{:S(2)}) collective-permute-start(bf16[80,384]{1,0:T(8,128)(2,1)S(1)} %get-tuple-element.198.refs_0_), channel_id=1, source_target_pairs={{0,4},{2,6},{4,0},{6,2},{8,12},{10,14},{12,8},{14,10},{16,20},{18,... | collective-permute-start | bytes 184328 | tf_op jit(solution)/shard_map/ppermute | solution.py:89
  54.5 6.4 %collective-permute-start.13 = (bf16[80,384]{1,0:T(8,128)(2,1)S(1)}, bf16[80,384]{1,0:T(8,128)(2,1)S(1)}, u32[]{:S(2)}, u32[]{:S(2)}) collective-permute-start(bf16[80,384]{1,0:T(8,128)(2,1)S(1)} %get-tuple-element.198.refs_0_), channel_id=1, source_target_pairs={{0,6},{2,0},{4,2},{6,4},{8,14},{10,8},{12,10},{14,12},{16,22},{18,... | collective-permute-start | bytes 184328 | tf_op jit(solution)/shard_map/ppermute | solution.py:89
  61.5 20.0 %collective-permute-start.19 = (bf16[8,48,1920]{2,1,0:T(8,128)(2,1)S(1)}, bf16[8,48,1920]{2,1,0:T(8,128)(2,1)S(1)}, u32[]{:S(2)}, u32[]{:S(2)}) collective-permute-start(bf16[8,48,1920]{2,1,0:T(8,128)(2,1)S(1)} %get-tuple-element.220), channel_id=1, source_target_pairs={{0,2},{1,5},{2,0},{3,7},{4,6},{5,1},{6,4},{7,3},{8,10},{9,13},{10,... | collective-permute-start | bytes 4423688 | tf_op jit(solution)/shard_map/ppermute | solution.py:129
  62.8 10.0 %collective-permute-start.18 = (bf16[80,384]{1,0:T(8,128)(2,1)S(1)}, bf16[80,384]{1,0:T(8,128)(2,1)S(1)}, u32[]{:S(2)}, u32[]{:S(2)}) collective-permute-start(bf16[80,384]{1,0:T(8,128)(2,1)S(1)} %get-tuple-element.209.refs_0_), channel_id=1, source_target_pairs={{0,8},{2,10},{4,12},{6,14},{8,16},{10,18},{12,20},{14,22},{16,24},... | collective-permute-start | bytes 184328 | tf_op jit(solution)/shard_map/ppermute | solution.py:89
  63.3 9.5 %collective-permute-start.17 = (bf16[80,384]{1,0:T(8,128)(2,1)S(1)}, bf16[80,384]{1,0:T(8,128)(2,1)S(1)}, u32[]{:S(2)}, u32[]{:S(2)}) collective-permute-start(bf16[80,384]{1,0:T(8,128)(2,1)S(1)} %get-tuple-element.209.refs_0_), channel_id=1, source_target_pairs={{0,16},{2,18},{4,20},{6,22},{8,24},{10,26},{12,28},{14,30},{16,0},... | collective-permute-start | bytes 184328 | tf_op jit(solution)/shard_map/ppermute | solution.py:89
  64.3 8.5 %collective-permute-start.16 = (bf16[80,384]{1,0:T(8,128)(2,1)S(1)}, bf16[80,384]{1,0:T(8,128)(2,1)S(1)}, u32[]{:S(2)}, u32[]{:S(2)}) collective-permute-start(bf16[80,384]{1,0:T(8,128)(2,1)S(1)} %get-tuple-element.209.refs_0_), channel_id=1, source_target_pairs={{0,24},{2,26},{4,28},{6,30},{8,0},{10,2},{12,4},{14,6},{16,8},{18,... | collective-permute-start | bytes 184328 | tf_op jit(solution)/shard_map/ppermute | solution.py:89
  72.3 29.3 %collective-permute-start.22 = (bf16[8,48,1536]{2,1,0:T(8,128)(2,1)S(1)}, bf16[8,48,1536]{2,1,0:T(8,128)(2,1)S(1)}, u32[]{:S(2)}, u32[]{:S(2)}) collective-permute-start(bf16[8,48,1536]{2,1,0:T(8,128)(2,1)S(1)} %get-tuple-element.237), channel_id=1, source_target_pairs={{0,8},{1,17},{2,10},{3,19},{4,12},{5,21},{6,14},{7,23},{8,0},{9,25... | collective-permute-start | bytes 3538952 | tf_op jit(solution)/shard_map/ppermute | solution.py:129
  75.1 18.5 %collective-permute-start.20 = (bf16[64,384]{1,0:T(8,128)(2,1)S(1)}, bf16[64,384]{1,0:T(8,128)(2,1)S(1)}, u32[]{:S(2)}, u32[]{:S(2)}) collective-permute-start(bf16[64,384]{1,0:T(8,128)(2,1)S(1)} %get-tuple-element.223), channel_id=1, source_target_pairs={{2,0},{4,2},{6,4},{8,6},{10,8},{12,10},{14,12},{16,14},{18,16},{20... | collective-permute-start | bytes 147464 | tf_op jit(solution)/shard_map/ppermute | solution.py:107
  78.1 18.7 %collective-permute-start.23 = (bf16[8,48,768]{2,1,0:T(8,128)(2,1)S(1)}, bf16[8,48,768]{2,1,0:T(8,128)(2,1)S(1)}, u32[]{:S(2)}, u32[]{:S(2)}) collective-permute-start(bf16[8,48,768]{2,1,0:T(8,128)(2,1)S(1)} %get-tuple-element.238), channel_id=1, source_target_pairs={{0,2},{1,5},{2,0},{3,7},{4,6},{5,1},{6,4},{7,3},{8,10},{9,13},{10,... | collective-permute-start | bytes 1769480 | tf_op jit(solution)/shard_map/ppermute | solution.py:129
  82.7 13.3 %collective-permute-start.24 = (bf16[4,48,1920]{2,1,0:T(8,128)(2,1)S(1)}, bf16[4,48,1920]{2,1,0:T(8,128)(2,1)S(1)}, u32[]{:S(2)}, u32[]{:S(2)}) collective-permute-start(bf16[4,48,1920]{2,1,0:T(8,128)(2,1)S(1)} %get-tuple-element.239), channel_id=1, source_target_pairs={{0,4},{1,3},{2,6},{3,1},{4,0},{5,7},{6,2},{7,5},{8,12},{9,11},{10,... | collective-permute-start | bytes 2211848 | tf_op jit(solution)/shard_map/ppermute | solution.py:129
  95.9 14.5 %collective-permute-start.21 = (bf16[520,768]{1,0:T(8,128)(2,1)S(1)}, bf16[520,768]{1,0:T(8,128)(2,1)S(1)}, u32[]{:S(2)}, u32[]{:S(2)}) collective-permute-start(bf16[520,768]{1,0:T(8,128)(2,1)S(1)} %get-tuple-element.231.part_ref), channel_id=1, source_target_pairs={{0,1},{1,0},{2,3},{3,2},{4,5},{5,4},{6,7},{7,6},{8,9},{9,8},{10,11... | collective-permute-start | bytes 2396168 | tf_op jit(solution)/shard_map/ppermute | solution.py:102
  97.6 16.6 %collective-permute-start.25 = (bf16[4,48,768]{2,1,0:T(8,128)(2,1)S(1)}, bf16[4,48,768]{2,1,0:T(8,128)(2,1)S(1)}, u32[]{:S(2)}, u32[]{:S(2)}) collective-permute-start(bf16[4,48,768]{2,1,0:T(8,128)(2,1)S(1)} %get-tuple-element.250), channel_id=1, source_target_pairs={{0,4},{1,3},{2,6},{3,1},{4,0},{5,7},{6,2},{7,5},{8,12},{9,11},{10,... | collective-permute-start | bytes 884744 | tf_op jit(solution)/shard_map/ppermute | solution.py:129
  101.7 17.3 %collective-permute-start.30 = (bf16[2,48,1920]{2,1,0:T(8,128)(2,1)S(1)}, bf16[2,48,1920]{2,1,0:T(8,128)(2,1)S(1)}, u32[]{:S(2)}, u32[]{:S(2)}) collective-permute-start(bf16[2,48,1920]{2,1,0:T(8,128)(2,1)S(1)} %get-tuple-element.259), channel_id=1, source_target_pairs={{0,8},{1,17},{2,10},{3,19},{4,12},{5,21},{6,14},{7,23},{8,0},{9,25... | collective-permute-start | bytes 1105928 | tf_op jit(solution)/shard_map/ppermute | solution.py:129
  106.9 11.3 %collective-permute-start.27 = (bf16[4,48,1536]{2,1,0:T(8,128)(2,1)S(1)}, bf16[4,48,1536]{2,1,0:T(8,128)(2,1)S(1)}, u32[]{:S(2)}, u32[]{:S(2)}) collective-permute-start(bf16[4,48,1536]{2,1,0:T(8,128)(2,1)S(1)} %get-tuple-element.254), channel_id=1, source_target_pairs={{0,2},{1,5},{2,0},{3,7},{4,6},{5,1},{6,4},{7,3},{8,10},{9,13},{10,... | collective-permute-start | bytes 1769480 | tf_op jit(solution)/shard_map/ppermute | solution.py:129
  111.6 10.4 %collective-permute-start.29 = (bf16[456,384]{1,0:T(8,128)(2,1)S(1)}, bf16[456,384]{1,0:T(8,128)(2,1)S(1)}, u32[]{:S(2)}, u32[]{:S(2)}) collective-permute-start(bf16[456,384]{1,0:T(8,128)(2,1)S(1)} %get-tuple-element.258), channel_id=1, source_target_pairs={{0,2},{1,5},{2,0},{3,7},{4,6},{5,1},{6,4},{7,3},{8,10},{9,13},{10,... | collective-permute-start | bytes 1050632 | tf_op jit(solution)/shard_map/ppermute | solution.py:129
  114.8 12.5 %collective-permute-start.26 = (bf16[2,48,768]{2,1,0:T(8,128)(2,1)S(1)}, bf16[2,48,768]{2,1,0:T(8,128)(2,1)S(1)}, u32[]{:S(2)}, u32[]{:S(2)}) collective-permute-start(bf16[2,48,768]{2,1,0:T(8,128)(2,1)S(1)} %get-tuple-element.253), channel_id=1, source_target_pairs={{0,8},{1,17},{2,10},{3,19},{4,12},{5,21},{6,14},{7,23},{8,0},{9,25... | collective-permute-start | bytes 442376 | tf_op jit(solution)/shard_map/ppermute | solution.py:129
  119.7 14.6 %collective-permute-start.34 = (bf16[1,48,1920]{2,1,0:T(8,128)(2,1)S(1)}, bf16[1,48,1920]{2,1,0:T(8,128)(2,1)S(1)}, u32[]{:S(2)}, u32[]{:S(2)}) collective-permute-start(bf16[1,48,1920]{2,1,0:T(8,128)(2,1)S(1)} %get-tuple-element.273), channel_id=1, source_target_pairs={{0,16},{1,9},{2,18},{3,11},{4,20},{5,13},{6,22},{7,15},{8,24},{9,1... | collective-permute-start | bytes 552968 | tf_op jit(solution)/shard_map/ppermute | solution.py:129
  119.8 6.8 %collective-permute-start.28 = (bf16[2,48,1536]{2,1,0:T(8,128)(2,1)S(1)}, bf16[2,48,1536]{2,1,0:T(8,128)(2,1)S(1)}, u32[]{:S(2)}, u32[]{:S(2)}) collective-permute-start(bf16[2,48,1536]{2,1,0:T(8,128)(2,1)S(1)} %get-tuple-element.257), channel_id=1, source_target_pairs={{0,4},{1,3},{2,6},{3,1},{4,0},{5,7},{6,2},{7,5},{8,12},{9,11},{10,... | collective-permute-start | bytes 884744 | tf_op jit(solution)/shard_map/ppermute | solution.py:129
  122.6 6.1 %collective-permute-start.32 = (bf16[264,384]{1,0:T(8,128)(2,1)S(1)}, bf16[264,384]{1,0:T(8,128)(2,1)S(1)}, u32[]{:S(2)}, u32[]{:S(2)}) collective-permute-start(bf16[264,384]{1,0:T(8,128)(2,1)S(1)} %get-tuple-element.269), channel_id=1, source_target_pairs={{0,4},{1,3},{2,6},{3,1},{4,0},{5,7},{6,2},{7,5},{8,12},{9,11},{10,... | collective-permute-start | bytes 608264 | tf_op jit(solution)/shard_map/ppermute | solution.py:129
  129.4 8.9 %collective-permute-start.33 = (bf16[168,384]{1,0:T(8,128)(2,1)S(1)}, bf16[168,384]{1,0:T(8,128)(2,1)S(1)}, u32[]{:S(2)}, u32[]{:S(2)}) collective-permute-start(bf16[168,384]{1,0:T(8,128)(2,1)S(1)} %get-tuple-element.272), channel_id=1, source_target_pairs={{0,8},{1,17},{2,10},{3,19},{4,12},{5,21},{6,14},{7,23},{8,0},{9,25... | collective-permute-start | bytes 387080 | tf_op jit(solution)/shard_map/ppermute | solution.py:129
  131.5 10.3 %collective-permute-start.36 = (bf16[1,48,1536]{2,1,0:T(8,128)(2,1)S(1)}, bf16[1,48,1536]{2,1,0:T(8,128)(2,1)S(1)}, u32[]{:S(2)}, u32[]{:S(2)}) collective-permute-start(bf16[1,48,1536]{2,1,0:T(8,128)(2,1)S(1)} %get-tuple-element.279), channel_id=1, source_target_pairs={{0,16},{1,9},{2,18},{3,11},{4,20},{5,13},{6,22},{7,15},{8,24},{9,1... | collective-permute-start | bytes 442376 | tf_op jit(solution)/shard_map/ppermute | solution.py:129
  138.8 6.5 %collective-permute-start.35 = (bf16[120,384]{1,0:T(8,128)(2,1)S(1)}, bf16[120,384]{1,0:T(8,128)(2,1)S(1)}, u32[]{:S(2)}, u32[]{:S(2)}) collective-permute-start(bf16[120,384]{1,0:T(8,128)(2,1)S(1)} %get-tuple-element.278), channel_id=1, source_target_pairs={{0,16},{1,9},{2,18},{3,11},{4,20},{5,13},{6,22},{7,15},{8,24},{9,1... | collective-permute-start | bytes 276488 | tf_op jit(solution)/shard_map/ppermute | solution.py:129
  140.1 6.5 %collective-permute-start.31 = (bf16[1,48,768]{2,1,0:T(8,128)(2,1)S(1)}, bf16[1,48,768]{2,1,0:T(8,128)(2,1)S(1)}, u32[]{:S(2)}, u32[]{:S(2)}) collective-permute-start(bf16[1,48,768]{2,1,0:T(8,128)(2,1)S(1)} %get-tuple-element.268), channel_id=1, source_target_pairs={{0,16},{1,9},{2,18},{3,11},{4,20},{5,13},{6,22},{7,15},{8,24},{9,1... | collective-permute-start | bytes 221192 | tf_op jit(solution)/shard_map/ppermute | solution.py:129
  146.6 1.2 collective-permute-start.37

commit v6 on v5

--- a/solution.py
+++ b/solution.py
@@ -633,16 +633,16 @@
 
     def group(a, acc):
         acc = list(acc)
-        for b in range(16):
-            j = a * 16 + b
+        for b in range(32):
+            j = a * 32 + b
             keep = ahead > j.astype(F32)
             for l in range(count):
-                u = jnp.where(keep, sg[l, pl.ds(s0 + a * 16 + b, SPAN), :], 0.0)
+                u = jnp.where(keep, sg[l, pl.ds(s0 + a * 32 + b, SPAN), :], 0.0)
                 acc[l] = acc[l] + u * taps[l, pl.ds(j, 1), :]
                 sums[l, j] += jnp.sum((held[l] * u).reshape(SPAN // 8, 8, LANES), axis=0)
         return tuple(acc)
 
-    return lax.fori_loop(0, STEP // 16, group, tuple(jnp.zeros((SPAN, LANES), F32) for _ in range(count)))
+    return lax.fori_loop(0, STEP // 32, group, tuple(jnp.zeros((SPAN, LANES), F32) for _ in range(count)))
 
 
 def reach(docr_ref, docc_ref, ahead_ref):

time: 149 us -> 149 us (level)
  transfers between devices with their start and end apart: 38 -> 38, of which waited for: 14 -> 14; matrix products, arithmetic and copies ran while one was open for 0% -> 0% of each run, Pallas kernels for 45% -> 44%
where the time goes in v6:
time: 149 us
  Pallas kernels  75.3 us (51%)
  starting transfers between devices  52 us (35%)
  waiting for transfers between devices  20.4 us (14%)
    pallas_call x36, Pallas kernels, run(): pl.pallas_call(body, out_shape=outs, grid=grid, in_specs=[FEW] * scalars...  75.3 us
    ppermute x16, starting transfers between devices, mirrored(): return lax.ppermute(array, ('seq', 'head'), pairs)  28.2 us
    ppermute x12, starting transfers between devices, turned(): return lax.ppermute(array, 'seq', pairs)  16.3 us
    ppermute x16, waiting for transfers between devices, mirrored(): return lax.ppermute(array, ('seq', 'head'), pairs)  13.3 us
    ppermute x2, starting transfers between devices, passed_along(): lax.ppermute(array, 'seq', [(i, i + by) for i in range(count) if 0 <= i +...  5.76 us
    ppermute x12, waiting for transfers between devices, turned(): return lax.ppermute(array, 'seq', pairs)  4.16 us
  transfers between devices with their start and end apart: 38, of which 14 were waited for; matrix products, arithmetic and copies ran while one was open for 0% of the time, Pallas kernels for 44%

profile of v6, /device:TPU:0, one launch (start us, length us, event | category | flops | bytes accessed | tf_op | source)
XLA Modules:
  0.0 149.0 jit_solution(8222902407560312381)
XLA Ops:
  1.8 3.2 %shard_map.246 = (f32[24,512]{1,0:T(8,128)S(1)}, f32[1536,128]{1,0:T(8,128)S(1)}, f32[8,512]{1,0:T(8,128)S(1)}, f32[512,128]{1,0:T(8,128)S(1)}, f32[512,128]{1,0...) custom-call(s32[512]{0:T(512)} %starts_ref.1, ...), custom_call_target="tpu_custom_call" | custom-call | flops 2700000000 | bytes 8100000 | tf_op jit(solution)/shard_map/pallas_call | solution.py:57
  5.1 2.3 %shard_map.247 = (bf16[512,768]{1,0:T(8,128)(2,1)S(1)}, bf16[512,384]{1,0:T(8,128)(2,1)S(1)}, bf16[512,384]{1,0:T(8,128)(2,1)S(1)}, bf16[512,384]{1,0:T(8,128)(2,1)S(1)}, bf16[64,384]{1,0:T(8,128)(2,1)S(1)}) custom-call(s32[2]{0:T(128)S(1)} %pad_add_fusion.place_ref, bf16[512,384]{1,0:T(8,128)(2,1)S(1)} %copy-done, ...), custom_call_target="tpu_custom_call" | custom-call | flops 3000000000 | bytes 9000000 | tf_op jit(solution)/shard_map/pallas_call | solution.py:57
  7.4 4.5 %collective-permute-start.1 = (bf16[64,384]{1,0:T(8,128)(2,1)S(1)}, bf16[64,384]{1,0:T(8,128)(2,1)S(1)}, u32[]{:S(2)}, u32[]{:S(2)}) collective-permute-start(bf16[64,384]{1,0:T(8,128)(2,1)S(1)} %get-tuple-element.159), channel_id=1, source_target_pairs={{0,2},{2,4},{4,6},{6,8},{8,10},{10,12},{12,14},{14,16},{16,18},{18... | collective-permute-start | bytes 147464 | tf_op jit(solution)/shard_map/ppermute | solution.py:107
  11.9 5.1 %shard_map.248.part_ref = bf16[512,384]{1,0:T(8,128)(2,1)S(1)} custom-call(bf16[512,384]{1,0:T(8,128)(2,1)S(1)} %get-tuple-element.156.k_ref, bf16[64,384]{1,0:T(8,128)(2,1)S(1)} %copy-done.9, f32[512,128]{1,0:T(8,128)S(1)} %get-tuple-element.157.dist_ref, f32[512,384]{1,0:T(8,128)S(1)} %get-tuple-element.158.beta_ref), custom_call_target="tpu_custom_call" | custom-call | flops 5400000000 | bytes 16200000 | tf_op jit(solution)/shard_map/pallas_call | solution.py:57
  17.0 1.1 shard_map.249
  18.1 2.5 %collective-permute-start.5 = (bf16[80,384]{1,0:T(8,128)(2,1)S(1)}, bf16[80,384]{1,0:T(8,128)(2,1)S(1)}, u32[]{:S(2)}, u32[]{:S(2)}) collective-permute-start(bf16[80,384]{1,0:T(8,128)(2,1)S(1)} %get-tuple-element.167.refs_0_), channel_id=1, source_target_pairs={{0,6},{2,0},{4,2},{6,4},{8,14},{10,8},{12,10},{14,12},{16,22},{18,... | collective-permute-start | bytes 184328 | tf_op jit(solution)/shard_map/ppermute | solution.py:89
  21.7 2.4 %shard_map.250 = (bf16[512,1536]{1,0:T(8,128)(2,1)S(1)}, bf16[512,768]{1,0:T(8,128)(2,1)S(1)}) custom-call(s32[2]{0:T(128)S(1)} %pad_add_fusion.place_ref, bf16[512,384]{1,0:T(8,128)(2,1)S(1)} %copy-done.8, bf16[512,384]{1,0:T(8,128)(2,1)S(1)} %collective-permute-done.2.other_ref, bf16[768,1536]{1,0:T(8,128)(2,1)S(1)} %copy-done.3), custom_call_target="tpu_custom_call" | custom-call | flops 2500000000 | bytes 7500000 | tf_op jit(solution)/shard_map/pallas_call | solution.py:57
  24.1 1.3 collective-permute-done.4.refs_2_
  25.5 0.7 collective-permute-done.3.refs_1_
  26.9 3.7 %collective-permute-start.8 = (bf16[80,384]{1,0:T(8,128)(2,1)S(1)}, bf16[80,384]{1,0:T(8,128)(2,1)S(1)}, u32[]{:S(2)}, u32[]{:S(2)}) collective-permute-start(bf16[80,384]{1,0:T(8,128)(2,1)S(1)} %get-tuple-element.178.refs_0_), channel_id=1, source_target_pairs={{0,24},{2,26},{4,28},{6,30},{8,0},{10,2},{12,4},{14,6},{16,8},{18,... | collective-permute-start | bytes 184328 | tf_op jit(solution)/shard_map/ppermute | solution.py:89
  30.5 1.0 collective-permute-start.6
  31.5 2.9 %shard_map.252.inside_ref = f32[512,384]{1,0:T(8,128)S(1)} custom-call(bf16[512,384]{1,0:T(8,128)(2,1)S(1)} %get-tuple-element.203.q_ref, bf16[512,384]{1,0:T(8,128)(2,1)S(1)} %get-tuple-element.173.k_ref, bf16[512,384]{1,0:T(8,128)(2,1)S(1)} %get-tuple-element.162.v_ref, f32[24,512]{1,0:T(8,128)S(1)} %get-tuple-element.174.lamr_ref, ...), custom_call_target="tpu_custom_call" | custom-call | flops 3500000000 | bytes 10500000 | tf_op jit(solution)/shard_map/pallas_call | solution.py:57
  34.5 1.1 collective-permute-done.7.refs_2_
  35.7 0.9 collective-permute-done.6.refs_1_
  36.6 0.8 shard_map.253
  37.5 1.7 %collective-permute-done.9.mix_other_ref = bf16[512,384]{1,0:T(8,128)(2,1)S(1)} collective-permute-done((bf16[512,384]{1,0:T(8,128)(2,1)S(1)}, bf16[512,384]{1,0:T(8,128)(2,1)S(1)}, u32[]{:S(2)}, u32[]{:S(2)}) %collective-permute-start.9) | collective-permute-done | bytes 393248 | tf_op jit(solution)/shard_map/ppermute | solution.py:102
  39.2 7.2 %shard_map.254 = (f32[512,768]{1,0:T(8,128)S(1)}, bf16[512,768]{1,0:T(8,128)(2,1)S(1)}, bf16[512,1536]{1,0:T(8,128)(2,1)S(1)}, bf16[512,1536]{1,0:T(8,128)(2,1)S(1)}, bf16[512,768]{1,0:T(8,128)(2,1)S(1)}) custom-call(s32[2]{0:T(128)S(1)} %pad_add_fusion.place_ref, bf16[512,384]{1,0:T(8,128)(2,1)S(1)} %copy-done, ...), custom_call_target="tpu_custom_call" | custom-call | flops 10800000000 | bytes 32400000 | tf_op jit(solution)/shard_map/pallas_call | solution.py:57
  46.6 3.7 %shard_map.255 = (bf16[8,48,1536]{2,1,0:T(8,128)(2,1)S(1)}, bf16[8,48,1536]{2,1,0:T(8,128)(2,1)S(1)}, f32[512,384]{1,0:T(8,128)S(1)}, bf16[512,384]{1,0:T(8,128)(2,1)S(1)}) custom-call(s32[2]{0:T(128)S(1)} %pad_add_fusion.place_ref, bf16[512,768]{1,0:T(8,128)(2,1)S(1)} %get-tuple-element.187.grad_ref, bf16[512,1536]{1,0:T(8,128)(2,1)S(1)} %get-tuple-element.188.hidden_ref, ...), custom_call_target="tpu_custom_call" | custom-call | flops 2460000000 | bytes 7380000 | tf_op jit(solution)/shard_map/pallas_call | solution.py:57
  50.8 2.6 %shard_map.256 = (f32[512,384]{1,0:T(8,128)S(1)}, bf16[512,768]{1,0:T(8,128)(2,1)S(1)}, bf16[512,384]{1,0:T(8,128)(2,1)S(1)}, f32[8,768]{1,0:T(8,128)S(1)}, bf16[80,384]{1,0:T(8,128)(2,1)S(1)}) custom-call(s32[2]{0:T(128)S(1)} %pad_add_fusion.place_ref, bf16[512,768]{1,0:T(8,128)(2,1)S(1)} %get-tuple-element.186.part_ref, ...), custom_call_target="tpu_custom_call" | custom-call | flops 2340000000 | bytes 7020000 | tf_op jit(solution)/shard_map/pallas_call | solution.py:57
  53.5 1.0 collective-permute-start.14
  54.5 2.8 %collective-permute-start.13 = (bf16[80,384]{1,0:T(8,128)(2,1)S(1)}, bf16[80,384]{1,0:T(8,128)(2,1)S(1)}, u32[]{:S(2)}, u32[]{:S(2)}) collective-permute-start(bf16[80,384]{1,0:T(8,128)(2,1)S(1)} %get-tuple-element.198.refs_0_), channel_id=1, source_target_pairs={{0,6},{2,0},{4,2},{6,4},{8,14},{10,8},{12,10},{14,12},{16,22},{18,... | collective-permute-start | bytes 184328 | tf_op jit(solution)/shard_map/ppermute | solution.py:89
  57.3 3.5 %shard_map.257 = (bf16[8,48,1920]{2,1,0:T(8,128)(2,1)S(1)}, bf16[8,48,1920]{2,1,0:T(8,128)(2,1)S(1)}, bf16[512,384]{1,0:T(8,128)(2,1)}) custom-call(s32[2]{0:T(128)S(1)} %pad_add_fusion.place_ref, bf16[512,768]{1,0:T(8,128)(2,1)S(1)} %get-tuple-element.193.refs_0_, bf16[512,768]{1,0:T(8,128)(2,1)S(1)} %get-tuple-element.194.refs_1_, ...), custom_call_target="tpu_custom_call" | custom-call | flops 1920000000 | bytes 5760000 | tf_op jit(solution)/shard_map/pallas_call | solution.py:57
  61.5 1.3 collective-permute-start.19
  63.3 1.0 collective-permute-start.17
  64.3 2.6 %collective-permute-start.16 = (bf16[80,384]{1,0:T(8,128)(2,1)S(1)}, bf16[80,384]{1,0:T(8,128)(2,1)S(1)}, u32[]{:S(2)}, u32[]{:S(2)}) collective-permute-start(bf16[80,384]{1,0:T(8,128)(2,1)S(1)} %get-tuple-element.209.refs_0_), channel_id=1, source_target_pairs={{0,24},{2,26},{4,28},{6,30},{8,0},{10,2},{12,4},{14,6},{16,8},{18,... | collective-permute-start | bytes 184328 | tf_op jit(solution)/shard_map/ppermute | solution.py:89
  66.9 5.5 %shard_map.259 = (bf16[512,384]{1,0:T(8,128)(2,1)S(1)}, f32[512,384]{1,0:T(8,128)S(1)}, f32[512,384]{1,0:T(8,128)S(1)}) custom-call(bf16[512,384]{1,0:T(8,128)(2,1)S(1)} %get-tuple-element.203.q_ref, bf16[512,384]{1,0:T(8,128)(2,1)S(1)} %get-tuple-element.173.k_ref, bf16[512,384]{1,0:T(8,128)(2,1)S(1)} %get-tuple-element.162.v_ref, ...), custom_call_target="tpu_custom_call" | custom-call | flops 1280000000 | bytes 3840000 | tf_op jit(solution)/shard_map/pallas_call | solution.py:57
  72.8 2.3 %shard_map.260 = (bf16[512,384]{1,0:T(8,128)(2,1)S(1)}, f32[3,640,128]{2,1,0:T(8,128)S(1)}, bf16[64,384]{1,0:T(8,128)(2,1)S(1)}, f32[3,64,8,128]{3,2,1,0:T(8,128)S(1)}, f32[576,128]{1,0:T(8,128)S(1)}) custom-call(s32[2]{0:T(128)S(1)} %pad_add_fusion.place_ref, f32[512,384]{1,0:T(8,128)S(1)} %get-tuple-element.206.dk_ref, ...), custom_call_target="tpu_custom_call" | custom-call | flops 1500000000 | bytes 4500000 | tf_op jit(solution)/shard_map/pallas_call | solution.py:57
  75.1 1.3 collective-permute-start.20
  76.4 1.7 %shard_map.261 = (bf16[8,48,768]{2,1,0:T(8,128)(2,1)S(1)}, bf16[8,48,768]{2,1,0:T(8,128)(2,1)S(1)}) custom-call(s32[2]{0:T(128)S(1)} %pad_add_fusion.place_ref, bf16[512,768]{1,0:T(8,128)(2,1)S(1)} %get-tuple-element.221.refs_0_.refs_1_.normed_ref, bf16[512,768]{1,0:T(8,128)(2,1)S(1)} %get-tuple-element.221.refs_0_.refs_1_.normed_ref, ...), custom_call_target="tpu_custom_call" | custom-call | flops 1140000000 | bytes 3419999 | tf_op jit(solution)/shard_map/pallas_call | solution.py:57
  78.1 2.7 %collective-permute-start.23 = (bf16[8,48,768]{2,1,0:T(8,128)(2,1)S(1)}, bf16[8,48,768]{2,1,0:T(8,128)(2,1)S(1)}, u32[]{:S(2)}, u32[]{:S(2)}) collective-permute-start(bf16[8,48,768]{2,1,0:T(8,128)(2,1)S(1)} %get-tuple-element.238), channel_id=1, source_target_pairs={{0,2},{1,5},{2,0},{3,7},{4,6},{5,1},{6,4},{7,3},{8,10},{9,13},{10,... | collective-permute-start | bytes 1769480 | tf_op jit(solution)/shard_map/ppermute | solution.py:129
  80.8 0.7 collective-permute-done.19.got_ref
  81.5 1.2 shard_map.262
  82.7 1.1 collective-permute-start.24
  83.8 9.6 %shard_map.263 = (f32[512,384]{1,0:T(8,128)S(1)}, f32[64,384]{1,0:T(8,128)S(1)}) custom-call(f32[3,640,128]{2,1,0:T(8,128)S(1)} %get-tuple-element.215.sg_ref, bf16[512,384]{1,0:T(8,128)(2,1)S(1)} %get-tuple-element.156.k_ref, f32[576,128]{1,0:T(8,128)S(1)} %get-tuple-element.216.ahead_ref, bf16[64,384]{1,0:T(8,128)(2,1)S(1)} %copy-done.9, ...), custom_call_target="tpu_custom_call" | custom-call | flops 7049999872 | bytes 21150000 | tf_op jit(solution)/shard_map/pallas_call | solution.py:57
  93.4 2.2 %shard_map.264 = (bf16[512,384]{1,0:T(8,128)(2,1)S(1)}, bf16[520,768]{1,0:T(8,128)(2,1)S(1)}) custom-call(s32[2]{0:T(128)S(1)} %pad_add_fusion.place_ref, f32[512,384]{1,0:T(8,128)S(1)} %get-tuple-element.229.grad_ref, bf16[64,384]{1,0:T(8,128)(2,1)S(1)} %collective-permute-done.20.edge_ref, f32[512,128]{1,0:T(8,128)S(1)} %get-tuple-element.153.docc_ref, ...), custom_call_target="tpu_custom_call" | custom-call | flops 2160000000 | bytes 6480000 | tf_op jit(solution)/shard_map/pallas_call | solution.py:57
  95.8 0.9 shard_map.265
  96.7 0.7 shard_map.266
  97.4 1.0 collective-permute-start.25
  98.4 3.3 %collective-permute-done.22.got_ref = bf16[8,48,1536]{2,1,0:T(8,128)(2,1)S(1)} collective-permute-done((bf16[8,48,1536]{2,1,0:T(8,128)(2,1)S(1)}, bf16[8,48,1536]{2,1,0:T(8,128)(2,1)S(1)}, u32[]{:S(2)}, u32[]{:S(2)}) %collective-permute-start.22) | collective-permute-done | bytes 1179680 | tf_op jit(solution)/shard_map/ppermute | solution.py:129
  101.7 4.2 %collective-permute-start.30 = (bf16[2,48,1920]{2,1,0:T(8,128)(2,1)S(1)}, bf16[2,48,1920]{2,1,0:T(8,128)(2,1)S(1)}, u32[]{:S(2)}, u32[]{:S(2)}) collective-permute-start(bf16[2,48,1920]{2,1,0:T(8,128)(2,1)S(1)} %get-tuple-element.259), channel_id=1, source_target_pairs={{0,8},{1,17},{2,10},{3,19},{4,12},{5,21},{6,14},{7,23},{8,0},{9,25... | collective-permute-start | bytes 1105928 | tf_op jit(solution)/shard_map/ppermute | solution.py:129
  105.9 1.0 shard_map.267
  106.9 3.5 %collective-permute-start.27 = (bf16[4,48,1536]{2,1,0:T(8,128)(2,1)S(1)}, bf16[4,48,1536]{2,1,0:T(8,128)(2,1)S(1)}, u32[]{:S(2)}, u32[]{:S(2)}) collective-permute-start(bf16[4,48,1536]{2,1,0:T(8,128)(2,1)S(1)} %get-tuple-element.254), channel_id=1, source_target_pairs={{0,2},{1,5},{2,0},{3,7},{4,6},{5,1},{6,4},{7,3},{8,10},{9,13},{10,... | collective-permute-start | bytes 1769480 | tf_op jit(solution)/shard_map/ppermute | solution.py:129
  110.4 1.2 shard_map.268
  111.7 2.5 %shard_map.269 = bf16[512,384]{1,0:T(8,128)(2,1)} custom-call(s32[2]{0:T(128)S(1)} %pad_add_fusion.place_ref, bf16[520,768]{1,0:T(8,128)(2,1)S(1)} %get-tuple-element.231.part_ref, bf16[520,768]{1,0:T(8,128)(2,1)S(1)} %collective-permute-done.21.got_ref, bf16[512,384]{1,0:T(8,128)(2,1)S(1)} %copy-done, bf16[512,384]{1,0:T(8,128)(2,1)S(1)} %collective-permute-done.other_ref, ...), custom_call_target="tpu_custom_call" | custom-call | flops 890000000 | bytes 2670000 | tf_op jit(solution)/shard_map/pallas_call | solution.py:57
  114.8 2.1 %collective-permute-start.26 = (bf16[2,48,768]{2,1,0:T(8,128)(2,1)S(1)}, bf16[2,48,768]{2,1,0:T(8,128)(2,1)S(1)}, u32[]{:S(2)}, u32[]{:S(2)}) collective-permute-start(bf16[2,48,768]{2,1,0:T(8,128)(2,1)S(1)} %get-tuple-element.253), channel_id=1, source_target_pairs={{0,8},{1,17},{2,10},{3,19},{4,12},{5,21},{6,14},{7,23},{8,0},{9,25... | collective-permute-start | bytes 442376 | tf_op jit(solution)/shard_map/ppermute | solution.py:129
  116.9 1.3 collective-permute-done.27.got_ref
  118.2 0.8 shard_map.271
  119.0 0.7 shard_map.272
  119.8 1.9 %collective-permute-start.28 = (bf16[2,48,1536]{2,1,0:T(8,128)(2,1)S(1)}, bf16[2,48,1536]{2,1,0:T(8,128)(2,1)S(1)}, u32[]{:S(2)}, u32[]{:S(2)}) collective-permute-start(bf16[2,48,1536]{2,1,0:T(8,128)(2,1)S(1)} %get-tuple-element.257), channel_id=1, source_target_pairs={{0,4},{1,3},{2,6},{3,1},{4,0},{5,7},{6,2},{7,5},{8,12},{9,11},{10,... | collective-permute-start | bytes 884744 | tf_op jit(solution)/shard_map/ppermute | solution.py:129
  122.6 1.9 %collective-permute-start.32 = (bf16[264,384]{1,0:T(8,128)(2,1)S(1)}, bf16[264,384]{1,0:T(8,128)(2,1)S(1)}, u32[]{:S(2)}, u32[]{:S(2)}) collective-permute-start(bf16[264,384]{1,0:T(8,128)(2,1)S(1)} %get-tuple-element.269), channel_id=1, source_target_pairs={{0,4},{1,3},{2,6},{3,1},{4,0},{5,7},{6,2},{7,5},{8,12},{9,11},{10,... | collective-permute-start | bytes 608264 | tf_op jit(solution)/shard_map/ppermute | solution.py:129
  124.6 2.0 %collective-permute-done.28.got_ref = bf16[2,48,1536]{2,1,0:T(8,128)(2,1)S(1)} collective-permute-done((bf16[2,48,1536]{2,1,0:T(8,128)(2,1)S(1)}, bf16[2,48,1536]{2,1,0:T(8,128)(2,1)S(1)}, u32[]{:S(2)}, u32[]{:S(2)}) %collective-permute-start.28) | collective-permute-done | bytes 294944 | tf_op jit(solution)/shard_map/ppermute | solution.py:129
  126.6 0.7 shard_map.274
  127.9 0.9 collective-permute-done.32.got_ref
  129.4 2.1 %collective-permute-start.33 = (bf16[168,384]{1,0:T(8,128)(2,1)S(1)}, bf16[168,384]{1,0:T(8,128)(2,1)S(1)}, u32[]{:S(2)}, u32[]{:S(2)}) collective-permute-start(bf16[168,384]{1,0:T(8,128)(2,1)S(1)} %get-tuple-element.272), channel_id=1, source_target_pairs={{0,8},{1,17},{2,10},{3,19},{4,12},{5,21},{6,14},{7,23},{8,0},{9,25... | collective-permute-start | bytes 387080 | tf_op jit(solution)/shard_map/ppermute | solution.py:129
  131.5 2.8 %collective-permute-start.36 = (bf16[1,48,1536]{2,1,0:T(8,128)(2,1)S(1)}, bf16[1,48,1536]{2,1,0:T(8,128)(2,1)S(1)}, u32[]{:S(2)}, u32[]{:S(2)}) collective-permute-start(bf16[1,48,1536]{2,1,0:T(8,128)(2,1)S(1)} %get-tuple-element.279), channel_id=1, source_target_pairs={{0,16},{1,9},{2,18},{3,11},{4,20},{5,13},{6,22},{7,15},{8,24},{9,1... | collective-permute-start | bytes 442376 | tf_op jit(solution)/shard_map/ppermute | solution.py:129
  134.3 1.3 shard_map.277
  135.6 2.6 %collective-permute-done.33.got_ref = bf16[168,384]{1,0:T(8,128)(2,1)S(1)} collective-permute-done((bf16[168,384]{1,0:T(8,128)(2,1)S(1)}, bf16[168,384]{1,0:T(8,128)(2,1)S(1)}, u32[]{:S(2)}, u32[]{:S(2)}) %collective-permute-start.33) | collective-permute-done | bytes 129056 | tf_op jit(solution)/shard_map/ppermute | solution.py:129
  138.8 1.2 collective-permute-start.35
  140.1 1.7 %collective-permute-start.31 = (bf16[1,48,768]{2,1,0:T(8,128)(2,1)S(1)}, bf16[1,48,768]{2,1,0:T(8,128)(2,1)S(1)}, u32[]{:S(2)}, u32[]{:S(2)}) collective-permute-start(bf16[1,48,768]{2,1,0:T(8,128)(2,1)S(1)} %get-tuple-element.268), channel_id=1, source_target_pairs={{0,16},{1,9},{2,18},{3,11},{4,20},{5,13},{6,22},{7,15},{8,24},{9,1... | collective-permute-start | bytes 221192 | tf_op jit(solution)/shard_map/ppermute | solution.py:129
  141.8 1.3 shard_map.279
  143.1 2.2 %collective-permute-done.35.got_ref = bf16[120,384]{1,0:T(8,128)(2,1)S(1)} collective-permute-done((bf16[120,384]{1,0:T(8,128)(2,1)S(1)}, bf16[120,384]{1,0:T(8,128)(2,1)S(1)}, u32[]{:S(2)}, u32[]{:S(2)}) %collective-permute-start.35) | collective-permute-done | bytes 92192 | tf_op jit(solution)/shard_map/ppermute | solution.py:129
  145.3 1.2 shard_map.280
  146.6 1.2 collective-permute-done.37.other_ref
  147.7 1.2 shard_map.281
  (75 shorter events, 8.8 us)
Async XLA Ops:
  0.6 4.3 %collective-permute-start = (bf16[512,384]{1,0:T(8,128)(2,1)}, bf16[512,384]{1,0:T(8,128)(2,1)S(1)}, u32[]{:S(2)}, u32[]{:S(2)}) collective-permute-start(bf16[512,384]{1,0:T(8,128)(2,1)} %own_ref.9), channel_id=1, source_target_pairs={{0,1},{1,0},{2,3},{3,2},{4,5},{5,4},{6,7},{7,6},{8,9},{9,8},{10,11... | collective-permute-start | bytes 1179656 | tf_op jit(solution)/shard_map/ppermute | solution.py:102
  1.2 20.5 %collective-permute-start.2 = (bf16[512,384]{1,0:T(8,128)(2,1)}, bf16[512,384]{1,0:T(8,128)(2,1)S(1)}, u32[]{:S(2)}, u32[]{:S(2)}) collective-permute-start(bf16[512,384]{1,0:T(8,128)(2,1)} %own_ref.6), channel_id=1, source_target_pairs={{0,1},{1,0},{2,3},{3,2},{4,5},{5,4},{6,7},{7,6},{8,9},{9,8},{10,11... | collective-permute-start | bytes 1179656 | tf_op jit(solution)/shard_map/ppermute | solution.py:102
  1.2 36.3 %collective-permute-start.10 = (bf16[768,384]{1,0:T(8,128)(2,1)}, bf16[768,384]{1,0:T(8,128)(2,1)S(1)}, u32[]{:S(2)}, u32[]{:S(2)}) collective-permute-start(bf16[768,384]{1,0:T(8,128)(2,1)} %out_w_ref.1), channel_id=1, source_target_pairs={{0,1},{1,0},{2,3},{3,2},{4,5},{5,4},{6,7},{7,6},{8,9},{9,8},{10,11... | collective-permute-start | bytes 1769480 | tf_op jit(solution)/shard_map/ppermute | solution.py:102
  1.7 3.2 %copy-start = (bf16[512,384]{1,0:T(8,128)(2,1)S(1)}, bf16[512,384]{1,0:T(8,128)(2,1)}, u32[]{:S(2)}) copy-start(bf16[512,384]{1,0:T(8,128)(2,1)} %own_ref.9) | copy-start | bytes 1179652
  1.7 3.2 %copy-start.1 = (f32[768]{0:T(1024)S(1)}, f32[768]{0:T(1024)}, u32[]{:S(2)}) copy-start(f32[768]{0:T(1024)} %gain_ref.7) | copy-start | bytes 9220
  1.8 3.3 %copy-start.5 = (bf16[768,384]{1,0:T(8,128)(2,1)S(1)}, bf16[768,384]{1,0:T(8,128)(2,1)}, u32[]{:S(2)}) copy-start(bf16[768,384]{1,0:T(8,128)(2,1)} %wq_ref.3) | copy-start | bytes 1769476
  1.8 3.3 %copy-start.6 = (bf16[768,384]{1,0:T(8,128)(2,1)S(1)}, bf16[768,384]{1,0:T(8,128)(2,1)}, u32[]{:S(2)}) copy-start(bf16[768,384]{1,0:T(8,128)(2,1)} %wk_ref.3) | copy-start | bytes 1769476
  1.8 3.3 %copy-start.7 = (bf16[768,384]{1,0:T(8,128)(2,1)S(1)}, bf16[768,384]{1,0:T(8,128)(2,1)}, u32[]{:S(2)}) copy-start(bf16[768,384]{1,0:T(8,128)(2,1)} %wv_ref.3) | copy-start | bytes 1769476
  1.8 3.3 %copy-start.10 = (f32[768]{0:T(1024)S(1)}, f32[768]{0:T(1024)}, u32[]{:S(2)}) copy-start(f32[768]{0:T(1024)} %bias_ref.2) | copy-start | bytes 9220
  5.0 6.8 %copy-start.9 = (bf16[64,384]{1,0:T(8,128)(2,1)S(1)}, bf16[64,384]{1,0:T(8,128)(2,1)}, u32[]{:S(2)}) copy-start(bf16[64,384]{1,0:T(8,128)(2,1)} %taps_ref.7) | copy-start | bytes 147460
  7.4 9.6 %collective-permute-start.1 = (bf16[64,384]{1,0:T(8,128)(2,1)S(1)}, bf16[64,384]{1,0:T(8,128)(2,1)S(1)}, u32[]{:S(2)}, u32[]{:S(2)}) collective-permute-start(bf16[64,384]{1,0:T(8,128)(2,1)S(1)} %get-tuple-element.159), channel_id=1, source_target_pairs={{0,2},{2,4},{4,6},{6,8},{8,10},{10,12},{12,14},{14,16},{16,18},{18... | collective-permute-start | bytes 147464 | tf_op jit(solution)/shard_map/ppermute | solution.py:107
  17.0 4.7 %copy-start.3 = (bf16[768,1536]{1,0:T(8,128)(2,1)S(1)}, bf16[768,1536]{1,0:T(8,128)(2,1)}, u32[]{:S(2)}) copy-start(bf16[768,1536]{1,0:T(8,128)(2,1)} %down_ref.3) | copy-start | bytes 7077892
  17.0 4.7 %copy-start.8 = (bf16[512,384]{1,0:T(8,128)(2,1)S(1)}, bf16[512,384]{1,0:T(8,128)(2,1)}, u32[]{:S(2)}) copy-start(bf16[512,384]{1,0:T(8,128)(2,1)} %own_ref.6) | copy-start | bytes 1179652
  18.1 6.0 %collective-permute-start.5 = (bf16[80,384]{1,0:T(8,128)(2,1)S(1)}, bf16[80,384]{1,0:T(8,128)(2,1)S(1)}, u32[]{:S(2)}, u32[]{:S(2)}) collective-permute-start(bf16[80,384]{1,0:T(8,128)(2,1)S(1)} %get-tuple-element.167.refs_0_), channel_id=1, source_target_pairs={{0,6},{2,0},{4,2},{6,4},{8,14},{10,8},{12,10},{14,12},{16,22},{18,... | collective-permute-start | bytes 184328 | tf_op jit(solution)/shard_map/ppermute | solution.py:89
  20.6 4.9 %collective-permute-start.4 = (bf16[80,384]{1,0:T(8,128)(2,1)S(1)}, bf16[80,384]{1,0:T(8,128)(2,1)S(1)}, u32[]{:S(2)}, u32[]{:S(2)}) collective-permute-start(bf16[80,384]{1,0:T(8,128)(2,1)S(1)} %get-tuple-element.167.refs_0_), channel_id=1, source_target_pairs={{0,4},{2,6},{4,0},{6,2},{8,12},{10,14},{12,8},{14,10},{16,20},{18,... | collective-permute-start | bytes 184328 | tf_op jit(solution)/shard_map/ppermute | solution.py:89
  21.1 5.1 %collective-permute-start.3 = (bf16[80,384]{1,0:T(8,128)(2,1)S(1)}, bf16[80,384]{1,0:T(8,128)(2,1)S(1)}, u32[]{:S(2)}, u32[]{:S(2)}) collective-permute-start(bf16[80,384]{1,0:T(8,128)(2,1)S(1)} %get-tuple-element.167.refs_0_), channel_id=1, source_target_pairs={{0,2},{2,4},{4,6},{6,0},{8,10},{10,12},{12,14},{14,8},{16,18},{18,... | collective-permute-start | bytes 184328 | tf_op jit(solution)/shard_map/ppermute | solution.py:89
  26.9 7.6 %collective-permute-start.8 = (bf16[80,384]{1,0:T(8,128)(2,1)S(1)}, bf16[80,384]{1,0:T(8,128)(2,1)S(1)}, u32[]{:S(2)}, u32[]{:S(2)}) collective-permute-start(bf16[80,384]{1,0:T(8,128)(2,1)S(1)} %get-tuple-element.178.refs_0_), channel_id=1, source_target_pairs={{0,24},{2,26},{4,28},{6,30},{8,0},{10,2},{12,4},{14,6},{16,8},{18,... | collective-permute-start | bytes 184328 | tf_op jit(solution)/shard_map/ppermute | solution.py:89
  30.5 5.1 %collective-permute-start.7 = (bf16[80,384]{1,0:T(8,128)(2,1)S(1)}, bf16[80,384]{1,0:T(8,128)(2,1)S(1)}, u32[]{:S(2)}, u32[]{:S(2)}) collective-permute-start(bf16[80,384]{1,0:T(8,128)(2,1)S(1)} %get-tuple-element.178.refs_0_), channel_id=1, source_target_pairs={{0,16},{2,18},{4,20},{6,22},{8,24},{10,26},{12,28},{14,30},{16,0},... | collective-permute-start | bytes 184328 | tf_op jit(solution)/shard_map/ppermute | solution.py:89
  30.5 6.0 %collective-permute-start.6 = (bf16[80,384]{1,0:T(8,128)(2,1)S(1)}, bf16[80,384]{1,0:T(8,128)(2,1)S(1)}, u32[]{:S(2)}, u32[]{:S(2)}) collective-permute-start(bf16[80,384]{1,0:T(8,128)(2,1)S(1)} %get-tuple-element.178.refs_0_), channel_id=1, source_target_pairs={{0,8},{2,10},{4,12},{6,14},{8,16},{10,18},{12,20},{14,22},{16,24},... | collective-permute-start | bytes 184328 | tf_op jit(solution)/shard_map/ppermute | solution.py:89
  36.6 2.6 %copy-start.2 = (bf16[768,1536]{1,0:T(8,128)(2,1)S(1)}, bf16[768,1536]{1,0:T(8,128)(2,1)}, u32[]{:S(2)}) copy-start(bf16[768,1536]{1,0:T(8,128)(2,1)} %up_ref.1) | copy-start | bytes 7077892
  36.6 2.6 %copy-start.4 = (bf16[768,384]{1,0:T(8,128)(2,1)S(1)}, bf16[768,384]{1,0:T(8,128)(2,1)}, u32[]{:S(2)}) copy-start(bf16[768,384]{1,0:T(8,128)(2,1)} %out_w_ref.1) | copy-start | bytes 1769476
  36.6 2.6 %copy-start.11 = (f32[768]{0:T(1024)S(1)}, f32[768]{0:T(1024)}, u32[]{:S(2)}) copy-start(f32[768]{0:T(1024)} %bias_ref.3) | copy-start | bytes 9220
  36.6 2.6 %copy-start.12 = (f32[768]{0:T(1024)S(1)}, f32[768]{0:T(1024)}, u32[]{:S(2)}) copy-start(f32[768]{0:T(1024)} %gain_ref.6) | copy-start | bytes 9220
  37.4 1.8 %collective-permute-start.9 = (bf16[512,384]{1,0:T(8,128)(2,1)S(1)}, bf16[512,384]{1,0:T(8,128)(2,1)S(1)}, u32[]{:S(2)}, u32[]{:S(2)}) collective-permute-start(bf16[512,384]{1,0:T(8,128)(2,1)S(1)} %get-tuple-element.184.mix_own_ref.refs_3_), channel_id=1, source_target_pairs={{0,1},{1,0},{2,3},{3,2},{4,5},{5,4},{6,7},{7,6},{8,9},{9,8},{10,11... | collective-permute-start | bytes 1179656 | tf_op jit(solution)/shard_map/ppermute | solution.py:102
  46.5 4.3 %collective-permute-start.11 = (bf16[512,768]{1,0:T(8,128)(2,1)S(1)}, bf16[512,768]{1,0:T(8,128)(2,1)S(1)}, u32[]{:S(2)}, u32[]{:S(2)}) collective-permute-start(bf16[512,768]{1,0:T(8,128)(2,1)S(1)} %get-tuple-element.186.part_ref), channel_id=1, source_target_pairs={{0,1},{1,0},{2,3},{3,2},{4,5},{5,4},{6,7},{7,6},{8,9},{9,8},{10,11... | collective-permute-start | bytes 2359304 | tf_op jit(solution)/shard_map/ppermute | solution.py:102
  50.4 7.0 %collective-permute-start.12 = (bf16[512,384]{1,0:T(8,128)(2,1)S(1)}, bf16[512,384]{1,0:T(8,128)(2,1)S(1)}, u32[]{:S(2)}, u32[]{:S(2)}) collective-permute-start(bf16[512,384]{1,0:T(8,128)(2,1)S(1)} %get-tuple-element.196), channel_id=1, source_target_pairs={{0,1},{1,0},{2,3},{3,2},{4,5},{5,4},{6,7},{7,6},{8,9},{9,8},{10,11... | collective-permute-start | bytes 1179656 | tf_op jit(solution)/shard_map/ppermute | solution.py:102
  53.4 7.4 %collective-permute-start.15 = (bf16[80,384]{1,0:T(8,128)(2,1)S(1)}, bf16[80,384]{1,0:T(8,128)(2,1)S(1)}, u32[]{:S(2)}, u32[]{:S(2)}) collective-permute-start(bf16[80,384]{1,0:T(8,128)(2,1)S(1)} %get-tuple-element.198.refs_0_), channel_id=1, source_target_pairs={{0,2},{2,4},{4,6},{6,0},{8,10},{10,12},{12,14},{14,8},{16,18},{18,... | collective-permute-start | bytes 184328 | tf_op jit(solution)/shard_map/ppermute | solution.py:89
  53.5 7.4 %collective-permute-start.14 = (bf16[80,384]{1,0:T(8,128)(2,1)S(1)}, bf16[80,384]{1,0:T(8,128)(2,1)S(1)}, u32[]{:S(2)}, u32[]{:S(2)}) collective-permute-start(bf16[80,384]{1,0:T(8,128)(2,1)S(1)} %get-tuple-element.198.refs_0_), channel_id=1, source_target_pairs={{0,4},{2,6},{4,0},{6,2},{8,12},{10,14},{12,8},{14,10},{16,20},{18,... | collective-permute-start | bytes 184328 | tf_op jit(solution)/shard_map/ppermute | solution.py:89
  54.5 6.4 %collective-permute-start.13 = (bf16[80,384]{1,0:T(8,128)(2,1)S(1)}, bf16[80,384]{1,0:T(8,128)(2,1)S(1)}, u32[]{:S(2)}, u32[]{:S(2)}) collective-permute-start(bf16[80,384]{1,0:T(8,128)(2,1)S(1)} %get-tuple-element.198.refs_0_), channel_id=1, source_target_pairs={{0,6},{2,0},{4,2},{6,4},{8,14},{10,8},{12,10},{14,12},{16,22},{18,... | collective-permute-start | bytes 184328 | tf_op jit(solution)/shard_map/ppermute | solution.py:89
  61.5 20.0 %collective-permute-start.19 = (bf16[8,48,1920]{2,1,0:T(8,128)(2,1)S(1)}, bf16[8,48,1920]{2,1,0:T(8,128)(2,1)S(1)}, u32[]{:S(2)}, u32[]{:S(2)}) collective-permute-start(bf16[8,48,1920]{2,1,0:T(8,128)(2,1)S(1)} %get-tuple-element.220), channel_id=1, source_target_pairs={{0,2},{1,5},{2,0},{3,7},{4,6},{5,1},{6,4},{7,3},{8,10},{9,13},{10,... | collective-permute-start | bytes 4423688 | tf_op jit(solution)/shard_map/ppermute | solution.py:129
  62.8 10.0 %collective-permute-start.18 = (bf16[80,384]{1,0:T(8,128)(2,1)S(1)}, bf16[80,384]{1,0:T(8,128)(2,1)S(1)}, u32[]{:S(2)}, u32[]{:S(2)}) collective-permute-start(bf16[80,384]{1,0:T(8,128)(2,1)S(1)} %get-tuple-element.209.refs_0_), channel_id=1, source_target_pairs={{0,8},{2,10},{4,12},{6,14},{8,16},{10,18},{12,20},{14,22},{16,24},... | collective-permute-start | bytes 184328 | tf_op jit(solution)/shard_map/ppermute | solution.py:89
  63.3 9.5 %collective-permute-start.17 = (bf16[80,384]{1,0:T(8,128)(2,1)S(1)}, bf16[80,384]{1,0:T(8,128)(2,1)S(1)}, u32[]{:S(2)}, u32[]{:S(2)}) collective-permute-start(bf16[80,384]{1,0:T(8,128)(2,1)S(1)} %get-tuple-element.209.refs_0_), channel_id=1, source_target_pairs={{0,16},{2,18},{4,20},{6,22},{8,24},{10,26},{12,28},{14,30},{16,0},... | collective-permute-start | bytes 184328 | tf_op jit(solution)/shard_map/ppermute | solution.py:89
  64.3 8.5 %collective-permute-start.16 = (bf16[80,384]{1,0:T(8,128)(2,1)S(1)}, bf16[80,384]{1,0:T(8,128)(2,1)S(1)}, u32[]{:S(2)}, u32[]{:S(2)}) collective-permute-start(bf16[80,384]{1,0:T(8,128)(2,1)S(1)} %get-tuple-element.209.refs_0_), channel_id=1, source_target_pairs={{0,24},{2,26},{4,28},{6,30},{8,0},{10,2},{12,4},{14,6},{16,8},{18,... | collective-permute-start | bytes 184328 | tf_op jit(solution)/shard_map/ppermute | solution.py:89
  72.3 29.3 %collective-permute-start.22 = (bf16[8,48,1536]{2,1,0:T(8,128)(2,1)S(1)}, bf16[8,48,1536]{2,1,0:T(8,128)(2,1)S(1)}, u32[]{:S(2)}, u32[]{:S(2)}) collective-permute-start(bf16[8,48,1536]{2,1,0:T(8,128)(2,1)S(1)} %get-tuple-element.237), channel_id=1, source_target_pairs={{0,8},{1,17},{2,10},{3,19},{4,12},{5,21},{6,14},{7,23},{8,0},{9,25... | collective-permute-start | bytes 3538952 | tf_op jit(solution)/shard_map/ppermute | solution.py:129
  75.1 18.3 %collective-permute-start.20 = (bf16[64,384]{1,0:T(8,128)(2,1)S(1)}, bf16[64,384]{1,0:T(8,128)(2,1)S(1)}, u32[]{:S(2)}, u32[]{:S(2)}) collective-permute-start(bf16[64,384]{1,0:T(8,128)(2,1)S(1)} %get-tuple-element.223), channel_id=1, source_target_pairs={{2,0},{4,2},{6,4},{8,6},{10,8},{12,10},{14,12},{16,14},{18,16},{20... | collective-permute-start | bytes 147464 | tf_op jit(solution)/shard_map/ppermute | solution.py:107
  78.1 18.6 %collective-permute-start.23 = (bf16[8,48,768]{2,1,0:T(8,128)(2,1)S(1)}, bf16[8,48,768]{2,1,0:T(8,128)(2,1)S(1)}, u32[]{:S(2)}, u32[]{:S(2)}) collective-permute-start(bf16[8,48,768]{2,1,0:T(8,128)(2,1)S(1)} %get-tuple-element.238), channel_id=1, source_target_pairs={{0,2},{1,5},{2,0},{3,7},{4,6},{5,1},{6,4},{7,3},{8,10},{9,13},{10,... | collective-permute-start | bytes 1769480 | tf_op jit(solution)/shard_map/ppermute | solution.py:129
  82.7 13.1 %collective-permute-start.24 = (bf16[4,48,1920]{2,1,0:T(8,128)(2,1)S(1)}, bf16[4,48,1920]{2,1,0:T(8,128)(2,1)S(1)}, u32[]{:S(2)}, u32[]{:S(2)}) collective-permute-start(bf16[4,48,1920]{2,1,0:T(8,128)(2,1)S(1)} %get-tuple-element.239), channel_id=1, source_target_pairs={{0,4},{1,3},{2,6},{3,1},{4,0},{5,7},{6,2},{7,5},{8,12},{9,11},{10,... | collective-permute-start | bytes 2211848 | tf_op jit(solution)/shard_map/ppermute | solution.py:129
  95.7 14.7 %collective-permute-start.21 = (bf16[520,768]{1,0:T(8,128)(2,1)S(1)}, bf16[520,768]{1,0:T(8,128)(2,1)S(1)}, u32[]{:S(2)}, u32[]{:S(2)}) collective-permute-start(bf16[520,768]{1,0:T(8,128)(2,1)S(1)} %get-tuple-element.231.part_ref), channel_id=1, source_target_pairs={{0,1},{1,0},{2,3},{3,2},{4,5},{5,4},{6,7},{7,6},{8,9},{9,8},{10,11... | collective-permute-start | bytes 2396168 | tf_op jit(solution)/shard_map/ppermute | solution.py:102
  97.4 16.8 %collective-permute-start.25 = (bf16[4,48,768]{2,1,0:T(8,128)(2,1)S(1)}, bf16[4,48,768]{2,1,0:T(8,128)(2,1)S(1)}, u32[]{:S(2)}, u32[]{:S(2)}) collective-permute-start(bf16[4,48,768]{2,1,0:T(8,128)(2,1)S(1)} %get-tuple-element.250), channel_id=1, source_target_pairs={{0,4},{1,3},{2,6},{3,1},{4,0},{5,7},{6,2},{7,5},{8,12},{9,11},{10,... | collective-permute-start | bytes 884744 | tf_op jit(solution)/shard_map/ppermute | solution.py:129
  101.7 17.3 %collective-permute-start.30 = (bf16[2,48,1920]{2,1,0:T(8,128)(2,1)S(1)}, bf16[2,48,1920]{2,1,0:T(8,128)(2,1)S(1)}, u32[]{:S(2)}, u32[]{:S(2)}) collective-permute-start(bf16[2,48,1920]{2,1,0:T(8,128)(2,1)S(1)} %get-tuple-element.259), channel_id=1, source_target_pairs={{0,8},{1,17},{2,10},{3,19},{4,12},{5,21},{6,14},{7,23},{8,0},{9,25... | collective-permute-start | bytes 1105928 | tf_op jit(solution)/shard_map/ppermute | solution.py:129
  106.9 11.3 %collective-permute-start.27 = (bf16[4,48,1536]{2,1,0:T(8,128)(2,1)S(1)}, bf16[4,48,1536]{2,1,0:T(8,128)(2,1)S(1)}, u32[]{:S(2)}, u32[]{:S(2)}) collective-permute-start(bf16[4,48,1536]{2,1,0:T(8,128)(2,1)S(1)} %get-tuple-element.254), channel_id=1, source_target_pairs={{0,2},{1,5},{2,0},{3,7},{4,6},{5,1},{6,4},{7,3},{8,10},{9,13},{10,... | collective-permute-start | bytes 1769480 | tf_op jit(solution)/shard_map/ppermute | solution.py:129
  111.6 10.4 %collective-permute-start.29 = (bf16[456,384]{1,0:T(8,128)(2,1)S(1)}, bf16[456,384]{1,0:T(8,128)(2,1)S(1)}, u32[]{:S(2)}, u32[]{:S(2)}) collective-permute-start(bf16[456,384]{1,0:T(8,128)(2,1)S(1)} %get-tuple-element.258), channel_id=1, source_target_pairs={{0,2},{1,5},{2,0},{3,7},{4,6},{5,1},{6,4},{7,3},{8,10},{9,13},{10,... | collective-permute-start | bytes 1050632 | tf_op jit(solution)/shard_map/ppermute | solution.py:129
  114.8 12.5 %collective-permute-start.26 = (bf16[2,48,768]{2,1,0:T(8,128)(2,1)S(1)}, bf16[2,48,768]{2,1,0:T(8,128)(2,1)S(1)}, u32[]{:S(2)}, u32[]{:S(2)}) collective-permute-start(bf16[2,48,768]{2,1,0:T(8,128)(2,1)S(1)} %get-tuple-element.253), channel_id=1, source_target_pairs={{0,8},{1,17},{2,10},{3,19},{4,12},{5,21},{6,14},{7,23},{8,0},{9,25... | collective-permute-start | bytes 442376 | tf_op jit(solution)/shard_map/ppermute | solution.py:129
  119.7 14.6 %collective-permute-start.34 = (bf16[1,48,1920]{2,1,0:T(8,128)(2,1)S(1)}, bf16[1,48,1920]{2,1,0:T(8,128)(2,1)S(1)}, u32[]{:S(2)}, u32[]{:S(2)}) collective-permute-start(bf16[1,48,1920]{2,1,0:T(8,128)(2,1)S(1)} %get-tuple-element.273), channel_id=1, source_target_pairs={{0,16},{1,9},{2,18},{3,11},{4,20},{5,13},{6,22},{7,15},{8,24},{9,1... | collective-permute-start | bytes 552968 | tf_op jit(solution)/shard_map/ppermute | solution.py:129
  119.8 6.8 %collective-permute-start.28 = (bf16[2,48,1536]{2,1,0:T(8,128)(2,1)S(1)}, bf16[2,48,1536]{2,1,0:T(8,128)(2,1)S(1)}, u32[]{:S(2)}, u32[]{:S(2)}) collective-permute-start(bf16[2,48,1536]{2,1,0:T(8,128)(2,1)S(1)} %get-tuple-element.257), channel_id=1, source_target_pairs={{0,4},{1,3},{2,6},{3,1},{4,0},{5,7},{6,2},{7,5},{8,12},{9,11},{10,... | collective-permute-start | bytes 884744 | tf_op jit(solution)/shard_map/ppermute | solution.py:129
  122.6 6.1 %collective-permute-start.32 = (bf16[264,384]{1,0:T(8,128)(2,1)S(1)}, bf16[264,384]{1,0:T(8,128)(2,1)S(1)}, u32[]{:S(2)}, u32[]{:S(2)}) collective-permute-start(bf16[264,384]{1,0:T(8,128)(2,1)S(1)} %get-tuple-element.269), channel_id=1, source_target_pairs={{0,4},{1,3},{2,6},{3,1},{4,0},{5,7},{6,2},{7,5},{8,12},{9,11},{10,... | collective-permute-start | bytes 608264 | tf_op jit(solution)/shard_map/ppermute | solution.py:129
  129.4 8.9 %collective-permute-start.33 = (bf16[168,384]{1,0:T(8,128)(2,1)S(1)}, bf16[168,384]{1,0:T(8,128)(2,1)S(1)}, u32[]{:S(2)}, u32[]{:S(2)}) collective-permute-start(bf16[168,384]{1,0:T(8,128)(2,1)S(1)} %get-tuple-element.272), channel_id=1, source_target_pairs={{0,8},{1,17},{2,10},{3,19},{4,12},{5,21},{6,14},{7,23},{8,0},{9,25... | collective-permute-start | bytes 387080 | tf_op jit(solution)/shard_map/ppermute | solution.py:129
  131.5 10.3 %collective-permute-start.36 = (bf16[1,48,1536]{2,1,0:T(8,128)(2,1)S(1)}, bf16[1,48,1536]{2,1,0:T(8,128)(2,1)S(1)}, u32[]{:S(2)}, u32[]{:S(2)}) collective-permute-start(bf16[1,48,1536]{2,1,0:T(8,128)(2,1)S(1)} %get-tuple-element.279), channel_id=1, source_target_pairs={{0,16},{1,9},{2,18},{3,11},{4,20},{5,13},{6,22},{7,15},{8,24},{9,1... | collective-permute-start | bytes 442376 | tf_op jit(solution)/shard_map/ppermute | solution.py:129
  138.8 6.5 %collective-permute-start.35 = (bf16[120,384]{1,0:T(8,128)(2,1)S(1)}, bf16[120,384]{1,0:T(8,128)(2,1)S(1)}, u32[]{:S(2)}, u32[]{:S(2)}) collective-permute-start(bf16[120,384]{1,0:T(8,128)(2,1)S(1)} %get-tuple-element.278), channel_id=1, source_target_pairs={{0,16},{1,9},{2,18},{3,11},{4,20},{5,13},{6,22},{7,15},{8,24},{9,1... | collective-permute-start | bytes 276488 | tf_op jit(solution)/shard_map/ppermute | solution.py:129
  140.1 6.5 %collective-permute-start.31 = (bf16[1,48,768]{2,1,0:T(8,128)(2,1)S(1)}, bf16[1,48,768]{2,1,0:T(8,128)(2,1)S(1)}, u32[]{:S(2)}, u32[]{:S(2)}) collective-permute-start(bf16[1,48,768]{2,1,0:T(8,128)(2,1)S(1)} %get-tuple-element.268), channel_id=1, source_target_pairs={{0,16},{1,9},{2,18},{3,11},{4,20},{5,13},{6,22},{7,15},{8,24},{9,1... | collective-permute-start | bytes 221192 | tf_op jit(solution)/shard_map/ppermute | solution.py:129
  146.6 1.2 collective-permute-start.37
